TPU v7x, 32 devices: a whole 2x2x4 slice. The times are simulated.
32 devices in a mesh: group: 4 (over z), seq: 2 (over x), head: 4 (over y, core).
Axes of the slice: x: 2, y: 2, z: 4, core: 2. Of those that a mesh axis runs over, the one named last changes fastest.
Arguments:
- latents: bfloat16 [256, 64], P('seq'), may hold values from -6 to 6
- noise: bfloat16 [256, 64], P('seq'), may hold values from -6 to 6
- step: int32 [1], replicated, may hold values from 50 to 950
- stream: bfloat16 [256, 5120], P('seq'), may hold values from -6 to 6
- patch_embed_weight: bfloat16 [64, 5120], replicated, may hold values from -0.75 to 0.75
- prenorm_gain_vector: float32 [5120], replicated, may hold values from 0.5 to 1.5
- query_matrix: bfloat16 [5120, 4096], P('seq', ('group', 'head')), may hold values from -0.08385255 to 0.08385255
- key_matrix: bfloat16 [5120, 4096], P('seq', ('group', 'head')), may hold values from -1.0481569 to 1.0481569
- value_matrix: bfloat16 [5120, 4096], P('seq', ('group', 'head')), may hold values from -0.078125 to 0.078125
- output_matrix: bfloat16 [4096, 5120], P(('group', 'head'), 'seq'), may hold values from -0.09375 to 0.09375
- velocity_readout_weight: bfloat16 [64, 5120], replicated, may hold values from -0.078125 to 0.078125
- adapter_query_down: bfloat16 [5120, 128], P('seq'), may hold values from -0.078125 to 0.078125
- adapter_query_up: bfloat16 [128, 4096], P(None, ('group', 'head')), may hold values from -0.5 to 0.5
- adapter_output_down: bfloat16 [4096, 128], P(('group', 'head')), may hold values from -0.09375 to 0.09375
- adapter_output_up: bfloat16 [128, 5120], replicated, may hold values from -0.5 to 0.5
Outputs:
- latent_grad: float32 [256, 64], P('seq')
All inputs are finite; a program needn't handle non-finite values. Where the computation divides by a largest or mean magnitude, that divisor is 1e-20 or more.
Results may differ from a plain program's by a relative error of at most 0.015.
Values may be sent and summed in bfloat16 or wider, within the bound.
No kernel may reach another device: no remote copies, remote signals or barrier semaphores. Data moves between devices by JAX's collectives and lax.ppermute only.
A program may use at most 64 MiB of HBM per device.

v0:
```python
import jax
import jax.numpy as jnp
from jax import lax
from jax.sharding import PartitionSpec as P

HEAD_SIZE = 128


def contract_final_axis(left, right):
    return lax.dot_general(
        left, right, (((1,), (1,)), ((), ())), preferred_element_type=jnp.float32
    )


def local(
    latents,
    noise,
    step,
    stream,
    patch_embed_weight,
    prenorm_gain_vector,
    query_matrix,
    key_matrix,
    value_matrix,
    output_matrix,
    velocity_readout_weight,
    adapter_query_down,
    adapter_query_up,
    adapter_output_down,
    adapter_output_up,
):
    tokens = latents.shape[0]
    width = query_matrix.shape[1]
    local_heads = width // HEAD_SIZE
    channels = velocity_readout_weight.shape[0]
    level = (step[0].astype(jnp.float32) + 1.0) / 1000.0
    sigma = 5.0 * level / (1.0 + 4.0 * level)
    noisy = (
        (1.0 - sigma) * latents.astype(jnp.float32) + sigma * noise.astype(jnp.float32)
    ).astype(jnp.bfloat16)
    hidden = (
        stream.astype(jnp.float32)
        + jnp.dot(noisy, patch_embed_weight, preferred_element_type=jnp.float32)
    ).astype(jnp.bfloat16)
    hidden_wide = hidden.astype(jnp.float32)
    normalized_tokens = (
        hidden_wide
        * lax.rsqrt(jnp.mean(hidden_wide * hidden_wide, axis=-1, keepdims=True) + 1e-06)
        * prenorm_gain_vector
    ).astype(jnp.bfloat16)
    pieces = (
        lax.all_gather(query_matrix, "seq", axis=0, tiled=True),
        lax.all_gather(key_matrix, "seq", axis=0, tiled=True),
        lax.all_gather(value_matrix, "seq", axis=0, tiled=True),
        lax.all_gather(adapter_query_down, "seq", axis=0, tiled=True),
    )
    base_query_rows, key_rows_whole, value_rows_whole, adapter_output_whole = tuple(
        (jnp.dot(normalized_tokens, piece, preferred_element_type=jnp.float32) for piece in pieces)
    )
    adapter_hidden_rows = adapter_output_whole.astype(jnp.bfloat16)
    logit_scale = HEAD_SIZE ** (-0.5)
    adapter_query_delta = jnp.dot(
        adapter_hidden_rows, adapter_query_up, preferred_element_type=jnp.float32
    )
    queries = (base_query_rows * logit_scale).astype(jnp.bfloat16)
    fake_query_rows = ((base_query_rows + adapter_query_delta) * logit_scale).astype(jnp.bfloat16)
    keys = key_rows_whole.astype(jnp.bfloat16)
    values = value_rows_whole.astype(jnp.bfloat16)
    both_sets = jnp.stack([queries, fake_query_rows]).reshape(2, tokens, local_heads, HEAD_SIZE)
    start_top = jnp.full((2, local_heads, tokens), -1e30, jnp.float32)
    pieces = (
        lax.all_gather(keys, "seq", axis=0, tiled=True),
        lax.all_gather(values, "seq", axis=0, tiled=True),
    )
    top = start_top
    key_rows = pieces[0].reshape(-1, local_heads, HEAD_SIZE)
    value_rows = pieces[1].reshape(-1, local_heads, HEAD_SIZE)
    scores = jnp.einsum("sthd,khd->shtk", both_sets, key_rows, preferred_element_type=jnp.float32)
    new_top = jnp.maximum(top, jnp.max(scores, axis=-1))
    weights = jnp.exp(scores - new_top[..., None])
    mass = jnp.sum(weights, axis=-1)
    added = jnp.einsum(
        "shtk,khd->sthd",
        weights.astype(jnp.bfloat16),
        value_rows,
        preferred_element_type=jnp.float32,
    )
    accum = added
    top, mass, accum = (new_top, mass, accum)
    attn = (
        (accum / mass.transpose(0, 2, 1)[..., None]).astype(jnp.bfloat16).reshape(2, tokens, width)
    )
    columns = output_matrix.shape[1]
    readout_part = lax.dynamic_slice_in_dim(
        velocity_readout_weight, lax.axis_index("seq") * columns, columns, 1
    )
    blended_heads_whole = lax.psum(contract_final_axis(output_matrix, readout_part), "seq")
    adapter_readout_delta = contract_final_axis(adapter_output_up, velocity_readout_weight).astype(
        jnp.bfloat16
    )
    mix = blended_heads_whole.astype(jnp.bfloat16)
    fake_head_blend = (
        blended_heads_whole
        + jnp.dot(adapter_output_down, adapter_readout_delta, preferred_element_type=jnp.float32)
    ).astype(jnp.bfloat16)
    real_term = jnp.dot(attn[0], mix, preferred_element_type=jnp.float32)
    fake_term = jnp.dot(attn[1], fake_head_blend, preferred_element_type=jnp.float32)
    real_sum, fake_sum = lax.psum((real_term, fake_term), ("group", "head"))
    base = contract_final_axis(hidden, velocity_readout_weight)
    noisy_wide = noisy.astype(jnp.float32)
    x0_real = noisy_wide - sigma * (base + real_sum)
    x0_fake = noisy_wide - sigma * (base + fake_sum)
    local_error = jnp.sum(jnp.abs(latents.astype(jnp.float32) - x0_real))
    weight = lax.psum(local_error, "seq") / (tokens * lax.axis_size("seq") * channels)
    return (x0_fake - x0_real) / weight


def solution(mesh):
    in_specs = (
        P("seq", None),
        P("seq", None),
        P(),
        P("seq", None),
        P(),
        P(),
        P("seq", ("group", "head")),
        P("seq", ("group", "head")),
        P("seq", ("group", "head")),
        P(("group", "head"), "seq"),
        P(),
        P("seq", None),
        P(None, ("group", "head")),
        P(("group", "head"), None),
        P(),
    )
    out_specs = P("seq", None)
    return jax.shard_map(local, mesh=mesh, in_specs=in_specs, out_specs=out_specs, check_vma=False)
```

profile of v0, /device:TPU:0, one launch (start us, length us, event | category | flops | bytes accessed | tf_op | source)
XLA Modules:
  0.0 293.7 jit_solution(10465976688104948731)
XLA Ops:
  6.5 1.3 copy-done
  7.9 2.1 convolution_bitcast_fusion.2
  10.0 0.0 all-gather.5.cloned.1.call-start
  10.0 0.7 all-gather.5.cloned.1.call-update
  10.8 0.7 all-gather.9.cloned.1.call-update
  11.5 0.5 all-gather.11.cloned.1.call-update
  12.1 0.5 all-gather.7.cloned.1.call-update
  13.4 2.2 fusion.1
  15.7 18.1 %all-reduce.4.cloned.1.call-done = f32[256,64]{0,1:T(8,128)} async-done(((f32[256,64]{0,1:T(8,128)}), f32[256,64]{0,1:T(8,128)}) %all-reduce.4.cloned.1.call-update) | async-done | bytes 65552 | tf_op jit(solution)/shard_map/psum | solution.py:97
  33.8 2.6 fusion.9
  36.4 38.0 %all-gather.5.cloned.1.call-done = bf16[5120,256]{1,0:T(8,128)(2,1)} async-done(((bf16[2560,256]{1,0:T(8,128)(2,1)}), bf16[5120,256]{1,0:T(8,128)(2,1)}) %all-gather.5.cloned.1.call-update) | async-done | bytes 2621456 | tf_op jit(solution)/shard_map/all_gather | solution.py:54
  74.4 2.3 convolution_convert_fusion.1
  76.7 4.9 %all_gather.19 = bf16[256,256]{1,0:T(8,128)(2,1)S(1)} all-gather(bf16[128,256]{1,0:T(8,128)(2,1)S(1)} %convolution_convert_fusion.1), channel_id=1, replica_groups=mesh['group'=4,'seq'=2,'head'=4] {'seq'}, dimensions={0}, use_global_device_ids=true | all-gather | bytes 196608 | tf_op jit(solution)/shard_map/all_gather | solution.py:73
  81.6 0.8 copy.24
  82.4 32.6 %all-gather.9.cloned.1.call-done = bf16[5120,256]{1,0:T(8,128)(2,1)} async-done(((bf16[2560,256]{1,0:T(8,128)(2,1)}), bf16[5120,256]{1,0:T(8,128)(2,1)}) %all-gather.9.cloned.1.call-update) | async-done | bytes 2621456 | tf_op jit(solution)/shard_map/all_gather | solution.py:52
  115.0 3.0 %multiply_convert_fusion = (bf16[128,256]{1,0:T(8,128)(2,1)S(1)}, f32[128,256]{1,0:T(8,128)}) fusion(bf16[5120,256]{1,0:T(8,128)(2,1)} %all-gather.9.cloned.1.call-done, bf16[128,5120]{1,0:T(8,128)(2,1)S(1)} %get-tuple-element.10, f32[5120]{0:T(1024)S(1)} %copy-done.12, f32[128]{0:T(128)S(1)} %add_rsqrt_fusion), kind=kOutput, calls=%fused_computation.31 | convolution fusion | flops 338231296 | bytes 4149760 | tf_op jit(solution)/shard_map/dot_general | solution.py:58
  117.9 22.7 %all-gather.11.cloned.1.call-done = bf16[5120,128]{1,0:T(8,128)(2,1)} async-done(((bf16[2560,128]{1,0:T(8,128)(2,1)}), bf16[5120,128]{1,0:T(8,128)(2,1)}) %all-gather.11.cloned.1.call-update) | async-done | bytes 1310736 | tf_op jit(solution)/shard_map/all_gather | solution.py:55
  140.6 2.0 fusion.7
  142.7 0.6 copy.17
  143.3 0.6 copy.16
  144.0 37.1 %all-gather.7.cloned.1.call-done = bf16[5120,256]{1,0:T(8,128)(2,1)} async-done(((bf16[2560,256]{1,0:T(8,128)(2,1)}), bf16[5120,256]{1,0:T(8,128)(2,1)}) %all-gather.7.cloned.1.call-update) | async-done | bytes 2621456 | tf_op jit(solution)/shard_map/all_gather | solution.py:53
  181.1 2.3 convolution_convert_fusion
  183.4 4.9 %all_gather.21 = bf16[256,256]{1,0:T(8,128)(2,1)S(1)} all-gather(bf16[128,256]{1,0:T(8,128)(2,1)S(1)} %convolution_convert_fusion), channel_id=1, replica_groups=mesh['group'=4,'seq'=2,'head'=4] {'seq'}, dimensions={0}, use_global_device_ids=true | all-gather | bytes 196608 | tf_op jit(solution)/shard_map/all_gather | solution.py:72
  188.4 1.2 fusion.37
  189.5 0.1 fusion.10
  189.7 0.2 fusion.5
  189.9 0.8 fusion.38
  190.7 0.7 fusion.25
  191.4 86.6 %all-reduce.6.cloned.1.call-done = (f32[128,64]{0,1:T(8,128)}, f32[128,64]{0,1:T(8,128)}) async-done(((f32[128,64]{0,1:T(8,128)}, f32[128,64]{0,1:T(8,128)}), (f32[128,64]{0,1:T(8,128)}, f32[128,64]{0,1:T(8,128)})) %all-reduce.6.cloned.1.call-update) | async-done | bytes 65552 | tf_op jit(solution)/shard_map/psum | solution.py:108
  278.1 2.0 fusion.22
  280.0 5.5 %psum.31 = f32[]{:T(128)} all-reduce(f32[]{:T(128)} %get-tuple-element.15), channel_id=1, replica_groups=mesh['group'=4,'seq'=2,'head'=4] {'seq'}, use_global_device_ids=true, to_apply=%region_7.0 | all-reduce | flops 1 | bytes 8 | tf_op jit(solution)/shard_map/psum | solution.py:114
  286.3 0.6 fusion.24
  (38 shorter events, 0.4 us)
Async XLA Ops:
  6.5 1.3 copy-start
  6.5 27.3 %all-reduce.4.cloned.1.call-start = ((), (), s32[]{:S(2)}) async-start(), calls=%async_computation.4 | async-start | bytes 131072 | tf_op jit(solution)/shard_map/psum | solution.py:97
  10.0 64.4 %all-gather.5.cloned.1.call-start = ((), (), s32[]{:S(2)}) async-start(), calls=%async_computation | async-start | bytes 3932160 | tf_op jit(solution)/shard_map/all_gather | solution.py:54
  10.7 104.2 %all-gather.9.cloned.1.call-start = ((), (), s32[]{:S(2)}) async-start(), calls=%async_computation.2 | async-start | bytes 3932160 | tf_op jit(solution)/shard_map/all_gather | solution.py:52
  11.5 1.9 copy-start.3
  11.5 1.9 copy-start.4
  11.5 129.1 %all-gather.11.cloned.1.call-start = ((), (), s32[]{:S(2)}) async-start(), calls=%async_computation.3 | async-start | bytes 1966080 | tf_op jit(solution)/shard_map/all_gather | solution.py:55
  12.1 169.0 %all-gather.7.cloned.1.call-start = ((), (), s32[]{:S(2)}) async-start(), calls=%async_computation.1 | async-start | bytes 3932160 | tf_op jit(solution)/shard_map/all_gather | solution.py:53
  12.7 265.4 %all-reduce.6.cloned.1.call-start = ((), (), s32[]{:S(2)}) async-start(), calls=%async_computation.5 | async-start | bytes 131072 | tf_op jit(solution)/shard_map/psum | solution.py:108
  13.4 20.4 %copy-start.1 = (bf16[64,5120]{1,0:T(8,128)(2,1)S(1)}, bf16[64,5120]{1,0:T(8,128)(2,1)}, u32[]{:S(2)}) copy-start(bf16[64,5120]{1,0:T(8,128)(2,1)} %param.25) | copy-start | bytes 1966084
  13.4 20.4 %copy-start.9 = (bf16[256,128]{1,0:T(8,128)(2,1)S(1)}, bf16[256,128]{1,0:T(8,128)(2,1)}, u32[]{:S(2)}) copy-start(bf16[256,128]{1,0:T(8,128)(2,1)} %param.28) | copy-start | bytes 196612
  15.7 58.7 %copy-start.12 = (f32[5120]{0:T(1024)S(1)}, f32[5120]{0:T(1024)}, u32[]{:S(2)}) copy-start(f32[5120]{0:T(1024)} %param.20) | copy-start | bytes 61444
  82.4 58.2 %copy-start.11 = (bf16[128,256]{1,0:T(8,128)(2,1)S(1)}, bf16[128,256]{1,0:T(8,128)(2,1)}, u32[]{:S(2)}) copy-start(bf16[128,256]{1,0:T(8,128)(2,1)} %param.27) | copy-start | bytes 196612
  188.3 1.3 copy-start.8
  188.3 1.6 copy-start.7
  189.5 1.2 copy-start.2
  189.5 88.5 %copy-start.5 = (bf16[128,64]{0,1:T(8,128)(2,1)S(1)}, bf16[128,64]{0,1:T(8,128)(2,1)}, u32[]{:S(2)}) copy-start(bf16[128,64]{0,1:T(8,128)(2,1)} %param.16) | copy-start | bytes 49156
  278.0 8.2 %copy-start.6 = (f32[128,64]{0,1:T(8,128)S(1)}, f32[128,64]{0,1:T(8,128)}, u32[]{:S(2)}) copy-start(f32[128,64]{0,1:T(8,128)} %get-tuple-element.6) | copy-start | bytes 98308
  278.0 8.2 %copy-start.10 = (f32[128,64]{0,1:T(8,128)S(1)}, f32[128,64]{0,1:T(8,128)}, u32[]{:S(2)}) copy-start(f32[128,64]{0,1:T(8,128)} %get-tuple-element.5) | copy-start | bytes 98308
Sparse Core Ops, SparseCore 0:
  10.1 23.6 all-reduce.3
  35.4 38.9 all-gather.4
  75.9 38.9 all-gather.8
  116.4 24.2 all-gather.10
  142.0 38.9 all-gather.6
  191.6 86.4 all-reduce.5
where the time goes:
time: 295 us; the launch traced here: 294 us
  waiting for transfers between devices  237 us (80%)
  matrix products  21.4 us (7%)
  blocking collectives  15.4 us (5%)
  between operations  15 us (5%)
  local copies, waits for them, and re-layouts  3.5 us (1%)
    psum x1, waiting for transfers between devices, local(): real_sum, fake_sum = lax.psum((real_term, fake_term), ('group', 'head'))  86.6 us
    all_gather x1, waiting for transfers between devices, local(): lax.all_gather(value_matrix, 'seq', axis=0, tiled=True)  38 us
    all_gather x1, waiting for transfers between devices, local(): lax.all_gather(key_matrix, 'seq', axis=0, tiled=True)  37.1 us
    all_gather x1, waiting for transfers between devices, local(): lax.all_gather(query_matrix, 'seq', axis=0, tiled=True)  32.6 us
    all_gather x1, waiting for transfers between devices, local(): lax.all_gather(adapter_query_down, 'seq', axis=0, tiled=True)  22.7 us
    psum x1, waiting for transfers between devices, local(): lax.psum(contract_final_axis(output_matrix, readout_part), 'seq')  18.1 us
    dot_general x3, matrix products, local(): jnp.dot(normalized_tokens, piece, preferred_element_type=jnp.float32)  7.54 us
  transfers between devices with their start and end apart: 6, of which 6 were waited for; matrix products, arithmetic and copies ran while one was open for 5% of the time, Pallas kernels for 0%

commit v1 on v0

v1 whole, which is shorter than its diff:
```python
import itertools

import jax
import jax.numpy as jnp
from jax import lax
from jax.sharding import PartitionSpec as P

HEAD_SIZE = 128
F32 = jnp.float32
BF16 = jnp.bfloat16


def contract_final_axis(left, right):
    return lax.dot_general(
        left, right, (((1,), (1,)), ((), ())), preferred_element_type=F32
    )


def dot(left, right):
    return jnp.dot(left, right, preferred_element_type=F32)


def noise_level(step):
    level = (step[0].astype(F32) + 1.0) / 1000.0
    return 5.0 * level / (1.0 + 4.0 * level)


def pairs(sizes, partner):
    def linear(coordinate):
        index = 0
        for value, size in zip(coordinate, sizes):
            index = index * size + value
        return index

    return [
        (linear(c), linear(partner(*c)))
        for c in itertools.product(*[range(n) for n in sizes])
    ]


def split_high_low(x):
    high = lax.reduce_precision(x, 8, 7)
    return high.astype(BF16), (x - high).astype(BF16)


def rows_of(x, index, count):
    return lax.dynamic_slice_in_dim(x, index * count, count, 0)


def columns_of(x, index, count):
    return lax.dynamic_slice_in_dim(x, index * count, count, 1)


def fold(x):
    half = x.shape[0] // 2
    return jnp.concatenate([x[:half], x[half:]], axis=1)


def unfold(x):
    half = x.shape[1] // 2
    return jnp.concatenate([x[:, :half], x[:, half:]], axis=0)


def paired_local(
    sizes,
    latents,
    noise,
    step,
    stream,
    patch_embed_weight,
    prenorm_gain_vector,
    query_matrix,
    key_matrix,
    value_matrix,
    output_matrix,
    velocity_readout_weight,
    adapter_query_down,
    adapter_query_up,
    adapter_output_down,
    adapter_output_up,
):
    groups, _, heads = sizes
    seq = lax.axis_index("seq")
    head = lax.axis_index("head")
    group = lax.axis_index("group")
    core = head % 2
    tokens, channels = latents.shape
    half_width = query_matrix.shape[0]
    quarter = half_width // 2
    columns = query_matrix.shape[1] // 2
    to_x = pairs((2,), lambda s: (s ^ 1,))
    to_core = pairs((heads,), lambda h: (h ^ 1,))
    to_y = pairs((heads,), lambda h: (h ^ 2,))
    to_xy = pairs((2, heads), lambda s, h: (s ^ 1, h ^ 2))

    sigma = noise_level(step)
    latents_wide = latents.astype(F32)
    noisy = ((1.0 - sigma) * latents_wide + sigma * noise.astype(F32)).astype(BF16)
    hidden = (stream.astype(F32) + dot(noisy, patch_embed_weight)).astype(BF16)
    hidden_wide = hidden.astype(F32)
    normed = (
        hidden_wide
        * lax.rsqrt(jnp.mean(hidden_wide * hidden_wide, axis=-1, keepdims=True) + 1e-06)
        * prenorm_gain_vector
    ).astype(BF16)

    message = jnp.concatenate(
        [columns_of(normed, (1 - seq) * 2 + core, quarter), noisy, latents], axis=1
    )
    received = lax.ppermute(message, "seq", to_x)
    near = received[:, :quarter]
    far = lax.ppermute(near, "head", to_core)
    other_noisy = received[:, quarter : quarter + channels]
    other_latents = received[:, quarter + channels :]

    own = columns_of(normed, seq, half_width)
    weights = (query_matrix, key_matrix, value_matrix)

    readout_half = columns_of(velocity_readout_weight, seq, half_width)
    mix_part = contract_final_axis(output_matrix, readout_half)

    def payload(q, k, v, lora, extra):
        def theirs(x):
            return columns_of(x, 1 - seq, columns)

        blocks = [
            *split_high_low(theirs(q)),
            *split_high_low(theirs(k)),
            theirs(v).astype(BF16),
            *split_high_low(lora),
            *extra,
        ]
        return jnp.concatenate(blocks, axis=1)

    def combined(q, k, v, lora, message):
        def mine(x):
            return columns_of(x, seq, columns)

        def part(index):
            return message[:, index * columns : (index + 1) * columns].astype(F32)

        rank = lora.shape[1]
        base = 5 * columns
        return (
            mine(q) + (part(0) + part(1)),
            (mine(k) + (part(2) + part(3))).astype(BF16),
            (mine(v) + part(4)).astype(BF16),
            (
                lora
                + (
                    message[:, base : base + rank].astype(F32)
                    + message[:, base + rank : base + 2 * rank].astype(F32)
                )
            ).astype(BF16),
        )

    own_parts = [dot(own, w) for w in (*weights, adapter_query_down)]
    mix_theirs = rows_of(mix_part, 1 - seq, columns)
    own_sent = payload(*own_parts, split_high_low(mix_theirs))
    own_received = lax.ppermute(own_sent, "seq", to_x)

    near_start = core * quarter
    far_start = (1 - core) * quarter

    def other_part(w):
        return dot(near, lax.dynamic_slice_in_dim(w, near_start, quarter, 0)) + dot(
            far, lax.dynamic_slice_in_dim(w, far_start, quarter, 0)
        )

    other_parts = [other_part(w) for w in (*weights, adapter_query_down)]
    other_sent = payload(*other_parts, ())
    other_received = lax.ppermute(other_sent, "seq", to_x)

    q_own, k_own, v_own, lora_own = combined(*own_parts, other_received)
    q_oth, k_oth, v_oth, lora_oth = combined(*other_parts, own_received)
    base_query = jnp.concatenate([q_own, q_oth], axis=0)
    keys = jnp.concatenate([k_own, k_oth], axis=0)
    values = jnp.concatenate([v_own, v_oth], axis=0)
    lora_hidden = jnp.concatenate([lora_own, lora_oth], axis=0)
    up = columns_of(adapter_query_up, seq, columns)
    scale = HEAD_SIZE ** (-0.5)
    queries = (base_query * scale).astype(BF16)
    fake_queries = ((base_query + dot(lora_hidden, up)) * scale).astype(BF16)

    def attend(query):
        outs = []
        for start in range(0, columns, HEAD_SIZE):
            part = slice(start, start + HEAD_SIZE)
            scores = contract_final_axis(query[:, part], keys[:, part])
            top = jnp.max(scores, axis=-1, keepdims=True)
            probs = jnp.exp(scores - top)
            mass = jnp.sum(probs, axis=-1, keepdims=True)
            outs.append((dot(probs.astype(BF16), values[:, part]) / mass).astype(BF16))
        return jnp.concatenate(outs, axis=1)

    mix_message = own_received[:, -2 * channels :].astype(F32)
    mix_full = rows_of(mix_part, seq, columns) + (
        mix_message[:, :channels] + mix_message[:, channels:]
    )
    lora_readout = contract_final_axis(adapter_output_up, velocity_readout_weight).astype(BF16)
    mix = mix_full.astype(BF16)
    fake_mix = (
        mix_full + dot(rows_of(adapter_output_down, seq, columns), lora_readout)
    ).astype(BF16)
    real = dot(attend(queries), mix)
    delta = dot(attend(fake_queries), fake_mix) - real

    base = contract_final_axis(hidden, velocity_readout_weight)
    base = jnp.where((group == 0) & (head == 0), base, 0.0)
    terms_own = jnp.concatenate([real[:tokens] + base, delta[:tokens]], axis=1)
    terms_oth = jnp.concatenate([real[tokens:], delta[tokens:]], axis=1)

    share = tokens // 2
    sent = jnp.concatenate(
        [rows_of(terms_own, 1 - core, share), rows_of(terms_oth, 1 - core, share)], axis=0
    )
    got = lax.ppermute(sent, "head", to_core)
    mine = rows_of(terms_own, core, share) + got[:share]
    theirs = rows_of(terms_oth, core, share) + got[share:]
    same = jnp.concatenate([mine, fold(theirs[:, :channels])], axis=0)
    cross = jnp.concatenate([theirs, fold(mine[:, :channels])], axis=0)
    from_x = lax.ppermute(cross, "seq", to_x)
    from_y = lax.ppermute(same, "head", to_y)
    from_xy = lax.ppermute(cross, ("seq", "head"), to_xy)
    total = (same + from_y) + (from_x + from_xy)
    stage = 1
    parts = [total] + [
        lax.ppermute(total, "group", pairs((groups,), lambda g, k=k: (g ^ k,)))
        for k in range(1, groups)
    ]
    while len(parts) > 1:
        parts = [a + b for a, b in zip(parts[::2], parts[1::2])]
    total = parts[0]

    real_own = total[:share, :channels]
    delta_own = total[:share, channels:]
    real_oth = unfold(total[share:])

    def error(latents_all, noisy_all, real_part):
        x0_real = rows_of(noisy_all, core, share).astype(F32) - sigma * real_part
        return jnp.sum(jnp.abs(rows_of(latents_all, core, share).astype(F32) - x0_real))

    local_error = error(latents, noisy, real_own) + error(other_latents, other_noisy, real_oth)
    packet = jnp.concatenate(
        [fold(delta_own), jnp.broadcast_to(local_error, (8, 2 * channels))], axis=0
    )
    answer = lax.ppermute(packet, "head", to_core)
    weight = (local_error + answer[-1, 0]) / (2 * tokens * channels)
    delta_partner = unfold(answer[: share // 2])
    first = jnp.where(core == 0, delta_own, delta_partner)
    second = jnp.where(core == 0, delta_partner, delta_own)
    return jnp.concatenate([first, second], axis=0) * (-sigma) / weight


def gathered_local(
    latents,
    noise,
    step,
    stream,
    patch_embed_weight,
    prenorm_gain_vector,
    query_matrix,
    key_matrix,
    value_matrix,
    output_matrix,
    velocity_readout_weight,
    adapter_query_down,
    adapter_query_up,
    adapter_output_down,
    adapter_output_up,
):
    tokens = latents.shape[0]
    width = query_matrix.shape[1]
    local_heads = width // HEAD_SIZE
    channels = velocity_readout_weight.shape[0]
    sigma = noise_level(step)
    noisy = (
        (1.0 - sigma) * latents.astype(F32) + sigma * noise.astype(F32)
    ).astype(BF16)
    hidden = (stream.astype(F32) + dot(noisy, patch_embed_weight)).astype(BF16)
    hidden_wide = hidden.astype(F32)
    normed = (
        hidden_wide
        * lax.rsqrt(jnp.mean(hidden_wide * hidden_wide, axis=-1, keepdims=True) + 1e-06)
        * prenorm_gain_vector
    ).astype(BF16)
    base_query, keys, values, lora_hidden = (
        dot(normed, lax.all_gather(piece, "seq", axis=0, tiled=True))
        for piece in (query_matrix, key_matrix, value_matrix, adapter_query_down)
    )
    scale = HEAD_SIZE ** (-0.5)
    lora_delta = dot(lora_hidden.astype(BF16), adapter_query_up)
    queries = (base_query * scale).astype(BF16)
    fake_queries = ((base_query + lora_delta) * scale).astype(BF16)
    both_sets = jnp.stack([queries, fake_queries]).reshape(2, tokens, local_heads, HEAD_SIZE)
    key_rows = lax.all_gather(keys.astype(BF16), "seq", axis=0, tiled=True)
    value_rows = lax.all_gather(values.astype(BF16), "seq", axis=0, tiled=True)
    key_rows = key_rows.reshape(-1, local_heads, HEAD_SIZE)
    value_rows = value_rows.reshape(-1, local_heads, HEAD_SIZE)
    scores = jnp.einsum("sthd,khd->shtk", both_sets, key_rows, preferred_element_type=F32)
    weights = jnp.exp(scores - jnp.max(scores, axis=-1, keepdims=True))
    mass = jnp.sum(weights, axis=-1)
    added = jnp.einsum(
        "shtk,khd->sthd", weights.astype(BF16), value_rows, preferred_element_type=F32
    )
    attn = (added / mass.transpose(0, 2, 1)[..., None]).astype(BF16).reshape(2, tokens, width)
    columns = output_matrix.shape[1]
    readout_part = columns_of(velocity_readout_weight, lax.axis_index("seq"), columns)
    mix_full = lax.psum(contract_final_axis(output_matrix, readout_part), "seq")
    lora_readout = contract_final_axis(adapter_output_up, velocity_readout_weight).astype(BF16)
    fake_mix = (mix_full + dot(adapter_output_down, lora_readout)).astype(BF16)
    real_sum, fake_sum = lax.psum(
        (dot(attn[0], mix_full.astype(BF16)), dot(attn[1], fake_mix)), ("group", "head")
    )
    base = contract_final_axis(hidden, velocity_readout_weight)
    noisy_wide = noisy.astype(F32)
    x0_real = noisy_wide - sigma * (base + real_sum)
    x0_fake = noisy_wide - sigma * (base + fake_sum)
    local_error = jnp.sum(jnp.abs(latents.astype(F32) - x0_real))
    weight = lax.psum(local_error, "seq") / (tokens * lax.axis_size("seq") * channels)
    return (x0_fake - x0_real) / weight


def solution(mesh):
    sizes = tuple(mesh.shape[name] for name in ("group", "seq", "head"))

    def local(*args):
        query_columns = args[6].shape[1]
        power = sizes[0] & (sizes[0] - 1) == 0
        paired = sizes[1] == 2 and sizes[2] == 4 and power
        if paired and (query_columns // HEAD_SIZE) % 2 == 0:
            return paired_local(sizes, *args)
        return gathered_local(*args)

    split = ("group", "head")
    in_specs = (
        P("seq", None),
        P("seq", None),
        P(),
        P("seq", None),
        P(),
        P(),
        P("seq", split),
        P("seq", split),
        P("seq", split),
        P(split, "seq"),
        P(),
        P("seq", None),
        P(None, split),
        P(split, None),
        P(),
    )
    return jax.shard_map(
        local, mesh=mesh, in_specs=in_specs, out_specs=P("seq", None), check_vma=False
    )
```

time: 295 us -> 80.6 us (0.27)
  waiting for transfers between devices: 237 us -> 29.2 us
  blocking collectives: 15.4 us -> 0 us
  starting transfers between devices: 0.2 us -> 14.9 us
  between operations: 15 us -> 3.28 us
  other arithmetic: 0.74 us -> 8.87 us
  matrix products: 21.4 us -> 16.9 us
  local copies, waits for them, and re-layouts: 3.5 us -> 6.74 us
    all_gather x4 -> x0, waiting for transfers between devices: 130 us -> none  [the longest x1 38 us: local(): lax.all_gather(value_matrix, 'seq', axis=0, tiled=True)]
    psum x2 -> x0, waiting for transfers between devices: 105 us -> none  [the longest x1 86.6 us: local(): real_sum, fake_sum = lax.psum((real_term, fake_term), ('group', 'head'))]
    ppermute x0 -> x12, waiting for transfers between devices: none -> 29.2 us  [the longest x1 6.07 us: paired_local(): own_received = lax.ppermute(own_sent, 'seq', to_x)]
    ppermute x0 -> x12, starting transfers between devices: none -> 14.9 us  [the longest x3 4.45 us: paired_local(): lax.ppermute(total, 'group', pairs((groups,), lambda g, k=k: (g ^ k,)))]
    all_gather x2 -> x0, blocking collectives: 9.87 us -> none  [the longest x1 4.93 us: local(): lax.all_gather(values, 'seq', axis=0, tiled=True)]
    convert_element_type x0 -> x5, other arithmetic: none -> 6.34 us  [the longest x1 3.25 us: paired_local(): normed = (hidden_wide * lax.rsqrt(jnp.mean(hidden_wide * hidden_wide, axi...]
    psum x1 -> x0, blocking collectives: 5.54 us -> none  [local(): lax.psum(local_error, 'seq') / (tokens * lax.axis_size('seq') * channels)]
    dot_general x10 -> x16, matrix products: 17.3 us -> 12.1 us  [dot(): return jnp.dot(left, right, preferred_element_type=F32)]
  transfers between devices with their start and end apart: 6 -> 12, of which waited for: 6 -> 12; matrix products, arithmetic and copies ran while one was open for 5% -> 6% of each run, Pallas kernels for 0% -> 0%
where the time goes in v1:
time: 80.6 us; the launch traced here: 79.9 us
  waiting for transfers between devices  29.2 us (36%)
  matrix products  16.9 us (21%)
  starting transfers between devices  14.9 us (18%)
  other arithmetic  8.87 us (11%)
  local copies, waits for them, and re-layouts  6.74 us (8%)
  between operations  3.28 us (4%)
    dot_general x16, matrix products, dot(): return jnp.dot(left, right, preferred_element_type=F32)  12.1 us
    ppermute x1, waiting for transfers between devices, paired_local(): own_received = lax.ppermute(own_sent, 'seq', to_x)  6.07 us
    ppermute x1, waiting for transfers between devices, paired_local(): other_received = lax.ppermute(other_sent, 'seq', to_x)  5.49 us
    ppermute x1, waiting for transfers between devices, paired_local(): received = lax.ppermute(message, 'seq', to_x)  5.29 us
    dot_general x4, matrix products, contract_final_axis(): lax.dot_general(left, right, (((1,), (1,)), ((), ())), preferred_element_...  4.83 us
    ppermute x3, starting transfers between devices, paired_local(): lax.ppermute(total, 'group', pairs((groups,), lambda g, k=k: (g ^ k,)))  4.45 us
    ppermute x3, waiting for transfers between devices, paired_local(): lax.ppermute(total, 'group', pairs((groups,), lambda g, k=k: (g ^ k,)))  4.38 us
    convert_element_type x1, other arithmetic, paired_local(): normed = (hidden_wide * lax.rsqrt(jnp.mean(hidden_wide * hidden_wide, axi...  3.25 us
  transfers between devices with their start and end apart: 12, of which 12 were waited for; matrix products, arithmetic and copies ran while one was open for 6% of the time, Pallas kernels for 0%

profile of v1, /device:TPU:0, one launch (start us, length us, event | category | flops | bytes accessed | tf_op | source)
XLA Modules:
  0.0 79.9 jit_solution(12154894186553307385)
XLA Ops:
  0.8 1.8 %copy.46 = bf16[128,5120]{0,1:T(8,128)(2,1)S(1)} copy(bf16[128,5120]{1,0:T(8,128)(2,1)} %param.18) | data formatting | bytes 2621440 | tf_op args[3]
  2.7 3.0 %fusion.1 = (f32[128]{0:T(128)S(1)}, bf16[128,5120]{0,1:T(8,128)(2,1)}) fusion(bf16[128,64]{0,1:T(8,128)(2,1)S(1)} %add_convert_fusion.6, bf16[64,5120]{1,0:T(8,128)(2,1)} %param.19, bf16[128,5120]{0,1:T(8,128)(2,1)S(1)} %copy.46), kind=kOutput, calls=%fused_computation.4 | convolution fusion | flops 87818112 | bytes 3293696 | tf_op jit(solution)/shard_map/dot_general | solution.py:20
  5.7 3.3 %fusion.3 = bf16[128,5120]{0,1:T(8,128)(2,1)S(1)} fusion(bf16[128,5120]{0,1:T(8,128)(2,1)} %get-tuple-element.40, f32[5120]{0:T(1024)S(1)} %copy-done.16, f32[128]{0:T(128)S(1)} %add_rsqrt_fusion), kind=kLoop, calls=%fused_computation.6 | loop fusion | flops 2621440 | bytes 2642432 | tf_op jit(solution)/shard_map/convert_element_type | solution.py:105
  9.1 3.0 %collective-permute-start = (bf16[128,1408]{0,1:T(8,128)(2,1)S(1)}, bf16[128,1408]{0,1:T(8,128)(2,1)S(1)}, u32[]{:S(2)}, u32[]{:S(2)}) collective-permute-start(bf16[128,1408]{0,1:T(8,128)(2,1)S(1)} %pad_maximum_fusion), channel_id=1, source_target_pairs={{0,4},{4,0},{1,5},{5,1},{2,6},{6,2},{3,7},{7,3},{8,12},{12,8},{9,1... | collective-permute-start | bytes 1081352 | tf_op jit(solution)/shard_map/ppermute | solution.py:110
  12.1 2.0 %fusion.29 = f32[64,256]{0,1:T(8,128)S(1)} fusion(bf16[256,2560]{1,0:T(8,128)(2,1)} %param.24, bf16[64,5120]{1,0:T(8,128)(2,1)} %param.25, s32[]{:T(128)S(6)} %select_n.43), kind=kOutput, calls=%fused_computation.44 | convolution fusion | flops 83886080 | bytes 1703940 | tf_op jit(solution)/shard_map/dot_general | solution.py:14
  15.2 5.3 %collective-permute-done = bf16[128,1408]{0,1:T(8,128)(2,1)S(1)} collective-permute-done((bf16[128,1408]{0,1:T(8,128)(2,1)S(1)}, bf16[128,1408]{0,1:T(8,128)(2,1)S(1)}, u32[]{:S(2)}, u32[]{:S(2)}) %collective-permute-start) | collective-permute-done | bytes 360480 | tf_op jit(solution)/shard_map/ppermute | solution.py:110
  25.2 1.8 %collective-permute-start.2 = (bf16[128,896]{1,0:T(8,128)(2,1)S(1)}, bf16[128,896]{1,0:T(8,128)(2,1)S(1)}, u32[]{:S(2)}, u32[]{:S(2)}) collective-permute-start(bf16[128,896]{1,0:T(8,128)(2,1)S(1)} %fusion.72), channel_id=1, source_target_pairs={{0,4},{4,0},{1,5},{5,1},{2,6},{6,2},{3,7},{7,3},{8,12},{12,8},{9,1... | collective-permute-start | bytes 688136 | tf_op jit(solution)/shard_map/ppermute | solution.py:172
  27.5 5.5 %collective-permute-done.2 = bf16[128,896]{1,0:T(8,128)(2,1)S(1)} collective-permute-done((bf16[128,896]{1,0:T(8,128)(2,1)S(1)}, bf16[128,896]{1,0:T(8,128)(2,1)S(1)}, u32[]{:S(2)}, u32[]{:S(2)}) %collective-permute-start.2) | collective-permute-done | bytes 229408 | tf_op jit(solution)/shard_map/ppermute | solution.py:172
  32.9 1.0 %add_convert_fusion.1 = (bf16[128,128]{1,0:T(8,128)(2,1)}, bf16[128,128]{1,0:T(8,128)(2,1)S(1)}, f32[128,128]{1,0:T(8,128)S(1)}, bf16[128,128]{1,0:T(8,128)(2,1)...) fusion(bf16[128,896]{1,0:T(8,128)(2,1)S(1)} %collective-permute, ...), kind=kOutput, calls=%fused_computation.111 | convolution fusion | flops 84361216 | bytes 2228236 | tf_op jit(solution)/shard_map/dot_general | solution.py:20
  33.9 1.6 %concatenate.59 = bf16[128,1024]{1,0:T(8,128)(2,1)} concatenate(bf16[128,128]{1,0:T(8,128)(2,1)S(1)} %get-tuple-element.16, bf16[128,128]{1,0:T(8,128)(2,1)S(1)} %get-tuple-element.15, bf16[128,128]{1,0:T(8,128)(2,1)} %get-tuple-element.18, bf16[128,128]{1,0:T(8,128)(2,1)S(1)} %get-tuple-element.17, bf16[128,128]{1,0:T(8,128)(2,1)} %dynamic-slice_convert_fusion, ...), dimensions={1} | concatenate | bytes 524288 | tf_op jit(solution)/shard_map/concatenate | solution.py:133
  35.6 1.7 %collective-permute-start.3 = (bf16[128,1024]{1,0:T(8,128)(2,1)}, bf16[128,1024]{1,0:T(8,128)(2,1)}, u32[]{:S(2)}, u32[]{:S(2)}) collective-permute-start(bf16[128,1024]{1,0:T(8,128)(2,1)} %concatenate.59), channel_id=1, source_target_pairs={{0,4},{4,0},{1,5},{5,1},{2,6},{6,2},{3,7},{7,3},{8,12},{12,8},{9,1... | collective-permute-start | bytes 786440 | tf_op jit(solution)/shard_map/ppermute | solution.py:160
  37.3 6.1 %collective-permute-done.3 = bf16[128,1024]{1,0:T(8,128)(2,1)} collective-permute-done((bf16[128,1024]{1,0:T(8,128)(2,1)}, bf16[128,1024]{1,0:T(8,128)(2,1)}, u32[]{:S(2)}, u32[]{:S(2)}) %collective-permute-start.3) | collective-permute-done | bytes 262176 | tf_op jit(solution)/shard_map/ppermute | solution.py:160
  43.4 1.6 %add_convert_fusion = (bf16[128,128]{1,0:T(8,128)(2,1)}, bf16[128,128]{1,0:T(8,128)(2,1)}, bf16[128,128]{1,0:T(8,128)(2,1)S(1)}, f32[128,128]{1,0:T(8,128)S(1)}) fusion(f32[128,128]{1,0:T(8,128)S(1)} %get-tuple-element.42, bf16[128,1024]{1,0:T(8,128)(2,1)} %collective-permute-done.3, f32[128,256]{1,0:T(8,128)} %copy-done.7, s32[]{:T(128)S(6)} %select_n.44, ...), kind=kLoop, calls=%fused_computation.110 | loop fusion | flops 278528 | bytes 655364 | tf_op jit(solution)/shard_map/convert_element_type | solution.py:154
  45.3 0.8 slice_convert_fusion
  46.7 1.9 %fusion.9 = f32[256,64]{0,1:T(8,128)} fusion(f32[256,256]{0,1:T(8,128)S(1)} %get-tuple-element.44, f32[256]{0:T(256)S(1)} %get-tuple-element.43, f32[256]{0:T(256)S(1)} %fusion.34, bf16[128,128]{1,0:T(8,128)(2,1)} %get-tuple-element.8, bf16[128,128]{1,0:T(8,128)(2,1)} %get-tuple-element.14, f32[128,128]{1,0:T(8,128)S(1)} %slice_convert_fusion, ...), kind=kOutput, calls=%fused_computation.21 | convolution fusion | flops 21323776 | bytes 591876 | tf_op jit(solution)/shard_map/dot_general | solution.py:20
  48.6 0.8 slice.190
  49.4 1.5 %fusion.11 = f32[128,64]{0,1:T(8,128)S(1)} fusion(bf16[64,5120]{1,0:T(8,128)(2,1)} %param.25, bf16[128,5120]{0,1:T(8,128)(2,1)S(1)} %copy-done.1, f32[256,64]{0,1:T(8,128)} %fusion.9, pred[]{:T(512)S(6)} %and.12), kind=kOutput, calls=%fused_computation.24 | convolution fusion | flops 83902464 | bytes 2031617 | tf_op jit(solution)/shard_map/dot_general | solution.py:14
  50.9 1.1 %fusion.130 = (f32[256]{0:T(256)S(1)}, f32[256,256]{0,1:T(8,128)S(1)}) fusion(bf16[128,128]{1,0:T(8,128)(2,1)S(1)} %get-tuple-element.9, bf16[128,128]{1,0:T(8,128)(2,1)S(1)} %get-tuple-element.12, f32[128,128]{1,0:T(8,128)S(1)} %get-tuple-element.10, f32[128,128]{1,0:T(8,128)S(1)} %get-tuple-element.13, bf16[128,128]{1,0:T(8,128)(2,1)S(1)} %copy-done.12, ...), kind=kOutput, calls=%fused_computation.186 | convolution fusion | flops 25624320 | bytes 558084 | tf_op jit(solution)/shard_map/dot_general | solution.py:14
  52.1 2.2 %fusion.10 = bf16[128,64]{1,0:T(8,128)(2,1)S(1)} fusion(bf16[128,5120]{1,0:T(8,128)(2,1)} %param.29, bf16[64,5120]{1,0:T(8,128)(2,1)} %param.25, bf16[256,128]{1,0:T(8,128)(2,1)} %param.28, s32[]{:T(128)S(6)} %select_n.44, f32[128,128]{1,0:T(8,128)S(1)} %copy-done.9, f32[64,256]{0,1:T(8,128)S(1)} %copy-done.6), kind=kOutput, calls=%fused_computation.22 | convolution fusion | flops 86024192 | bytes 2114560 | tf_op jit(solution)/shard_map/dot_general | solution.py:20
  55.1 1.2 %collective-permute-done.4 = f32[128,128]{0,1:T(8,128)S(1)} collective-permute-done((f32[128,128]{0,1:T(8,128)S(1)}, f32[128,128]{0,1:T(8,128)S(1)}, u32[]{:S(2)}, u32[]{:S(2)}) %collective-permute-start.4) | collective-permute-done | bytes 65568 | tf_op jit(solution)/shard_map/ppermute | solution.py:217
  56.7 1.8 %collective-permute-start.5 = (f32[96,128]{0,1:T(8,128)S(1)}, f32[96,128]{0,1:T(8,128)S(1)}, u32[]{:S(2)}, u32[]{:S(2)}) collective-permute-start(f32[96,128]{0,1:T(8,128)S(1)} %maximum_maximum_fusion), channel_id=1, source_target_pairs={{0,2},{1,3},{2,0},{3,1},{4,6},{5,7},{6,4},{7,5},{8,10},{9,11},{10,... | collective-permute-start | bytes 147464 | tf_op jit(solution)/shard_map/ppermute | solution.py:223
  58.6 1.6 %collective-permute-start.6 = (f32[96,128]{0,1:T(8,128)S(1)}, f32[96,128]{0,1:T(8,128)S(1)}, u32[]{:S(2)}, u32[]{:S(2)}) collective-permute-start(f32[96,128]{0,1:T(8,128)S(1)} %maximum_maximum_fusion.1), channel_id=1, source_target_pairs={{0,4},{4,0},{1,5},{5,1},{2,6},{6,2},{3,7},{7,3},{8,12},{12,8},{9,1... | collective-permute-start | bytes 147464 | tf_op jit(solution)/shard_map/ppermute | solution.py:222
  61.1 2.6 %collective-permute-done.6 = f32[96,128]{0,1:T(8,128)S(1)} collective-permute-done((f32[96,128]{0,1:T(8,128)S(1)}, f32[96,128]{0,1:T(8,128)S(1)}, u32[]{:S(2)}, u32[]{:S(2)}) %collective-permute-start.6) | collective-permute-done | bytes 49184 | tf_op jit(solution)/shard_map/ppermute | solution.py:222
  63.6 1.8 %collective-permute-done.7 = f32[96,128]{0,1:T(8,128)S(1)} collective-permute-done((f32[96,128]{0,1:T(8,128)S(1)}, f32[96,128]{0,1:T(8,128)S(1)}, u32[]{:S(2)}, u32[]{:S(2)}) %collective-permute-start.7) | collective-permute-done | bytes 49184 | tf_op jit(solution)/shard_map/ppermute | solution.py:224
  65.5 3.7 %collective-permute-start.10 = (f32[96,128]{0,1:T(8,128)S(1)}, f32[96,128]{0,1:T(8,128)S(1)}, u32[]{:S(2)}, u32[]{:S(2)}) collective-permute-start(f32[96,128]{0,1:T(8,128)S(1)} %add_add_fusion.1), channel_id=1, source_target_pairs={{0,24},{8,16},{16,8},{24,0},{1,25},{9,17},{17,9},{25,1},{2,26},{10... | collective-permute-start | bytes 147464 | tf_op jit(solution)/shard_map/ppermute | solution.py:228
  69.1 0.8 collective-permute-start.9
  69.9 1.8 %collective-permute-done.10 = f32[96,128]{0,1:T(8,128)S(1)} collective-permute-done((f32[96,128]{0,1:T(8,128)S(1)}, f32[96,128]{0,1:T(8,128)S(1)}, u32[]{:S(2)}, u32[]{:S(2)}) %collective-permute-start.10) | collective-permute-done | bytes 49184 | tf_op jit(solution)/shard_map/ppermute | solution.py:228
  71.7 1.7 %collective-permute-done.8 = f32[96,128]{0,1:T(8,128)S(1)} collective-permute-done((f32[96,128]{0,1:T(8,128)S(1)}, f32[96,128]{0,1:T(8,128)S(1)}, u32[]{:S(2)}, u32[]{:S(2)}) %collective-permute-start.8) | collective-permute-done | bytes 49184 | tf_op jit(solution)/shard_map/ppermute | solution.py:228
  73.4 0.9 %collective-permute-done.9 = f32[96,128]{0,1:T(8,128)S(1)} collective-permute-done((f32[96,128]{0,1:T(8,128)S(1)}, f32[96,128]{0,1:T(8,128)S(1)}, u32[]{:S(2)}, u32[]{:S(2)}) %collective-permute-start.9) | collective-permute-done | bytes 49184 | tf_op jit(solution)/shard_map/ppermute | solution.py:228
  74.4 0.8 fusion.81
  76.7 1.2 %collective-permute-done.11 = f32[40,128]{0,1:T(8,128)S(1)} collective-permute-done((f32[40,128]{0,1:T(8,128)S(1)}, f32[40,128]{0,1:T(8,128)S(1)}, u32[]{:S(2)}, u32[]{:S(2)}) %collective-permute-start.11) | collective-permute-done | bytes 20512 | tf_op jit(solution)/shard_map/ppermute | solution.py:247
  79.2 0.7 fusion.86
  (88 shorter events, 10.2 us)
Async XLA Ops:
  0.0 21.2 %copy-start = (bf16[2560,256]{1,0:T(8,128)(2,1)S(1)}, bf16[2560,256]{1,0:T(8,128)(2,1)}, u32[]{:S(2)}) copy-start(bf16[2560,256]{1,0:T(8,128)(2,1)} %param.22) | copy-start | bytes 3932164
  0.8 1.8 %copy-start.10 = (bf16[128,64]{0,1:T(8,128)(2,1)S(1)}, bf16[128,64]{0,1:T(8,128)(2,1)}, u32[]{:S(2)}) copy-start(bf16[128,64]{0,1:T(8,128)(2,1)} %param.15) | copy-start | bytes 49156
  0.8 1.8 %copy-start.17 = (bf16[128,64]{0,1:T(8,128)(2,1)S(1)}, bf16[128,64]{0,1:T(8,128)(2,1)}, u32[]{:S(2)}) copy-start(bf16[128,64]{0,1:T(8,128)(2,1)} %param.16) | copy-start | bytes 49156
  2.7 3.1 %copy-start.16 = (f32[5120]{0:T(1024)S(1)}, f32[5120]{0:T(1024)}, u32[]{:S(2)}) copy-start(f32[5120]{0:T(1024)} %param.20) | copy-start | bytes 61444
  9.1 11.4 %collective-permute-start = (bf16[128,1408]{0,1:T(8,128)(2,1)S(1)}, bf16[128,1408]{0,1:T(8,128)(2,1)S(1)}, u32[]{:S(2)}, u32[]{:S(2)}) collective-permute-start(bf16[128,1408]{0,1:T(8,128)(2,1)S(1)} %pad_maximum_fusion), channel_id=1, source_target_pairs={{0,4},{4,0},{1,5},{5,1},{2,6},{6,2},{3,7},{7,3},{8,12},{12,8},{9,1... | collective-permute-start | bytes 1081352 | tf_op jit(solution)/shard_map/ppermute | solution.py:110
  12.1 2.7 %copy-start.2 = (bf16[2560,256]{1,0:T(8,128)(2,1)S(1)}, bf16[2560,256]{1,0:T(8,128)(2,1)}, u32[]{:S(2)}) copy-start(bf16[2560,256]{1,0:T(8,128)(2,1)} %param.23) | copy-start | bytes 3932164
  14.1 0.7 copy-start.5
  15.2 7.0 %copy-start.3 = (bf16[2560,256]{1,0:T(8,128)(2,1)S(1)}, bf16[2560,256]{1,0:T(8,128)(2,1)}, u32[]{:S(2)}) copy-start(bf16[2560,256]{1,0:T(8,128)(2,1)} %param.21) | copy-start | bytes 3932164
  20.5 1.7 %collective-permute-start.1 = (bf16[128,1280]{0,1:T(8,128)(2,1)S(1)}, bf16[128,1280]{0,1:T(8,128)(2,1)S(1)}, u32[]{:S(2)}, u32[]{:S(2)}) collective-permute-start(bf16[128,1280]{0,1:T(8,128)(2,1)S(1)} %slice.170), channel_id=1, source_target_pairs={{0,1},{1,0},{2,3},{3,2},{4,5},{5,4},{6,7},{7,6},{8,9},{9,8},{10,11... | collective-permute-start | bytes 983048 | tf_op jit(solution)/shard_map/ppermute | solution.py:112
  23.5 1.1 %copy-start.4 = (bf16[2560,128]{1,0:T(8,128)(2,1)S(1)}, bf16[2560,128]{1,0:T(8,128)(2,1)}, u32[]{:S(2)}) copy-start(bf16[2560,128]{1,0:T(8,128)(2,1)} %param.26) | copy-start | bytes 1966084
  24.2 3.3 %copy-start.7 = (f32[128,256]{1,0:T(8,128)}, f32[128,256]{1,0:T(8,128)S(1)}, u32[]{:S(2)}) copy-start(f32[128,256]{1,0:T(8,128)S(1)} %convolution_add_fusion.1) | copy-start | bytes 393220
  25.2 7.7 %collective-permute-start.2 = (bf16[128,896]{1,0:T(8,128)(2,1)S(1)}, bf16[128,896]{1,0:T(8,128)(2,1)S(1)}, u32[]{:S(2)}, u32[]{:S(2)}) collective-permute-start(bf16[128,896]{1,0:T(8,128)(2,1)S(1)} %fusion.72), channel_id=1, source_target_pairs={{0,4},{4,0},{1,5},{5,1},{2,6},{6,2},{3,7},{7,3},{8,12},{12,8},{9,1... | collective-permute-start | bytes 688136 | tf_op jit(solution)/shard_map/ppermute | solution.py:172
  35.6 13.8 %copy-start.1 = (bf16[128,5120]{0,1:T(8,128)(2,1)S(1)}, bf16[128,5120]{0,1:T(8,128)(2,1)}, u32[]{:S(2)}) copy-start(bf16[128,5120]{0,1:T(8,128)(2,1)} %get-tuple-element.40) | copy-start | bytes 3932164
  35.6 7.8 %collective-permute-start.3 = (bf16[128,1024]{1,0:T(8,128)(2,1)}, bf16[128,1024]{1,0:T(8,128)(2,1)}, u32[]{:S(2)}, u32[]{:S(2)}) collective-permute-start(bf16[128,1024]{1,0:T(8,128)(2,1)} %concatenate.59), channel_id=1, source_target_pairs={{0,4},{4,0},{1,5},{5,1},{2,6},{6,2},{3,7},{7,3},{8,12},{12,8},{9,1... | collective-permute-start | bytes 786440 | tf_op jit(solution)/shard_map/ppermute | solution.py:160
  46.1 0.6 copy-start.8
  48.6 2.3 %copy-start.11 = (bf16[128,128]{1,0:T(8,128)(2,1)S(1)}, bf16[128,128]{1,0:T(8,128)(2,1)}, u32[]{:S(2)}) copy-start(bf16[128,128]{1,0:T(8,128)(2,1)} %get-tuple-element.11) | copy-start | bytes 98308
  48.6 2.3 %copy-start.12 = (bf16[128,128]{1,0:T(8,128)(2,1)S(1)}, bf16[128,128]{1,0:T(8,128)(2,1)}, u32[]{:S(2)}) copy-start(bf16[128,128]{1,0:T(8,128)(2,1)} %get-tuple-element.7) | copy-start | bytes 98308
  49.3 2.8 %copy-start.6 = (f32[64,256]{0,1:T(8,128)S(1)}, f32[64,256]{0,1:T(8,128)}, u32[]{:S(2)}) copy-start(f32[64,256]{0,1:T(8,128)} %copy-done.5) | copy-start | bytes 196612
  49.4 2.8 %copy-start.9 = (f32[128,128]{1,0:T(8,128)S(1)}, f32[128,128]{1,0:T(8,128)}, u32[]{:S(2)}) copy-start(f32[128,128]{1,0:T(8,128)} %copy-done.8) | copy-start | bytes 196612
  52.0 2.3 %copy-start.13 = (f32[256,64]{0,1:T(8,128)S(1)}, f32[256,64]{0,1:T(8,128)}, u32[]{:S(2)}) copy-start(f32[256,64]{0,1:T(8,128)} %fusion.9) | copy-start | bytes 196612
  52.0 2.3 %copy-start.14 = (bf16[128,128]{1,0:T(8,128)(2,1)S(1)}, bf16[128,128]{1,0:T(8,128)(2,1)}, u32[]{:S(2)}) copy-start(bf16[128,128]{1,0:T(8,128)(2,1)} %get-tuple-element.14) | copy-start | bytes 98308
  52.0 2.3 %copy-start.15 = (bf16[128,128]{1,0:T(8,128)(2,1)S(1)}, bf16[128,128]{1,0:T(8,128)(2,1)}, u32[]{:S(2)}) copy-start(bf16[128,128]{1,0:T(8,128)(2,1)} %get-tuple-element.8) | copy-start | bytes 98308
  55.0 1.3 %collective-permute-start.4 = (f32[128,128]{0,1:T(8,128)S(1)}, f32[128,128]{0,1:T(8,128)S(1)}, u32[]{:S(2)}, u32[]{:S(2)}) collective-permute-start(f32[128,128]{0,1:T(8,128)S(1)} %pad_maximum_fusion.5), channel_id=1, source_target_pairs={{0,1},{1,0},{2,3},{3,2},{4,5},{5,4},{6,7},{7,6},{8,9},{9,8},{10,11... | collective-permute-start | bytes 196616 | tf_op jit(solution)/shard_map/ppermute | solution.py:217
  56.7 4.3 %collective-permute-start.5 = (f32[96,128]{0,1:T(8,128)S(1)}, f32[96,128]{0,1:T(8,128)S(1)}, u32[]{:S(2)}, u32[]{:S(2)}) collective-permute-start(f32[96,128]{0,1:T(8,128)S(1)} %maximum_maximum_fusion), channel_id=1, source_target_pairs={{0,2},{1,3},{2,0},{3,1},{4,6},{5,7},{6,4},{7,5},{8,10},{9,11},{10,... | collective-permute-start | bytes 147464 | tf_op jit(solution)/shard_map/ppermute | solution.py:223
  58.6 5.0 %collective-permute-start.6 = (f32[96,128]{0,1:T(8,128)S(1)}, f32[96,128]{0,1:T(8,128)S(1)}, u32[]{:S(2)}, u32[]{:S(2)}) collective-permute-start(f32[96,128]{0,1:T(8,128)S(1)} %maximum_maximum_fusion.1), channel_id=1, source_target_pairs={{0,4},{4,0},{1,5},{5,1},{2,6},{6,2},{3,7},{7,3},{8,12},{12,8},{9,1... | collective-permute-start | bytes 147464 | tf_op jit(solution)/shard_map/ppermute | solution.py:222
  60.2 5.2 %collective-permute-start.7 = (f32[96,128]{0,1:T(8,128)S(1)}, f32[96,128]{0,1:T(8,128)S(1)}, u32[]{:S(2)}, u32[]{:S(2)}) collective-permute-start(f32[96,128]{0,1:T(8,128)S(1)} %maximum_maximum_fusion.1), channel_id=1, source_target_pairs={{0,6},{1,7},{2,4},{3,5},{4,2},{5,3},{6,0},{7,1},{8,14},{9,15},{10,... | collective-permute-start | bytes 147464 | tf_op jit(solution)/shard_map/ppermute | solution.py:224
  65.5 6.2 %collective-permute-start.10 = (f32[96,128]{0,1:T(8,128)S(1)}, f32[96,128]{0,1:T(8,128)S(1)}, u32[]{:S(2)}, u32[]{:S(2)}) collective-permute-start(f32[96,128]{0,1:T(8,128)S(1)} %add_add_fusion.1), channel_id=1, source_target_pairs={{0,24},{8,16},{16,8},{24,0},{1,25},{9,17},{17,9},{25,1},{2,26},{10... | collective-permute-start | bytes 147464 | tf_op jit(solution)/shard_map/ppermute | solution.py:228
  69.1 4.3 %collective-permute-start.8 = (f32[96,128]{0,1:T(8,128)S(1)}, f32[96,128]{0,1:T(8,128)S(1)}, u32[]{:S(2)}, u32[]{:S(2)}) collective-permute-start(f32[96,128]{0,1:T(8,128)S(1)} %add_add_fusion.1), channel_id=1, source_target_pairs={{0,8},{8,0},{16,24},{24,16},{1,9},{9,1},{17,25},{25,17},{2,10},{10... | collective-permute-start | bytes 147464 | tf_op jit(solution)/shard_map/ppermute | solution.py:228
  69.1 5.2 %collective-permute-start.9 = (f32[96,128]{0,1:T(8,128)S(1)}, f32[96,128]{0,1:T(8,128)S(1)}, u32[]{:S(2)}, u32[]{:S(2)}) collective-permute-start(f32[96,128]{0,1:T(8,128)S(1)} %add_add_fusion.1), channel_id=1, source_target_pairs={{0,16},{8,24},{16,0},{24,8},{1,17},{9,25},{17,1},{25,9},{2,18},{10... | collective-permute-start | bytes 147464 | tf_op jit(solution)/shard_map/ppermute | solution.py:228
  76.6 1.3 %collective-permute-start.11 = (f32[40,128]{0,1:T(8,128)S(1)}, f32[40,128]{0,1:T(8,128)S(1)}, u32[]{:S(2)}, u32[]{:S(2)}) collective-permute-start(f32[40,128]{0,1:T(8,128)S(1)} %select_maximum_fusion), channel_id=1, source_target_pairs={{0,1},{1,0},{2,3},{3,2},{4,5},{5,4},{6,7},{7,6},{8,9},{9,8},{10,11... | collective-permute-start | bytes 61448 | tf_op jit(solution)/shard_map/ppermute | solution.py:247

commit v2 on v1

v2 whole, which is shorter than its diff:
```python
import itertools

import jax
import jax.numpy as jnp
from jax import lax
from jax.experimental import pallas as pl
from jax.experimental.pallas import tpu as pltpu
from jax.sharding import PartitionSpec as P

HEAD_SIZE = 128
F32 = jnp.float32
BF16 = jnp.bfloat16


def contract_final_axis(left, right):
    return lax.dot_general(
        left, right, (((1,), (1,)), ((), ())), preferred_element_type=F32
    )


def dot(left, right):
    return jnp.dot(left, right, preferred_element_type=F32)


def noise_level(step):
    level = (step[0].astype(F32) + 1.0) / 1000.0
    return 5.0 * level / (1.0 + 4.0 * level)


def pairs(sizes, partner):
    def linear(coordinate):
        index = 0
        for value, size in zip(coordinate, sizes):
            index = index * size + value
        return index

    return [
        (linear(c), linear(partner(*c)))
        for c in itertools.product(*[range(n) for n in sizes])
    ]


def columns_of(x, index, count):
    return lax.dynamic_slice_in_dim(x, index * count, count, 1)


VMEM = pl.BlockSpec(memory_space=pltpu.VMEM)
SMEM = pl.BlockSpec(memory_space=pltpu.SMEM)
HBM = pl.BlockSpec(memory_space=pltpu.HBM)


def run(kernel, outs, args, specs=None, scratch=(), flops=0, limit=8 << 20, moved=None):
    shapes = [jax.ShapeDtypeStruct(shape, kind) for shape, kind in outs]
    if moved is None:
        moved = sum(a.size * a.dtype.itemsize for a in (*args, *shapes))
    return pl.pallas_call(
        kernel,
        out_shape=shapes,
        in_specs=specs or [VMEM] * len(args),
        out_specs=[VMEM] * len(shapes),
        scratch_shapes=list(scratch),
        cost_estimate=pl.CostEstimate(flops=flops, bytes_accessed=moved, transcendentals=0),
        compiler_params=pltpu.CompilerParams(vmem_limit_bytes=limit),
    )(*args)


def aligned(index, count):
    return pl.ds(pl.multiple_of(index * count, count), count)


def fold(low, high):
    lane = lax.broadcasted_iota(jnp.int32, low.shape, 1)
    return jnp.where(lane < low.shape[1] // 2, low, high)


def swap_halves(x):
    return pltpu.roll(x, x.shape[1] // 2, 1)


def high_low(x):
    high = x.astype(BF16)
    return high, (x - high.astype(F32)).astype(BF16)


def first_kernel(
    step_hbm, latents_hbm, noise_hbm, gain_hbm, stream_hbm, patch_hbm,
    message_ref, hidden_ref, inverse_ref, gap_ref, sigma_ref,
    step_s, latents_v, noise_v, gain_v, stream_v, patch_v, sems,
):
    parts, tokens, quarter = hidden_ref.shape
    channels = latents_v.shape[1]
    seq = lax.axis_index("seq")
    core = lax.axis_index("head") % 2
    small = [
        pltpu.make_async_copy(step_hbm, step_s, sems.at[0]),
        pltpu.make_async_copy(latents_hbm, latents_v, sems.at[1]),
        pltpu.make_async_copy(noise_hbm, noise_v, sems.at[2]),
    ]
    large = []
    for j in range(parts):
        span = pl.ds(j * quarter, quarter)
        large.append((
            pltpu.make_async_copy(stream_hbm.at[:, span], stream_v.at[j], sems.at[4 + 2 * j]),
            pltpu.make_async_copy(patch_hbm.at[:, span], patch_v.at[j], sems.at[5 + 2 * j]),
        ))
    gain_copy = pltpu.make_async_copy(gain_hbm, gain_v, sems.at[3])
    for copy in small:
        copy.start()
    for pair in large:
        for copy in pair:
            copy.start()
    gain_copy.start()
    for copy in small:
        copy.wait()
    level = (jnp.full((8, 128), step_s[0], jnp.int32).astype(F32) + 1.0) / 1000.0
    sigma = 5.0 * level / (1.0 + 4.0 * level)
    sigma_ref[...] = sigma
    sigma = jnp.broadcast_to(sigma[:1, :1], (tokens, channels))
    latents = latents_v[...].astype(F32)
    noisy = ((1.0 - sigma) * latents + sigma * noise_v[...].astype(F32)).astype(BF16)
    noisy_wide = noisy.astype(F32)
    gap_ref[...] = latents - noisy_wide
    message_ref[:, quarter:] = jnp.concatenate([noisy_wide, latents], axis=1).astype(BF16)
    squares = jnp.zeros((tokens, 128), F32)
    for j in range(parts):
        for copy in large[j]:
            copy.wait()
        hidden = (stream_v[j].astype(F32) + dot(noisy, patch_v[j])).astype(BF16)
        hidden_ref[j] = hidden
        wide = hidden.astype(F32)
        wide = wide * wide
        for i in range(quarter // 128):
            squares = squares + wide[:, i * 128 : (i + 1) * 128]
    mean = jnp.sum(squares, axis=1, keepdims=True) / (parts * quarter)
    inverse = lax.rsqrt(mean + 1e-06)
    inverse_ref[...] = jnp.broadcast_to(inverse, inverse_ref.shape)
    gain_copy.wait()
    target = (1 - seq) * 2 + core
    for j in range(parts):

        @pl.when(target == j)
        def _(j=j):
            gain = gain_v[j * quarter : (j + 1) * quarter][None, :]
            message_ref[:, :quarter] = (hidden_ref[j].astype(F32) * inverse * gain).astype(BF16)


def pick(index, x):
    half = x.shape[1] // 2
    return jnp.where(index == 0, x[:, :half], x[:, half:])


def partial_outputs(parts, seq, sent_ref, kept_ref):
    q, k, v, lora = parts
    columns = q.shape[1] // 2
    blocks = [*high_low(pick(1 - seq, q)), *high_low(pick(1 - seq, k))]
    blocks += [pick(1 - seq, v).astype(BF16), *high_low(lora)]
    for i, block in enumerate(blocks):
        sent_ref[:, i * columns : (i + 1) * columns] = block
    for i, block in enumerate((pick(seq, q), pick(seq, k), pick(seq, v), lora)):
        kept_ref[:, i * columns : (i + 1) * columns] = block


def own_kernel(
    hidden_ref, inverse_ref, gain_ref, q_ref, k_ref, v_ref, down_ref, output_ref, readout_ref,
    sent_ref, kept_ref, mix_ref, normed_v, mix_v,
):
    _, tokens, quarter = hidden_ref.shape
    seq = lax.axis_index("seq")
    inverse = inverse_ref[:, :1]
    for i in range(2):
        gain = gain_ref[pl.ds(2 * seq + i, 1), :]
        hidden = hidden_ref[2 * seq + i].astype(F32)
        normed_v[:, i * quarter : (i + 1) * quarter] = (hidden * inverse * gain).astype(BF16)
    normed = normed_v[...]
    parts = [dot(normed, w[...]) for w in (q_ref, k_ref, v_ref, down_ref)]
    partial_outputs(parts, seq, sent_ref, kept_ref)
    half_width = 2 * quarter
    readout = readout_ref[:, aligned(seq, half_width)]
    mix_v[...] = contract_final_axis(output_ref[...], readout)
    rows, channels = mix_ref.shape
    theirs = mix_v[aligned(1 - seq, rows), :]
    high = theirs.astype(BF16).astype(F32)
    both = jnp.concatenate([high, theirs - high], axis=1)
    sent_ref[:, -2 * channels :] = both.astype(BF16)
    mix_ref[...] = mix_v[aligned(seq, rows), :]


def side_kernel(hidden_ref, up_ref, readout_ref, readout_of_up_ref, base_ref):
    parts, tokens, quarter = hidden_ref.shape
    readout_of_up_ref[...] = contract_final_axis(up_ref[...], readout_ref[...]).astype(BF16)
    base = jnp.zeros(base_ref.shape, F32)
    for j in range(parts):
        base += contract_final_axis(
            hidden_ref[j], readout_ref[:, j * quarter : (j + 1) * quarter]
        )
    once = (lax.axis_index("group") == 0) & (lax.axis_index("head") == 0)
    base_ref[...] = jnp.where(once, base, 0.0)


def other_kernel(near_ref, far_ref, q_ref, k_ref, v_ref, down_ref, sent_ref, kept_ref):
    quarter = q_ref.shape[0] // 2
    core = lax.axis_index("head") % 2
    near = near_ref[:, :quarter]
    far = far_ref[:, :quarter]
    parts = [
        dot(near, w[aligned(core, quarter), :]) + dot(far, w[aligned(1 - core, quarter), :])
        for w in (q_ref, k_ref, v_ref, down_ref)
    ]
    partial_outputs(parts, lax.axis_index("seq"), sent_ref, kept_ref)


def finish(kept_ref, got_ref, up):
    tokens = kept_ref.shape[0]
    columns = up.shape[1]

    def got(i):
        return got_ref[:, i * columns : (i + 1) * columns].astype(F32)

    def kept(i):
        return kept_ref[:, i * columns : (i + 1) * columns]

    scale = HEAD_SIZE ** (-0.5)
    base = kept(0) + (got(0) + got(1))
    lora = (kept(3) + (got(5) + got(6))).astype(BF16)
    return (
        (base * scale).astype(BF16),
        ((base + dot(lora, up)) * scale).astype(BF16),
        (kept(1) + (got(2) + got(3))).astype(BF16),
        (kept(2) + got(4)).astype(BF16),
    )


def half_kernel(
    kept_ref, got_ref, up_ref, mix_ref, down_ref, readout_of_up_ref, near_ref,
    set_ref, mixes_ref, gap_ref,
):
    seq = lax.axis_index("seq")
    rows, channels = mix_ref.shape
    up = up_ref[:, aligned(seq, rows)]
    for i, block in enumerate(finish(kept_ref, got_ref, up)):
        set_ref[i] = block
    got = got_ref[:, -2 * channels :].astype(F32)
    mix_full = mix_ref[...] + (got[:, :channels] + swap_halves(got)[:, :channels])
    low_rank = dot(down_ref[aligned(seq, rows), :], readout_of_up_ref[...])
    mix = mix_full.astype(BF16).astype(F32)
    fake = (mix_full + low_rank).astype(BF16).astype(F32)
    mixes_ref[0] = jnp.concatenate([mix, -mix], axis=1).astype(BF16)
    mixes_ref[1] = jnp.concatenate([jnp.zeros_like(fake), fake], axis=1).astype(BF16)
    pair = near_ref[:, -2 * channels :].astype(F32)
    gap_ref[...] = (swap_halves(pair) - pair)[:, :channels]


def attention_kernel(
    kept_ref, got_ref, up_ref, set_ref, mixes_ref, base_ref,
    sent_ref, stay_ref, sets_v, terms_v,
):
    seq = lax.axis_index("seq")
    core = lax.axis_index("head") % 2
    tokens, channels = base_ref.shape
    columns = set_ref.shape[2]
    up = up_ref[:, aligned(seq, columns)]
    for i, block in enumerate(finish(kept_ref, got_ref, up)):
        sets_v[i, :tokens] = block
        sets_v[i, tokens:] = set_ref[i]
    terms = jnp.zeros(terms_v.shape, F32)
    for start in range(0, columns, HEAD_SIZE):
        span = slice(start, start + HEAD_SIZE)
        keys, values = sets_v[2, :, span], sets_v[3, :, span]
        for kind in range(2):
            scores = contract_final_axis(sets_v[kind, :, span], keys)
            top = jnp.max(scores, axis=1, keepdims=True)
            probs = jnp.exp(scores - top)
            mass = jnp.sum(probs, axis=1, keepdims=True)
            attn = (dot(probs.astype(BF16), values) / mass).astype(BF16)
            terms = terms + dot(attn, mixes_ref[kind, span, :])
    terms_v[...] = terms
    terms_v[:tokens, :channels] = terms[:tokens, :channels] + base_ref[...]
    share = tokens // 2
    sent_ref[:share] = terms_v[aligned(1 - core, share), :]
    sent_ref[share:] = terms_v[aligned(3 - core, share), :]
    stay_ref[:share] = terms_v[aligned(core, share), :]
    stay_ref[share:] = terms_v[aligned(2 + core, share), :]


def pack_kernel(stay_ref, got_ref, same_ref, cross_ref):
    share = stay_ref.shape[0] // 2
    mine = stay_ref[:share] + got_ref[:share]
    theirs = stay_ref[share:] + got_ref[share:]
    half = share // 2
    same_ref[:share] = mine
    same_ref[share:] = fold(theirs[:half], swap_halves(theirs[half:]))
    cross_ref[:share] = theirs
    cross_ref[share:] = fold(mine[:half], swap_halves(mine[half:]))


def error_kernel(*refs):
    *parts, gap_own_ref, gap_other_ref, sigma_ref, packet_ref = refs
    parts = [ref[...] for ref in parts]
    while len(parts) > 1:
        parts = [a + b for a, b in zip(parts[::2], parts[1::2])]
    total = parts[0]
    core = lax.axis_index("head") % 2
    tokens, channels = gap_own_ref.shape
    share = tokens // 2
    half = share // 2
    sigma = sigma_ref[:1, :1]
    own = total[:share]
    gap = gap_other_ref[aligned(core, share), :]
    folded = total[share:]
    error = jnp.abs(gap_own_ref[aligned(core, share), :] + sigma * own[:, :channels])
    low = jnp.abs(gap[:half] + sigma * folded[:, :channels])
    high = jnp.abs(gap[half:] + sigma * swap_halves(folded)[:, :channels])
    error = error[:half] + error[half:] + low + high
    packet_ref[:half] = fold(swap_halves(own[:half]), own[half:])
    packet_ref[half:] = jnp.full((8, 2 * channels), jnp.sum(error), F32)


def last_kernel(mine_ref, theirs_ref, sigma_ref, out_ref):
    core = lax.axis_index("head") % 2
    tokens, channels = out_ref.shape
    share = tokens // 2
    half = share // 2
    weight = (mine_ref[half:] + theirs_ref[half:]) / (2 * tokens * channels)
    factor = (-sigma_ref[...] / weight)[:1, :1]
    for ref, index in ((mine_ref, core), (theirs_ref, 1 - core)):
        packet = ref[:half] * factor
        both = jnp.concatenate([packet, swap_halves(packet)], axis=0)
        out_ref[aligned(index, share), :] = both[:, :channels]


def paired_local(
    sizes,
    latents,
    noise,
    step,
    stream,
    patch_embed_weight,
    prenorm_gain_vector,
    query_matrix,
    key_matrix,
    value_matrix,
    output_matrix,
    velocity_readout_weight,
    adapter_query_down,
    adapter_query_up,
    adapter_output_down,
    adapter_output_up,
):
    groups, _, heads = sizes
    tokens, channels = latents.shape
    half_width, local_columns = query_matrix.shape
    quarter = half_width // 2
    columns = local_columns // 2
    rank = adapter_query_down.shape[1]
    share = tokens // 2
    to_x = pairs((2,), lambda s: (s ^ 1,))
    to_core = pairs((heads,), lambda h: (h ^ 1,))
    to_y = pairs((heads,), lambda h: (h ^ 2,))
    to_xy = pairs((2, heads), lambda s, h: (s ^ 1, h ^ 2))
    weights = (query_matrix, key_matrix, value_matrix, adapter_query_down)
    partial_flops = 2 * tokens * half_width * (3 * local_columns + rank)

    copies = 4 + 2 * 4
    message, hidden, inverse, gap_own, sigma = run(
        first_kernel,
        [
            ((tokens, quarter + 2 * channels), BF16),
            ((4, tokens, quarter), BF16),
            ((tokens, 128), F32),
            ((tokens, channels), F32),
            ((8, 128), F32),
        ],
        (step, latents, noise, prenorm_gain_vector, stream, patch_embed_weight),
        [HBM] * 6,
        [
            pltpu.SMEM((1,), jnp.int32),
            pltpu.VMEM((tokens, channels), BF16),
            pltpu.VMEM((tokens, channels), BF16),
            pltpu.VMEM((4 * quarter,), F32),
            pltpu.VMEM((4, tokens, quarter), BF16),
            pltpu.VMEM((4, channels, quarter), BF16),
            pltpu.SemaphoreType.DMA((copies,)),
        ],
    )
    near = lax.ppermute(message, "seq", to_x)
    own_sent, own_kept, mix_part = run(
        own_kernel,
        [
            ((tokens, 7 * columns + 2 * channels), BF16),
            ((tokens, 4 * columns), F32),
            ((columns, channels), F32),
        ],
        (
            hidden, inverse, prenorm_gain_vector.reshape(4, quarter), *weights,
            output_matrix, velocity_readout_weight,
        ),
        scratch=[
            pltpu.VMEM((tokens, half_width), BF16),
            pltpu.VMEM((local_columns, channels), F32),
        ],
        flops=partial_flops,
    )
    own_got = lax.ppermute(own_sent, "seq", to_x)
    readout_of_up, base = run(
        side_kernel,
        [((rank, channels), BF16), ((tokens, channels), F32)],
        (hidden, adapter_output_up, velocity_readout_weight),
        flops=8 * tokens * half_width * channels,
    )
    far = lax.ppermute(near, "head", to_core)
    other_sent, other_kept = run(
        other_kernel,
        [((tokens, 7 * columns), BF16), ((tokens, 4 * columns), F32)],
        (near, far, *weights),
        flops=partial_flops,
    )
    other_got = lax.ppermute(other_sent, "seq", to_x)
    half_set, mixes, gap_other = run(
        half_kernel,
        [
            ((4, tokens, columns), BF16),
            ((2, columns, 2 * channels), BF16),
            ((tokens, channels), F32),
        ],
        (
            other_kept, own_got, adapter_query_up, mix_part,
            adapter_output_down, readout_of_up, near,
        ),
    )
    sent, stay = run(
        attention_kernel,
        [((tokens, 2 * channels), F32)] * 2,
        (own_kept, other_got, adapter_query_up, half_set, mixes, base),
        scratch=[
            pltpu.VMEM((4, 2 * tokens, columns), BF16),
            pltpu.VMEM((2 * tokens, 2 * channels), F32),
        ],
    )

    got = lax.ppermute(sent, "head", to_core)
    packed = ((share + share // 2, 2 * channels), F32)
    same, cross = run(pack_kernel, [packed, packed], (stay, got))
    from_x = lax.ppermute(cross, "seq", to_x)
    from_y = lax.ppermute(same, "head", to_y)
    from_xy = lax.ppermute(cross, ("seq", "head"), to_xy)
    total = (same + from_y) + (from_x + from_xy)
    totals = [total] + [
        lax.ppermute(total, "group", pairs((groups,), lambda g, k=k: (g ^ k,)))
        for k in range(1, groups)
    ]
    (packet,) = run(
        error_kernel,
        [((share // 2 + 8, 2 * channels), F32)],
        (*totals, gap_own, gap_other, sigma),
    )
    answer = lax.ppermute(packet, "head", to_core)
    (out,) = run(last_kernel, [((tokens, channels), F32)], (packet, answer, sigma))
    return out


def gathered_local(
    latents,
    noise,
    step,
    stream,
    patch_embed_weight,
    prenorm_gain_vector,
    query_matrix,
    key_matrix,
    value_matrix,
    output_matrix,
    velocity_readout_weight,
    adapter_query_down,
    adapter_query_up,
    adapter_output_down,
    adapter_output_up,
):
    tokens = latents.shape[0]
    width = query_matrix.shape[1]
    local_heads = width // HEAD_SIZE
    channels = velocity_readout_weight.shape[0]
    sigma = noise_level(step)
    noisy = (
        (1.0 - sigma) * latents.astype(F32) + sigma * noise.astype(F32)
    ).astype(BF16)
    hidden = (stream.astype(F32) + dot(noisy, patch_embed_weight)).astype(BF16)
    hidden_wide = hidden.astype(F32)
    normed = (
        hidden_wide
        * lax.rsqrt(jnp.mean(hidden_wide * hidden_wide, axis=-1, keepdims=True) + 1e-06)
        * prenorm_gain_vector
    ).astype(BF16)
    base_query, keys, values, lora_hidden = (
        dot(normed, lax.all_gather(piece, "seq", axis=0, tiled=True))
        for piece in (query_matrix, key_matrix, value_matrix, adapter_query_down)
    )
    scale = HEAD_SIZE ** (-0.5)
    lora_delta = dot(lora_hidden.astype(BF16), adapter_query_up)
    queries = (base_query * scale).astype(BF16)
    fake_queries = ((base_query + lora_delta) * scale).astype(BF16)
    both_sets = jnp.stack([queries, fake_queries]).reshape(2, tokens, local_heads, HEAD_SIZE)
    key_rows = lax.all_gather(keys.astype(BF16), "seq", axis=0, tiled=True)
    value_rows = lax.all_gather(values.astype(BF16), "seq", axis=0, tiled=True)
    key_rows = key_rows.reshape(-1, local_heads, HEAD_SIZE)
    value_rows = value_rows.reshape(-1, local_heads, HEAD_SIZE)
    scores = jnp.einsum("sthd,khd->shtk", both_sets, key_rows, preferred_element_type=F32)
    weights = jnp.exp(scores - jnp.max(scores, axis=-1, keepdims=True))
    mass = jnp.sum(weights, axis=-1)
    added = jnp.einsum(
        "shtk,khd->sthd", weights.astype(BF16), value_rows, preferred_element_type=F32
    )
    attn = (added / mass.transpose(0, 2, 1)[..., None]).astype(BF16).reshape(2, tokens, width)
    columns = output_matrix.shape[1]
    readout_part = columns_of(velocity_readout_weight, lax.axis_index("seq"), columns)
    mix_full = lax.psum(contract_final_axis(output_matrix, readout_part), "seq")
    lora_readout = contract_final_axis(adapter_output_up, velocity_readout_weight).astype(BF16)
    fake_mix = (mix_full + dot(adapter_output_down, lora_readout)).astype(BF16)
    real_sum, fake_sum = lax.psum(
        (dot(attn[0], mix_full.astype(BF16)), dot(attn[1], fake_mix)), ("group", "head")
    )
    base = contract_final_axis(hidden, velocity_readout_weight)
    noisy_wide = noisy.astype(F32)
    x0_real = noisy_wide - sigma * (base + real_sum)
    x0_fake = noisy_wide - sigma * (base + fake_sum)
    local_error = jnp.sum(jnp.abs(latents.astype(F32) - x0_real))
    weight = lax.psum(local_error, "seq") / (tokens * lax.axis_size("seq") * channels)
    return (x0_fake - x0_real) / weight


def solution(mesh):
    sizes = tuple(mesh.shape[name] for name in ("group", "seq", "head"))

    def local(*args):
        query_columns = args[6].shape[1]
        power = sizes[0] & (sizes[0] - 1) == 0
        paired = sizes[1] == 2 and sizes[2] == 4 and power
        if paired and (query_columns // HEAD_SIZE) % 2 == 0:
            return paired_local(sizes, *args)
        return gathered_local(*args)

    split = ("group", "head")
    in_specs = (
        P("seq", None),
        P("seq", None),
        P(),
        P("seq", None),
        P(),
        P(),
        P("seq", split),
        P("seq", split),
        P("seq", split),
        P(split, "seq"),
        P(),
        P("seq", None),
        P(None, split),
        P(split, None),
        P(),
    )
    return jax.shard_map(
        local, mesh=mesh, in_specs=in_specs, out_specs=P("seq", None), check_vma=False
    )
```

time: 80.6 us -> 60.2 us (0.75)
  matrix products: 16.9 us -> 0 us
  other arithmetic: 8.87 us -> 0.01 us
  Pallas kernels: 0 us -> 8.48 us
  local copies, waits for them, and re-layouts: 6.74 us -> 10.6 us
  waiting for transfers between devices: 29.2 us -> 26.4 us
  between operations: 3.28 us -> 0.94 us
  starting transfers between devices: 14.9 us -> 13.3 us
    dot_general x20 -> x0, matrix products: 16.9 us -> none  [the longest x16 12.1 us: dot(): return jnp.dot(left, right, preferred_element_type=F32)]
    pallas_call x0 -> x9, Pallas kernels: none -> 8.48 us  [run(): pl.pallas_call(kernel, out_shape=shapes, in_specs=specs or [VMEM] * len(a...]
    unnamed x38 -> x28, local copies, waits for them, and re-layouts: 2.85 us -> 9.85 us
    convert_element_type x5 -> x0, other arithmetic: 6.34 us -> none  [the longest x1 3.25 us: paired_local(): normed = (hidden_wide * lax.rsqrt(jnp.mean(hidden_wide * hidden_wide, axi...]
    ppermute x1, waiting for transfers between devices: 2.55 us -> 0.13 us  [paired_local(): from_x = lax.ppermute(cross, 'seq', to_x)]
    concatenate x1 -> x0, local copies, waits for them, and re-layouts: 1.63 us -> none  [payload(): return jnp.concatenate(blocks, axis=1)]
    slice x9 -> x0, local copies, waits for them, and re-layouts: 1.62 us -> none  [the longest x2 0.77 us: paired_local(): terms_oth = jnp.concatenate([real[tokens:], delta[tokens:]], axis=1)]
    ppermute x3, starting transfers between devices: 6.57 us -> 5.22 us  [the longest x1 3.03 us: paired_local(): near = lax.ppermute(message, 'seq', to_x)]
  transfers between devices with their start and end apart: 12 -> 12, of which waited for: 12 -> 10; matrix products, arithmetic and copies ran while one was open for 6% -> 0% of each run, Pallas kernels for 0% -> 9%
where the time goes in v2:
time: 60.2 us; the launch traced here: 59.7 us
  waiting for transfers between devices  26.4 us (44%)
  starting transfers between devices  13.3 us (22%)
  local copies, waits for them, and re-layouts  10.6 us (18%)
  Pallas kernels  8.48 us (14%)
  between operations  0.94 us (2%)
    unnamed x28, local copies, waits for them, and re-layouts  9.85 us
    ppermute x1, waiting for transfers between devices, paired_local(): near = lax.ppermute(message, 'seq', to_x)  8.52 us
    pallas_call x9, Pallas kernels, run(): pl.pallas_call(kernel, out_shape=shapes, in_specs=specs or [VMEM] * len(a...  8.48 us
    ppermute x3, starting transfers between devices, paired_local(): lax.ppermute(total, 'group', pairs((groups,), lambda g, k=k: (g ^ k,)))  4.45 us
    ppermute x1, waiting for transfers between devices, paired_local(): own_got = lax.ppermute(own_sent, 'seq', to_x)  4.23 us
    ppermute x3, waiting for transfers between devices, paired_local(): lax.ppermute(total, 'group', pairs((groups,), lambda g, k=k: (g ^ k,)))  4.21 us
    ppermute x1, waiting for transfers between devices, paired_local(): other_got = lax.ppermute(other_sent, 'seq', to_x)  3.22 us
    ppermute x1, waiting for transfers between devices, paired_local(): from_xy = lax.ppermute(cross, ('seq', 'head'), to_xy)  3.07 us
  transfers between devices with their start and end apart: 12, of which 10 were waited for; matrix products, arithmetic and copies ran while one was open for 0% of the time, Pallas kernels for 9%

profile of v2, /device:TPU:0, one launch (start us, length us, event | category | flops | bytes accessed | tf_op | source)
XLA Modules:
  0.0 59.7 jit_solution(6856514240435181316)
XLA Ops:
  0.8 0.8 %copy.16.latents_hbm = bf16[128,64]{1,0:T(8,128)(2,1)S(1)} copy(bf16[128,64]{0,1:T(8,128)(2,1)} %param.15) | data formatting | bytes 32768 | tf_op args[0]
  1.6 0.8 %copy.17.noise_hbm = bf16[128,64]{1,0:T(8,128)(2,1)S(1)} copy(bf16[128,64]{0,1:T(8,128)(2,1)} %param.16) | data formatting | bytes 32768 | tf_op args[1]
  2.5 1.3 %copy-done.7 = bf16[128,5120]{1,0:T(8,128)(2,1)S(1)} copy-done((bf16[128,5120]{1,0:T(8,128)(2,1)S(1)}, bf16[128,5120]{1,0:T(8,128)(2,1)}, u32[]{:S(2)}) %copy-start.7) | copy-done | bytes 1310744
  3.8 1.1 %copy-done.8 = bf16[64,5120]{1,0:T(8,128)(2,1)S(1)} copy-done((bf16[64,5120]{1,0:T(8,128)(2,1)S(1)}, bf16[64,5120]{1,0:T(8,128)(2,1)}, u32[]{:S(2)}) %copy-start.8) | copy-done | bytes 655384
  4.9 0.7 %copy-done.10 = f32[5120]{0:T(1024)S(1)} copy-done((f32[5120]{0:T(1024)S(1)}, f32[5120]{0:T(1024)}, u32[]{:S(2)}) %copy-start.10) | copy-done | bytes 20504
  5.6 1.9 %shard_map.145 = (bf16[128,1408]{1,0:T(8,128)(2,1)S(1)}, bf16[4,128,1280]{2,1,0:T(8,128)(2,1)S(1)}, f32[128,128]{1,0:T(8,128)S(1)}, f32[128,64]{1,0:T(8,128)S(1)}, f32[8,128]{1,0:T(8,128)S(1)}) custom-call(s32[1]{0:T(128)S(6)} %copy.19.step_hbm, bf16[128,64]{1,0:T(8,128)(2,1)S(1)} %copy.16.latents_hbm, bf16[128,64]{1,0:T(8,128)(2,1)S(1)} %copy.17.noise_hbm, ...), custom_call_target="tpu_custom_call" | custom-call | bytes 3792900 | tf_op jit(solution)/shard_map/pallas_call | solution.py:56
  7.5 3.0 %collective-permute-start = (bf16[128,1408]{1,0:T(8,128)(2,1)S(1)}, bf16[128,1408]{1,0:T(8,128)(2,1)}, u32[]{:S(2)}, u32[]{:S(2)}) collective-permute-start(bf16[128,1408]{1,0:T(8,128)(2,1)S(1)} %get-tuple-element.27), channel_id=1, source_target_pairs={{0,4},{4,0},{1,5},{5,1},{2,6},{6,2},{3,7},{7,3},{8,12},{12,8},{9,1... | collective-permute-start | bytes 1081352 | tf_op jit(solution)/shard_map/ppermute | solution.py:385
  10.5 8.5 %collective-permute-done.near_ref = bf16[128,1408]{1,0:T(8,128)(2,1)} collective-permute-done((bf16[128,1408]{1,0:T(8,128)(2,1)S(1)}, bf16[128,1408]{1,0:T(8,128)(2,1)}, u32[]{:S(2)}, u32[]{:S(2)}) %collective-permute-start) | collective-permute-done | bytes 360480 | tf_op jit(solution)/shard_map/ppermute | solution.py:385
  19.1 1.3 %copy-done.1 = bf16[2560,256]{1,0:T(8,128)(2,1)S(1)} copy-done((bf16[2560,256]{1,0:T(8,128)(2,1)S(1)}, bf16[2560,256]{1,0:T(8,128)(2,1)}, u32[]{:S(2)}) %copy-start.1) | copy-done | bytes 1310744
  20.4 1.3 %copy-done.2 = bf16[2560,256]{1,0:T(8,128)(2,1)S(1)} copy-done((bf16[2560,256]{1,0:T(8,128)(2,1)S(1)}, bf16[2560,256]{1,0:T(8,128)(2,1)}, u32[]{:S(2)}) %copy-start.2) | copy-done | bytes 1310744
  21.7 1.1 %copy-done.4 = bf16[2560,128]{1,0:T(8,128)(2,1)S(1)} copy-done((bf16[2560,128]{1,0:T(8,128)(2,1)S(1)}, bf16[2560,128]{1,0:T(8,128)(2,1)}, u32[]{:S(2)}) %copy-start.4) | copy-done | bytes 655384
  22.8 1.3 %copy-done.5 = bf16[256,2560]{1,0:T(8,128)(2,1)S(1)} copy-done((bf16[256,2560]{1,0:T(8,128)(2,1)S(1)}, bf16[256,2560]{1,0:T(8,128)(2,1)}, u32[]{:S(2)}) %copy-start.5) | copy-done | bytes 1310744
  24.1 1.4 %shard_map.146 = (bf16[128,1024]{1,0:T(8,128)(2,1)S(1)}, f32[128,512]{1,0:T(8,128)S(1)}, f32[128,64]{1,0:T(8,128)S(1)}) custom-call(bf16[4,128,1280]{2,1,0:T(8,128)(2,1)S(1)} %get-tuple-element.24.hidden_ref, f32[128,128]{1,0:T(8,128)S(1)} %get-tuple-element.25.inverse_ref, f32[4,1280]{1,0:T(4,128)S(1)} %reshape.3.gain_ref, bf16[2560,256]{1,0:T(8,128)(2,1)S(1)} %copy-done, ...), custom_call_target="tpu_custom_call" | custom-call | flops 587202560 | bytes 8507392 | tf_op jit(solution)/shard_map/pallas_call | solution.py:56
  25.5 1.8 %collective-permute-start.3 = (bf16[128,1024]{1,0:T(8,128)(2,1)S(1)}, bf16[128,1024]{1,0:T(8,128)(2,1)S(1)}, u32[]{:S(2)}, u32[]{:S(2)}) collective-permute-start(bf16[128,1024]{1,0:T(8,128)(2,1)S(1)} %get-tuple-element.30), channel_id=1, source_target_pairs={{0,4},{4,0},{1,5},{5,1},{2,6},{6,2},{3,7},{7,3},{8,12},{12,8},{9,1... | collective-permute-start | bytes 786440 | tf_op jit(solution)/shard_map/ppermute | solution.py:403
  27.3 2.0 %shard_map.147 = (bf16[128,896]{1,0:T(8,128)(2,1)S(1)}, f32[128,512]{1,0:T(8,128)S(1)}) custom-call(bf16[128,1408]{1,0:T(8,128)(2,1)} %collective-permute-done.near_ref, bf16[128,1408]{1,0:T(8,128)(2,1)} %collective-permute-done.1.far_ref, bf16[2560,256]{1,0:T(8,128)(2,1)S(1)} %copy-done, bf16[2560,256]{1,0:T(8,128)(2,1)S(1)} %copy-done.1, ...), custom_call_target="tpu_custom_call" | custom-call | flops 587202560 | bytes 5799936 | tf_op jit(solution)/shard_map/pallas_call | solution.py:56
  29.3 0.4 collective-permute-start.2
  29.7 0.8 %shard_map.148 = (bf16[128,64]{1,0:T(8,128)(2,1)S(1)}, f32[128,64]{1,0:T(8,128)S(1)}) custom-call(bf16[4,128,1280]{2,1,0:T(8,128)(2,1)S(1)} %get-tuple-element.24.hidden_ref, bf16[128,5120]{1,0:T(8,128)(2,1)S(1)} %copy-done.6, bf16[64,5120]{1,0:T(8,128)(2,1)S(1)} %copy-done.3), custom_call_target="tpu_custom_call" | custom-call | flops 167772160 | bytes 3325952 | tf_op jit(solution)/shard_map/pallas_call | solution.py:56
  30.5 4.2 %collective-permute-done.3.got_ref = bf16[128,1024]{1,0:T(8,128)(2,1)S(1)} collective-permute-done((bf16[128,1024]{1,0:T(8,128)(2,1)S(1)}, bf16[128,1024]{1,0:T(8,128)(2,1)S(1)}, u32[]{:S(2)}, u32[]{:S(2)}) %collective-permute-start.3) | collective-permute-done | bytes 262176 | tf_op jit(solution)/shard_map/ppermute | solution.py:403
  34.7 1.2 %shard_map.149 = (bf16[4,128,128]{2,1,0:T(8,128)(2,1)S(1)}, bf16[2,128,128]{2,1,0:T(8,128)(2,1)S(1)}, f32[128,64]{1,0:T(8,128)S(1)}) custom-call(f32[128,512]{1,0:T(8,128)S(1)} %get-tuple-element.29.kept_ref, bf16[128,1024]{1,0:T(8,128)(2,1)S(1)} %collective-permute-done.3.got_ref, bf16[128,256]{1,0:T(8,128)(2,1)S(1)} %copy-done.9, ...), custom_call_target="tpu_custom_call" | custom-call | bytes 1294336 | tf_op jit(solution)/shard_map/pallas_call | solution.py:56
  36.0 3.2 %collective-permute-done.2.got_ref = bf16[128,896]{1,0:T(8,128)(2,1)S(1)} collective-permute-done((bf16[128,896]{1,0:T(8,128)(2,1)S(1)}, bf16[128,896]{1,0:T(8,128)(2,1)S(1)}, u32[]{:S(2)}, u32[]{:S(2)}) %collective-permute-start.2) | collective-permute-done | bytes 229408 | tf_op jit(solution)/shard_map/ppermute | solution.py:417
  39.2 0.9 %shard_map.150 = (f32[128,128]{1,0:T(8,128)S(1)}, f32[128,128]{1,0:T(8,128)S(1)}) custom-call(f32[128,512]{1,0:T(8,128)S(1)} %get-tuple-element.26.kept_ref, bf16[128,896]{1,0:T(8,128)(2,1)S(1)} %collective-permute-done.2.got_ref, bf16[128,256]{1,0:T(8,128)(2,1)S(1)} %copy-done.9, bf16[4,128,128]{2,1,0:T(8,128)(2,1)S(1)} %get-tuple-element.33.set_ref, ...), custom_call_target="tpu_custom_call" | custom-call | bytes 917504 | tf_op jit(solution)/shard_map/pallas_call | solution.py:56
  40.1 1.2 %collective-permute-done.4.got_ref = f32[128,128]{1,0:T(8,128)S(1)} collective-permute-done((f32[128,128]{1,0:T(8,128)S(1)}, f32[128,128]{1,0:T(8,128)S(1)}, u32[]{:S(2)}, u32[]{:S(2)}) %collective-permute-start.4) | collective-permute-done | bytes 65568 | tf_op jit(solution)/shard_map/ppermute | solution.py:440
  41.4 1.8 %collective-permute-start.5 = (f32[96,128]{1,0:T(8,128)S(1)}, f32[96,128]{1,0:T(8,128)S(1)}, u32[]{:S(2)}, u32[]{:S(2)}) collective-permute-start(f32[96,128]{1,0:T(8,128)S(1)} %get-tuple-element.38), channel_id=1, source_target_pairs={{0,2},{1,3},{2,0},{3,1},{4,6},{5,7},{6,4},{7,5},{8,10},{9,11},{10,... | collective-permute-start | bytes 147464 | tf_op jit(solution)/shard_map/ppermute | solution.py:444
  43.2 1.4 %collective-permute-start.7 = (f32[96,128]{1,0:T(8,128)S(1)}, f32[96,128]{1,0:T(8,128)S(1)}, u32[]{:S(2)}, u32[]{:S(2)}) collective-permute-start(f32[96,128]{1,0:T(8,128)S(1)} %get-tuple-element.39), channel_id=1, source_target_pairs={{0,6},{1,7},{2,4},{3,5},{4,2},{5,3},{6,0},{7,1},{8,14},{9,15},{10,... | collective-permute-start | bytes 147464 | tf_op jit(solution)/shard_map/ppermute | solution.py:445
  45.0 0.6 %collective-permute-done.5 = f32[96,128]{1,0:T(8,128)S(1)} collective-permute-done((f32[96,128]{1,0:T(8,128)S(1)}, f32[96,128]{1,0:T(8,128)S(1)}, u32[]{:S(2)}, u32[]{:S(2)}) %collective-permute-start.5) | collective-permute-done | bytes 49184 | tf_op jit(solution)/shard_map/ppermute | solution.py:444
  45.6 3.1 %collective-permute-done.7 = f32[96,128]{1,0:T(8,128)S(1)} collective-permute-done((f32[96,128]{1,0:T(8,128)S(1)}, f32[96,128]{1,0:T(8,128)S(1)}, u32[]{:S(2)}, u32[]{:S(2)}) %collective-permute-start.7) | collective-permute-done | bytes 49184 | tf_op jit(solution)/shard_map/ppermute | solution.py:445
  48.8 3.7 %collective-permute-start.10 = (f32[96,128]{1,0:T(8,128)S(1)}, f32[96,128]{1,0:T(8,128)S(1)}, u32[]{:S(2)}, u32[]{:S(2)}) collective-permute-start(f32[96,128]{1,0:T(8,128)S(1)} %add_add_fusion.refs_0_), channel_id=1, source_target_pairs={{0,24},{8,16},{16,8},{24,0},{1,25},{9,17},{17,9},{25,1},{2,26},{10... | collective-permute-start | bytes 147464 | tf_op jit(solution)/shard_map/ppermute | solution.py:448
  52.4 0.8 %collective-permute-start.8 = (f32[96,128]{1,0:T(8,128)S(1)}, f32[96,128]{1,0:T(8,128)S(1)}, u32[]{:S(2)}, u32[]{:S(2)}) collective-permute-start(f32[96,128]{1,0:T(8,128)S(1)} %add_add_fusion.refs_0_), channel_id=1, source_target_pairs={{0,8},{8,0},{16,24},{24,16},{1,9},{9,1},{17,25},{25,17},{2,10},{10... | collective-permute-start | bytes 147464 | tf_op jit(solution)/shard_map/ppermute | solution.py:448
  53.2 1.7 %collective-permute-done.10.refs_3_ = f32[96,128]{1,0:T(8,128)S(1)} collective-permute-done((f32[96,128]{1,0:T(8,128)S(1)}, f32[96,128]{1,0:T(8,128)S(1)}, u32[]{:S(2)}, u32[]{:S(2)}) %collective-permute-start.10) | collective-permute-done | bytes 49184 | tf_op jit(solution)/shard_map/ppermute | solution.py:448
  55.0 2.5 %collective-permute-done.9.refs_2_ = f32[96,128]{1,0:T(8,128)S(1)} collective-permute-done((f32[96,128]{1,0:T(8,128)S(1)}, f32[96,128]{1,0:T(8,128)S(1)}, u32[]{:S(2)}, u32[]{:S(2)}) %collective-permute-start.9) | collective-permute-done | bytes 49184 | tf_op jit(solution)/shard_map/ppermute | solution.py:448
  57.7 1.2 %collective-permute-done.11.theirs_ref = f32[40,128]{1,0:T(8,128)S(1)} collective-permute-done((f32[40,128]{1,0:T(8,128)S(1)}, f32[40,128]{1,0:T(8,128)S(1)}, u32[]{:S(2)}, u32[]{:S(2)}) %collective-permute-start.11) | collective-permute-done | bytes 20512 | tf_op jit(solution)/shard_map/ppermute | solution.py:456
  59.0 0.7 %copy.18 = f32[128,64]{0,1:T(8,128)} copy(f32[128,64]{1,0:T(8,128)S(1)} %shard_map.153) | data formatting | bytes 65536 | tf_op jit(solution)/shard_map/pallas_call | solution.py:56
  (32 shorter events, 1.0 us)
Async XLA Ops:
  0.0 19.1 %copy-start.3 = (bf16[64,5120]{1,0:T(8,128)(2,1)S(1)}, bf16[64,5120]{1,0:T(8,128)(2,1)}, u32[]{:S(2)}) copy-start(bf16[64,5120]{1,0:T(8,128)(2,1)} %readout_ref.3) | copy-start | bytes 1966084
  0.0 19.1 %copy-start = (bf16[2560,256]{1,0:T(8,128)(2,1)S(1)}, bf16[2560,256]{1,0:T(8,128)(2,1)}, u32[]{:S(2)}) copy-start(bf16[2560,256]{1,0:T(8,128)(2,1)} %q_ref.3) | copy-start | bytes 3932164
  2.5 1.3 %copy-start.7 = (bf16[128,5120]{1,0:T(8,128)(2,1)S(1)}, bf16[128,5120]{1,0:T(8,128)(2,1)}, u32[]{:S(2)}) copy-start(bf16[128,5120]{1,0:T(8,128)(2,1)} %stream_hbm.1) | copy-start | bytes 3932164
  3.8 1.1 %copy-start.8 = (bf16[64,5120]{1,0:T(8,128)(2,1)S(1)}, bf16[64,5120]{1,0:T(8,128)(2,1)}, u32[]{:S(2)}) copy-start(bf16[64,5120]{1,0:T(8,128)(2,1)} %patch_hbm.1) | copy-start | bytes 1966084
  4.9 0.7 %copy-start.10 = (f32[5120]{0:T(1024)S(1)}, f32[5120]{0:T(1024)}, u32[]{:S(2)}) copy-start(f32[5120]{0:T(1024)} %gain_hbm.1) | copy-start | bytes 61444
  5.6 13.4 %copy-start.11 = (f32[5120]{0:T(1024)S(1)}, f32[5120]{0:T(1024)}, u32[]{:S(2)}) copy-start(f32[5120]{0:T(1024)} %gain_hbm.1) | copy-start | bytes 61444
  7.5 11.6 %collective-permute-start = (bf16[128,1408]{1,0:T(8,128)(2,1)S(1)}, bf16[128,1408]{1,0:T(8,128)(2,1)}, u32[]{:S(2)}, u32[]{:S(2)}) collective-permute-start(bf16[128,1408]{1,0:T(8,128)(2,1)S(1)} %get-tuple-element.27), channel_id=1, source_target_pairs={{0,4},{4,0},{1,5},{5,1},{2,6},{6,2},{3,7},{7,3},{8,12},{12,8},{9,1... | collective-permute-start | bytes 1081352 | tf_op jit(solution)/shard_map/ppermute | solution.py:385
  19.0 8.2 %collective-permute-start.1 = (bf16[128,1408]{1,0:T(8,128)(2,1)}, bf16[128,1408]{1,0:T(8,128)(2,1)}, u32[]{:S(2)}, u32[]{:S(2)}) collective-permute-start(bf16[128,1408]{1,0:T(8,128)(2,1)} %collective-permute-done.near_ref), channel_id=1, source_target_pairs={{0,1},{1,0},{2,3},{3,2},{4,5},{5,4},{6,7},{7,6},{8,9},{9,8},{10,11... | collective-permute-start | bytes 1081352 | tf_op jit(solution)/shard_map/ppermute | solution.py:410
  19.1 1.3 %copy-start.1 = (bf16[2560,256]{1,0:T(8,128)(2,1)S(1)}, bf16[2560,256]{1,0:T(8,128)(2,1)}, u32[]{:S(2)}) copy-start(bf16[2560,256]{1,0:T(8,128)(2,1)} %k_ref.3) | copy-start | bytes 3932164
  20.4 1.3 %copy-start.2 = (bf16[2560,256]{1,0:T(8,128)(2,1)S(1)}, bf16[2560,256]{1,0:T(8,128)(2,1)}, u32[]{:S(2)}) copy-start(bf16[2560,256]{1,0:T(8,128)(2,1)} %v_ref.3) | copy-start | bytes 3932164
  21.7 1.1 %copy-start.4 = (bf16[2560,128]{1,0:T(8,128)(2,1)S(1)}, bf16[2560,128]{1,0:T(8,128)(2,1)}, u32[]{:S(2)}) copy-start(bf16[2560,128]{1,0:T(8,128)(2,1)} %down_ref.4) | copy-start | bytes 1966084
  22.8 1.3 %copy-start.5 = (bf16[256,2560]{1,0:T(8,128)(2,1)S(1)}, bf16[256,2560]{1,0:T(8,128)(2,1)}, u32[]{:S(2)}) copy-start(bf16[256,2560]{1,0:T(8,128)(2,1)} %output_ref.1) | copy-start | bytes 3932164
  25.5 4.2 %copy-start.6 = (bf16[128,5120]{1,0:T(8,128)(2,1)S(1)}, bf16[128,5120]{1,0:T(8,128)(2,1)}, u32[]{:S(2)}) copy-start(bf16[128,5120]{1,0:T(8,128)(2,1)} %up_ref.3) | copy-start | bytes 3932164
  25.5 9.2 %collective-permute-start.3 = (bf16[128,1024]{1,0:T(8,128)(2,1)S(1)}, bf16[128,1024]{1,0:T(8,128)(2,1)S(1)}, u32[]{:S(2)}, u32[]{:S(2)}) collective-permute-start(bf16[128,1024]{1,0:T(8,128)(2,1)S(1)} %get-tuple-element.30), channel_id=1, source_target_pairs={{0,4},{4,0},{1,5},{5,1},{2,6},{6,2},{3,7},{7,3},{8,12},{12,8},{9,1... | collective-permute-start | bytes 786440 | tf_op jit(solution)/shard_map/ppermute | solution.py:403
  29.3 5.5 %copy-start.9 = (bf16[128,256]{1,0:T(8,128)(2,1)S(1)}, bf16[128,256]{1,0:T(8,128)(2,1)}, u32[]{:S(2)}) copy-start(bf16[128,256]{1,0:T(8,128)(2,1)} %up_ref.5) | copy-start | bytes 196612
  29.3 5.5 %copy-start.12 = (bf16[256,128]{1,0:T(8,128)(2,1)S(1)}, bf16[256,128]{1,0:T(8,128)(2,1)}, u32[]{:S(2)}) copy-start(bf16[256,128]{1,0:T(8,128)(2,1)} %down_ref.5) | copy-start | bytes 196612
  29.3 9.9 %collective-permute-start.2 = (bf16[128,896]{1,0:T(8,128)(2,1)S(1)}, bf16[128,896]{1,0:T(8,128)(2,1)S(1)}, u32[]{:S(2)}, u32[]{:S(2)}) collective-permute-start(bf16[128,896]{1,0:T(8,128)(2,1)S(1)} %get-tuple-element.28), channel_id=1, source_target_pairs={{0,4},{4,0},{1,5},{5,1},{2,6},{6,2},{3,7},{7,3},{8,12},{12,8},{9,1... | collective-permute-start | bytes 688136 | tf_op jit(solution)/shard_map/ppermute | solution.py:417
  40.0 1.3 %collective-permute-start.4 = (f32[128,128]{1,0:T(8,128)S(1)}, f32[128,128]{1,0:T(8,128)S(1)}, u32[]{:S(2)}, u32[]{:S(2)}) collective-permute-start(f32[128,128]{1,0:T(8,128)S(1)} %get-tuple-element.37), channel_id=1, source_target_pairs={{0,1},{1,0},{2,3},{3,2},{4,5},{5,4},{6,7},{7,6},{8,9},{9,8},{10,11... | collective-permute-start | bytes 196616 | tf_op jit(solution)/shard_map/ppermute | solution.py:440
  41.4 4.1 %collective-permute-start.5 = (f32[96,128]{1,0:T(8,128)S(1)}, f32[96,128]{1,0:T(8,128)S(1)}, u32[]{:S(2)}, u32[]{:S(2)}) collective-permute-start(f32[96,128]{1,0:T(8,128)S(1)} %get-tuple-element.38), channel_id=1, source_target_pairs={{0,2},{1,3},{2,0},{3,1},{4,6},{5,7},{6,4},{7,5},{8,10},{9,11},{10,... | collective-permute-start | bytes 147464 | tf_op jit(solution)/shard_map/ppermute | solution.py:444
  43.2 5.4 %collective-permute-start.7 = (f32[96,128]{1,0:T(8,128)S(1)}, f32[96,128]{1,0:T(8,128)S(1)}, u32[]{:S(2)}, u32[]{:S(2)}) collective-permute-start(f32[96,128]{1,0:T(8,128)S(1)} %get-tuple-element.39), channel_id=1, source_target_pairs={{0,6},{1,7},{2,4},{3,5},{4,2},{5,3},{6,0},{7,1},{8,14},{9,15},{10,... | collective-permute-start | bytes 147464 | tf_op jit(solution)/shard_map/ppermute | solution.py:445
  44.7 4.1 %collective-permute-start.6 = (f32[96,128]{1,0:T(8,128)S(1)}, f32[96,128]{1,0:T(8,128)S(1)}, u32[]{:S(2)}, u32[]{:S(2)}) collective-permute-start(f32[96,128]{1,0:T(8,128)S(1)} %get-tuple-element.39), channel_id=1, source_target_pairs={{0,4},{4,0},{1,5},{5,1},{2,6},{6,2},{3,7},{7,3},{8,12},{12,8},{9,1... | collective-permute-start | bytes 147464 | tf_op jit(solution)/shard_map/ppermute | solution.py:443
  48.8 6.2 %collective-permute-start.10 = (f32[96,128]{1,0:T(8,128)S(1)}, f32[96,128]{1,0:T(8,128)S(1)}, u32[]{:S(2)}, u32[]{:S(2)}) collective-permute-start(f32[96,128]{1,0:T(8,128)S(1)} %add_add_fusion.refs_0_), channel_id=1, source_target_pairs={{0,24},{8,16},{16,8},{24,0},{1,25},{9,17},{17,9},{25,1},{2,26},{10... | collective-permute-start | bytes 147464 | tf_op jit(solution)/shard_map/ppermute | solution.py:448
  52.4 5.0 %collective-permute-start.9 = (f32[96,128]{1,0:T(8,128)S(1)}, f32[96,128]{1,0:T(8,128)S(1)}, u32[]{:S(2)}, u32[]{:S(2)}) collective-permute-start(f32[96,128]{1,0:T(8,128)S(1)} %add_add_fusion.refs_0_), channel_id=1, source_target_pairs={{0,16},{8,24},{16,0},{24,8},{1,17},{9,25},{17,1},{25,9},{2,18},{10... | collective-permute-start | bytes 147464 | tf_op jit(solution)/shard_map/ppermute | solution.py:448
  52.4 5.0 %collective-permute-start.8 = (f32[96,128]{1,0:T(8,128)S(1)}, f32[96,128]{1,0:T(8,128)S(1)}, u32[]{:S(2)}, u32[]{:S(2)}) collective-permute-start(f32[96,128]{1,0:T(8,128)S(1)} %add_add_fusion.refs_0_), channel_id=1, source_target_pairs={{0,8},{8,0},{16,24},{24,16},{1,9},{9,1},{17,25},{25,17},{2,10},{10... | collective-permute-start | bytes 147464 | tf_op jit(solution)/shard_map/ppermute | solution.py:448
  57.6 1.3 %collective-permute-start.11 = (f32[40,128]{1,0:T(8,128)S(1)}, f32[40,128]{1,0:T(8,128)S(1)}, u32[]{:S(2)}, u32[]{:S(2)}) collective-permute-start(f32[40,128]{1,0:T(8,128)S(1)} %shard_map.152.mine_ref), channel_id=1, source_target_pairs={{0,1},{1,0},{2,3},{3,2},{4,5},{5,4},{6,7},{7,6},{8,9},{9,8},{10,11... | collective-permute-start | bytes 61448 | tf_op jit(solution)/shard_map/ppermute | solution.py:456

commit v3 on v2

--- a/solution.py
+++ b/solution.py
@@ -6,6 +6,7 @@
 from jax.experimental import pallas as pl
 from jax.experimental.pallas import tpu as pltpu
 from jax.sharding import PartitionSpec as P
+
 
 HEAD_SIZE = 128
 F32 = jnp.float32
@@ -83,27 +84,25 @@
 
 
 def first_kernel(
-    step_hbm, latents_hbm, noise_hbm, gain_hbm, stream_hbm, patch_hbm,
-    message_ref, hidden_ref, inverse_ref, gap_ref, sigma_ref,
-    step_s, latents_v, noise_v, gain_v, stream_v, patch_v, sems,
+    step_ref, latents_hbm, noise_hbm, gain_hbm, stream_hbm, patch_hbm,
+    message_ref, hidden_ref, inverse_ref, gap_ref,
+    latents_v, noise_v, gain_v, stream_v, patch_v, sems,
 ):
     parts, tokens, quarter = hidden_ref.shape
-    channels = latents_v.shape[1]
     seq = lax.axis_index("seq")
     core = lax.axis_index("head") % 2
     small = [
-        pltpu.make_async_copy(step_hbm, step_s, sems.at[0]),
-        pltpu.make_async_copy(latents_hbm, latents_v, sems.at[1]),
-        pltpu.make_async_copy(noise_hbm, noise_v, sems.at[2]),
+        pltpu.make_async_copy(latents_hbm, latents_v, sems.at[0]),
+        pltpu.make_async_copy(noise_hbm, noise_v, sems.at[1]),
     ]
     large = []
     for j in range(parts):
         span = pl.ds(j * quarter, quarter)
         large.append((
-            pltpu.make_async_copy(stream_hbm.at[:, span], stream_v.at[j], sems.at[4 + 2 * j]),
-            pltpu.make_async_copy(patch_hbm.at[:, span], patch_v.at[j], sems.at[5 + 2 * j]),
+            pltpu.make_async_copy(stream_hbm.at[:, span], stream_v.at[j], sems.at[3 + 2 * j]),
+            pltpu.make_async_copy(patch_hbm.at[:, span], patch_v.at[j], sems.at[4 + 2 * j]),
         ))
-    gain_copy = pltpu.make_async_copy(gain_hbm, gain_v, sems.at[3])
+    gain_copy = pltpu.make_async_copy(gain_hbm, gain_v, sems.at[2])
     for copy in small:
         copy.start()
     for pair in large:
@@ -112,20 +111,19 @@
     gain_copy.start()
     for copy in small:
         copy.wait()
-    level = (jnp.full((8, 128), step_s[0], jnp.int32).astype(F32) + 1.0) / 1000.0
-    sigma = 5.0 * level / (1.0 + 4.0 * level)
-    sigma_ref[...] = sigma
-    sigma = jnp.broadcast_to(sigma[:1, :1], (tokens, channels))
+    level = (jnp.full((8, 128), step_ref[0], jnp.int32).astype(F32) + 1.0) / 1000.0
+    sigma = (5.0 * level / (1.0 + 4.0 * level))[:1, :1]
     latents = latents_v[...].astype(F32)
     noisy = ((1.0 - sigma) * latents + sigma * noise_v[...].astype(F32)).astype(BF16)
-    noisy_wide = noisy.astype(F32)
-    gap_ref[...] = latents - noisy_wide
-    message_ref[:, quarter:] = jnp.concatenate([noisy_wide, latents], axis=1).astype(BF16)
+    gap_ref[...] = (latents - noisy.astype(F32)) / sigma
     squares = jnp.zeros((tokens, 128), F32)
     for j in range(parts):
         for copy in large[j]:
             copy.wait()
-        hidden = (stream_v[j].astype(F32) + dot(noisy, patch_v[j])).astype(BF16)
+        embedded = lax.dot_general(
+            noisy, patch_v[j], (((0,), (0,)), ((), ())), preferred_element_type=F32
+        )
+        hidden = (stream_v[j].astype(F32) + embedded).astype(BF16)
         hidden_ref[j] = hidden
         wide = hidden.astype(F32)
         wide = wide * wide
@@ -141,7 +139,7 @@
         @pl.when(target == j)
         def _(j=j):
             gain = gain_v[j * quarter : (j + 1) * quarter][None, :]
-            message_ref[:, :quarter] = (hidden_ref[j].astype(F32) * inverse * gain).astype(BF16)
+            message_ref[...] = (hidden_ref[j].astype(F32) * inverse * gain).astype(BF16)
 
 
 def pick(index, x):
@@ -164,7 +162,7 @@
     hidden_ref, inverse_ref, gain_ref, q_ref, k_ref, v_ref, down_ref, output_ref, readout_ref,
     sent_ref, kept_ref, mix_ref, normed_v, mix_v,
 ):
-    _, tokens, quarter = hidden_ref.shape
+    _, _, quarter = hidden_ref.shape
     seq = lax.axis_index("seq")
     inverse = inverse_ref[:, :1]
     for i in range(2):
@@ -185,23 +183,23 @@
     mix_ref[...] = mix_v[aligned(seq, rows), :]
 
 
-def side_kernel(hidden_ref, up_ref, readout_ref, readout_of_up_ref, base_ref):
-    parts, tokens, quarter = hidden_ref.shape
+def side_kernel(hidden_ref, up_ref, readout_ref, gap_ref, readout_of_up_ref, base_ref):
+    parts, _, quarter = hidden_ref.shape
     readout_of_up_ref[...] = contract_final_axis(up_ref[...], readout_ref[...]).astype(BF16)
-    base = jnp.zeros(base_ref.shape, F32)
+    base = gap_ref[...]
     for j in range(parts):
         base += contract_final_axis(
-            hidden_ref[j], readout_ref[:, j * quarter : (j + 1) * quarter]
+            readout_ref[:, j * quarter : (j + 1) * quarter], hidden_ref[j]
         )
     once = (lax.axis_index("group") == 0) & (lax.axis_index("head") == 0)
-    base_ref[...] = jnp.where(once, base, 0.0)
+    base_ref[...] = jnp.where(once, base, 0.0).T
 
 
 def other_kernel(near_ref, far_ref, q_ref, k_ref, v_ref, down_ref, sent_ref, kept_ref):
     quarter = q_ref.shape[0] // 2
     core = lax.axis_index("head") % 2
-    near = near_ref[:, :quarter]
-    far = far_ref[:, :quarter]
+    near = near_ref[...]
+    far = far_ref[...]
     parts = [
         dot(near, w[aligned(core, quarter), :]) + dot(far, w[aligned(1 - core, quarter), :])
         for w in (q_ref, k_ref, v_ref, down_ref)
@@ -210,7 +208,6 @@
 
 
 def finish(kept_ref, got_ref, up):
-    tokens = kept_ref.shape[0]
     columns = up.shape[1]
 
     def got(i):
@@ -231,8 +228,8 @@
 
 
 def half_kernel(
-    kept_ref, got_ref, up_ref, mix_ref, down_ref, readout_of_up_ref, near_ref,
-    set_ref, mixes_ref, gap_ref,
+    kept_ref, got_ref, up_ref, mix_ref, down_ref, readout_of_up_ref,
+    set_ref, mixes_ref,
 ):
     seq = lax.axis_index("seq")
     rows, channels = mix_ref.shape
@@ -246,8 +243,6 @@
     fake = (mix_full + low_rank).astype(BF16).astype(F32)
     mixes_ref[0] = jnp.concatenate([mix, -mix], axis=1).astype(BF16)
     mixes_ref[1] = jnp.concatenate([jnp.zeros_like(fake), fake], axis=1).astype(BF16)
-    pair = near_ref[:, -2 * channels :].astype(F32)
-    gap_ref[...] = (swap_halves(pair) - pair)[:, :channels]
 
 
 def attention_kernel(
@@ -287,45 +282,39 @@
     mine = stay_ref[:share] + got_ref[:share]
     theirs = stay_ref[share:] + got_ref[share:]
     half = share // 2
-    same_ref[:share] = mine
-    same_ref[share:] = fold(theirs[:half], swap_halves(theirs[half:]))
-    cross_ref[:share] = theirs
-    cross_ref[share:] = fold(mine[:half], swap_halves(mine[half:]))
+    same_ref[:share] = mine.astype(BF16)
+    same_ref[share:] = fold(theirs[:half], swap_halves(theirs[half:])).astype(BF16)
+    cross_ref[:share] = theirs.astype(BF16)
+    cross_ref[share:] = fold(mine[:half], swap_halves(mine[half:])).astype(BF16)
 
 
 def error_kernel(*refs):
-    *parts, gap_own_ref, gap_other_ref, sigma_ref, packet_ref = refs
-    parts = [ref[...] for ref in parts]
+    *parts, packet_ref = refs
+    parts = [ref[...].astype(F32) for ref in parts]
     while len(parts) > 1:
         parts = [a + b for a, b in zip(parts[::2], parts[1::2])]
     total = parts[0]
+    half = packet_ref.shape[0] - 8
+    share = 2 * half
+    own = jnp.abs(total[:half]) + jnp.abs(total[half:share])
+    own = fold(own, jnp.zeros_like(own)) + jnp.abs(total[share:])
+    packet_ref[:half] = fold(swap_halves(total[:half]), total[half:share])
+    packet_ref[half:] = jnp.full((8, packet_ref.shape[1]), jnp.sum(own), F32)
+
+
+def last_kernel(mine_ref, theirs_ref, out_ref, both_v):
     core = lax.axis_index("head") % 2
-    tokens, channels = gap_own_ref.shape
-    share = tokens // 2
-    half = share // 2
-    sigma = sigma_ref[:1, :1]
-    own = total[:share]
-    gap = gap_other_ref[aligned(core, share), :]
-    folded = total[share:]
-    error = jnp.abs(gap_own_ref[aligned(core, share), :] + sigma * own[:, :channels])
-    low = jnp.abs(gap[:half] + sigma * folded[:, :channels])
-    high = jnp.abs(gap[half:] + sigma * swap_halves(folded)[:, :channels])
-    error = error[:half] + error[half:] + low + high
-    packet_ref[:half] = fold(swap_halves(own[:half]), own[half:])
-    packet_ref[half:] = jnp.full((8, 2 * channels), jnp.sum(error), F32)
-
-
-def last_kernel(mine_ref, theirs_ref, sigma_ref, out_ref):
-    core = lax.axis_index("head") % 2
-    tokens, channels = out_ref.shape
+    channels, tokens = out_ref.shape
     share = tokens // 2
     half = share // 2
     weight = (mine_ref[half:] + theirs_ref[half:]) / (2 * tokens * channels)
-    factor = (-sigma_ref[...] / weight)[:1, :1]
+    weight = weight[:1, :1]
     for ref, index in ((mine_ref, core), (theirs_ref, 1 - core)):
-        packet = ref[:half] * factor
-        both = jnp.concatenate([packet, swap_halves(packet)], axis=0)
-        out_ref[aligned(index, share), :] = both[:, :channels]
+        packet = -ref[:half] / weight
+        start = pl.multiple_of(index * share, share)
+        both_v[pl.ds(start, half)] = packet
+        both_v[pl.ds(start + half, half)] = swap_halves(packet)
+    out_ref[...] = both_v[...].T[:channels]
 
 
 def paired_local(
@@ -360,22 +349,22 @@
     weights = (query_matrix, key_matrix, value_matrix, adapter_query_down)
     partial_flops = 2 * tokens * half_width * (3 * local_columns + rank)
 
-    copies = 4 + 2 * 4
-    message, hidden, inverse, gap_own, sigma = run(
+    copies = 3 + 2 * 4
+    inputs = (step, latents.T, noise.T, prenorm_gain_vector, stream, patch_embed_weight)
+    message, hidden, inverse, gap = run(
         first_kernel,
         [
-            ((tokens, quarter + 2 * channels), BF16),
+            ((tokens, quarter), BF16),
             ((4, tokens, quarter), BF16),
             ((tokens, 128), F32),
-            ((tokens, channels), F32),
-            ((8, 128), F32),
+            ((channels, tokens), F32),
         ],
-        (step, latents, noise, prenorm_gain_vector, stream, patch_embed_weight),
-        [HBM] * 6,
+        [inputs[0]]
+        + [pltpu.with_memory_space_constraint(x, pltpu.HBM) for x in inputs[1:]],
+        [SMEM] + [HBM] * 5,
         [
-            pltpu.SMEM((1,), jnp.int32),
-            pltpu.VMEM((tokens, channels), BF16),
-            pltpu.VMEM((tokens, channels), BF16),
+            pltpu.VMEM((channels, tokens), BF16),
+            pltpu.VMEM((channels, tokens), BF16),
             pltpu.VMEM((4 * quarter,), F32),
             pltpu.VMEM((4, tokens, quarter), BF16),
             pltpu.VMEM((4, channels, quarter), BF16),
@@ -404,7 +393,7 @@
     readout_of_up, base = run(
         side_kernel,
         [((rank, channels), BF16), ((tokens, channels), F32)],
-        (hidden, adapter_output_up, velocity_readout_weight),
+        (hidden, adapter_output_up, velocity_readout_weight, gap),
         flops=8 * tokens * half_width * channels,
     )
     far = lax.ppermute(near, "head", to_core)
@@ -415,16 +404,12 @@
         flops=partial_flops,
     )
     other_got = lax.ppermute(other_sent, "seq", to_x)
-    half_set, mixes, gap_other = run(
+    half_set, mixes = run(
         half_kernel,
-        [
-            ((4, tokens, columns), BF16),
-            ((2, columns, 2 * channels), BF16),
-            ((tokens, channels), F32),
-        ],
+        [((4, tokens, columns), BF16), ((2, columns, 2 * channels), BF16)],
         (
             other_kept, own_got, adapter_query_up, mix_part,
-            adapter_output_down, readout_of_up, near,
+            adapter_output_down, readout_of_up,
         ),
     )
     sent, stay = run(
@@ -438,24 +423,28 @@
     )
 
     got = lax.ppermute(sent, "head", to_core)
-    packed = ((share + share // 2, 2 * channels), F32)
+    packed = ((share + share // 2, 2 * channels), BF16)
     same, cross = run(pack_kernel, [packed, packed], (stay, got))
     from_x = lax.ppermute(cross, "seq", to_x)
     from_y = lax.ppermute(same, "head", to_y)
     from_xy = lax.ppermute(cross, ("seq", "head"), to_xy)
-    total = (same + from_y) + (from_x + from_xy)
+    total = (same.astype(F32) + from_y.astype(F32)) + (
+        from_x.astype(F32) + from_xy.astype(F32)
+    )
+    total = total.astype(BF16)
     totals = [total] + [
         lax.ppermute(total, "group", pairs((groups,), lambda g, k=k: (g ^ k,)))
         for k in range(1, groups)
     ]
-    (packet,) = run(
-        error_kernel,
-        [((share // 2 + 8, 2 * channels), F32)],
-        (*totals, gap_own, gap_other, sigma),
-    )
+    (packet,) = run(error_kernel, [((share // 2 + 8, 2 * channels), F32)], totals)
     answer = lax.ppermute(packet, "head", to_core)
-    (out,) = run(last_kernel, [((tokens, channels), F32)], (packet, answer, sigma))
-    return out
+    (out,) = run(
+        last_kernel,
+        [((channels, tokens), F32)],
+        (packet, answer),
+        scratch=[pltpu.VMEM((tokens, 2 * channels), F32)],
+    )
+    return out.T
 
 
 def gathered_local(

time: 60.2 us -> 54.4 us (0.904)
  local copies, waits for them, and re-layouts: 10.6 us -> 5.07 us
    unnamed x28 -> x24, local copies, waits for them, and re-layouts: 9.85 us -> 5.06 us
    ppermute x1, waiting for transfers between devices: 3.22 us -> 4.24 us  [paired_local(): other_got = lax.ppermute(other_sent, 'seq', to_x)]
    ppermute x1, waiting for transfers between devices: 8.52 us -> 7.81 us  [paired_local(): near = lax.ppermute(message, 'seq', to_x)]
    pallas_call x1 -> x0, local copies, waits for them, and re-layouts: 0.7 us -> none  [run(): pl.pallas_call(kernel, out_shape=shapes, in_specs=specs or [VMEM] * len(a...]
  transfers between devices with their start and end apart: 12 -> 12, of which waited for: 10 -> 10; matrix products, arithmetic and copies ran while one was open for 0% -> 0% of each run, Pallas kernels for 9% -> 8%
where the time goes in v3:
time: 54.4 us; the launch traced here: 54.1 us
  waiting for transfers between devices  26 us (48%)
  starting transfers between devices  13.3 us (24%)
  Pallas kernels  8.73 us (16%)
  local copies, waits for them, and re-layouts  5.07 us (9%)
  between operations  0.91 us (2%)
    pallas_call x9, Pallas kernels, run(): pl.pallas_call(kernel, out_shape=shapes, in_specs=specs or [VMEM] * len(a...  8.73 us
    ppermute x1, waiting for transfers between devices, paired_local(): near = lax.ppermute(message, 'seq', to_x)  7.81 us
    unnamed x24, local copies, waits for them, and re-layouts  5.06 us
    ppermute x3, starting transfers between devices, paired_local(): lax.ppermute(total, 'group', pairs((groups,), lambda g, k=k: (g ^ k,)))  4.45 us
    ppermute x1, waiting for transfers between devices, paired_local(): other_got = lax.ppermute(other_sent, 'seq', to_x)  4.24 us
    ppermute x1, waiting for transfers between devices, paired_local(): own_got = lax.ppermute(own_sent, 'seq', to_x)  4.1 us
    ppermute x3, waiting for transfers between devices, paired_local(): lax.ppermute(total, 'group', pairs((groups,), lambda g, k=k: (g ^ k,)))  3.94 us
    ppermute x1, starting transfers between devices, paired_local(): near = lax.ppermute(message, 'seq', to_x)  3.04 us
  transfers between devices with their start and end apart: 12, of which 10 were waited for; matrix products, arithmetic and copies ran while one was open for 0% of the time, Pallas kernels for 8%

profile of v3, /device:TPU:0, one launch (start us, length us, event | category | flops | bytes accessed | tf_op | source)
XLA Modules:
  0.0 54.1 jit_solution(6984814208889234981)
XLA Ops:
  0.8 2.3 %shard_map.145 = (bf16[128,1280]{1,0:T(8,128)(2,1)S(1)}, bf16[4,128,1280]{2,1,0:T(8,128)(2,1)S(1)}, f32[128,128]{1,0:T(8,128)S(1)}, f32[64,128]{1,0:T(8,128)S(1)}) custom-call(s32[1]{0:T(128)S(6)} %copy.16.step_ref, bf16[64,128]{1,0:T(8,128)(2,1)} %bitcast.3, bf16[64,128]{1,0:T(8,128)(2,1)} %bitcast.4, f32[5120]{0:T(1024)} %gain_hbm.1, ...), custom_call_target="tpu_custom_call" | custom-call | bytes 3756036 | tf_op jit(solution)/shard_map/pallas_call | solution.py:57
  3.1 3.0 %collective-permute-start = (bf16[128,1280]{1,0:T(8,128)(2,1)S(1)}, bf16[128,1280]{1,0:T(8,128)(2,1)}, u32[]{:S(2)}, u32[]{:S(2)}) collective-permute-start(bf16[128,1280]{1,0:T(8,128)(2,1)S(1)} %get-tuple-element.25), channel_id=1, source_target_pairs={{0,4},{4,0},{1,5},{5,1},{2,6},{6,2},{3,7},{7,3},{8,12},{12,8},{9,1... | collective-permute-start | bytes 983048 | tf_op jit(solution)/shard_map/ppermute | solution.py:374
  6.2 7.8 %collective-permute-done.near_ref = bf16[128,1280]{1,0:T(8,128)(2,1)} collective-permute-done((bf16[128,1280]{1,0:T(8,128)(2,1)S(1)}, bf16[128,1280]{1,0:T(8,128)(2,1)}, u32[]{:S(2)}, u32[]{:S(2)}) %collective-permute-start) | collective-permute-done | bytes 327712 | tf_op jit(solution)/shard_map/ppermute | solution.py:374
  14.0 1.3 %copy-done.1 = bf16[2560,256]{1,0:T(8,128)(2,1)S(1)} copy-done((bf16[2560,256]{1,0:T(8,128)(2,1)S(1)}, bf16[2560,256]{1,0:T(8,128)(2,1)}, u32[]{:S(2)}) %copy-start.1) | copy-done | bytes 1310744
  15.4 1.3 %copy-done.3 = bf16[2560,256]{1,0:T(8,128)(2,1)S(1)} copy-done((bf16[2560,256]{1,0:T(8,128)(2,1)S(1)}, bf16[2560,256]{1,0:T(8,128)(2,1)}, u32[]{:S(2)}) %copy-start.3) | copy-done | bytes 1310744
  16.7 1.1 %copy-done.6 = bf16[64,5120]{1,0:T(8,128)(2,1)S(1)} copy-done((bf16[64,5120]{1,0:T(8,128)(2,1)S(1)}, bf16[64,5120]{1,0:T(8,128)(2,1)}, u32[]{:S(2)}) %copy-start.6) | copy-done | bytes 655384
  17.8 1.3 %copy-done.7 = bf16[256,2560]{1,0:T(8,128)(2,1)S(1)} copy-done((bf16[256,2560]{1,0:T(8,128)(2,1)S(1)}, bf16[256,2560]{1,0:T(8,128)(2,1)}, u32[]{:S(2)}) %copy-start.7) | copy-done | bytes 1310744
  19.1 1.4 %shard_map.146 = (bf16[128,1024]{1,0:T(8,128)(2,1)S(1)}, f32[128,512]{1,0:T(8,128)S(1)}, f32[128,64]{1,0:T(8,128)S(1)}) custom-call(bf16[4,128,1280]{2,1,0:T(8,128)(2,1)S(1)} %get-tuple-element.22.hidden_ref, f32[128,128]{1,0:T(8,128)S(1)} %get-tuple-element.23.inverse_ref, f32[4,1280]{1,0:T(4,128)S(1)} %reshape.3.gain_ref, bf16[2560,256]{1,0:T(8,128)(2,1)S(1)} %copy-done, ...), custom_call_target="tpu_custom_call" | custom-call | flops 587202560 | bytes 8507392 | tf_op jit(solution)/shard_map/pallas_call | solution.py:57
  20.5 1.8 %collective-permute-start.3 = (bf16[128,1024]{1,0:T(8,128)(2,1)S(1)}, bf16[128,1024]{1,0:T(8,128)(2,1)S(1)}, u32[]{:S(2)}, u32[]{:S(2)}) collective-permute-start(bf16[128,1024]{1,0:T(8,128)(2,1)S(1)} %get-tuple-element.28), channel_id=1, source_target_pairs={{0,4},{4,0},{1,5},{5,1},{2,6},{6,2},{3,7},{7,3},{8,12},{12,8},{9,1... | collective-permute-start | bytes 786440 | tf_op jit(solution)/shard_map/ppermute | solution.py:392
  22.3 2.0 %shard_map.147 = (bf16[128,896]{1,0:T(8,128)(2,1)S(1)}, f32[128,512]{1,0:T(8,128)S(1)}) custom-call(bf16[128,1280]{1,0:T(8,128)(2,1)} %collective-permute-done.near_ref, bf16[128,1280]{1,0:T(8,128)(2,1)} %collective-permute-done.1.far_ref, bf16[2560,256]{1,0:T(8,128)(2,1)S(1)} %copy-done, bf16[2560,256]{1,0:T(8,128)(2,1)S(1)} %copy-done.2, ...), custom_call_target="tpu_custom_call" | custom-call | flops 587202560 | bytes 5734400 | tf_op jit(solution)/shard_map/pallas_call | solution.py:57
  24.2 0.4 collective-permute-start.2
  24.6 1.0 %shard_map.148 = (bf16[128,64]{1,0:T(8,128)(2,1)S(1)}, f32[128,64]{1,0:T(8,128)S(1)}) custom-call(bf16[4,128,1280]{2,1,0:T(8,128)(2,1)S(1)} %get-tuple-element.22.hidden_ref, bf16[128,5120]{1,0:T(8,128)(2,1)S(1)} %copy-done.8, bf16[64,5120]{1,0:T(8,128)(2,1)S(1)} %copy-done.6, f32[64,128]{1,0:T(8,128)S(1)} %get-tuple-element.30.gap_ref), custom_call_target="tpu_custom_call" | custom-call | flops 167772160 | bytes 3358720 | tf_op jit(solution)/shard_map/pallas_call | solution.py:57
  25.6 4.1 %collective-permute-done.3.got_ref = bf16[128,1024]{1,0:T(8,128)(2,1)S(1)} collective-permute-done((bf16[128,1024]{1,0:T(8,128)(2,1)S(1)}, bf16[128,1024]{1,0:T(8,128)(2,1)S(1)}, u32[]{:S(2)}, u32[]{:S(2)}) %collective-permute-start.3) | collective-permute-done | bytes 262176 | tf_op jit(solution)/shard_map/ppermute | solution.py:392
  29.7 0.2 shard_map.149
  29.9 4.2 %collective-permute-done.2.got_ref = bf16[128,896]{1,0:T(8,128)(2,1)S(1)} collective-permute-done((bf16[128,896]{1,0:T(8,128)(2,1)S(1)}, bf16[128,896]{1,0:T(8,128)(2,1)S(1)}, u32[]{:S(2)}, u32[]{:S(2)}) %collective-permute-start.2) | collective-permute-done | bytes 229408 | tf_op jit(solution)/shard_map/ppermute | solution.py:406
  34.2 0.9 %shard_map.150 = (f32[128,128]{1,0:T(8,128)S(1)}, f32[128,128]{1,0:T(8,128)S(1)}) custom-call(f32[128,512]{1,0:T(8,128)S(1)} %get-tuple-element.24.kept_ref, bf16[128,896]{1,0:T(8,128)(2,1)S(1)} %collective-permute-done.2.got_ref, bf16[128,256]{1,0:T(8,128)(2,1)S(1)} %copy-done.9, bf16[4,128,128]{2,1,0:T(8,128)(2,1)S(1)} %get-tuple-element.32.set_ref, ...), custom_call_target="tpu_custom_call" | custom-call | bytes 917504 | tf_op jit(solution)/shard_map/pallas_call | solution.py:57
  35.0 0.1 collective-permute-start.4
  35.1 1.2 %collective-permute-done.4.got_ref = f32[128,128]{1,0:T(8,128)S(1)} collective-permute-done((f32[128,128]{1,0:T(8,128)S(1)}, f32[128,128]{1,0:T(8,128)S(1)}, u32[]{:S(2)}, u32[]{:S(2)}) %collective-permute-start.4) | collective-permute-done | bytes 65568 | tf_op jit(solution)/shard_map/ppermute | solution.py:425
  36.3 0.1 shard_map.151
  36.4 1.8 %collective-permute-start.5 = (bf16[96,128]{1,0:T(8,128)(2,1)S(1)}, bf16[96,128]{1,0:T(8,128)(2,1)S(1)}, u32[]{:S(2)}, u32[]{:S(2)}) collective-permute-start(bf16[96,128]{1,0:T(8,128)(2,1)S(1)} %get-tuple-element.37), channel_id=1, source_target_pairs={{0,2},{1,3},{2,0},{3,1},{4,6},{5,7},{6,4},{7,5},{8,10},{9,11},{10,... | collective-permute-start | bytes 73736 | tf_op jit(solution)/shard_map/ppermute | solution.py:429
  38.2 1.4 %collective-permute-start.7 = (bf16[96,128]{1,0:T(8,128)(2,1)S(1)}, bf16[96,128]{1,0:T(8,128)(2,1)S(1)}, u32[]{:S(2)}, u32[]{:S(2)}) collective-permute-start(bf16[96,128]{1,0:T(8,128)(2,1)S(1)} %get-tuple-element.38), channel_id=1, source_target_pairs={{0,6},{1,7},{2,4},{3,5},{4,2},{5,3},{6,0},{7,1},{8,14},{9,15},{10,... | collective-permute-start | bytes 73736 | tf_op jit(solution)/shard_map/ppermute | solution.py:430
  39.6 0.3 collective-permute-start.6
  39.9 0.3 collective-permute-done.5
  40.3 2.8 %collective-permute-done.7 = bf16[96,128]{1,0:T(8,128)(2,1)S(1)} collective-permute-done((bf16[96,128]{1,0:T(8,128)(2,1)S(1)}, bf16[96,128]{1,0:T(8,128)(2,1)S(1)}, u32[]{:S(2)}, u32[]{:S(2)}) %collective-permute-start.7) | collective-permute-done | bytes 24608 | tf_op jit(solution)/shard_map/ppermute | solution.py:430
  43.1 0.4 collective-permute-done.6
  43.5 3.7 %collective-permute-start.10 = (bf16[96,128]{1,0:T(8,128)(2,1)S(1)}, bf16[96,128]{1,0:T(8,128)(2,1)S(1)}, u32[]{:S(2)}, u32[]{:S(2)}) collective-permute-start(bf16[96,128]{1,0:T(8,128)(2,1)S(1)} %add_convert_fusion.refs_0_), channel_id=1, source_target_pairs={{0,24},{8,16},{16,8},{24,0},{1,25},{9,17},{17,9},{25,1},{2,26},{10... | collective-permute-start | bytes 73736 | tf_op jit(solution)/shard_map/ppermute | solution.py:436
  47.1 0.8 %collective-permute-start.8 = (bf16[96,128]{1,0:T(8,128)(2,1)S(1)}, bf16[96,128]{1,0:T(8,128)(2,1)S(1)}, u32[]{:S(2)}, u32[]{:S(2)}) collective-permute-start(bf16[96,128]{1,0:T(8,128)(2,1)S(1)} %add_convert_fusion.refs_0_), channel_id=1, source_target_pairs={{0,8},{8,0},{16,24},{24,16},{1,9},{9,1},{17,25},{25,17},{2,10},{10... | collective-permute-start | bytes 73736 | tf_op jit(solution)/shard_map/ppermute | solution.py:436
  47.9 1.3 %collective-permute-done.10.refs_3_ = bf16[96,128]{1,0:T(8,128)(2,1)S(1)} collective-permute-done((bf16[96,128]{1,0:T(8,128)(2,1)S(1)}, bf16[96,128]{1,0:T(8,128)(2,1)S(1)}, u32[]{:S(2)}, u32[]{:S(2)}) %collective-permute-start.10) | collective-permute-done | bytes 24608 | tf_op jit(solution)/shard_map/ppermute | solution.py:436
  49.2 2.7 %collective-permute-done.9.refs_2_ = bf16[96,128]{1,0:T(8,128)(2,1)S(1)} collective-permute-done((bf16[96,128]{1,0:T(8,128)(2,1)S(1)}, bf16[96,128]{1,0:T(8,128)(2,1)S(1)}, u32[]{:S(2)}, u32[]{:S(2)}) %collective-permute-start.9) | collective-permute-done | bytes 24608 | tf_op jit(solution)/shard_map/ppermute | solution.py:436
  51.9 0.1 shard_map.152.mine_ref
  52.1 1.2 %collective-permute-done.11.theirs_ref = f32[40,128]{1,0:T(8,128)S(1)} collective-permute-done((f32[40,128]{1,0:T(8,128)S(1)}, f32[40,128]{1,0:T(8,128)S(1)}, u32[]{:S(2)}, u32[]{:S(2)}) %collective-permute-start.11) | collective-permute-done | bytes 20512 | tf_op jit(solution)/shard_map/ppermute | solution.py:440
  53.3 0.8 %shard_map.153 = f32[64,128]{1,0:T(8,128)} custom-call(f32[40,128]{1,0:T(8,128)S(1)} %shard_map.152.mine_ref, f32[40,128]{1,0:T(8,128)S(1)} %collective-permute-done.11.theirs_ref), custom_call_target="tpu_custom_call" | custom-call | bytes 73728 | tf_op jit(solution)/shard_map/pallas_call | solution.py:57
  (27 shorter events, 0.2 us)
Async XLA Ops:
  0.0 14.0 %copy-start.11 = (f32[5120]{0:T(1024)S(1)}, f32[5120]{0:T(1024)}, u32[]{:S(2)}) copy-start(f32[5120]{0:T(1024)} %gain_hbm.1) | copy-start | bytes 61444
  0.0 14.0 %copy-start.5 = (bf16[2560,128]{1,0:T(8,128)(2,1)S(1)}, bf16[2560,128]{1,0:T(8,128)(2,1)}, u32[]{:S(2)}) copy-start(bf16[2560,128]{1,0:T(8,128)(2,1)} %down_ref.4) | copy-start | bytes 1966084
  0.0 14.0 %copy-start = (bf16[2560,256]{1,0:T(8,128)(2,1)S(1)}, bf16[2560,256]{1,0:T(8,128)(2,1)}, u32[]{:S(2)}) copy-start(bf16[2560,256]{1,0:T(8,128)(2,1)} %q_ref.3) | copy-start | bytes 3932164
  3.1 10.8 %collective-permute-start = (bf16[128,1280]{1,0:T(8,128)(2,1)S(1)}, bf16[128,1280]{1,0:T(8,128)(2,1)}, u32[]{:S(2)}, u32[]{:S(2)}) collective-permute-start(bf16[128,1280]{1,0:T(8,128)(2,1)S(1)} %get-tuple-element.25), channel_id=1, source_target_pairs={{0,4},{4,0},{1,5},{5,1},{2,6},{6,2},{3,7},{7,3},{8,12},{12,8},{9,1... | collective-permute-start | bytes 983048 | tf_op jit(solution)/shard_map/ppermute | solution.py:374
  14.0 8.3 %collective-permute-start.1 = (bf16[128,1280]{1,0:T(8,128)(2,1)}, bf16[128,1280]{1,0:T(8,128)(2,1)}, u32[]{:S(2)}, u32[]{:S(2)}) collective-permute-start(bf16[128,1280]{1,0:T(8,128)(2,1)} %collective-permute-done.near_ref), channel_id=1, source_target_pairs={{0,1},{1,0},{2,3},{3,2},{4,5},{5,4},{6,7},{7,6},{8,9},{9,8},{10,11... | collective-permute-start | bytes 983048 | tf_op jit(solution)/shard_map/ppermute | solution.py:399
  14.0 1.3 %copy-start.1 = (bf16[2560,256]{1,0:T(8,128)(2,1)S(1)}, bf16[2560,256]{1,0:T(8,128)(2,1)}, u32[]{:S(2)}) copy-start(bf16[2560,256]{1,0:T(8,128)(2,1)} %k_ref.3) | copy-start | bytes 3932164
  15.4 1.3 %copy-start.3 = (bf16[2560,256]{1,0:T(8,128)(2,1)S(1)}, bf16[2560,256]{1,0:T(8,128)(2,1)}, u32[]{:S(2)}) copy-start(bf16[2560,256]{1,0:T(8,128)(2,1)} %v_ref.3) | copy-start | bytes 3932164
  16.7 1.1 %copy-start.6 = (bf16[64,5120]{1,0:T(8,128)(2,1)S(1)}, bf16[64,5120]{1,0:T(8,128)(2,1)}, u32[]{:S(2)}) copy-start(bf16[64,5120]{1,0:T(8,128)(2,1)} %readout_ref.3) | copy-start | bytes 1966084
  17.8 1.3 %copy-start.7 = (bf16[256,2560]{1,0:T(8,128)(2,1)S(1)}, bf16[256,2560]{1,0:T(8,128)(2,1)}, u32[]{:S(2)}) copy-start(bf16[256,2560]{1,0:T(8,128)(2,1)} %output_ref.1) | copy-start | bytes 3932164
  19.1 3.2 %copy-start.2 = (bf16[2560,256]{1,0:T(8,128)(2,1)S(1)}, bf16[2560,256]{1,0:T(8,128)(2,1)}, u32[]{:S(2)}) copy-start(bf16[2560,256]{1,0:T(8,128)(2,1)} %k_ref.3) | copy-start | bytes 3932164
  19.1 3.2 %copy-start.4 = (bf16[2560,256]{1,0:T(8,128)(2,1)S(1)}, bf16[2560,256]{1,0:T(8,128)(2,1)}, u32[]{:S(2)}) copy-start(bf16[2560,256]{1,0:T(8,128)(2,1)} %v_ref.3) | copy-start | bytes 3932164
  20.4 4.2 %copy-start.8 = (bf16[128,5120]{1,0:T(8,128)(2,1)S(1)}, bf16[128,5120]{1,0:T(8,128)(2,1)}, u32[]{:S(2)}) copy-start(bf16[128,5120]{1,0:T(8,128)(2,1)} %up_ref.3) | copy-start | bytes 3932164
  20.5 9.2 %collective-permute-start.3 = (bf16[128,1024]{1,0:T(8,128)(2,1)S(1)}, bf16[128,1024]{1,0:T(8,128)(2,1)S(1)}, u32[]{:S(2)}, u32[]{:S(2)}) collective-permute-start(bf16[128,1024]{1,0:T(8,128)(2,1)S(1)} %get-tuple-element.28), channel_id=1, source_target_pairs={{0,4},{4,0},{1,5},{5,1},{2,6},{6,2},{3,7},{7,3},{8,12},{12,8},{9,1... | collective-permute-start | bytes 786440 | tf_op jit(solution)/shard_map/ppermute | solution.py:392
  24.2 9.9 %collective-permute-start.2 = (bf16[128,896]{1,0:T(8,128)(2,1)S(1)}, bf16[128,896]{1,0:T(8,128)(2,1)S(1)}, u32[]{:S(2)}, u32[]{:S(2)}) collective-permute-start(bf16[128,896]{1,0:T(8,128)(2,1)S(1)} %get-tuple-element.26), channel_id=1, source_target_pairs={{0,4},{4,0},{1,5},{5,1},{2,6},{6,2},{3,7},{7,3},{8,12},{12,8},{9,1... | collective-permute-start | bytes 688136 | tf_op jit(solution)/shard_map/ppermute | solution.py:406
  24.6 5.1 %copy-start.9 = (bf16[128,256]{1,0:T(8,128)(2,1)S(1)}, bf16[128,256]{1,0:T(8,128)(2,1)}, u32[]{:S(2)}) copy-start(bf16[128,256]{1,0:T(8,128)(2,1)} %up_ref.5) | copy-start | bytes 196612
  24.6 5.1 %copy-start.10 = (bf16[256,128]{1,0:T(8,128)(2,1)S(1)}, bf16[256,128]{1,0:T(8,128)(2,1)}, u32[]{:S(2)}) copy-start(bf16[256,128]{1,0:T(8,128)(2,1)} %down_ref.5) | copy-start | bytes 196612
  35.0 1.3 %collective-permute-start.4 = (f32[128,128]{1,0:T(8,128)S(1)}, f32[128,128]{1,0:T(8,128)S(1)}, u32[]{:S(2)}, u32[]{:S(2)}) collective-permute-start(f32[128,128]{1,0:T(8,128)S(1)} %get-tuple-element.36), channel_id=1, source_target_pairs={{0,1},{1,0},{2,3},{3,2},{4,5},{5,4},{6,7},{7,6},{8,9},{9,8},{10,11... | collective-permute-start | bytes 196616 | tf_op jit(solution)/shard_map/ppermute | solution.py:425
  36.4 3.8 %collective-permute-start.5 = (bf16[96,128]{1,0:T(8,128)(2,1)S(1)}, bf16[96,128]{1,0:T(8,128)(2,1)S(1)}, u32[]{:S(2)}, u32[]{:S(2)}) collective-permute-start(bf16[96,128]{1,0:T(8,128)(2,1)S(1)} %get-tuple-element.37), channel_id=1, source_target_pairs={{0,2},{1,3},{2,0},{3,1},{4,6},{5,7},{6,4},{7,5},{8,10},{9,11},{10,... | collective-permute-start | bytes 73736 | tf_op jit(solution)/shard_map/ppermute | solution.py:429
  38.2 4.9 %collective-permute-start.7 = (bf16[96,128]{1,0:T(8,128)(2,1)S(1)}, bf16[96,128]{1,0:T(8,128)(2,1)S(1)}, u32[]{:S(2)}, u32[]{:S(2)}) collective-permute-start(bf16[96,128]{1,0:T(8,128)(2,1)S(1)} %get-tuple-element.38), channel_id=1, source_target_pairs={{0,6},{1,7},{2,4},{3,5},{4,2},{5,3},{6,0},{7,1},{8,14},{9,15},{10,... | collective-permute-start | bytes 73736 | tf_op jit(solution)/shard_map/ppermute | solution.py:430
  39.6 3.8 %collective-permute-start.6 = (bf16[96,128]{1,0:T(8,128)(2,1)S(1)}, bf16[96,128]{1,0:T(8,128)(2,1)S(1)}, u32[]{:S(2)}, u32[]{:S(2)}) collective-permute-start(bf16[96,128]{1,0:T(8,128)(2,1)S(1)} %get-tuple-element.38), channel_id=1, source_target_pairs={{0,4},{4,0},{1,5},{5,1},{2,6},{6,2},{3,7},{7,3},{8,12},{12,8},{9,1... | collective-permute-start | bytes 73736 | tf_op jit(solution)/shard_map/ppermute | solution.py:428
  43.5 5.7 %collective-permute-start.10 = (bf16[96,128]{1,0:T(8,128)(2,1)S(1)}, bf16[96,128]{1,0:T(8,128)(2,1)S(1)}, u32[]{:S(2)}, u32[]{:S(2)}) collective-permute-start(bf16[96,128]{1,0:T(8,128)(2,1)S(1)} %add_convert_fusion.refs_0_), channel_id=1, source_target_pairs={{0,24},{8,16},{16,8},{24,0},{1,25},{9,17},{17,9},{25,1},{2,26},{10... | collective-permute-start | bytes 73736 | tf_op jit(solution)/shard_map/ppermute | solution.py:436
  47.1 4.7 %collective-permute-start.9 = (bf16[96,128]{1,0:T(8,128)(2,1)S(1)}, bf16[96,128]{1,0:T(8,128)(2,1)S(1)}, u32[]{:S(2)}, u32[]{:S(2)}) collective-permute-start(bf16[96,128]{1,0:T(8,128)(2,1)S(1)} %add_convert_fusion.refs_0_), channel_id=1, source_target_pairs={{0,16},{8,24},{16,0},{24,8},{1,17},{9,25},{17,1},{25,9},{2,18},{10... | collective-permute-start | bytes 73736 | tf_op jit(solution)/shard_map/ppermute | solution.py:436
  47.1 4.7 %collective-permute-start.8 = (bf16[96,128]{1,0:T(8,128)(2,1)S(1)}, bf16[96,128]{1,0:T(8,128)(2,1)S(1)}, u32[]{:S(2)}, u32[]{:S(2)}) collective-permute-start(bf16[96,128]{1,0:T(8,128)(2,1)S(1)} %add_convert_fusion.refs_0_), channel_id=1, source_target_pairs={{0,8},{8,0},{16,24},{24,16},{1,9},{9,1},{17,25},{25,17},{2,10},{10... | collective-permute-start | bytes 73736 | tf_op jit(solution)/shard_map/ppermute | solution.py:436
  52.0 1.3 %collective-permute-start.11 = (f32[40,128]{1,0:T(8,128)S(1)}, f32[40,128]{1,0:T(8,128)S(1)}, u32[]{:S(2)}, u32[]{:S(2)}) collective-permute-start(f32[40,128]{1,0:T(8,128)S(1)} %shard_map.152.mine_ref), channel_id=1, source_target_pairs={{0,1},{1,0},{2,3},{3,2},{4,5},{5,4},{6,7},{7,6},{8,9},{9,8},{10,11... | collective-permute-start | bytes 61448 | tf_op jit(solution)/shard_map/ppermute | solution.py:440

commit v4 on v3

--- a/solution.py
+++ b/solution.py
@@ -46,7 +46,6 @@
 
 
 VMEM = pl.BlockSpec(memory_space=pltpu.VMEM)
-SMEM = pl.BlockSpec(memory_space=pltpu.SMEM)
 HBM = pl.BlockSpec(memory_space=pltpu.HBM)
 
 
@@ -83,39 +82,50 @@
     return high, (x - high.astype(F32)).astype(BF16)
 
 
+def slice_kernel(stream_hbm, message_ref, sem):
+    quarter = message_ref.shape[1]
+    target = (1 - lax.axis_index("seq")) * 2 + lax.axis_index("head") % 2
+    copy = pltpu.make_async_copy(stream_hbm.at[:, aligned(target, quarter)], message_ref, sem)
+    copy.start()
+    copy.wait()
+
+
 def first_kernel(
-    step_ref, latents_hbm, noise_hbm, gain_hbm, stream_hbm, patch_hbm,
-    message_ref, hidden_ref, inverse_ref, gap_ref,
-    latents_v, noise_v, gain_v, stream_v, patch_v, sems,
-):
-    parts, tokens, quarter = hidden_ref.shape
+    step_any, latents_hbm, noise_hbm, stream_hbm, patch_hbm, readout_hbm, gain_hbm,
+    normed_ref, rows_ref, base_ref, gain_ref,
+    step_s, latents_v, noise_v, stream_v, patch_v, readout_v, gain_v, hidden_v, sems,
+):
+    parts, tokens, quarter = stream_v.shape
+    channels = latents_v.shape[0]
     seq = lax.axis_index("seq")
-    core = lax.axis_index("head") % 2
     small = [
         pltpu.make_async_copy(latents_hbm, latents_v, sems.at[0]),
         pltpu.make_async_copy(noise_hbm, noise_v, sems.at[1]),
+        pltpu.make_async_copy(step_any, step_s, sems.at[2]),
     ]
+    gain_copy = pltpu.make_async_copy(gain_hbm, gain_v, sems.at[3])
     large = []
     for j in range(parts):
         span = pl.ds(j * quarter, quarter)
-        large.append((
-            pltpu.make_async_copy(stream_hbm.at[:, span], stream_v.at[j], sems.at[3 + 2 * j]),
-            pltpu.make_async_copy(patch_hbm.at[:, span], patch_v.at[j], sems.at[4 + 2 * j]),
-        ))
-    gain_copy = pltpu.make_async_copy(gain_hbm, gain_v, sems.at[2])
+        large.append([
+            pltpu.make_async_copy(source.at[:, span], target.at[j], sems.at[4 + 3 * j + i])
+            for i, (source, target) in enumerate(
+                ((stream_hbm, stream_v), (patch_hbm, patch_v), (readout_hbm, readout_v))
+            )
+        ])
     for copy in small:
         copy.start()
-    for pair in large:
-        for copy in pair:
+    for j in range(parts):
+        for copy in large[j]:
             copy.start()
     gain_copy.start()
     for copy in small:
         copy.wait()
-    level = (jnp.full((8, 128), step_ref[0], jnp.int32).astype(F32) + 1.0) / 1000.0
+    level = (jnp.full((8, 128), step_s[0], jnp.int32).astype(F32) + 1.0) / 1000.0
     sigma = (5.0 * level / (1.0 + 4.0 * level))[:1, :1]
     latents = latents_v[...].astype(F32)
     noisy = ((1.0 - sigma) * latents + sigma * noise_v[...].astype(F32)).astype(BF16)
-    gap_ref[...] = (latents - noisy.astype(F32)) / sigma
+    base = (latents - noisy.astype(F32)) / sigma
     squares = jnp.zeros((tokens, 128), F32)
     for j in range(parts):
         for copy in large[j]:
@@ -124,22 +134,31 @@
             noisy, patch_v[j], (((0,), (0,)), ((), ())), preferred_element_type=F32
         )
         hidden = (stream_v[j].astype(F32) + embedded).astype(BF16)
-        hidden_ref[j] = hidden
+        hidden_v[j] = hidden
+        base += contract_final_axis(readout_v[j], hidden)
         wide = hidden.astype(F32)
         wide = wide * wide
         for i in range(quarter // 128):
             squares = squares + wide[:, i * 128 : (i + 1) * 128]
     mean = jnp.sum(squares, axis=1, keepdims=True) / (parts * quarter)
     inverse = lax.rsqrt(mean + 1e-06)
-    inverse_ref[...] = jnp.broadcast_to(inverse, inverse_ref.shape)
+    rows_ref[:channels] = noisy.astype(F32)
+    rows_ref[channels:] = jnp.broadcast_to(inverse, (tokens, tokens)).T[
+        : rows_ref.shape[0] - channels
+    ]
+    once = (lax.axis_index("group") == 0) & (lax.axis_index("head") == 0)
+    base_ref[...] = jnp.where(once, base, 0.0).T
     gain_copy.wait()
-    target = (1 - seq) * 2 + core
     for j in range(parts):
 
-        @pl.when(target == j)
+        @pl.when(seq == j // 2)
         def _(j=j):
             gain = gain_v[j * quarter : (j + 1) * quarter][None, :]
-            message_ref[...] = (hidden_ref[j].astype(F32) * inverse * gain).astype(BF16)
+            start = (j % 2) * quarter
+            gain_ref[j % 2 : j % 2 + 1] = gain
+            normed_ref[:, start : start + quarter] = (
+                hidden_v[j].astype(F32) * inverse * gain
+            ).astype(BF16)
 
 
 def pick(index, x):
@@ -159,21 +178,14 @@
 
 
 def own_kernel(
-    hidden_ref, inverse_ref, gain_ref, q_ref, k_ref, v_ref, down_ref, output_ref, readout_ref,
-    sent_ref, kept_ref, mix_ref, normed_v, mix_v,
-):
-    _, _, quarter = hidden_ref.shape
+    normed_ref, q_ref, k_ref, v_ref, down_ref, output_ref, readout_ref,
+    sent_ref, kept_ref, mix_ref, mix_v,
+):
     seq = lax.axis_index("seq")
-    inverse = inverse_ref[:, :1]
-    for i in range(2):
-        gain = gain_ref[pl.ds(2 * seq + i, 1), :]
-        hidden = hidden_ref[2 * seq + i].astype(F32)
-        normed_v[:, i * quarter : (i + 1) * quarter] = (hidden * inverse * gain).astype(BF16)
-    normed = normed_v[...]
+    normed = normed_ref[...]
     parts = [dot(normed, w[...]) for w in (q_ref, k_ref, v_ref, down_ref)]
     partial_outputs(parts, seq, sent_ref, kept_ref)
-    half_width = 2 * quarter
-    readout = readout_ref[:, aligned(seq, half_width)]
+    readout = readout_ref[:, aligned(seq, normed.shape[1])]
     mix_v[...] = contract_final_axis(output_ref[...], readout)
     rows, channels = mix_ref.shape
     theirs = mix_v[aligned(1 - seq, rows), :]
@@ -183,27 +195,42 @@
     mix_ref[...] = mix_v[aligned(seq, rows), :]
 
 
-def side_kernel(hidden_ref, up_ref, readout_ref, gap_ref, readout_of_up_ref, base_ref):
-    parts, _, quarter = hidden_ref.shape
+def side_kernel(up_ref, readout_ref, readout_of_up_ref):
     readout_of_up_ref[...] = contract_final_axis(up_ref[...], readout_ref[...]).astype(BF16)
-    base = gap_ref[...]
-    for j in range(parts):
-        base += contract_final_axis(
-            readout_ref[:, j * quarter : (j + 1) * quarter], hidden_ref[j]
-        )
-    once = (lax.axis_index("group") == 0) & (lax.axis_index("head") == 0)
-    base_ref[...] = jnp.where(once, base, 0.0).T
-
-
-def other_kernel(near_ref, far_ref, q_ref, k_ref, v_ref, down_ref, sent_ref, kept_ref):
-    quarter = q_ref.shape[0] // 2
+
+
+def other_parts(part, raw_ref, rows_ref, patch_ref, gain_ref, weights):
+    tokens, quarter = raw_ref.shape
+    channels = patch_ref.shape[0]
+    quarters = lax.axis_index("seq") * 2 + part
+    noisy = rows_ref[:channels].astype(BF16)
+    inverse = jnp.broadcast_to(rows_ref[channels : channels + 1], (tokens, tokens)).T[:, :1]
+    embedded = lax.dot_general(
+        noisy, patch_ref[:, aligned(quarters, quarter)],
+        (((0,), (0,)), ((), ())), preferred_element_type=F32,
+    )
+    hidden = (raw_ref[...].astype(F32) + embedded).astype(BF16).astype(F32)
+    normed = (hidden * inverse * gain_ref[pl.ds(part, 1), :]).astype(BF16)
+    return [dot(normed, w[aligned(part, quarter), :]) for w in weights]
+
+
+def near_kernel(raw_ref, rows_ref, patch_ref, gain_ref, q_ref, k_ref, v_ref, down_ref, *outs):
     core = lax.axis_index("head") % 2
-    near = near_ref[...]
-    far = far_ref[...]
-    parts = [
-        dot(near, w[aligned(core, quarter), :]) + dot(far, w[aligned(1 - core, quarter), :])
-        for w in (q_ref, k_ref, v_ref, down_ref)
-    ]
+    weights = (q_ref, k_ref, v_ref, down_ref)
+    parts = other_parts(core, raw_ref, rows_ref, patch_ref, gain_ref, weights)
+    for out, part in zip(outs, parts):
+        out[...] = part
+
+
+def far_kernel(
+    raw_ref, rows_ref, patch_ref, gain_ref, q_ref, k_ref, v_ref, down_ref,
+    near_q_ref, near_k_ref, near_v_ref, near_down_ref, sent_ref, kept_ref,
+):
+    core = lax.axis_index("head") % 2
+    weights = (q_ref, k_ref, v_ref, down_ref)
+    parts = other_parts(1 - core, raw_ref, rows_ref, patch_ref, gain_ref, weights)
+    near = (near_q_ref, near_k_ref, near_v_ref, near_down_ref)
+    parts = [part + ref[...] for part, ref in zip(parts, near)]
     partial_outputs(parts, lax.axis_index("seq"), sent_ref, kept_ref)
 
 
@@ -349,29 +376,43 @@
     weights = (query_matrix, key_matrix, value_matrix, adapter_query_down)
     partial_flops = 2 * tokens * half_width * (3 * local_columns + rank)
 
-    copies = 3 + 2 * 4
-    inputs = (step, latents.T, noise.T, prenorm_gain_vector, stream, patch_embed_weight)
-    message, hidden, inverse, gap = run(
+    in_hbm = pltpu.with_memory_space_constraint(stream, pltpu.HBM)
+    (message,) = run(
+        slice_kernel,
+        [((tokens, quarter), BF16)],
+        (in_hbm,),
+        [HBM],
+        [pltpu.SemaphoreType.DMA],
+        moved=4 * tokens * quarter,
+    )
+    near = lax.ppermute(message, "seq", to_x)
+    inputs = (
+        latents.T, noise.T, stream, patch_embed_weight, velocity_readout_weight,
+        prenorm_gain_vector,
+    )
+    normed, rows, base, gain = run(
         first_kernel,
         [
-            ((tokens, quarter), BF16),
-            ((4, tokens, quarter), BF16),
-            ((tokens, 128), F32),
-            ((channels, tokens), F32),
+            ((tokens, half_width), BF16),
+            ((channels + 8, tokens), F32),
+            ((tokens, channels), F32),
+            ((2, quarter), F32),
         ],
-        [inputs[0]]
-        + [pltpu.with_memory_space_constraint(x, pltpu.HBM) for x in inputs[1:]],
-        [SMEM] + [HBM] * 5,
+        [step, *(pltpu.with_memory_space_constraint(x, pltpu.HBM) for x in inputs)],
+        [pl.BlockSpec(memory_space=pl.ANY)] + [HBM] * 6,
         [
+            pltpu.SMEM((1,), jnp.int32),
             pltpu.VMEM((channels, tokens), BF16),
             pltpu.VMEM((channels, tokens), BF16),
+            pltpu.VMEM((4, tokens, quarter), BF16),
+            pltpu.VMEM((4, channels, quarter), BF16),
+            pltpu.VMEM((4, channels, quarter), BF16),
             pltpu.VMEM((4 * quarter,), F32),
             pltpu.VMEM((4, tokens, quarter), BF16),
-            pltpu.VMEM((4, channels, quarter), BF16),
-            pltpu.SemaphoreType.DMA((copies,)),
+            pltpu.SemaphoreType.DMA((4 + 3 * 4,)),
         ],
     )
-    near = lax.ppermute(message, "seq", to_x)
+    other_rows = lax.ppermute(rows, "seq", to_x)
     own_sent, own_kept, mix_part = run(
         own_kernel,
         [
@@ -379,29 +420,30 @@
             ((tokens, 4 * columns), F32),
             ((columns, channels), F32),
         ],
-        (
-            hidden, inverse, prenorm_gain_vector.reshape(4, quarter), *weights,
-            output_matrix, velocity_readout_weight,
-        ),
-        scratch=[
-            pltpu.VMEM((tokens, half_width), BF16),
-            pltpu.VMEM((local_columns, channels), F32),
-        ],
+        (normed, *weights, output_matrix, velocity_readout_weight),
+        scratch=[pltpu.VMEM((local_columns, channels), F32)],
         flops=partial_flops,
     )
     own_got = lax.ppermute(own_sent, "seq", to_x)
-    readout_of_up, base = run(
+    (readout_of_up,) = run(
         side_kernel,
-        [((rank, channels), BF16), ((tokens, channels), F32)],
-        (hidden, adapter_output_up, velocity_readout_weight, gap),
-        flops=8 * tokens * half_width * channels,
+        [((rank, channels), BF16)],
+        (adapter_output_up, velocity_readout_weight),
+        flops=4 * rank * half_width * channels,
     )
     far = lax.ppermute(near, "head", to_core)
+    shared = (other_rows, patch_embed_weight, gain, *weights)
+    near_parts = run(
+        near_kernel,
+        [((tokens, w.shape[1]), F32) for w in weights],
+        (near, *shared),
+        flops=partial_flops // 2,
+    )
     other_sent, other_kept = run(
-        other_kernel,
+        far_kernel,
         [((tokens, 7 * columns), BF16), ((tokens, 4 * columns), F32)],
-        (near, far, *weights),
-        flops=partial_flops,
+        (far, *shared, *near_parts),
+        flops=partial_flops // 2,
     )
     other_got = lax.ppermute(other_sent, "seq", to_x)
     half_set, mixes = run(

time: 54.4 us -> 57.2 us (1.051)
  waiting for transfers between devices: 26 us -> 27.9 us
  starting transfers between devices: 13.3 us -> 15.1 us
  local copies, waits for them, and re-layouts: 5.07 us -> 3.52 us
  Pallas kernels: 8.73 us -> 9.61 us
    ppermute x0 -> x1, starting transfers between devices: none -> 1.81 us  [paired_local(): other_rows = lax.ppermute(rows, 'seq', to_x)]
    ppermute x1, waiting for transfers between devices: 2.81 us -> 1.24 us  [paired_local(): from_xy = lax.ppermute(cross, ('seq', 'head'), to_xy)]
    unnamed x24 -> x20, local copies, waits for them, and re-layouts: 5.06 us -> 3.52 us
    ppermute x1, starting transfers between devices: 1.81 us -> 0.35 us  [paired_local(): own_got = lax.ppermute(own_sent, 'seq', to_x)]
    ppermute x3, waiting for transfers between devices: 3.94 us -> 5.4 us  [paired_local(): lax.ppermute(total, 'group', pairs((groups,), lambda g, k=k: (g ^ k,)))]
    ppermute x1, starting transfers between devices: 0.38 us -> 1.81 us  [paired_local(): other_got = lax.ppermute(other_sent, 'seq', to_x)]
    ppermute x1, starting transfers between devices: 1.77 us -> 0.51 us  [paired_local(): from_y = lax.ppermute(same, 'head', to_y)]
    ppermute x1, starting transfers between devices: 0.3 us -> 1.49 us  [paired_local(): from_x = lax.ppermute(cross, 'seq', to_x)]
  transfers between devices with their start and end apart: 12 -> 13, of which waited for: 10 -> 10; matrix products, arithmetic and copies ran while one was open for 0% -> 0% of each run, Pallas kernels for 8% -> 12%
where the time goes in v4:
time: 57.2 us; the launch traced here: 57 us
  waiting for transfers between devices  27.9 us (49%)
  starting transfers between devices  15.1 us (26%)
  Pallas kernels  9.61 us (17%)
  local copies, waits for them, and re-layouts  3.52 us (6%)
  between operations  0.81 us (1%)
    pallas_call x11, Pallas kernels, run(): pl.pallas_call(kernel, out_shape=shapes, in_specs=specs or [VMEM] * len(a...  9.61 us
    ppermute x1, waiting for transfers between devices, paired_local(): near = lax.ppermute(message, 'seq', to_x)  7.71 us
    ppermute x3, waiting for transfers between devices, paired_local(): lax.ppermute(total, 'group', pairs((groups,), lambda g, k=k: (g ^ k,)))  5.4 us
    ppermute x1, waiting for transfers between devices, paired_local(): own_got = lax.ppermute(own_sent, 'seq', to_x)  5.13 us
    ppermute x3, starting transfers between devices, paired_local(): lax.ppermute(total, 'group', pairs((groups,), lambda g, k=k: (g ^ k,)))  4.45 us
    ppermute x1, waiting for transfers between devices, paired_local(): other_got = lax.ppermute(other_sent, 'seq', to_x)  3.94 us
    unnamed x20, local copies, waits for them, and re-layouts  3.52 us
    ppermute x1, starting transfers between devices, paired_local(): near = lax.ppermute(message, 'seq', to_x)  3.03 us
  transfers between devices with their start and end apart: 13, of which 10 were waited for; matrix products, arithmetic and copies ran while one was open for 0% of the time, Pallas kernels for 12%

profile of v4, /device:TPU:0, one launch (start us, length us, event | category | flops | bytes accessed | tf_op | source)
XLA Modules:
  0.0 57.0 jit_solution(15197048545182172086)
XLA Ops:
  0.0 1.1 %shard_map.147 = bf16[128,1280]{1,0:T(8,128)(2,1)S(1)} custom-call(bf16[128,5120]{1,0:T(8,128)(2,1)} %stream_hbm.3), custom_call_target="tpu_custom_call" | custom-call | bytes 655360 | tf_op jit(solution)/shard_map/pallas_call | solution.py:56
  1.1 3.0 %collective-permute-start = (bf16[128,1280]{1,0:T(8,128)(2,1)S(1)}, bf16[128,1280]{1,0:T(8,128)(2,1)S(1)}, u32[]{:S(2)}, u32[]{:S(2)}) collective-permute-start(bf16[128,1280]{1,0:T(8,128)(2,1)S(1)} %shard_map.147), channel_id=1, source_target_pairs={{0,4},{4,0},{1,5},{5,1},{2,6},{6,2},{3,7},{7,3},{8,12},{12,8},{9,1... | collective-permute-start | bytes 983048 | tf_op jit(solution)/shard_map/ppermute | solution.py:388
  4.1 7.7 %collective-permute-done.raw_ref = bf16[128,1280]{1,0:T(8,128)(2,1)S(1)} collective-permute-done((bf16[128,1280]{1,0:T(8,128)(2,1)S(1)}, bf16[128,1280]{1,0:T(8,128)(2,1)S(1)}, u32[]{:S(2)}, u32[]{:S(2)}) %collective-permute-start) | collective-permute-done | bytes 327712 | tf_op jit(solution)/shard_map/ppermute | solution.py:388
  12.5 3.3 %shard_map.145 = (bf16[128,2560]{1,0:T(8,128)(2,1)S(1)}, f32[72,128]{1,0:T(8,128)S(1)}, f32[128,64]{1,0:T(8,128)S(1)}, f32[2,1280]{1,0:T(2,128)S(1)}) custom-call(s32[1]{0:T(128)S(6)} %copy.16.step_any, bf16[64,128]{1,0:T(8,128)(2,1)} %bitcast.3, bf16[64,128]{1,0:T(8,128)(2,1)} %bitcast.4, bf16[128,5120]{1,0:T(8,128)(2,1)} %stream_hbm.3, ...), custom_call_target="tpu_custom_call" | custom-call | bytes 3409924 | tf_op jit(solution)/shard_map/pallas_call | solution.py:56
  15.8 1.8 %collective-permute-start.2 = (f32[72,128]{1,0:T(8,128)S(1)}, f32[72,128]{1,0:T(8,128)S(1)}, u32[]{:S(2)}, u32[]{:S(2)}) collective-permute-start(f32[72,128]{1,0:T(8,128)S(1)} %get-tuple-element.26), channel_id=1, source_target_pairs={{0,4},{4,0},{1,5},{5,1},{2,6},{6,2},{3,7},{7,3},{8,12},{12,8},{9,1... | collective-permute-start | bytes 110600 | tf_op jit(solution)/shard_map/ppermute | solution.py:415
  17.6 1.1 %copy-done.3 = bf16[2560,128]{1,0:T(8,128)(2,1)S(1)} copy-done((bf16[2560,128]{1,0:T(8,128)(2,1)S(1)}, bf16[2560,128]{1,0:T(8,128)(2,1)}, u32[]{:S(2)}) %copy-start.3) | copy-done | bytes 655384
  18.7 1.1 %copy-done.5 = bf16[64,5120]{1,0:T(8,128)(2,1)S(1)} copy-done((bf16[64,5120]{1,0:T(8,128)(2,1)S(1)}, bf16[64,5120]{1,0:T(8,128)(2,1)}, u32[]{:S(2)}) %copy-start.5) | copy-done | bytes 655384
  19.8 1.3 %copy-done.6 = bf16[256,2560]{1,0:T(8,128)(2,1)S(1)} copy-done((bf16[256,2560]{1,0:T(8,128)(2,1)S(1)}, bf16[256,2560]{1,0:T(8,128)(2,1)}, u32[]{:S(2)}) %copy-start.6) | copy-done | bytes 1310744
  21.1 1.3 %shard_map.146 = (bf16[128,1024]{1,0:T(8,128)(2,1)S(1)}, f32[128,512]{1,0:T(8,128)S(1)}, f32[128,64]{1,0:T(8,128)S(1)}) custom-call(bf16[128,2560]{1,0:T(8,128)(2,1)S(1)} %get-tuple-element.24.normed_ref, bf16[2560,256]{1,0:T(8,128)(2,1)S(1)} %copy-done, bf16[2560,256]{1,0:T(8,128)(2,1)S(1)} %copy-done.1, bf16[2560,256]{1,0:T(8,128)(2,1)S(1)} %copy-done.2, ...), custom_call_target="tpu_custom_call" | custom-call | flops 587202560 | bytes 7766016 | tf_op jit(solution)/shard_map/pallas_call | solution.py:56
  22.4 0.3 collective-permute-start.4
  22.8 0.7 %shard_map.148 = (f32[128,256]{1,0:T(8,128)S(1)}, f32[128,256]{1,0:T(8,128)S(1)}, f32[128,256]{1,0:T(8,128)S(1)}, f32[128,128]{1,0:T(8,128)S(1)}) custom-call(bf16[128,1280]{1,0:T(8,128)(2,1)S(1)} %collective-permute-done.raw_ref, f32[72,128]{1,0:T(8,128)S(1)} %collective-permute-done.2.rows_ref, bf16[64,5120]{1,0:T(8,128)(2,1)S(1)} %copy-done.4, ...), custom_call_target="tpu_custom_call" | custom-call | flops 293601280 | bytes 6076416 | tf_op jit(solution)/shard_map/pallas_call | solution.py:56
  23.5 0.7 %shard_map.149 = (bf16[128,896]{1,0:T(8,128)(2,1)S(1)}, f32[128,512]{1,0:T(8,128)S(1)}) custom-call(bf16[128,1280]{1,0:T(8,128)(2,1)S(1)} %collective-permute-done.1.raw_ref, f32[72,128]{1,0:T(8,128)S(1)} %collective-permute-done.2.rows_ref, bf16[64,5120]{1,0:T(8,128)(2,1)S(1)} %copy-done.4, f32[2,1280]{1,0:T(2,128)S(1)} %get-tuple-element.27.gain_ref, ...), custom_call_target="tpu_custom_call" | custom-call | flops 293601280 | bytes 6567936 | tf_op jit(solution)/shard_map/pallas_call | solution.py:56
  24.2 1.8 %collective-permute-start.3 = (bf16[128,896]{1,0:T(8,128)(2,1)S(1)}, bf16[128,896]{1,0:T(8,128)(2,1)S(1)}, u32[]{:S(2)}, u32[]{:S(2)}) collective-permute-start(bf16[128,896]{1,0:T(8,128)(2,1)S(1)} %get-tuple-element.32), channel_id=1, source_target_pairs={{0,4},{4,0},{1,5},{5,1},{2,6},{6,2},{3,7},{7,3},{8,12},{12,8},{9,1... | collective-permute-start | bytes 688136 | tf_op jit(solution)/shard_map/ppermute | solution.py:448
  26.0 0.5 shard_map.150.readout_of_up_ref
  26.5 5.1 %collective-permute-done.4.got_ref = bf16[128,1024]{1,0:T(8,128)(2,1)S(1)} collective-permute-done((bf16[128,1024]{1,0:T(8,128)(2,1)S(1)}, bf16[128,1024]{1,0:T(8,128)(2,1)S(1)}, u32[]{:S(2)}, u32[]{:S(2)}) %collective-permute-start.4) | collective-permute-done | bytes 262176 | tf_op jit(solution)/shard_map/ppermute | solution.py:427
  31.7 0.2 shard_map.151
  31.9 3.9 %collective-permute-done.3.got_ref = bf16[128,896]{1,0:T(8,128)(2,1)S(1)} collective-permute-done((bf16[128,896]{1,0:T(8,128)(2,1)S(1)}, bf16[128,896]{1,0:T(8,128)(2,1)S(1)}, u32[]{:S(2)}, u32[]{:S(2)}) %collective-permute-start.3) | collective-permute-done | bytes 229408 | tf_op jit(solution)/shard_map/ppermute | solution.py:448
  35.8 0.9 %shard_map.152 = (f32[128,128]{1,0:T(8,128)S(1)}, f32[128,128]{1,0:T(8,128)S(1)}) custom-call(f32[128,512]{1,0:T(8,128)S(1)} %get-tuple-element.25.kept_ref, bf16[128,896]{1,0:T(8,128)(2,1)S(1)} %collective-permute-done.3.got_ref, bf16[128,256]{1,0:T(8,128)(2,1)S(1)} %copy-done.8, bf16[4,128,128]{2,1,0:T(8,128)(2,1)S(1)} %get-tuple-element.36.set_ref, ...), custom_call_target="tpu_custom_call" | custom-call | bytes 917504 | tf_op jit(solution)/shard_map/pallas_call | solution.py:56
  36.8 1.2 %collective-permute-done.5.got_ref = f32[128,128]{1,0:T(8,128)S(1)} collective-permute-done((f32[128,128]{1,0:T(8,128)S(1)}, f32[128,128]{1,0:T(8,128)S(1)}, u32[]{:S(2)}, u32[]{:S(2)}) %collective-permute-start.5) | collective-permute-done | bytes 65568 | tf_op jit(solution)/shard_map/ppermute | solution.py:467
  38.1 1.5 %collective-permute-start.8 = (bf16[96,128]{1,0:T(8,128)(2,1)S(1)}, bf16[96,128]{1,0:T(8,128)(2,1)S(1)}, u32[]{:S(2)}, u32[]{:S(2)}) collective-permute-start(bf16[96,128]{1,0:T(8,128)(2,1)S(1)} %get-tuple-element.42), channel_id=1, source_target_pairs={{0,6},{1,7},{2,4},{3,5},{4,2},{5,3},{6,0},{7,1},{8,14},{9,15},{10,... | collective-permute-start | bytes 73736 | tf_op jit(solution)/shard_map/ppermute | solution.py:472
  39.6 1.5 %collective-permute-start.7 = (bf16[96,128]{1,0:T(8,128)(2,1)S(1)}, bf16[96,128]{1,0:T(8,128)(2,1)S(1)}, u32[]{:S(2)}, u32[]{:S(2)}) collective-permute-start(bf16[96,128]{1,0:T(8,128)(2,1)S(1)} %get-tuple-element.42), channel_id=1, source_target_pairs={{0,4},{4,0},{1,5},{5,1},{2,6},{6,2},{3,7},{7,3},{8,12},{12,8},{9,1... | collective-permute-start | bytes 73736 | tf_op jit(solution)/shard_map/ppermute | solution.py:470
  41.1 0.5 collective-permute-start.6
  41.6 1.2 %collective-permute-done.8 = bf16[96,128]{1,0:T(8,128)(2,1)S(1)} collective-permute-done((bf16[96,128]{1,0:T(8,128)(2,1)S(1)}, bf16[96,128]{1,0:T(8,128)(2,1)S(1)}, u32[]{:S(2)}, u32[]{:S(2)}) %collective-permute-start.8) | collective-permute-done | bytes 24608 | tf_op jit(solution)/shard_map/ppermute | solution.py:472
  42.8 0.6 %collective-permute-done.7 = bf16[96,128]{1,0:T(8,128)(2,1)S(1)} collective-permute-done((bf16[96,128]{1,0:T(8,128)(2,1)S(1)}, bf16[96,128]{1,0:T(8,128)(2,1)S(1)}, u32[]{:S(2)}, u32[]{:S(2)}) %collective-permute-start.7) | collective-permute-done | bytes 24608 | tf_op jit(solution)/shard_map/ppermute | solution.py:470
  43.4 1.5 %collective-permute-done.6 = bf16[96,128]{1,0:T(8,128)(2,1)S(1)} collective-permute-done((bf16[96,128]{1,0:T(8,128)(2,1)S(1)}, bf16[96,128]{1,0:T(8,128)(2,1)S(1)}, u32[]{:S(2)}, u32[]{:S(2)}) %collective-permute-start.6) | collective-permute-done | bytes 24608 | tf_op jit(solution)/shard_map/ppermute | solution.py:471
  44.9 1.6 %collective-permute-start.9 = (bf16[96,128]{1,0:T(8,128)(2,1)S(1)}, bf16[96,128]{1,0:T(8,128)(2,1)S(1)}, u32[]{:S(2)}, u32[]{:S(2)}) collective-permute-start(bf16[96,128]{1,0:T(8,128)(2,1)S(1)} %add_convert_fusion.refs_0_), channel_id=1, source_target_pairs={{0,8},{8,0},{16,24},{24,16},{1,9},{9,1},{17,25},{25,17},{2,10},{10... | collective-permute-start | bytes 73736 | tf_op jit(solution)/shard_map/ppermute | solution.py:478
  46.6 2.6 %collective-permute-start.10 = (bf16[96,128]{1,0:T(8,128)(2,1)S(1)}, bf16[96,128]{1,0:T(8,128)(2,1)S(1)}, u32[]{:S(2)}, u32[]{:S(2)}) collective-permute-start(bf16[96,128]{1,0:T(8,128)(2,1)S(1)} %add_convert_fusion.refs_0_), channel_id=1, source_target_pairs={{0,16},{8,24},{16,0},{24,8},{1,17},{9,25},{17,1},{25,9},{2,18},{10... | collective-permute-start | bytes 73736 | tf_op jit(solution)/shard_map/ppermute | solution.py:478
  49.1 0.2 collective-permute-start.11
  49.4 2.1 %collective-permute-done.10.refs_2_ = bf16[96,128]{1,0:T(8,128)(2,1)S(1)} collective-permute-done((bf16[96,128]{1,0:T(8,128)(2,1)S(1)}, bf16[96,128]{1,0:T(8,128)(2,1)S(1)}, u32[]{:S(2)}, u32[]{:S(2)}) %collective-permute-start.10) | collective-permute-done | bytes 24608 | tf_op jit(solution)/shard_map/ppermute | solution.py:478
  51.4 3.3 %collective-permute-done.11.refs_3_ = bf16[96,128]{1,0:T(8,128)(2,1)S(1)} collective-permute-done((bf16[96,128]{1,0:T(8,128)(2,1)S(1)}, bf16[96,128]{1,0:T(8,128)(2,1)S(1)}, u32[]{:S(2)}, u32[]{:S(2)}) %collective-permute-start.11) | collective-permute-done | bytes 24608 | tf_op jit(solution)/shard_map/ppermute | solution.py:478
  55.0 1.2 %collective-permute-done.12.theirs_ref = f32[40,128]{1,0:T(8,128)S(1)} collective-permute-done((f32[40,128]{1,0:T(8,128)S(1)}, f32[40,128]{1,0:T(8,128)S(1)}, u32[]{:S(2)}, u32[]{:S(2)}) %collective-permute-start.12) | collective-permute-done | bytes 20512 | tf_op jit(solution)/shard_map/ppermute | solution.py:482
  56.2 0.8 %shard_map.155 = f32[64,128]{1,0:T(8,128)} custom-call(f32[40,128]{1,0:T(8,128)S(1)} %shard_map.154.mine_ref, f32[40,128]{1,0:T(8,128)S(1)} %collective-permute-done.12.theirs_ref), custom_call_target="tpu_custom_call" | custom-call | bytes 73728 | tf_op jit(solution)/shard_map/pallas_call | solution.py:56
  (26 shorter events, 0.4 us)
Async XLA Ops:
  0.0 17.6 %copy-start.2 = (bf16[2560,256]{1,0:T(8,128)(2,1)S(1)}, bf16[2560,256]{1,0:T(8,128)(2,1)}, u32[]{:S(2)}) copy-start(bf16[2560,256]{1,0:T(8,128)(2,1)} %v_ref.5) | copy-start | bytes 3932164
  1.1 10.7 %collective-permute-start = (bf16[128,1280]{1,0:T(8,128)(2,1)S(1)}, bf16[128,1280]{1,0:T(8,128)(2,1)S(1)}, u32[]{:S(2)}, u32[]{:S(2)}) collective-permute-start(bf16[128,1280]{1,0:T(8,128)(2,1)S(1)} %shard_map.147), channel_id=1, source_target_pairs={{0,4},{4,0},{1,5},{5,1},{2,6},{6,2},{3,7},{7,3},{8,12},{12,8},{9,1... | collective-permute-start | bytes 983048 | tf_op jit(solution)/shard_map/ppermute | solution.py:388
  11.8 11.6 %collective-permute-start.1 = (bf16[128,1280]{1,0:T(8,128)(2,1)S(1)}, bf16[128,1280]{1,0:T(8,128)(2,1)S(1)}, u32[]{:S(2)}, u32[]{:S(2)}) collective-permute-start(bf16[128,1280]{1,0:T(8,128)(2,1)S(1)} %collective-permute-done.raw_ref), channel_id=1, source_target_pairs={{0,1},{1,0},{2,3},{3,2},{4,5},{5,4},{6,7},{7,6},{8,9},{9,8},{10,11... | collective-permute-start | bytes 983048 | tf_op jit(solution)/shard_map/ppermute | solution.py:434
  12.5 5.1 %copy-start = (bf16[2560,256]{1,0:T(8,128)(2,1)S(1)}, bf16[2560,256]{1,0:T(8,128)(2,1)}, u32[]{:S(2)}) copy-start(bf16[2560,256]{1,0:T(8,128)(2,1)} %q_ref.5) | copy-start | bytes 3932164
  12.5 5.1 %copy-start.1 = (bf16[2560,256]{1,0:T(8,128)(2,1)S(1)}, bf16[2560,256]{1,0:T(8,128)(2,1)}, u32[]{:S(2)}) copy-start(bf16[2560,256]{1,0:T(8,128)(2,1)} %k_ref.5) | copy-start | bytes 3932164
  15.8 7.0 %collective-permute-start.2 = (f32[72,128]{1,0:T(8,128)S(1)}, f32[72,128]{1,0:T(8,128)S(1)}, u32[]{:S(2)}, u32[]{:S(2)}) collective-permute-start(f32[72,128]{1,0:T(8,128)S(1)} %get-tuple-element.26), channel_id=1, source_target_pairs={{0,4},{4,0},{1,5},{5,1},{2,6},{6,2},{3,7},{7,3},{8,12},{12,8},{9,1... | collective-permute-start | bytes 110600 | tf_op jit(solution)/shard_map/ppermute | solution.py:415
  17.6 1.1 %copy-start.3 = (bf16[2560,128]{1,0:T(8,128)(2,1)S(1)}, bf16[2560,128]{1,0:T(8,128)(2,1)}, u32[]{:S(2)}) copy-start(bf16[2560,128]{1,0:T(8,128)(2,1)} %down_ref.6) | copy-start | bytes 1966084
  18.7 1.1 %copy-start.5 = (bf16[64,5120]{1,0:T(8,128)(2,1)S(1)}, bf16[64,5120]{1,0:T(8,128)(2,1)}, u32[]{:S(2)}) copy-start(bf16[64,5120]{1,0:T(8,128)(2,1)} %readout_ref.3) | copy-start | bytes 1966084
  19.8 1.3 %copy-start.6 = (bf16[256,2560]{1,0:T(8,128)(2,1)S(1)}, bf16[256,2560]{1,0:T(8,128)(2,1)}, u32[]{:S(2)}) copy-start(bf16[256,2560]{1,0:T(8,128)(2,1)} %output_ref.1) | copy-start | bytes 3932164
  21.1 1.6 %copy-start.4 = (bf16[64,5120]{1,0:T(8,128)(2,1)S(1)}, bf16[64,5120]{1,0:T(8,128)(2,1)}, u32[]{:S(2)}) copy-start(bf16[64,5120]{1,0:T(8,128)(2,1)} %patch_ref.3) | copy-start | bytes 1966084
  22.4 9.2 %collective-permute-start.4 = (bf16[128,1024]{1,0:T(8,128)(2,1)S(1)}, bf16[128,1024]{1,0:T(8,128)(2,1)S(1)}, u32[]{:S(2)}, u32[]{:S(2)}) collective-permute-start(bf16[128,1024]{1,0:T(8,128)(2,1)S(1)} %get-tuple-element.34), channel_id=1, source_target_pairs={{0,4},{4,0},{1,5},{5,1},{2,6},{6,2},{3,7},{7,3},{8,12},{12,8},{9,1... | collective-permute-start | bytes 786440 | tf_op jit(solution)/shard_map/ppermute | solution.py:427
  23.5 2.6 %copy-start.7 = (bf16[128,5120]{1,0:T(8,128)(2,1)S(1)}, bf16[128,5120]{1,0:T(8,128)(2,1)}, u32[]{:S(2)}) copy-start(bf16[128,5120]{1,0:T(8,128)(2,1)} %up_ref.3) | copy-start | bytes 3932164
  24.2 7.5 %copy-start.8 = (bf16[128,256]{1,0:T(8,128)(2,1)S(1)}, bf16[128,256]{1,0:T(8,128)(2,1)}, u32[]{:S(2)}) copy-start(bf16[128,256]{1,0:T(8,128)(2,1)} %up_ref.5) | copy-start | bytes 196612
  24.2 7.4 %copy-start.9 = (bf16[256,128]{1,0:T(8,128)(2,1)S(1)}, bf16[256,128]{1,0:T(8,128)(2,1)}, u32[]{:S(2)}) copy-start(bf16[256,128]{1,0:T(8,128)(2,1)} %down_ref.7) | copy-start | bytes 196612
  24.2 11.6 %collective-permute-start.3 = (bf16[128,896]{1,0:T(8,128)(2,1)S(1)}, bf16[128,896]{1,0:T(8,128)(2,1)S(1)}, u32[]{:S(2)}, u32[]{:S(2)}) collective-permute-start(bf16[128,896]{1,0:T(8,128)(2,1)S(1)} %get-tuple-element.32), channel_id=1, source_target_pairs={{0,4},{4,0},{1,5},{5,1},{2,6},{6,2},{3,7},{7,3},{8,12},{12,8},{9,1... | collective-permute-start | bytes 688136 | tf_op jit(solution)/shard_map/ppermute | solution.py:448
  36.7 1.3 %collective-permute-start.5 = (f32[128,128]{1,0:T(8,128)S(1)}, f32[128,128]{1,0:T(8,128)S(1)}, u32[]{:S(2)}, u32[]{:S(2)}) collective-permute-start(f32[128,128]{1,0:T(8,128)S(1)} %get-tuple-element.40), channel_id=1, source_target_pairs={{0,1},{1,0},{2,3},{3,2},{4,5},{5,4},{6,7},{7,6},{8,9},{9,8},{10,11... | collective-permute-start | bytes 196616 | tf_op jit(solution)/shard_map/ppermute | solution.py:467
  38.1 4.7 %collective-permute-start.8 = (bf16[96,128]{1,0:T(8,128)(2,1)S(1)}, bf16[96,128]{1,0:T(8,128)(2,1)S(1)}, u32[]{:S(2)}, u32[]{:S(2)}) collective-permute-start(bf16[96,128]{1,0:T(8,128)(2,1)S(1)} %get-tuple-element.42), channel_id=1, source_target_pairs={{0,6},{1,7},{2,4},{3,5},{4,2},{5,3},{6,0},{7,1},{8,14},{9,15},{10,... | collective-permute-start | bytes 73736 | tf_op jit(solution)/shard_map/ppermute | solution.py:472
  39.6 3.8 %collective-permute-start.7 = (bf16[96,128]{1,0:T(8,128)(2,1)S(1)}, bf16[96,128]{1,0:T(8,128)(2,1)S(1)}, u32[]{:S(2)}, u32[]{:S(2)}) collective-permute-start(bf16[96,128]{1,0:T(8,128)(2,1)S(1)} %get-tuple-element.42), channel_id=1, source_target_pairs={{0,4},{4,0},{1,5},{5,1},{2,6},{6,2},{3,7},{7,3},{8,12},{12,8},{9,1... | collective-permute-start | bytes 73736 | tf_op jit(solution)/shard_map/ppermute | solution.py:470
  41.1 3.8 %collective-permute-start.6 = (bf16[96,128]{1,0:T(8,128)(2,1)S(1)}, bf16[96,128]{1,0:T(8,128)(2,1)S(1)}, u32[]{:S(2)}, u32[]{:S(2)}) collective-permute-start(bf16[96,128]{1,0:T(8,128)(2,1)S(1)} %get-tuple-element.41), channel_id=1, source_target_pairs={{0,2},{1,3},{2,0},{3,1},{4,6},{5,7},{6,4},{7,5},{8,10},{9,11},{10,... | collective-permute-start | bytes 73736 | tf_op jit(solution)/shard_map/ppermute | solution.py:471
  44.9 4.5 %collective-permute-start.9 = (bf16[96,128]{1,0:T(8,128)(2,1)S(1)}, bf16[96,128]{1,0:T(8,128)(2,1)S(1)}, u32[]{:S(2)}, u32[]{:S(2)}) collective-permute-start(bf16[96,128]{1,0:T(8,128)(2,1)S(1)} %add_convert_fusion.refs_0_), channel_id=1, source_target_pairs={{0,8},{8,0},{16,24},{24,16},{1,9},{9,1},{17,25},{25,17},{2,10},{10... | collective-permute-start | bytes 73736 | tf_op jit(solution)/shard_map/ppermute | solution.py:478
  46.6 4.9 %collective-permute-start.10 = (bf16[96,128]{1,0:T(8,128)(2,1)S(1)}, bf16[96,128]{1,0:T(8,128)(2,1)S(1)}, u32[]{:S(2)}, u32[]{:S(2)}) collective-permute-start(bf16[96,128]{1,0:T(8,128)(2,1)S(1)} %add_convert_fusion.refs_0_), channel_id=1, source_target_pairs={{0,16},{8,24},{16,0},{24,8},{1,17},{9,25},{17,1},{25,9},{2,18},{10... | collective-permute-start | bytes 73736 | tf_op jit(solution)/shard_map/ppermute | solution.py:478
  49.1 5.6 %collective-permute-start.11 = (bf16[96,128]{1,0:T(8,128)(2,1)S(1)}, bf16[96,128]{1,0:T(8,128)(2,1)S(1)}, u32[]{:S(2)}, u32[]{:S(2)}) collective-permute-start(bf16[96,128]{1,0:T(8,128)(2,1)S(1)} %add_convert_fusion.refs_0_), channel_id=1, source_target_pairs={{0,24},{8,16},{16,8},{24,0},{1,25},{9,17},{17,9},{25,1},{2,26},{10... | collective-permute-start | bytes 73736 | tf_op jit(solution)/shard_map/ppermute | solution.py:478
  54.9 1.3 %collective-permute-start.12 = (f32[40,128]{1,0:T(8,128)S(1)}, f32[40,128]{1,0:T(8,128)S(1)}, u32[]{:S(2)}, u32[]{:S(2)}) collective-permute-start(f32[40,128]{1,0:T(8,128)S(1)} %shard_map.154.mine_ref), channel_id=1, source_target_pairs={{0,1},{1,0},{2,3},{3,2},{4,5},{5,4},{6,7},{7,6},{8,9},{9,8},{10,11... | collective-permute-start | bytes 61448 | tf_op jit(solution)/shard_map/ppermute | solution.py:482

commit v5 on v4

--- a/solution.py
+++ b/solution.py
@@ -142,10 +142,14 @@
             squares = squares + wide[:, i * 128 : (i + 1) * 128]
     mean = jnp.sum(squares, axis=1, keepdims=True) / (parts * quarter)
     inverse = lax.rsqrt(mean + 1e-06)
-    rows_ref[:channels] = noisy.astype(F32)
-    rows_ref[channels:] = jnp.broadcast_to(inverse, (tokens, tokens)).T[
-        : rows_ref.shape[0] - channels
-    ]
+    rows_ref[:channels] = noisy
+    scale = jnp.broadcast_to(inverse, (tokens, tokens)).T[:8]
+    first, _ = high_low(scale)
+    second, third = high_low(scale - first.astype(F32))
+    row = lax.broadcasted_iota(jnp.int32, (16, tokens), 0)
+    terms = [jnp.concatenate([x.astype(F32)] * 2, axis=0) for x in (first, second, third)]
+    terms = jnp.where(row == 0, terms[0], jnp.where(row == 1, terms[1], terms[2]))
+    rows_ref[channels:] = terms.astype(BF16)
     once = (lax.axis_index("group") == 0) & (lax.axis_index("head") == 0)
     base_ref[...] = jnp.where(once, base, 0.0).T
     gain_copy.wait()
@@ -178,15 +182,28 @@
 
 
 def own_kernel(
-    normed_ref, q_ref, k_ref, v_ref, down_ref, output_ref, readout_ref,
-    sent_ref, kept_ref, mix_ref, mix_v,
+    normed_ref, q_ref, k_ref, v_ref, down_hbm, output_hbm, readout_hbm,
+    sent_ref, kept_ref, mix_ref,
+    down_v, output_v, readout_v, mix_v, sems,
 ):
     seq = lax.axis_index("seq")
+    copies = [
+        pltpu.make_async_copy(down_hbm, down_v, sems.at[0]),
+        pltpu.make_async_copy(output_hbm, output_v, sems.at[1]),
+        pltpu.make_async_copy(
+            readout_hbm.at[:, aligned(seq, readout_v.shape[1])], readout_v, sems.at[2]
+        ),
+    ]
+    for copy in copies:
+        copy.start()
     normed = normed_ref[...]
-    parts = [dot(normed, w[...]) for w in (q_ref, k_ref, v_ref, down_ref)]
+    parts = [dot(normed, w[...]) for w in (q_ref, k_ref, v_ref)]
+    copies[0].wait()
+    parts.append(dot(normed, down_v[...]))
     partial_outputs(parts, seq, sent_ref, kept_ref)
-    readout = readout_ref[:, aligned(seq, normed.shape[1])]
-    mix_v[...] = contract_final_axis(output_ref[...], readout)
+    for copy in copies[1:]:
+        copy.wait()
+    mix_v[...] = contract_final_axis(output_v[...], readout_v[...])
     rows, channels = mix_ref.shape
     theirs = mix_v[aligned(1 - seq, rows), :]
     high = theirs.astype(BF16).astype(F32)
@@ -203,8 +220,10 @@
     tokens, quarter = raw_ref.shape
     channels = patch_ref.shape[0]
     quarters = lax.axis_index("seq") * 2 + part
-    noisy = rows_ref[:channels].astype(BF16)
-    inverse = jnp.broadcast_to(rows_ref[channels : channels + 1], (tokens, tokens)).T[:, :1]
+    noisy = rows_ref[:channels]
+    terms = rows_ref[channels:].astype(F32)
+    scale = (terms[:1] + terms[1:2]) + terms[2:3]
+    inverse = jnp.broadcast_to(scale, (tokens, tokens)).T[:, :1]
     embedded = lax.dot_general(
         noisy, patch_ref[:, aligned(quarters, quarter)],
         (((0,), (0,)), ((), ())), preferred_element_type=F32,
@@ -394,7 +413,7 @@
         first_kernel,
         [
             ((tokens, half_width), BF16),
-            ((channels + 8, tokens), F32),
+            ((channels + 16, tokens), BF16),
             ((tokens, channels), F32),
             ((2, quarter), F32),
         ],
@@ -420,8 +439,21 @@
             ((tokens, 4 * columns), F32),
             ((columns, channels), F32),
         ],
-        (normed, *weights, output_matrix, velocity_readout_weight),
-        scratch=[pltpu.VMEM((local_columns, channels), F32)],
+        (
+            normed, *weights[:3],
+            *(
+                pltpu.with_memory_space_constraint(x, pltpu.HBM)
+                for x in (adapter_query_down, output_matrix, velocity_readout_weight)
+            ),
+        ),
+        [VMEM] * 4 + [HBM] * 3,
+        scratch=[
+            pltpu.VMEM(adapter_query_down.shape, BF16),
+            pltpu.VMEM(output_matrix.shape, BF16),
+            pltpu.VMEM((channels, half_width), BF16),
+            pltpu.VMEM((local_columns, channels), F32),
+            pltpu.SemaphoreType.DMA((3,)),
+        ],
         flops=partial_flops,
     )
     own_got = lax.ppermute(own_sent, "seq", to_x)
@@ -474,10 +506,10 @@
         from_x.astype(F32) + from_xy.astype(F32)
     )
     total = total.astype(BF16)
-    totals = [total] + [
-        lax.ppermute(total, "group", pairs((groups,), lambda g, k=k: (g ^ k,)))
-        for k in range(1, groups)
-    ]
+    totals = [total]
+    for k in range(1, groups):
+        to_group = pairs((groups,), lambda g, k=k: (g ^ k,))
+        totals.append(lax.ppermute(total, "group", to_group))
     (packet,) = run(error_kernel, [((share // 2 + 8, 2 * channels), F32)], totals)
     answer = lax.ppermute(packet, "head", to_core)
     (out,) = run(

time: 57.2 us -> 55.1 us (0.963)
  local copies, waits for them, and re-layouts: 3.52 us -> 0.05 us
  Pallas kernels: 9.61 us -> 11.1 us
    unnamed x20 -> x18, local copies, waits for them, and re-layouts: 3.52 us -> 0.05 us
    pallas_call x11, Pallas kernels: 9.61 us -> 11.1 us  [run(): pl.pallas_call(kernel, out_shape=shapes, in_specs=specs or [VMEM] * len(a...]
  transfers between devices with their start and end apart: 13 -> 13, of which waited for: 10 -> 10; matrix products, arithmetic and copies ran while one was open for 0% -> 0% of each run, Pallas kernels for 12% -> 15%
where the time goes in v5:
time: 55.1 us; the launch traced here: 54.9 us
  waiting for transfers between devices  27.9 us (51%)
  starting transfers between devices  15.1 us (27%)
  Pallas kernels  11.1 us (20%)
  between operations  0.83 us (2%)
    pallas_call x11, Pallas kernels, run(): pl.pallas_call(kernel, out_shape=shapes, in_specs=specs or [VMEM] * len(a...  11.1 us
    ppermute x1, waiting for transfers between devices, paired_local(): near = lax.ppermute(message, 'seq', to_x)  7.71 us
    ppermute x3, waiting for transfers between devices, paired_local(): totals.append(lax.ppermute(total, 'group', to_group))  5.41 us
    ppermute x1, waiting for transfers between devices, paired_local(): own_got = lax.ppermute(own_sent, 'seq', to_x)  5.06 us
    ppermute x3, starting transfers between devices, paired_local(): totals.append(lax.ppermute(total, 'group', to_group))  4.45 us
    ppermute x1, waiting for transfers between devices, paired_local(): other_got = lax.ppermute(other_sent, 'seq', to_x)  3.95 us
    ppermute x1, starting transfers between devices, paired_local(): near = lax.ppermute(message, 'seq', to_x)  3.03 us
    ppermute x1, starting transfers between devices, paired_local(): other_rows = lax.ppermute(rows, 'seq', to_x)  1.81 us
  transfers between devices with their start and end apart: 13, of which 10 were waited for; matrix products, arithmetic and copies ran while one was open for 0% of the time, Pallas kernels for 15%

profile of v5, /device:TPU:0, one launch (start us, length us, event | category | flops | bytes accessed | tf_op | source)
XLA Modules:
  0.0 54.9 jit_solution(9662297061163883927)
XLA Ops:
  0.0 1.1 %shard_map.147 = bf16[128,1280]{1,0:T(8,128)(2,1)S(1)} custom-call(bf16[128,5120]{1,0:T(8,128)(2,1)} %stream_hbm.3), custom_call_target="tpu_custom_call" | custom-call | bytes 655360 | tf_op jit(solution)/shard_map/pallas_call | solution.py:56
  1.1 3.0 %collective-permute-start = (bf16[128,1280]{1,0:T(8,128)(2,1)S(1)}, bf16[128,1280]{1,0:T(8,128)(2,1)S(1)}, u32[]{:S(2)}, u32[]{:S(2)}) collective-permute-start(bf16[128,1280]{1,0:T(8,128)(2,1)S(1)} %shard_map.147), channel_id=1, source_target_pairs={{0,4},{4,0},{1,5},{5,1},{2,6},{6,2},{3,7},{7,3},{8,12},{12,8},{9,1... | collective-permute-start | bytes 983048 | tf_op jit(solution)/shard_map/ppermute | solution.py:407
  4.1 7.7 %collective-permute-done.raw_ref = bf16[128,1280]{1,0:T(8,128)(2,1)S(1)} collective-permute-done((bf16[128,1280]{1,0:T(8,128)(2,1)S(1)}, bf16[128,1280]{1,0:T(8,128)(2,1)S(1)}, u32[]{:S(2)}, u32[]{:S(2)}) %collective-permute-start) | collective-permute-done | bytes 327712 | tf_op jit(solution)/shard_map/ppermute | solution.py:407
  12.5 3.3 %shard_map.145 = (bf16[128,2560]{1,0:T(8,128)(2,1)S(1)}, bf16[80,128]{1,0:T(8,128)(2,1)S(1)}, f32[128,64]{1,0:T(8,128)S(1)}, f32[2,1280]{1,0:T(2,128)S(1)}) custom-call(s32[1]{0:T(128)S(6)} %copy.16.step_any, bf16[64,128]{1,0:T(8,128)(2,1)} %bitcast.3, bf16[64,128]{1,0:T(8,128)(2,1)} %bitcast.4, bf16[128,5120]{1,0:T(8,128)(2,1)} %stream_hbm.3, ...), custom_call_target="tpu_custom_call" | custom-call | bytes 3393540 | tf_op jit(solution)/shard_map/pallas_call | solution.py:56
  15.8 1.8 %collective-permute-start.2 = (bf16[80,128]{1,0:T(8,128)(2,1)S(1)}, bf16[80,128]{1,0:T(8,128)(2,1)S(1)}, u32[]{:S(2)}, u32[]{:S(2)}) collective-permute-start(bf16[80,128]{1,0:T(8,128)(2,1)S(1)} %get-tuple-element.26), channel_id=1, source_target_pairs={{0,4},{4,0},{1,5},{5,1},{2,6},{6,2},{3,7},{7,3},{8,12},{12,8},{9,1... | collective-permute-start | bytes 61448 | tf_op jit(solution)/shard_map/ppermute | solution.py:434
  17.6 2.7 %shard_map.146 = (bf16[128,1024]{1,0:T(8,128)(2,1)S(1)}, f32[128,512]{1,0:T(8,128)S(1)}, f32[128,64]{1,0:T(8,128)S(1)}) custom-call(bf16[128,2560]{1,0:T(8,128)(2,1)S(1)} %get-tuple-element.24.normed_ref, bf16[2560,256]{1,0:T(8,128)(2,1)S(1)} %copy-done, bf16[2560,256]{1,0:T(8,128)(2,1)S(1)} %copy-done.1, bf16[2560,256]{1,0:T(8,128)(2,1)S(1)} %copy-done.2, ...), custom_call_target="tpu_custom_call" | custom-call | flops 587202560 | bytes 7766016 | tf_op jit(solution)/shard_map/pallas_call | solution.py:56
  20.3 0.4 collective-permute-start.4
  20.7 0.7 %shard_map.148 = (f32[128,256]{1,0:T(8,128)S(1)}, f32[128,256]{1,0:T(8,128)S(1)}, f32[128,256]{1,0:T(8,128)S(1)}, f32[128,128]{1,0:T(8,128)S(1)}) custom-call(bf16[128,1280]{1,0:T(8,128)(2,1)S(1)} %collective-permute-done.raw_ref, bf16[80,128]{1,0:T(8,128)(2,1)S(1)} %collective-permute-done.2.rows_ref, bf16[64,5120]{1,0:T(8,128)(2,1)S(1)} %copy-done.4, ...), custom_call_target="tpu_custom_call" | custom-call | flops 293601280 | bytes 6060032 | tf_op jit(solution)/shard_map/pallas_call | solution.py:56
  21.5 0.7 %shard_map.149 = (bf16[128,896]{1,0:T(8,128)(2,1)S(1)}, f32[128,512]{1,0:T(8,128)S(1)}) custom-call(bf16[128,1280]{1,0:T(8,128)(2,1)S(1)} %collective-permute-done.1.raw_ref, bf16[80,128]{1,0:T(8,128)(2,1)S(1)} %collective-permute-done.2.rows_ref, bf16[64,5120]{1,0:T(8,128)(2,1)S(1)} %copy-done.4, f32[2,1280]{1,0:T(2,128)S(1)} %get-tuple-element.27.gain_ref, ...), custom_call_target="tpu_custom_call" | custom-call | flops 293601280 | bytes 6551552 | tf_op jit(solution)/shard_map/pallas_call | solution.py:56
  22.2 1.8 %collective-permute-start.3 = (bf16[128,896]{1,0:T(8,128)(2,1)S(1)}, bf16[128,896]{1,0:T(8,128)(2,1)S(1)}, u32[]{:S(2)}, u32[]{:S(2)}) collective-permute-start(bf16[128,896]{1,0:T(8,128)(2,1)S(1)} %get-tuple-element.32), channel_id=1, source_target_pairs={{0,4},{4,0},{1,5},{5,1},{2,6},{6,2},{3,7},{7,3},{8,12},{12,8},{9,1... | collective-permute-start | bytes 688136 | tf_op jit(solution)/shard_map/ppermute | solution.py:480
  24.0 0.5 shard_map.150.readout_of_up_ref
  24.5 5.1 %collective-permute-done.4.got_ref = bf16[128,1024]{1,0:T(8,128)(2,1)S(1)} collective-permute-done((bf16[128,1024]{1,0:T(8,128)(2,1)S(1)}, bf16[128,1024]{1,0:T(8,128)(2,1)S(1)}, u32[]{:S(2)}, u32[]{:S(2)}) %collective-permute-start.4) | collective-permute-done | bytes 262176 | tf_op jit(solution)/shard_map/ppermute | solution.py:459
  29.6 0.2 shard_map.151
  29.8 3.9 %collective-permute-done.3.got_ref = bf16[128,896]{1,0:T(8,128)(2,1)S(1)} collective-permute-done((bf16[128,896]{1,0:T(8,128)(2,1)S(1)}, bf16[128,896]{1,0:T(8,128)(2,1)S(1)}, u32[]{:S(2)}, u32[]{:S(2)}) %collective-permute-start.3) | collective-permute-done | bytes 229408 | tf_op jit(solution)/shard_map/ppermute | solution.py:480
  33.8 0.9 %shard_map.152 = (f32[128,128]{1,0:T(8,128)S(1)}, f32[128,128]{1,0:T(8,128)S(1)}) custom-call(f32[128,512]{1,0:T(8,128)S(1)} %get-tuple-element.25.kept_ref, bf16[128,896]{1,0:T(8,128)(2,1)S(1)} %collective-permute-done.3.got_ref, bf16[128,256]{1,0:T(8,128)(2,1)S(1)} %copy-done.7, bf16[4,128,128]{2,1,0:T(8,128)(2,1)S(1)} %get-tuple-element.36.set_ref, ...), custom_call_target="tpu_custom_call" | custom-call | bytes 917504 | tf_op jit(solution)/shard_map/pallas_call | solution.py:56
  34.6 0.1 collective-permute-start.5
  34.7 1.2 %collective-permute-done.5.got_ref = f32[128,128]{1,0:T(8,128)S(1)} collective-permute-done((f32[128,128]{1,0:T(8,128)S(1)}, f32[128,128]{1,0:T(8,128)S(1)}, u32[]{:S(2)}, u32[]{:S(2)}) %collective-permute-start.5) | collective-permute-done | bytes 65568 | tf_op jit(solution)/shard_map/ppermute | solution.py:499
  35.9 0.1 shard_map.153
  36.0 1.5 %collective-permute-start.8 = (bf16[96,128]{1,0:T(8,128)(2,1)S(1)}, bf16[96,128]{1,0:T(8,128)(2,1)S(1)}, u32[]{:S(2)}, u32[]{:S(2)}) collective-permute-start(bf16[96,128]{1,0:T(8,128)(2,1)S(1)} %get-tuple-element.42), channel_id=1, source_target_pairs={{0,6},{1,7},{2,4},{3,5},{4,2},{5,3},{6,0},{7,1},{8,14},{9,15},{10,... | collective-permute-start | bytes 73736 | tf_op jit(solution)/shard_map/ppermute | solution.py:504
  37.5 1.5 %collective-permute-start.7 = (bf16[96,128]{1,0:T(8,128)(2,1)S(1)}, bf16[96,128]{1,0:T(8,128)(2,1)S(1)}, u32[]{:S(2)}, u32[]{:S(2)}) collective-permute-start(bf16[96,128]{1,0:T(8,128)(2,1)S(1)} %get-tuple-element.42), channel_id=1, source_target_pairs={{0,4},{4,0},{1,5},{5,1},{2,6},{6,2},{3,7},{7,3},{8,12},{12,8},{9,1... | collective-permute-start | bytes 73736 | tf_op jit(solution)/shard_map/ppermute | solution.py:502
  39.0 0.5 collective-permute-start.6
  39.5 1.2 %collective-permute-done.8 = bf16[96,128]{1,0:T(8,128)(2,1)S(1)} collective-permute-done((bf16[96,128]{1,0:T(8,128)(2,1)S(1)}, bf16[96,128]{1,0:T(8,128)(2,1)S(1)}, u32[]{:S(2)}, u32[]{:S(2)}) %collective-permute-start.8) | collective-permute-done | bytes 24608 | tf_op jit(solution)/shard_map/ppermute | solution.py:504
  40.7 0.6 %collective-permute-done.7 = bf16[96,128]{1,0:T(8,128)(2,1)S(1)} collective-permute-done((bf16[96,128]{1,0:T(8,128)(2,1)S(1)}, bf16[96,128]{1,0:T(8,128)(2,1)S(1)}, u32[]{:S(2)}, u32[]{:S(2)}) %collective-permute-start.7) | collective-permute-done | bytes 24608 | tf_op jit(solution)/shard_map/ppermute | solution.py:502
  41.3 1.5 %collective-permute-done.6 = bf16[96,128]{1,0:T(8,128)(2,1)S(1)} collective-permute-done((bf16[96,128]{1,0:T(8,128)(2,1)S(1)}, bf16[96,128]{1,0:T(8,128)(2,1)S(1)}, u32[]{:S(2)}, u32[]{:S(2)}) %collective-permute-start.6) | collective-permute-done | bytes 24608 | tf_op jit(solution)/shard_map/ppermute | solution.py:503
  42.8 1.6 %collective-permute-start.9 = (bf16[96,128]{1,0:T(8,128)(2,1)S(1)}, bf16[96,128]{1,0:T(8,128)(2,1)S(1)}, u32[]{:S(2)}, u32[]{:S(2)}) collective-permute-start(bf16[96,128]{1,0:T(8,128)(2,1)S(1)} %add_convert_fusion.refs_0_), channel_id=1, source_target_pairs={{0,8},{8,0},{16,24},{24,16},{1,9},{9,1},{17,25},{25,17},{2,10},{10... | collective-permute-start | bytes 73736 | tf_op jit(solution)/shard_map/ppermute | solution.py:512
  44.5 2.6 %collective-permute-start.10 = (bf16[96,128]{1,0:T(8,128)(2,1)S(1)}, bf16[96,128]{1,0:T(8,128)(2,1)S(1)}, u32[]{:S(2)}, u32[]{:S(2)}) collective-permute-start(bf16[96,128]{1,0:T(8,128)(2,1)S(1)} %add_convert_fusion.refs_0_), channel_id=1, source_target_pairs={{0,16},{8,24},{16,0},{24,8},{1,17},{9,25},{17,1},{25,9},{2,18},{10... | collective-permute-start | bytes 73736 | tf_op jit(solution)/shard_map/ppermute | solution.py:512
  47.1 0.2 collective-permute-start.11
  47.3 2.1 %collective-permute-done.10.refs_2_ = bf16[96,128]{1,0:T(8,128)(2,1)S(1)} collective-permute-done((bf16[96,128]{1,0:T(8,128)(2,1)S(1)}, bf16[96,128]{1,0:T(8,128)(2,1)S(1)}, u32[]{:S(2)}, u32[]{:S(2)}) %collective-permute-start.10) | collective-permute-done | bytes 24608 | tf_op jit(solution)/shard_map/ppermute | solution.py:512
  49.4 3.3 %collective-permute-done.11.refs_3_ = bf16[96,128]{1,0:T(8,128)(2,1)S(1)} collective-permute-done((bf16[96,128]{1,0:T(8,128)(2,1)S(1)}, bf16[96,128]{1,0:T(8,128)(2,1)S(1)}, u32[]{:S(2)}, u32[]{:S(2)}) %collective-permute-start.11) | collective-permute-done | bytes 24608 | tf_op jit(solution)/shard_map/ppermute | solution.py:512
  52.7 0.1 shard_map.154.mine_ref
  52.9 1.2 %collective-permute-done.12.theirs_ref = f32[40,128]{1,0:T(8,128)S(1)} collective-permute-done((f32[40,128]{1,0:T(8,128)S(1)}, f32[40,128]{1,0:T(8,128)S(1)}, u32[]{:S(2)}, u32[]{:S(2)}) %collective-permute-start.12) | collective-permute-done | bytes 20512 | tf_op jit(solution)/shard_map/ppermute | solution.py:514
  54.1 0.8 %shard_map.155 = f32[64,128]{1,0:T(8,128)} custom-call(f32[40,128]{1,0:T(8,128)S(1)} %shard_map.154.mine_ref, f32[40,128]{1,0:T(8,128)S(1)} %collective-permute-done.12.theirs_ref), custom_call_target="tpu_custom_call" | custom-call | bytes 73728 | tf_op jit(solution)/shard_map/pallas_call | solution.py:56
  (24 shorter events, 0.2 us)
Async XLA Ops:
  0.0 17.6 %copy-start.2 = (bf16[2560,256]{1,0:T(8,128)(2,1)S(1)}, bf16[2560,256]{1,0:T(8,128)(2,1)}, u32[]{:S(2)}) copy-start(bf16[2560,256]{1,0:T(8,128)(2,1)} %v_ref.5) | copy-start | bytes 3932164
  1.1 10.7 %collective-permute-start = (bf16[128,1280]{1,0:T(8,128)(2,1)S(1)}, bf16[128,1280]{1,0:T(8,128)(2,1)S(1)}, u32[]{:S(2)}, u32[]{:S(2)}) collective-permute-start(bf16[128,1280]{1,0:T(8,128)(2,1)S(1)} %shard_map.147), channel_id=1, source_target_pairs={{0,4},{4,0},{1,5},{5,1},{2,6},{6,2},{3,7},{7,3},{8,12},{12,8},{9,1... | collective-permute-start | bytes 983048 | tf_op jit(solution)/shard_map/ppermute | solution.py:407
  11.8 9.6 %collective-permute-start.1 = (bf16[128,1280]{1,0:T(8,128)(2,1)S(1)}, bf16[128,1280]{1,0:T(8,128)(2,1)S(1)}, u32[]{:S(2)}, u32[]{:S(2)}) collective-permute-start(bf16[128,1280]{1,0:T(8,128)(2,1)S(1)} %collective-permute-done.raw_ref), channel_id=1, source_target_pairs={{0,1},{1,0},{2,3},{3,2},{4,5},{5,4},{6,7},{7,6},{8,9},{9,8},{10,11... | collective-permute-start | bytes 983048 | tf_op jit(solution)/shard_map/ppermute | solution.py:466
  12.5 5.1 %copy-start = (bf16[2560,256]{1,0:T(8,128)(2,1)S(1)}, bf16[2560,256]{1,0:T(8,128)(2,1)}, u32[]{:S(2)}) copy-start(bf16[2560,256]{1,0:T(8,128)(2,1)} %q_ref.5) | copy-start | bytes 3932164
  12.5 5.1 %copy-start.1 = (bf16[2560,256]{1,0:T(8,128)(2,1)S(1)}, bf16[2560,256]{1,0:T(8,128)(2,1)}, u32[]{:S(2)}) copy-start(bf16[2560,256]{1,0:T(8,128)(2,1)} %k_ref.5) | copy-start | bytes 3932164
  15.8 4.9 %collective-permute-start.2 = (bf16[80,128]{1,0:T(8,128)(2,1)S(1)}, bf16[80,128]{1,0:T(8,128)(2,1)S(1)}, u32[]{:S(2)}, u32[]{:S(2)}) collective-permute-start(bf16[80,128]{1,0:T(8,128)(2,1)S(1)} %get-tuple-element.26), channel_id=1, source_target_pairs={{0,4},{4,0},{1,5},{5,1},{2,6},{6,2},{3,7},{7,3},{8,12},{12,8},{9,1... | collective-permute-start | bytes 61448 | tf_op jit(solution)/shard_map/ppermute | solution.py:434
  17.6 3.1 %copy-start.3 = (bf16[2560,128]{1,0:T(8,128)(2,1)S(1)}, bf16[2560,128]{1,0:T(8,128)(2,1)}, u32[]{:S(2)}) copy-start(bf16[2560,128]{1,0:T(8,128)(2,1)} %down_ref.4) | copy-start | bytes 1966084
  17.6 3.1 %copy-start.4 = (bf16[64,5120]{1,0:T(8,128)(2,1)S(1)}, bf16[64,5120]{1,0:T(8,128)(2,1)}, u32[]{:S(2)}) copy-start(bf16[64,5120]{1,0:T(8,128)(2,1)} %patch_ref.3) | copy-start | bytes 1966084
  20.3 9.2 %collective-permute-start.4 = (bf16[128,1024]{1,0:T(8,128)(2,1)S(1)}, bf16[128,1024]{1,0:T(8,128)(2,1)S(1)}, u32[]{:S(2)}, u32[]{:S(2)}) collective-permute-start(bf16[128,1024]{1,0:T(8,128)(2,1)S(1)} %get-tuple-element.34), channel_id=1, source_target_pairs={{0,4},{4,0},{1,5},{5,1},{2,6},{6,2},{3,7},{7,3},{8,12},{12,8},{9,1... | collective-permute-start | bytes 786440 | tf_op jit(solution)/shard_map/ppermute | solution.py:459
  21.4 2.6 %copy-start.5 = (bf16[64,5120]{1,0:T(8,128)(2,1)S(1)}, bf16[64,5120]{1,0:T(8,128)(2,1)}, u32[]{:S(2)}) copy-start(bf16[64,5120]{1,0:T(8,128)(2,1)} %readout_ref.1) | copy-start | bytes 1966084
  21.4 2.6 %copy-start.6 = (bf16[128,5120]{1,0:T(8,128)(2,1)S(1)}, bf16[128,5120]{1,0:T(8,128)(2,1)}, u32[]{:S(2)}) copy-start(bf16[128,5120]{1,0:T(8,128)(2,1)} %up_ref.3) | copy-start | bytes 3932164
  22.2 7.4 %copy-start.7 = (bf16[128,256]{1,0:T(8,128)(2,1)S(1)}, bf16[128,256]{1,0:T(8,128)(2,1)}, u32[]{:S(2)}) copy-start(bf16[128,256]{1,0:T(8,128)(2,1)} %up_ref.5) | copy-start | bytes 196612
  22.2 7.4 %copy-start.8 = (bf16[256,128]{1,0:T(8,128)(2,1)S(1)}, bf16[256,128]{1,0:T(8,128)(2,1)}, u32[]{:S(2)}) copy-start(bf16[256,128]{1,0:T(8,128)(2,1)} %down_ref.5) | copy-start | bytes 196612
  22.2 11.5 %collective-permute-start.3 = (bf16[128,896]{1,0:T(8,128)(2,1)S(1)}, bf16[128,896]{1,0:T(8,128)(2,1)S(1)}, u32[]{:S(2)}, u32[]{:S(2)}) collective-permute-start(bf16[128,896]{1,0:T(8,128)(2,1)S(1)} %get-tuple-element.32), channel_id=1, source_target_pairs={{0,4},{4,0},{1,5},{5,1},{2,6},{6,2},{3,7},{7,3},{8,12},{12,8},{9,1... | collective-permute-start | bytes 688136 | tf_op jit(solution)/shard_map/ppermute | solution.py:480
  34.6 1.3 %collective-permute-start.5 = (f32[128,128]{1,0:T(8,128)S(1)}, f32[128,128]{1,0:T(8,128)S(1)}, u32[]{:S(2)}, u32[]{:S(2)}) collective-permute-start(f32[128,128]{1,0:T(8,128)S(1)} %get-tuple-element.40), channel_id=1, source_target_pairs={{0,1},{1,0},{2,3},{3,2},{4,5},{5,4},{6,7},{7,6},{8,9},{9,8},{10,11... | collective-permute-start | bytes 196616 | tf_op jit(solution)/shard_map/ppermute | solution.py:499
  36.0 4.7 %collective-permute-start.8 = (bf16[96,128]{1,0:T(8,128)(2,1)S(1)}, bf16[96,128]{1,0:T(8,128)(2,1)S(1)}, u32[]{:S(2)}, u32[]{:S(2)}) collective-permute-start(bf16[96,128]{1,0:T(8,128)(2,1)S(1)} %get-tuple-element.42), channel_id=1, source_target_pairs={{0,6},{1,7},{2,4},{3,5},{4,2},{5,3},{6,0},{7,1},{8,14},{9,15},{10,... | collective-permute-start | bytes 73736 | tf_op jit(solution)/shard_map/ppermute | solution.py:504
  37.5 3.8 %collective-permute-start.7 = (bf16[96,128]{1,0:T(8,128)(2,1)S(1)}, bf16[96,128]{1,0:T(8,128)(2,1)S(1)}, u32[]{:S(2)}, u32[]{:S(2)}) collective-permute-start(bf16[96,128]{1,0:T(8,128)(2,1)S(1)} %get-tuple-element.42), channel_id=1, source_target_pairs={{0,4},{4,0},{1,5},{5,1},{2,6},{6,2},{3,7},{7,3},{8,12},{12,8},{9,1... | collective-permute-start | bytes 73736 | tf_op jit(solution)/shard_map/ppermute | solution.py:502
  39.0 3.8 %collective-permute-start.6 = (bf16[96,128]{1,0:T(8,128)(2,1)S(1)}, bf16[96,128]{1,0:T(8,128)(2,1)S(1)}, u32[]{:S(2)}, u32[]{:S(2)}) collective-permute-start(bf16[96,128]{1,0:T(8,128)(2,1)S(1)} %get-tuple-element.41), channel_id=1, source_target_pairs={{0,2},{1,3},{2,0},{3,1},{4,6},{5,7},{6,4},{7,5},{8,10},{9,11},{10,... | collective-permute-start | bytes 73736 | tf_op jit(solution)/shard_map/ppermute | solution.py:503
  42.8 4.5 %collective-permute-start.9 = (bf16[96,128]{1,0:T(8,128)(2,1)S(1)}, bf16[96,128]{1,0:T(8,128)(2,1)S(1)}, u32[]{:S(2)}, u32[]{:S(2)}) collective-permute-start(bf16[96,128]{1,0:T(8,128)(2,1)S(1)} %add_convert_fusion.refs_0_), channel_id=1, source_target_pairs={{0,8},{8,0},{16,24},{24,16},{1,9},{9,1},{17,25},{25,17},{2,10},{10... | collective-permute-start | bytes 73736 | tf_op jit(solution)/shard_map/ppermute | solution.py:512
  44.5 4.9 %collective-permute-start.10 = (bf16[96,128]{1,0:T(8,128)(2,1)S(1)}, bf16[96,128]{1,0:T(8,128)(2,1)S(1)}, u32[]{:S(2)}, u32[]{:S(2)}) collective-permute-start(bf16[96,128]{1,0:T(8,128)(2,1)S(1)} %add_convert_fusion.refs_0_), channel_id=1, source_target_pairs={{0,16},{8,24},{16,0},{24,8},{1,17},{9,25},{17,1},{25,9},{2,18},{10... | collective-permute-start | bytes 73736 | tf_op jit(solution)/shard_map/ppermute | solution.py:512
  47.1 5.6 %collective-permute-start.11 = (bf16[96,128]{1,0:T(8,128)(2,1)S(1)}, bf16[96,128]{1,0:T(8,128)(2,1)S(1)}, u32[]{:S(2)}, u32[]{:S(2)}) collective-permute-start(bf16[96,128]{1,0:T(8,128)(2,1)S(1)} %add_convert_fusion.refs_0_), channel_id=1, source_target_pairs={{0,24},{8,16},{16,8},{24,0},{1,25},{9,17},{17,9},{25,1},{2,26},{10... | collective-permute-start | bytes 73736 | tf_op jit(solution)/shard_map/ppermute | solution.py:512
  52.8 1.3 %collective-permute-start.12 = (f32[40,128]{1,0:T(8,128)S(1)}, f32[40,128]{1,0:T(8,128)S(1)}, u32[]{:S(2)}, u32[]{:S(2)}) collective-permute-start(f32[40,128]{1,0:T(8,128)S(1)} %shard_map.154.mine_ref), channel_id=1, source_target_pairs={{0,1},{1,0},{2,3},{3,2},{4,5},{5,4},{6,7},{7,6},{8,9},{9,8},{10,11... | collective-permute-start | bytes 61448 | tf_op jit(solution)/shard_map/ppermute | solution.py:514

commit v6 on v5

--- a/solution.py
+++ b/solution.py
@@ -82,18 +82,29 @@
     return high, (x - high.astype(F32)).astype(BF16)
 
 
-def slice_kernel(stream_hbm, message_ref, sem):
-    quarter = message_ref.shape[1]
+def slice_kernel(stream_hbm, message_ref, sems):
+    tokens, quarter = message_ref.shape
     target = (1 - lax.axis_index("seq")) * 2 + lax.axis_index("head") % 2
-    copy = pltpu.make_async_copy(stream_hbm.at[:, aligned(target, quarter)], message_ref, sem)
-    copy.start()
-    copy.wait()
+    pieces = sems.shape[0]
+    rows = tokens // pieces
+    copies = [
+        pltpu.make_async_copy(
+            stream_hbm.at[pl.ds(i * rows, rows), aligned(target, quarter)],
+            message_ref.at[pl.ds(i * rows, rows)],
+            sems.at[i],
+        )
+        for i in range(pieces)
+    ]
+    for copy in copies:
+        copy.start()
+    for copy in copies:
+        copy.wait()
 
 
 def first_kernel(
-    step_any, latents_hbm, noise_hbm, stream_hbm, patch_hbm, readout_hbm, gain_hbm,
-    normed_ref, rows_ref, base_ref, gain_ref,
-    step_s, latents_v, noise_v, stream_v, patch_v, readout_v, gain_v, hidden_v, sems,
+    step_any, latents_hbm, noise_hbm, stream_hbm, patch_hbm, gain_hbm, value_hbm,
+    normed_ref, rows_ref, gap_ref, hidden_ref, gain_ref, patch_ref, value_ref,
+    step_s, latents_v, noise_v, stream_v, patch_v, gain_v, sems,
 ):
     parts, tokens, quarter = stream_v.shape
     channels = latents_v.shape[0]
@@ -108,9 +119,9 @@
     for j in range(parts):
         span = pl.ds(j * quarter, quarter)
         large.append([
-            pltpu.make_async_copy(source.at[:, span], target.at[j], sems.at[4 + 3 * j + i])
+            pltpu.make_async_copy(source.at[:, span], target.at[j], sems.at[4 + 2 * j + i])
             for i, (source, target) in enumerate(
-                ((stream_hbm, stream_v), (patch_hbm, patch_v), (readout_hbm, readout_v))
+                ((stream_hbm, stream_v), (patch_hbm, patch_v))
             )
         ])
     for copy in small:
@@ -119,13 +130,15 @@
         for copy in large[j]:
             copy.start()
     gain_copy.start()
+    value_copy = pltpu.make_async_copy(value_hbm, value_ref, sems.at[sems.shape[0] - 1])
+    value_copy.start()
     for copy in small:
         copy.wait()
     level = (jnp.full((8, 128), step_s[0], jnp.int32).astype(F32) + 1.0) / 1000.0
     sigma = (5.0 * level / (1.0 + 4.0 * level))[:1, :1]
     latents = latents_v[...].astype(F32)
     noisy = ((1.0 - sigma) * latents + sigma * noise_v[...].astype(F32)).astype(BF16)
-    base = (latents - noisy.astype(F32)) / sigma
+    gap_ref[...] = (latents - noisy.astype(F32)) / sigma
     squares = jnp.zeros((tokens, 128), F32)
     for j in range(parts):
         for copy in large[j]:
@@ -134,8 +147,7 @@
             noisy, patch_v[j], (((0,), (0,)), ((), ())), preferred_element_type=F32
         )
         hidden = (stream_v[j].astype(F32) + embedded).astype(BF16)
-        hidden_v[j] = hidden
-        base += contract_final_axis(readout_v[j], hidden)
+        hidden_ref[j] = hidden
         wide = hidden.astype(F32)
         wide = wide * wide
         for i in range(quarter // 128):
@@ -150,8 +162,6 @@
     terms = [jnp.concatenate([x.astype(F32)] * 2, axis=0) for x in (first, second, third)]
     terms = jnp.where(row == 0, terms[0], jnp.where(row == 1, terms[1], terms[2]))
     rows_ref[channels:] = terms.astype(BF16)
-    once = (lax.axis_index("group") == 0) & (lax.axis_index("head") == 0)
-    base_ref[...] = jnp.where(once, base, 0.0).T
     gain_copy.wait()
     for j in range(parts):
 
@@ -160,9 +170,12 @@
             gain = gain_v[j * quarter : (j + 1) * quarter][None, :]
             start = (j % 2) * quarter
             gain_ref[j % 2 : j % 2 + 1] = gain
+            patch_ref[j % 2] = patch_v[j]
             normed_ref[:, start : start + quarter] = (
-                hidden_v[j].astype(F32) * inverse * gain
+                hidden_ref[j].astype(F32) * inverse * gain
             ).astype(BF16)
+
+    value_copy.wait()
 
 
 def pick(index, x):
@@ -170,11 +183,11 @@
     return jnp.where(index == 0, x[:, :half], x[:, half:])
 
 
-def partial_outputs(parts, seq, sent_ref, kept_ref):
+def partial_outputs(parts, seq, lora_blocks, sent_ref, kept_ref):
     q, k, v, lora = parts
     columns = q.shape[1] // 2
     blocks = [*high_low(pick(1 - seq, q)), *high_low(pick(1 - seq, k))]
-    blocks += [pick(1 - seq, v).astype(BF16), *high_low(lora)]
+    blocks += [pick(1 - seq, v).astype(BF16), *lora_blocks]
     for i, block in enumerate(blocks):
         sent_ref[:, i * columns : (i + 1) * columns] = block
     for i, block in enumerate((pick(seq, q), pick(seq, k), pick(seq, v), lora)):
@@ -183,8 +196,8 @@
 
 def own_kernel(
     normed_ref, q_ref, k_ref, v_ref, down_hbm, output_hbm, readout_hbm,
-    sent_ref, kept_ref, mix_ref,
-    down_v, output_v, readout_v, mix_v, sems,
+    sent_ref, kept_ref, mix_ref, down_v,
+    output_v, readout_v, mix_v, sems,
 ):
     seq = lax.axis_index("seq")
     copies = [
@@ -199,8 +212,13 @@
     normed = normed_ref[...]
     parts = [dot(normed, w[...]) for w in (q_ref, k_ref, v_ref)]
     copies[0].wait()
-    parts.append(dot(normed, down_v[...]))
-    partial_outputs(parts, seq, sent_ref, kept_ref)
+    lora = dot(normed, down_v[...])
+    share = lora.shape[0] // 2
+    half = jnp.where(lax.axis_index("head") % 2 == 0, lora[:share], lora[share:])
+    high, low = high_low(half)
+    parts.append(lora)
+    both = jnp.concatenate([high, low], axis=0)
+    partial_outputs(parts, seq, [both], sent_ref, kept_ref)
     for copy in copies[1:]:
         copy.wait()
     mix_v[...] = contract_final_axis(output_v[...], readout_v[...])
@@ -212,20 +230,27 @@
     mix_ref[...] = mix_v[aligned(seq, rows), :]
 
 
-def side_kernel(up_ref, readout_ref, readout_of_up_ref):
+def side_kernel(hidden_ref, up_ref, readout_ref, gap_ref, readout_of_up_ref, base_ref):
+    parts, _, quarter = hidden_ref.shape
     readout_of_up_ref[...] = contract_final_axis(up_ref[...], readout_ref[...]).astype(BF16)
+    base = gap_ref[...]
+    for j in range(parts):
+        base += contract_final_axis(
+            readout_ref[:, j * quarter : (j + 1) * quarter], hidden_ref[j]
+        )
+    once = (lax.axis_index("group") == 0) & (lax.axis_index("head") == 0)
+    base_ref[...] = jnp.where(once, base, 0.0).T
 
 
 def other_parts(part, raw_ref, rows_ref, patch_ref, gain_ref, weights):
     tokens, quarter = raw_ref.shape
-    channels = patch_ref.shape[0]
-    quarters = lax.axis_index("seq") * 2 + part
+    channels = patch_ref.shape[1]
     noisy = rows_ref[:channels]
     terms = rows_ref[channels:].astype(F32)
     scale = (terms[:1] + terms[1:2]) + terms[2:3]
     inverse = jnp.broadcast_to(scale, (tokens, tokens)).T[:, :1]
     embedded = lax.dot_general(
-        noisy, patch_ref[:, aligned(quarters, quarter)],
+        noisy, patch_ref[part],
         (((0,), (0,)), ((), ())), preferred_element_type=F32,
     )
     hidden = (raw_ref[...].astype(F32) + embedded).astype(BF16).astype(F32)
@@ -250,10 +275,11 @@
     parts = other_parts(1 - core, raw_ref, rows_ref, patch_ref, gain_ref, weights)
     near = (near_q_ref, near_k_ref, near_v_ref, near_down_ref)
     parts = [part + ref[...] for part, ref in zip(parts, near)]
-    partial_outputs(parts, lax.axis_index("seq"), sent_ref, kept_ref)
-
-
-def finish(kept_ref, got_ref, up):
+    lora = high_low(parts[3])
+    partial_outputs(parts, lax.axis_index("seq"), lora, sent_ref, kept_ref)
+
+
+def finish(kept_ref, got_ref, up, lora):
     columns = up.shape[1]
 
     def got(i):
@@ -264,7 +290,6 @@
 
     scale = HEAD_SIZE ** (-0.5)
     base = kept(0) + (got(0) + got(1))
-    lora = (kept(3) + (got(5) + got(6))).astype(BF16)
     return (
         (base * scale).astype(BF16),
         ((base + dot(lora, up)) * scale).astype(BF16),
@@ -273,14 +298,25 @@
     )
 
 
+def lora_kernel(kept_ref, got_ref, lora_ref):
+    share, rank = lora_ref.shape
+    got = got_ref[:, 5 * rank : 6 * rank].astype(F32)
+    core = lax.axis_index("head") % 2
+    kept = kept_ref[aligned(core, share), 3 * rank :]
+    lora_ref[...] = (kept + (got[:share] + got[share:])).astype(BF16)
+
+
 def half_kernel(
-    kept_ref, got_ref, up_ref, mix_ref, down_ref, readout_of_up_ref,
+    kept_ref, got_ref, lora_ref, lora_far_ref, up_ref, mix_ref, down_ref, readout_of_up_ref,
     set_ref, mixes_ref,
 ):
     seq = lax.axis_index("seq")
     rows, channels = mix_ref.shape
     up = up_ref[:, aligned(seq, rows)]
-    for i, block in enumerate(finish(kept_ref, got_ref, up)):
+    mine, far = lora_ref[...], lora_far_ref[...]
+    first = lax.axis_index("head") % 2 == 0
+    lora = jnp.concatenate([jnp.where(first, mine, far), jnp.where(first, far, mine)], axis=0)
+    for i, block in enumerate(finish(kept_ref, got_ref, up, lora)):
         set_ref[i] = block
     got = got_ref[:, -2 * channels :].astype(F32)
     mix_full = mix_ref[...] + (got[:, :channels] + swap_halves(got)[:, :channels])
@@ -300,7 +336,10 @@
     tokens, channels = base_ref.shape
     columns = set_ref.shape[2]
     up = up_ref[:, aligned(seq, columns)]
-    for i, block in enumerate(finish(kept_ref, got_ref, up)):
+    rank = got_ref.shape[1] - 5 * columns
+    got = got_ref[:, 5 * columns :].astype(F32)
+    lora = kept_ref[:, 3 * columns :] + (got[:, : rank // 2] + got[:, rank // 2 :])
+    for i, block in enumerate(finish(kept_ref, got_ref, up, lora.astype(BF16))):
         sets_v[i, :tokens] = block
         sets_v[i, tokens:] = set_ref[i]
     terms = jnp.zeros(terms_v.shape, F32)
@@ -392,7 +431,6 @@
     to_core = pairs((heads,), lambda h: (h ^ 1,))
     to_y = pairs((heads,), lambda h: (h ^ 2,))
     to_xy = pairs((2, heads), lambda s, h: (s ^ 1, h ^ 2))
-    weights = (query_matrix, key_matrix, value_matrix, adapter_query_down)
     partial_flops = 2 * tokens * half_width * (3 * local_columns + rank)
 
     in_hbm = pltpu.with_memory_space_constraint(stream, pltpu.HBM)
@@ -401,21 +439,23 @@
         [((tokens, quarter), BF16)],
         (in_hbm,),
         [HBM],
-        [pltpu.SemaphoreType.DMA],
+        [pltpu.SemaphoreType.DMA((4,))],
         moved=4 * tokens * quarter,
     )
     near = lax.ppermute(message, "seq", to_x)
     inputs = (
-        latents.T, noise.T, stream, patch_embed_weight, velocity_readout_weight,
-        prenorm_gain_vector,
-    )
-    normed, rows, base, gain = run(
+        latents.T, noise.T, stream, patch_embed_weight, prenorm_gain_vector, value_matrix,
+    )
+    normed, rows, gap, hidden, gain, patch, value = run(
         first_kernel,
         [
             ((tokens, half_width), BF16),
             ((channels + 16, tokens), BF16),
-            ((tokens, channels), F32),
+            ((channels, tokens), F32),
+            ((4, tokens, quarter), BF16),
             ((2, quarter), F32),
+            ((2, channels, quarter), BF16),
+            (value_matrix.shape, BF16),
         ],
         [step, *(pltpu.with_memory_space_constraint(x, pltpu.HBM) for x in inputs)],
         [pl.BlockSpec(memory_space=pl.ANY)] + [HBM] * 6,
@@ -425,22 +465,21 @@
             pltpu.VMEM((channels, tokens), BF16),
             pltpu.VMEM((4, tokens, quarter), BF16),
             pltpu.VMEM((4, channels, quarter), BF16),
-            pltpu.VMEM((4, channels, quarter), BF16),
             pltpu.VMEM((4 * quarter,), F32),
-            pltpu.VMEM((4, tokens, quarter), BF16),
-            pltpu.SemaphoreType.DMA((4 + 3 * 4,)),
+            pltpu.SemaphoreType.DMA((5 + 2 * 4,)),
         ],
     )
     other_rows = lax.ppermute(rows, "seq", to_x)
-    own_sent, own_kept, mix_part = run(
+    own_sent, own_kept, mix_part, down = run(
         own_kernel,
         [
-            ((tokens, 7 * columns + 2 * channels), BF16),
+            ((tokens, 6 * columns + 2 * channels), BF16),
             ((tokens, 4 * columns), F32),
             ((columns, channels), F32),
+            (adapter_query_down.shape, BF16),
         ],
         (
-            normed, *weights[:3],
+            normed, query_matrix, key_matrix, value,
             *(
                 pltpu.with_memory_space_constraint(x, pltpu.HBM)
                 for x in (adapter_query_down, output_matrix, velocity_readout_weight)
@@ -448,7 +487,6 @@
         ),
         [VMEM] * 4 + [HBM] * 3,
         scratch=[
-            pltpu.VMEM(adapter_query_down.shape, BF16),
             pltpu.VMEM(output_matrix.shape, BF16),
             pltpu.VMEM((channels, half_width), BF16),
             pltpu.VMEM((local_columns, channels), F32),
@@ -457,14 +495,15 @@
         flops=partial_flops,
     )
     own_got = lax.ppermute(own_sent, "seq", to_x)
-    (readout_of_up,) = run(
+    readout_of_up, base = run(
         side_kernel,
-        [((rank, channels), BF16)],
-        (adapter_output_up, velocity_readout_weight),
-        flops=4 * rank * half_width * channels,
+        [((rank, channels), BF16), ((tokens, channels), F32)],
+        (hidden, adapter_output_up, velocity_readout_weight, gap),
+        flops=8 * tokens * half_width * channels,
     )
     far = lax.ppermute(near, "head", to_core)
-    shared = (other_rows, patch_embed_weight, gain, *weights)
+    weights = (query_matrix, key_matrix, value, down)
+    shared = (other_rows, patch, gain, *weights)
     near_parts = run(
         near_kernel,
         [((tokens, w.shape[1]), F32) for w in weights],
@@ -478,11 +517,13 @@
         flops=partial_flops // 2,
     )
     other_got = lax.ppermute(other_sent, "seq", to_x)
+    (lora,) = run(lora_kernel, [((share, rank), BF16)], (other_kept, own_got))
+    lora_far = lax.ppermute(lora, "head", to_core)
     half_set, mixes = run(
         half_kernel,
         [((4, tokens, columns), BF16), ((2, columns, 2 * channels), BF16)],
         (
-            other_kept, own_got, adapter_query_up, mix_part,
+            other_kept, own_got, lora, lora_far, adapter_query_up, mix_part,
             adapter_output_down, readout_of_up,
         ),
     )

time: 55.1 us -> 51.4 us (0.933)
  waiting for transfers between devices: 27.9 us -> 24.6 us
    ppermute x3, waiting for transfers between devices: 5.41 us -> 3.94 us  [paired_local(): totals.append(lax.ppermute(total, 'group', to_group))]
    ppermute x1, waiting for transfers between devices: 3.95 us -> 2.68 us  [paired_local(): other_got = lax.ppermute(other_sent, 'seq', to_x)]
    ppermute x1, starting transfers between devices: 1.5 us -> 0.27 us  [paired_local(): from_xy = lax.ppermute(cross, ('seq', 'head'), to_xy)]
    ppermute x1, waiting for transfers between devices: 1.24 us -> 2.43 us  [paired_local(): from_xy = lax.ppermute(cross, ('seq', 'head'), to_xy)]
    ppermute x1, waiting for transfers between devices: 1.49 us -> 0.34 us  [paired_local(): from_y = lax.ppermute(same, 'head', to_y)]
    ppermute x1, starting transfers between devices: 0.51 us -> 1.53 us  [paired_local(): from_y = lax.ppermute(same, 'head', to_y)]
    ppermute x1, waiting for transfers between devices: 0.59 us -> 0.01 us  [paired_local(): from_x = lax.ppermute(cross, 'seq', to_x)]
    pallas_call x11 -> x12, Pallas kernels: 11.1 us -> 10.6 us  [run(): pl.pallas_call(kernel, out_shape=shapes, in_specs=specs or [VMEM] * len(a...]
  transfers between devices with their start and end apart: 13 -> 14, of which waited for: 10 -> 10; matrix products, arithmetic and copies ran while one was open for 0% -> 0% of each run, Pallas kernels for 15% -> 15%
where the time goes in v6:
time: 51.4 us; the launch traced here: 51.2 us
  waiting for transfers between devices  24.6 us (48%)
  starting transfers between devices  15.2 us (30%)
  Pallas kernels  10.6 us (21%)
  between operations  0.83 us (2%)
    pallas_call x12, Pallas kernels, run(): pl.pallas_call(kernel, out_shape=shapes, in_specs=specs or [VMEM] * len(a...  10.6 us
    ppermute x1, waiting for transfers between devices, paired_local(): near = lax.ppermute(message, 'seq', to_x)  7.71 us
    ppermute x1, waiting for transfers between devices, paired_local(): own_got = lax.ppermute(own_sent, 'seq', to_x)  4.91 us
    ppermute x3, starting transfers between devices, paired_local(): totals.append(lax.ppermute(total, 'group', to_group))  4.45 us
    ppermute x3, waiting for transfers between devices, paired_local(): totals.append(lax.ppermute(total, 'group', to_group))  3.94 us
    ppermute x1, starting transfers between devices, paired_local(): near = lax.ppermute(message, 'seq', to_x)  3.03 us
    ppermute x1, waiting for transfers between devices, paired_local(): other_got = lax.ppermute(other_sent, 'seq', to_x)  2.68 us
    ppermute x1, waiting for transfers between devices, paired_local(): from_xy = lax.ppermute(cross, ('seq', 'head'), to_xy)  2.43 us
  transfers between devices with their start and end apart: 14, of which 10 were waited for; matrix products, arithmetic and copies ran while one was open for 0% of the time, Pallas kernels for 15%

profile of v6, /device:TPU:0, one launch (start us, length us, event | category | flops | bytes accessed | tf_op | source)
XLA Modules:
  0.0 51.2 jit_solution(10563954276577031017)
XLA Ops:
  0.0 1.0 %shard_map.147 = bf16[128,1280]{1,0:T(8,128)(2,1)S(1)} custom-call(bf16[128,5120]{1,0:T(8,128)(2,1)} %stream_hbm.3), custom_call_target="tpu_custom_call" | custom-call | bytes 655360 | tf_op jit(solution)/shard_map/pallas_call | solution.py:56
  1.0 3.0 %collective-permute-start = (bf16[128,1280]{1,0:T(8,128)(2,1)S(1)}, bf16[128,1280]{1,0:T(8,128)(2,1)S(1)}, u32[]{:S(2)}, u32[]{:S(2)}) collective-permute-start(bf16[128,1280]{1,0:T(8,128)(2,1)S(1)} %shard_map.147), channel_id=1, source_target_pairs={{0,4},{4,0},{1,5},{5,1},{2,6},{6,2},{3,7},{7,3},{8,12},{12,8},{9,1... | collective-permute-start | bytes 983048 | tf_op jit(solution)/shard_map/ppermute | solution.py:445
  4.1 7.7 %collective-permute-done.raw_ref = bf16[128,1280]{1,0:T(8,128)(2,1)S(1)} collective-permute-done((bf16[128,1280]{1,0:T(8,128)(2,1)S(1)}, bf16[128,1280]{1,0:T(8,128)(2,1)S(1)}, u32[]{:S(2)}, u32[]{:S(2)}) %collective-permute-start) | collective-permute-done | bytes 327712 | tf_op jit(solution)/shard_map/ppermute | solution.py:445
  12.5 2.6 %shard_map.145 = (bf16[128,2560]{1,0:T(8,128)(2,1)S(1)}, bf16[80,128]{1,0:T(8,128)(2,1)S(1)}, f32[64,128]{1,0:T(8,128)S(1)}, bf16[4,128,1280]{2,1,0:T(8,128)(2,1...) custom-call(s32[1]{0:T(128)S(6)} %copy.16.step_any, ...), custom_call_target="tpu_custom_call" | custom-call | bytes 6998020 | tf_op jit(solution)/shard_map/pallas_call | solution.py:56
  15.1 1.8 %collective-permute-start.2 = (bf16[80,128]{1,0:T(8,128)(2,1)S(1)}, bf16[80,128]{1,0:T(8,128)(2,1)S(1)}, u32[]{:S(2)}, u32[]{:S(2)}) collective-permute-start(bf16[80,128]{1,0:T(8,128)(2,1)S(1)} %get-tuple-element.33), channel_id=1, source_target_pairs={{0,4},{4,0},{1,5},{5,1},{2,6},{6,2},{3,7},{7,3},{8,12},{12,8},{9,1... | collective-permute-start | bytes 61448 | tf_op jit(solution)/shard_map/ppermute | solution.py:472
  16.9 2.4 %shard_map.146 = (bf16[128,896]{1,0:T(8,128)(2,1)S(1)}, f32[128,512]{1,0:T(8,128)S(1)}, f32[128,64]{1,0:T(8,128)S(1)}, bf16[2560,128]{1,0:T(8,128)(2,1)S(1)}) custom-call(bf16[128,2560]{1,0:T(8,128)(2,1)S(1)} %get-tuple-element.30.normed_ref, bf16[2560,256]{1,0:T(8,128)(2,1)S(1)} %copy-done, bf16[2560,256]{1,0:T(8,128)(2,1)S(1)} %copy-done.1, ...), custom_call_target="tpu_custom_call" | custom-call | flops 587202560 | bytes 8388608 | tf_op jit(solution)/shard_map/pallas_call | solution.py:56
  19.4 0.3 collective-permute-start.4
  19.7 0.7 %shard_map.148 = (f32[128,256]{1,0:T(8,128)S(1)}, f32[128,256]{1,0:T(8,128)S(1)}, f32[128,256]{1,0:T(8,128)S(1)}, f32[128,128]{1,0:T(8,128)S(1)}) custom-call(bf16[128,1280]{1,0:T(8,128)(2,1)S(1)} %collective-permute-done.raw_ref, bf16[80,128]{1,0:T(8,128)(2,1)S(1)} %collective-permute-done.2.rows_ref, bf16[2,64,1280]{2,1,0:T(8,128)(2,1)S(1)} %get-tuple-element.34.patch_ref, ...), custom_call_target="tpu_custom_call" | custom-call | flops 293601280 | bytes 5732352 | tf_op jit(solution)/shard_map/pallas_call | solution.py:56
  20.5 0.7 %shard_map.149 = (bf16[128,896]{1,0:T(8,128)(2,1)S(1)}, f32[128,512]{1,0:T(8,128)S(1)}) custom-call(bf16[128,1280]{1,0:T(8,128)(2,1)S(1)} %collective-permute-done.1.raw_ref, bf16[80,128]{1,0:T(8,128)(2,1)S(1)} %collective-permute-done.2.rows_ref, bf16[2,64,1280]{2,1,0:T(8,128)(2,1)S(1)} %get-tuple-element.34.patch_ref, ...), custom_call_target="tpu_custom_call" | custom-call | flops 293601280 | bytes 6223872 | tf_op jit(solution)/shard_map/pallas_call | solution.py:56
  21.2 1.8 %collective-permute-start.3 = (bf16[128,896]{1,0:T(8,128)(2,1)S(1)}, bf16[128,896]{1,0:T(8,128)(2,1)S(1)}, u32[]{:S(2)}, u32[]{:S(2)}) collective-permute-start(bf16[128,896]{1,0:T(8,128)(2,1)S(1)} %get-tuple-element.41), channel_id=1, source_target_pairs={{0,4},{4,0},{1,5},{5,1},{2,6},{6,2},{3,7},{7,3},{8,12},{12,8},{9,1... | collective-permute-start | bytes 688136 | tf_op jit(solution)/shard_map/ppermute | solution.py:519
  23.0 4.9 %collective-permute-done.4.got_ref = bf16[128,896]{1,0:T(8,128)(2,1)S(1)} collective-permute-done((bf16[128,896]{1,0:T(8,128)(2,1)S(1)}, bf16[128,896]{1,0:T(8,128)(2,1)S(1)}, u32[]{:S(2)}, u32[]{:S(2)}) %collective-permute-start.4) | collective-permute-done | bytes 229408 | tf_op jit(solution)/shard_map/ppermute | solution.py:497
  27.9 0.1 collective-permute-start.5
  28.1 1.0 %shard_map.151 = (bf16[128,64]{1,0:T(8,128)(2,1)S(1)}, f32[128,64]{1,0:T(8,128)S(1)}) custom-call(bf16[4,128,1280]{2,1,0:T(8,128)(2,1)S(1)} %get-tuple-element.45.hidden_ref, bf16[128,5120]{1,0:T(8,128)(2,1)S(1)} %copy-done.3, bf16[64,5120]{1,0:T(8,128)(2,1)S(1)} %copy-done.2, f32[64,128]{1,0:T(8,128)S(1)} %get-tuple-element.46.gap_ref), custom_call_target="tpu_custom_call" | custom-call | flops 167772160 | bytes 3358720 | tf_op jit(solution)/shard_map/pallas_call | solution.py:56
  29.0 0.2 collective-permute-done.5.lora_far_ref
  29.2 0.2 shard_map.152
  29.4 2.7 %collective-permute-done.3.got_ref = bf16[128,896]{1,0:T(8,128)(2,1)S(1)} collective-permute-done((bf16[128,896]{1,0:T(8,128)(2,1)S(1)}, bf16[128,896]{1,0:T(8,128)(2,1)S(1)}, u32[]{:S(2)}, u32[]{:S(2)}) %collective-permute-start.3) | collective-permute-done | bytes 229408 | tf_op jit(solution)/shard_map/ppermute | solution.py:519
  32.1 0.9 %shard_map.153 = (f32[128,128]{1,0:T(8,128)S(1)}, f32[128,128]{1,0:T(8,128)S(1)}) custom-call(f32[128,512]{1,0:T(8,128)S(1)} %get-tuple-element.32.kept_ref, bf16[128,896]{1,0:T(8,128)(2,1)S(1)} %collective-permute-done.3.got_ref, bf16[128,256]{1,0:T(8,128)(2,1)S(1)} %copy-done.4, bf16[4,128,128]{2,1,0:T(8,128)(2,1)S(1)} %get-tuple-element.48.set_ref, ...), custom_call_target="tpu_custom_call" | custom-call | bytes 917504 | tf_op jit(solution)/shard_map/pallas_call | solution.py:56
  32.9 0.1 collective-permute-start.6
  33.0 1.2 %collective-permute-done.6.got_ref = f32[128,128]{1,0:T(8,128)S(1)} collective-permute-done((f32[128,128]{1,0:T(8,128)S(1)}, f32[128,128]{1,0:T(8,128)S(1)}, u32[]{:S(2)}, u32[]{:S(2)}) %collective-permute-start.6) | collective-permute-done | bytes 65568 | tf_op jit(solution)/shard_map/ppermute | solution.py:540
  34.3 0.1 shard_map.154
  34.3 1.5 %collective-permute-start.7 = (bf16[96,128]{1,0:T(8,128)(2,1)S(1)}, bf16[96,128]{1,0:T(8,128)(2,1)S(1)}, u32[]{:S(2)}, u32[]{:S(2)}) collective-permute-start(bf16[96,128]{1,0:T(8,128)(2,1)S(1)} %get-tuple-element.53), channel_id=1, source_target_pairs={{0,2},{1,3},{2,0},{3,1},{4,6},{5,7},{6,4},{7,5},{8,10},{9,11},{10,... | collective-permute-start | bytes 73736 | tf_op jit(solution)/shard_map/ppermute | solution.py:544
  35.9 0.3 collective-permute-start.9
  36.2 1.7 %collective-permute-start.8 = (bf16[96,128]{1,0:T(8,128)(2,1)S(1)}, bf16[96,128]{1,0:T(8,128)(2,1)S(1)}, u32[]{:S(2)}, u32[]{:S(2)}) collective-permute-start(bf16[96,128]{1,0:T(8,128)(2,1)S(1)} %get-tuple-element.54), channel_id=1, source_target_pairs={{0,4},{4,0},{1,5},{5,1},{2,6},{6,2},{3,7},{7,3},{8,12},{12,8},{9,1... | collective-permute-start | bytes 73736 | tf_op jit(solution)/shard_map/ppermute | solution.py:543
  37.8 0.3 collective-permute-done.7
  38.2 2.4 %collective-permute-done.9 = bf16[96,128]{1,0:T(8,128)(2,1)S(1)} collective-permute-done((bf16[96,128]{1,0:T(8,128)(2,1)S(1)}, bf16[96,128]{1,0:T(8,128)(2,1)S(1)}, u32[]{:S(2)}, u32[]{:S(2)}) %collective-permute-start.9) | collective-permute-done | bytes 24608 | tf_op jit(solution)/shard_map/ppermute | solution.py:545
  40.6 3.7 %collective-permute-start.12 = (bf16[96,128]{1,0:T(8,128)(2,1)S(1)}, bf16[96,128]{1,0:T(8,128)(2,1)S(1)}, u32[]{:S(2)}, u32[]{:S(2)}) collective-permute-start(bf16[96,128]{1,0:T(8,128)(2,1)S(1)} %add_convert_fusion.refs_0_), channel_id=1, source_target_pairs={{0,24},{8,16},{16,8},{24,0},{1,25},{9,17},{17,9},{25,1},{2,26},{10... | collective-permute-start | bytes 73736 | tf_op jit(solution)/shard_map/ppermute | solution.py:553
  44.3 0.8 %collective-permute-start.10 = (bf16[96,128]{1,0:T(8,128)(2,1)S(1)}, bf16[96,128]{1,0:T(8,128)(2,1)S(1)}, u32[]{:S(2)}, u32[]{:S(2)}) collective-permute-start(bf16[96,128]{1,0:T(8,128)(2,1)S(1)} %add_convert_fusion.refs_0_), channel_id=1, source_target_pairs={{0,8},{8,0},{16,24},{24,16},{1,9},{9,1},{17,25},{25,17},{2,10},{10... | collective-permute-start | bytes 73736 | tf_op jit(solution)/shard_map/ppermute | solution.py:553
  45.1 1.2 %collective-permute-done.12.refs_3_ = bf16[96,128]{1,0:T(8,128)(2,1)S(1)} collective-permute-done((bf16[96,128]{1,0:T(8,128)(2,1)S(1)}, bf16[96,128]{1,0:T(8,128)(2,1)S(1)}, u32[]{:S(2)}, u32[]{:S(2)}) %collective-permute-start.12) | collective-permute-done | bytes 24608 | tf_op jit(solution)/shard_map/ppermute | solution.py:553
  46.3 2.7 %collective-permute-done.11.refs_2_ = bf16[96,128]{1,0:T(8,128)(2,1)S(1)} collective-permute-done((bf16[96,128]{1,0:T(8,128)(2,1)S(1)}, bf16[96,128]{1,0:T(8,128)(2,1)S(1)}, u32[]{:S(2)}, u32[]{:S(2)}) %collective-permute-start.11) | collective-permute-done | bytes 24608 | tf_op jit(solution)/shard_map/ppermute | solution.py:553
  49.0 0.1 shard_map.155.mine_ref
  49.2 1.2 %collective-permute-done.13.theirs_ref = f32[40,128]{1,0:T(8,128)S(1)} collective-permute-done((f32[40,128]{1,0:T(8,128)S(1)}, f32[40,128]{1,0:T(8,128)S(1)}, u32[]{:S(2)}, u32[]{:S(2)}) %collective-permute-start.13) | collective-permute-done | bytes 20512 | tf_op jit(solution)/shard_map/ppermute | solution.py:555
  50.4 0.8 %shard_map.156 = f32[64,128]{1,0:T(8,128)} custom-call(f32[40,128]{1,0:T(8,128)S(1)} %shard_map.155.mine_ref, f32[40,128]{1,0:T(8,128)S(1)} %collective-permute-done.13.theirs_ref), custom_call_target="tpu_custom_call" | custom-call | bytes 73728 | tf_op jit(solution)/shard_map/pallas_call | solution.py:56
  (21 shorter events, 0.2 us)
Async XLA Ops:
  1.0 10.7 %collective-permute-start = (bf16[128,1280]{1,0:T(8,128)(2,1)S(1)}, bf16[128,1280]{1,0:T(8,128)(2,1)S(1)}, u32[]{:S(2)}, u32[]{:S(2)}) collective-permute-start(bf16[128,1280]{1,0:T(8,128)(2,1)S(1)} %shard_map.147), channel_id=1, source_target_pairs={{0,4},{4,0},{1,5},{5,1},{2,6},{6,2},{3,7},{7,3},{8,12},{12,8},{9,1... | collective-permute-start | bytes 983048 | tf_op jit(solution)/shard_map/ppermute | solution.py:445
  11.8 8.7 %collective-permute-start.1 = (bf16[128,1280]{1,0:T(8,128)(2,1)S(1)}, bf16[128,1280]{1,0:T(8,128)(2,1)S(1)}, u32[]{:S(2)}, u32[]{:S(2)}) collective-permute-start(bf16[128,1280]{1,0:T(8,128)(2,1)S(1)} %collective-permute-done.raw_ref), channel_id=1, source_target_pairs={{0,1},{1,0},{2,3},{3,2},{4,5},{5,4},{6,7},{7,6},{8,9},{9,8},{10,11... | collective-permute-start | bytes 983048 | tf_op jit(solution)/shard_map/ppermute | solution.py:504
  12.4 4.5 %copy-start = (bf16[2560,256]{1,0:T(8,128)(2,1)S(1)}, bf16[2560,256]{1,0:T(8,128)(2,1)}, u32[]{:S(2)}) copy-start(bf16[2560,256]{1,0:T(8,128)(2,1)} %q_ref.5) | copy-start | bytes 3932164
  12.5 4.5 %copy-start.1 = (bf16[2560,256]{1,0:T(8,128)(2,1)S(1)}, bf16[2560,256]{1,0:T(8,128)(2,1)}, u32[]{:S(2)}) copy-start(bf16[2560,256]{1,0:T(8,128)(2,1)} %k_ref.5) | copy-start | bytes 3932164
  15.1 4.6 %collective-permute-start.2 = (bf16[80,128]{1,0:T(8,128)(2,1)S(1)}, bf16[80,128]{1,0:T(8,128)(2,1)S(1)}, u32[]{:S(2)}, u32[]{:S(2)}) collective-permute-start(bf16[80,128]{1,0:T(8,128)(2,1)S(1)} %get-tuple-element.33), channel_id=1, source_target_pairs={{0,4},{4,0},{1,5},{5,1},{2,6},{6,2},{3,7},{7,3},{8,12},{12,8},{9,1... | collective-permute-start | bytes 61448 | tf_op jit(solution)/shard_map/ppermute | solution.py:472
  19.4 8.5 %collective-permute-start.4 = (bf16[128,896]{1,0:T(8,128)(2,1)S(1)}, bf16[128,896]{1,0:T(8,128)(2,1)S(1)}, u32[]{:S(2)}, u32[]{:S(2)}) collective-permute-start(bf16[128,896]{1,0:T(8,128)(2,1)S(1)} %get-tuple-element.43), channel_id=1, source_target_pairs={{0,4},{4,0},{1,5},{5,1},{2,6},{6,2},{3,7},{7,3},{8,12},{12,8},{9,1... | collective-permute-start | bytes 688136 | tf_op jit(solution)/shard_map/ppermute | solution.py:497
  20.5 7.6 %copy-start.2 = (bf16[64,5120]{1,0:T(8,128)(2,1)S(1)}, bf16[64,5120]{1,0:T(8,128)(2,1)}, u32[]{:S(2)}) copy-start(bf16[64,5120]{1,0:T(8,128)(2,1)} %readout_ref.1) | copy-start | bytes 1966084
  20.5 7.6 %copy-start.3 = (bf16[128,5120]{1,0:T(8,128)(2,1)S(1)}, bf16[128,5120]{1,0:T(8,128)(2,1)}, u32[]{:S(2)}) copy-start(bf16[128,5120]{1,0:T(8,128)(2,1)} %up_ref.3) | copy-start | bytes 3932164
  21.2 10.9 %collective-permute-start.3 = (bf16[128,896]{1,0:T(8,128)(2,1)S(1)}, bf16[128,896]{1,0:T(8,128)(2,1)S(1)}, u32[]{:S(2)}, u32[]{:S(2)}) collective-permute-start(bf16[128,896]{1,0:T(8,128)(2,1)S(1)} %get-tuple-element.41), channel_id=1, source_target_pairs={{0,4},{4,0},{1,5},{5,1},{2,6},{6,2},{3,7},{7,3},{8,12},{12,8},{9,1... | collective-permute-start | bytes 688136 | tf_op jit(solution)/shard_map/ppermute | solution.py:519
  27.9 1.2 %collective-permute-start.5 = (bf16[64,128]{1,0:T(8,128)(2,1)S(1)}, bf16[64,128]{1,0:T(8,128)(2,1)S(1)}, u32[]{:S(2)}, u32[]{:S(2)}) collective-permute-start(bf16[64,128]{1,0:T(8,128)(2,1)S(1)} %shard_map.150.lora_ref), channel_id=1, source_target_pairs={{0,1},{1,0},{2,3},{3,2},{4,5},{5,4},{6,7},{7,6},{8,9},{9,8},{10,11... | collective-permute-start | bytes 49160 | tf_op jit(solution)/shard_map/ppermute | solution.py:521
  28.0 1.2 %copy-start.4 = (bf16[128,256]{1,0:T(8,128)(2,1)S(1)}, bf16[128,256]{1,0:T(8,128)(2,1)}, u32[]{:S(2)}) copy-start(bf16[128,256]{1,0:T(8,128)(2,1)} %up_ref.5) | copy-start | bytes 196612
  28.0 1.1 %copy-start.5 = (bf16[256,128]{1,0:T(8,128)(2,1)S(1)}, bf16[256,128]{1,0:T(8,128)(2,1)}, u32[]{:S(2)}) copy-start(bf16[256,128]{1,0:T(8,128)(2,1)} %down_ref.1) | copy-start | bytes 196612
  32.9 1.3 %collective-permute-start.6 = (f32[128,128]{1,0:T(8,128)S(1)}, f32[128,128]{1,0:T(8,128)S(1)}, u32[]{:S(2)}, u32[]{:S(2)}) collective-permute-start(f32[128,128]{1,0:T(8,128)S(1)} %get-tuple-element.52), channel_id=1, source_target_pairs={{0,1},{1,0},{2,3},{3,2},{4,5},{5,4},{6,7},{7,6},{8,9},{9,8},{10,11... | collective-permute-start | bytes 196616 | tf_op jit(solution)/shard_map/ppermute | solution.py:540
  34.3 3.8 %collective-permute-start.7 = (bf16[96,128]{1,0:T(8,128)(2,1)S(1)}, bf16[96,128]{1,0:T(8,128)(2,1)S(1)}, u32[]{:S(2)}, u32[]{:S(2)}) collective-permute-start(bf16[96,128]{1,0:T(8,128)(2,1)S(1)} %get-tuple-element.53), channel_id=1, source_target_pairs={{0,2},{1,3},{2,0},{3,1},{4,6},{5,7},{6,4},{7,5},{8,10},{9,11},{10,... | collective-permute-start | bytes 73736 | tf_op jit(solution)/shard_map/ppermute | solution.py:544
  35.9 4.7 %collective-permute-start.9 = (bf16[96,128]{1,0:T(8,128)(2,1)S(1)}, bf16[96,128]{1,0:T(8,128)(2,1)S(1)}, u32[]{:S(2)}, u32[]{:S(2)}) collective-permute-start(bf16[96,128]{1,0:T(8,128)(2,1)S(1)} %get-tuple-element.54), channel_id=1, source_target_pairs={{0,6},{1,7},{2,4},{3,5},{4,2},{5,3},{6,0},{7,1},{8,14},{9,15},{10,... | collective-permute-start | bytes 73736 | tf_op jit(solution)/shard_map/ppermute | solution.py:545
  36.2 4.5 %collective-permute-start.8 = (bf16[96,128]{1,0:T(8,128)(2,1)S(1)}, bf16[96,128]{1,0:T(8,128)(2,1)S(1)}, u32[]{:S(2)}, u32[]{:S(2)}) collective-permute-start(bf16[96,128]{1,0:T(8,128)(2,1)S(1)} %get-tuple-element.54), channel_id=1, source_target_pairs={{0,4},{4,0},{1,5},{5,1},{2,6},{6,2},{3,7},{7,3},{8,12},{12,8},{9,1... | collective-permute-start | bytes 73736 | tf_op jit(solution)/shard_map/ppermute | solution.py:543
  40.6 5.7 %collective-permute-start.12 = (bf16[96,128]{1,0:T(8,128)(2,1)S(1)}, bf16[96,128]{1,0:T(8,128)(2,1)S(1)}, u32[]{:S(2)}, u32[]{:S(2)}) collective-permute-start(bf16[96,128]{1,0:T(8,128)(2,1)S(1)} %add_convert_fusion.refs_0_), channel_id=1, source_target_pairs={{0,24},{8,16},{16,8},{24,0},{1,25},{9,17},{17,9},{25,1},{2,26},{10... | collective-permute-start | bytes 73736 | tf_op jit(solution)/shard_map/ppermute | solution.py:553
  44.3 4.7 %collective-permute-start.11 = (bf16[96,128]{1,0:T(8,128)(2,1)S(1)}, bf16[96,128]{1,0:T(8,128)(2,1)S(1)}, u32[]{:S(2)}, u32[]{:S(2)}) collective-permute-start(bf16[96,128]{1,0:T(8,128)(2,1)S(1)} %add_convert_fusion.refs_0_), channel_id=1, source_target_pairs={{0,16},{8,24},{16,0},{24,8},{1,17},{9,25},{17,1},{25,9},{2,18},{10... | collective-permute-start | bytes 73736 | tf_op jit(solution)/shard_map/ppermute | solution.py:553
  44.3 4.7 %collective-permute-start.10 = (bf16[96,128]{1,0:T(8,128)(2,1)S(1)}, bf16[96,128]{1,0:T(8,128)(2,1)S(1)}, u32[]{:S(2)}, u32[]{:S(2)}) collective-permute-start(bf16[96,128]{1,0:T(8,128)(2,1)S(1)} %add_convert_fusion.refs_0_), channel_id=1, source_target_pairs={{0,8},{8,0},{16,24},{24,16},{1,9},{9,1},{17,25},{25,17},{2,10},{10... | collective-permute-start | bytes 73736 | tf_op jit(solution)/shard_map/ppermute | solution.py:553
  49.2 1.3 %collective-permute-start.13 = (f32[40,128]{1,0:T(8,128)S(1)}, f32[40,128]{1,0:T(8,128)S(1)}, u32[]{:S(2)}, u32[]{:S(2)}) collective-permute-start(f32[40,128]{1,0:T(8,128)S(1)} %shard_map.155.mine_ref), channel_id=1, source_target_pairs={{0,1},{1,0},{2,3},{3,2},{4,5},{5,4},{6,7},{7,6},{8,9},{9,8},{10,11... | collective-permute-start | bytes 61448 | tf_op jit(solution)/shard_map/ppermute | solution.py:555

commit v7 on v6

--- a/solution.py
+++ b/solution.py
@@ -80,25 +80,6 @@
 def high_low(x):
     high = x.astype(BF16)
     return high, (x - high.astype(F32)).astype(BF16)
-
-
-def slice_kernel(stream_hbm, message_ref, sems):
-    tokens, quarter = message_ref.shape
-    target = (1 - lax.axis_index("seq")) * 2 + lax.axis_index("head") % 2
-    pieces = sems.shape[0]
-    rows = tokens // pieces
-    copies = [
-        pltpu.make_async_copy(
-            stream_hbm.at[pl.ds(i * rows, rows), aligned(target, quarter)],
-            message_ref.at[pl.ds(i * rows, rows)],
-            sems.at[i],
-        )
-        for i in range(pieces)
-    ]
-    for copy in copies:
-        copy.start()
-    for copy in copies:
-        copy.wait()
 
 
 def first_kernel(
@@ -194,6 +175,12 @@
         kept_ref[:, i * columns : (i + 1) * columns] = block
 
 
+def half_rows(x):
+    share = x.shape[0] // 2
+    half = jnp.where(lax.axis_index("head") % 2 == 0, x[:share], x[share:])
+    return jnp.concatenate(high_low(half), axis=0)
+
+
 def own_kernel(
     normed_ref, q_ref, k_ref, v_ref, down_hbm, output_hbm, readout_hbm,
     sent_ref, kept_ref, mix_ref, down_v,
@@ -213,12 +200,8 @@
     parts = [dot(normed, w[...]) for w in (q_ref, k_ref, v_ref)]
     copies[0].wait()
     lora = dot(normed, down_v[...])
-    share = lora.shape[0] // 2
-    half = jnp.where(lax.axis_index("head") % 2 == 0, lora[:share], lora[share:])
-    high, low = high_low(half)
     parts.append(lora)
-    both = jnp.concatenate([high, low], axis=0)
-    partial_outputs(parts, seq, [both], sent_ref, kept_ref)
+    partial_outputs(parts, seq, [half_rows(lora)], sent_ref, kept_ref)
     for copy in copies[1:]:
         copy.wait()
     mix_v[...] = contract_final_axis(output_v[...], readout_v[...])
@@ -268,19 +251,20 @@
 
 def far_kernel(
     raw_ref, rows_ref, patch_ref, gain_ref, q_ref, k_ref, v_ref, down_ref,
-    near_q_ref, near_k_ref, near_v_ref, near_down_ref, sent_ref, kept_ref,
+    near_q_ref, near_k_ref, near_v_ref, near_down_ref,
+    small_ref, sent_ref, kept_ref,
 ):
     core = lax.axis_index("head") % 2
     weights = (q_ref, k_ref, v_ref, down_ref)
     parts = other_parts(1 - core, raw_ref, rows_ref, patch_ref, gain_ref, weights)
     near = (near_q_ref, near_k_ref, near_v_ref, near_down_ref)
     parts = [part + ref[...] for part, ref in zip(parts, near)]
-    lora = high_low(parts[3])
-    partial_outputs(parts, lax.axis_index("seq"), lora, sent_ref, kept_ref)
-
-
-def finish(kept_ref, got_ref, up, lora):
-    columns = up.shape[1]
+    small_ref[...] = half_rows(parts[3])
+    partial_outputs(parts, lax.axis_index("seq"), [], sent_ref, kept_ref)
+
+
+def finish(kept_ref, got_ref, low_rank):
+    columns = low_rank.shape[1]
 
     def got(i):
         return got_ref[:, i * columns : (i + 1) * columns].astype(F32)
@@ -292,31 +276,42 @@
     base = kept(0) + (got(0) + got(1))
     return (
         (base * scale).astype(BF16),
-        ((base + dot(lora, up)) * scale).astype(BF16),
+        ((base + low_rank) * scale).astype(BF16),
         (kept(1) + (got(2) + got(3))).astype(BF16),
         (kept(2) + got(4)).astype(BF16),
     )
 
 
-def lora_kernel(kept_ref, got_ref, lora_ref):
-    share, rank = lora_ref.shape
-    got = got_ref[:, 5 * rank : 6 * rank].astype(F32)
+def lora_kernel(own_kept_ref, small_got_ref, other_kept_ref, own_got_ref, lora_ref):
+    rank = lora_ref.shape[1]
+    share = lora_ref.shape[0] // 2
     core = lax.axis_index("head") % 2
-    kept = kept_ref[aligned(core, share), 3 * rank :]
-    lora_ref[...] = (kept + (got[:share] + got[share:])).astype(BF16)
+    for i, (kept_ref, got) in enumerate((
+        (own_kept_ref, small_got_ref[...]),
+        (other_kept_ref, own_got_ref[:, 5 * rank : 6 * rank]),
+    )):
+        kept = kept_ref[aligned(core, share), kept_ref.shape[1] - rank :]
+        got = got.astype(F32)
+        lora_ref[i * share : (i + 1) * share] = (
+            kept + (got[:share] + got[share:])
+        ).astype(BF16)
 
 
 def half_kernel(
-    kept_ref, got_ref, lora_ref, lora_far_ref, up_ref, mix_ref, down_ref, readout_of_up_ref,
-    set_ref, mixes_ref,
+    kept_ref, got_ref, lora_ref, lora_far_ref, up_ref, mix_ref, down_ref,
+    readout_of_up_ref, set_ref, mixes_ref, low_rank_ref,
 ):
     seq = lax.axis_index("seq")
     rows, channels = mix_ref.shape
     up = up_ref[:, aligned(seq, rows)]
     mine, far = lora_ref[...], lora_far_ref[...]
+    share = mine.shape[0] // 2
     first = lax.axis_index("head") % 2 == 0
-    lora = jnp.concatenate([jnp.where(first, mine, far), jnp.where(first, far, mine)], axis=0)
-    for i, block in enumerate(finish(kept_ref, got_ref, up, lora)):
+    low, high = jnp.where(first, mine, far), jnp.where(first, far, mine)
+    own = jnp.concatenate([low[:share], high[:share]], axis=0)
+    other = jnp.concatenate([low[share:], high[share:]], axis=0)
+    low_rank_ref[...] = dot(own, up)
+    for i, block in enumerate(finish(kept_ref, got_ref, dot(other, up))):
         set_ref[i] = block
     got = got_ref[:, -2 * channels :].astype(F32)
     mix_full = mix_ref[...] + (got[:, :channels] + swap_halves(got)[:, :channels])
@@ -328,18 +323,13 @@
 
 
 def attention_kernel(
-    kept_ref, got_ref, up_ref, set_ref, mixes_ref, base_ref,
+    kept_ref, got_ref, low_rank_ref, set_ref, mixes_ref, base_ref,
     sent_ref, stay_ref, sets_v, terms_v,
 ):
-    seq = lax.axis_index("seq")
     core = lax.axis_index("head") % 2
     tokens, channels = base_ref.shape
     columns = set_ref.shape[2]
-    up = up_ref[:, aligned(seq, columns)]
-    rank = got_ref.shape[1] - 5 * columns
-    got = got_ref[:, 5 * columns :].astype(F32)
-    lora = kept_ref[:, 3 * columns :] + (got[:, : rank // 2] + got[:, rank // 2 :])
-    for i, block in enumerate(finish(kept_ref, got_ref, up, lora.astype(BF16))):
+    for i, block in enumerate(finish(kept_ref, got_ref, low_rank_ref[...])):
         sets_v[i, :tokens] = block
         sets_v[i, tokens:] = set_ref[i]
     terms = jnp.zeros(terms_v.shape, F32)
@@ -433,15 +423,8 @@
     to_xy = pairs((2, heads), lambda s, h: (s ^ 1, h ^ 2))
     partial_flops = 2 * tokens * half_width * (3 * local_columns + rank)
 
-    in_hbm = pltpu.with_memory_space_constraint(stream, pltpu.HBM)
-    (message,) = run(
-        slice_kernel,
-        [((tokens, quarter), BF16)],
-        (in_hbm,),
-        [HBM],
-        [pltpu.SemaphoreType.DMA((4,))],
-        moved=4 * tokens * quarter,
-    )
+    target = (1 - lax.axis_index("seq")) * 2 + lax.axis_index("head") % 2
+    message = columns_of(stream, target, quarter)
     near = lax.ppermute(message, "seq", to_x)
     inputs = (
         latents.T, noise.T, stream, patch_embed_weight, prenorm_gain_vector, value_matrix,
@@ -510,18 +493,27 @@
         (near, *shared),
         flops=partial_flops // 2,
     )
-    other_sent, other_kept = run(
+    small_sent, other_sent, other_kept = run(
         far_kernel,
-        [((tokens, 7 * columns), BF16), ((tokens, 4 * columns), F32)],
+        [
+            ((tokens, rank), BF16),
+            ((tokens, 5 * columns), BF16),
+            ((tokens, 4 * columns), F32),
+        ],
         (far, *shared, *near_parts),
         flops=partial_flops // 2,
     )
+    small_got = lax.ppermute(small_sent, "seq", to_x)
     other_got = lax.ppermute(other_sent, "seq", to_x)
-    (lora,) = run(lora_kernel, [((share, rank), BF16)], (other_kept, own_got))
+    (lora,) = run(lora_kernel, [((tokens, rank), BF16)], (own_kept, small_got, other_kept, own_got))
     lora_far = lax.ppermute(lora, "head", to_core)
-    half_set, mixes = run(
+    half_set, mixes, low_rank = run(
         half_kernel,
-        [((4, tokens, columns), BF16), ((2, columns, 2 * channels), BF16)],
+        [
+            ((4, tokens, columns), BF16),
+            ((2, columns, 2 * channels), BF16),
+            ((tokens, columns), F32),
+        ],
         (
             other_kept, own_got, lora, lora_far, adapter_query_up, mix_part,
             adapter_output_down, readout_of_up,
@@ -530,7 +522,7 @@
     sent, stay = run(
         attention_kernel,
         [((tokens, 2 * channels), F32)] * 2,
-        (own_kept, other_got, adapter_query_up, half_set, mixes, base),
+        (own_kept, other_got, low_rank, half_set, mixes, base),
         scratch=[
             pltpu.VMEM((4, 2 * tokens, columns), BF16),
             pltpu.VMEM((2 * tokens, 2 * channels), F32),
@@ -638,6 +630,7 @@
         query_columns = args[6].shape[1]
         power = sizes[0] & (sizes[0] - 1) == 0
         paired = sizes[1] == 2 and sizes[2] == 4 and power
+        paired = paired and args[0].shape[0] == query_columns // 2
         if paired and (query_columns // HEAD_SIZE) % 2 == 0:
             return paired_local(sizes, *args)
         return gathered_local(*args)

time: 51.4 us -> 55.9 us (1.088)
  waiting for transfers between devices: 24.6 us -> 28.4 us
  local copies, waits for them, and re-layouts: 0.04 us -> 1.12 us
  Pallas kernels: 10.6 us -> 9.65 us
    ppermute x1, waiting for transfers between devices: 0.01 us -> 6.44 us  [paired_local(): other_rows = lax.ppermute(rows, 'seq', to_x)]
    ppermute x1, waiting for transfers between devices: 4.91 us -> 0.01 us  [paired_local(): own_got = lax.ppermute(own_sent, 'seq', to_x)]
    ppermute x0 -> x1, waiting for transfers between devices: none -> 4.45 us  [paired_local(): small_got = lax.ppermute(small_sent, 'seq', to_x)]
    ppermute x1, waiting for transfers between devices: 2.68 us -> 0.01 us  [paired_local(): other_got = lax.ppermute(other_sent, 'seq', to_x)]
    ppermute x1, starting transfers between devices: 1.81 us -> 0.29 us  [paired_local(): other_rows = lax.ppermute(rows, 'seq', to_x)]
    ppermute x1, starting transfers between devices: 0.35 us -> 1.8 us  [paired_local(): own_got = lax.ppermute(own_sent, 'seq', to_x)]
    ppermute x1, starting transfers between devices: 1.69 us -> 0.29 us  [paired_local(): from_x = lax.ppermute(cross, 'seq', to_x)]
    ppermute x1, starting transfers between devices: 0.27 us -> 1.43 us  [paired_local(): from_xy = lax.ppermute(cross, ('seq', 'head'), to_xy)]
  transfers between devices with their start and end apart: 14 -> 15, of which waited for: 10 -> 11; matrix products, arithmetic and copies ran while one was open for 0% -> 0% of each run, Pallas kernels for 15% -> 14%
where the time goes in v7:
time: 55.9 us; the launch traced here: 55.7 us
  waiting for transfers between devices  28.4 us (51%)
  starting transfers between devices  15.7 us (28%)
  Pallas kernels  9.65 us (17%)
  local copies, waits for them, and re-layouts  1.12 us (2%)
  between operations  0.83 us (1%)
    pallas_call x11, Pallas kernels, run(): pl.pallas_call(kernel, out_shape=shapes, in_specs=specs or [VMEM] * len(a...  9.65 us
    ppermute x1, waiting for transfers between devices, paired_local(): near = lax.ppermute(message, 'seq', to_x)  7.71 us
    ppermute x1, waiting for transfers between devices, paired_local(): other_rows = lax.ppermute(rows, 'seq', to_x)  6.44 us
    ppermute x3, starting transfers between devices, paired_local(): totals.append(lax.ppermute(total, 'group', to_group))  4.45 us
    ppermute x1, waiting for transfers between devices, paired_local(): small_got = lax.ppermute(small_sent, 'seq', to_x)  4.45 us
    ppermute x3, waiting for transfers between devices, paired_local(): totals.append(lax.ppermute(total, 'group', to_group))  3.92 us
    ppermute x1, starting transfers between devices, paired_local(): near = lax.ppermute(message, 'seq', to_x)  3.03 us
    ppermute x1, waiting for transfers between devices, paired_local(): from_xy = lax.ppermute(cross, ('seq', 'head'), to_xy)  2.7 us
  transfers between devices with their start and end apart: 15, of which 11 were waited for; matrix products, arithmetic and copies ran while one was open for 0% of the time, Pallas kernels for 14%

profile of v7, /device:TPU:0, one launch (start us, length us, event | category | flops | bytes accessed | tf_op | source)
XLA Modules:
  0.0 55.7 jit_solution(14666373462759096765)
XLA Ops:
  0.0 1.0 %constant_dynamic-slice_fusion = bf16[128,1280]{1,0:T(8,128)(2,1)S(1)} fusion(bf16[128,5120]{1,0:T(8,128)(2,1)} %stream_hbm.1, s32[]{:T(128)S(6)} %select_n.11), kind=kLoop, calls=%fused_computation.1 | loop fusion | bytes 655364 | tf_op jit(solution)/shard_map/dynamic_slice | solution.py:45
  1.0 3.0 %collective-permute-start = (bf16[128,1280]{1,0:T(8,128)(2,1)S(1)}, bf16[128,1280]{1,0:T(8,128)(2,1)S(1)}, u32[]{:S(2)}, u32[]{:S(2)}) collective-permute-start(bf16[128,1280]{1,0:T(8,128)(2,1)S(1)} %constant_dynamic-slice_fusion), channel_id=1, source_target_pairs={{0,4},{4,0},{1,5},{5,1},{2,6},{6,2},{3,7},{7,3},{8,12},{12,8},{9,1... | collective-permute-start | bytes 983048 | tf_op jit(solution)/shard_map/ppermute | solution.py:428
  4.0 7.7 %collective-permute-done.raw_ref = bf16[128,1280]{1,0:T(8,128)(2,1)S(1)} collective-permute-done((bf16[128,1280]{1,0:T(8,128)(2,1)S(1)}, bf16[128,1280]{1,0:T(8,128)(2,1)S(1)}, u32[]{:S(2)}, u32[]{:S(2)}) %collective-permute-start) | collective-permute-done | bytes 327712 | tf_op jit(solution)/shard_map/ppermute | solution.py:428
  12.4 2.6 %shard_map.145 = (bf16[128,2560]{1,0:T(8,128)(2,1)S(1)}, bf16[80,128]{1,0:T(8,128)(2,1)S(1)}, f32[64,128]{1,0:T(8,128)S(1)}, bf16[4,128,1280]{2,1,0:T(8,128)(2,1...) custom-call(s32[1]{0:T(128)S(6)} %copy.16.step_any, ...), custom_call_target="tpu_custom_call" | custom-call | bytes 6998020 | tf_op jit(solution)/shard_map/pallas_call | solution.py:56
  15.2 2.5 %shard_map.146 = (bf16[128,896]{1,0:T(8,128)(2,1)S(1)}, f32[128,512]{1,0:T(8,128)S(1)}, f32[128,64]{1,0:T(8,128)S(1)}, bf16[2560,128]{1,0:T(8,128)(2,1)S(1)}) custom-call(bf16[128,2560]{1,0:T(8,128)(2,1)S(1)} %get-tuple-element.32.normed_ref, bf16[2560,256]{1,0:T(8,128)(2,1)S(1)} %copy-done, bf16[2560,256]{1,0:T(8,128)(2,1)S(1)} %copy-done.1, ...), custom_call_target="tpu_custom_call" | custom-call | flops 587202560 | bytes 8388608 | tf_op jit(solution)/shard_map/pallas_call | solution.py:56
  17.6 1.8 %collective-permute-start.4 = (bf16[128,896]{1,0:T(8,128)(2,1)S(1)}, bf16[128,896]{1,0:T(8,128)(2,1)S(1)}, u32[]{:S(2)}, u32[]{:S(2)}) collective-permute-start(bf16[128,896]{1,0:T(8,128)(2,1)S(1)} %get-tuple-element.45), channel_id=1, source_target_pairs={{0,4},{4,0},{1,5},{5,1},{2,6},{6,2},{3,7},{7,3},{8,12},{12,8},{9,1... | collective-permute-start | bytes 688136 | tf_op jit(solution)/shard_map/ppermute | solution.py:480
  19.4 0.3 collective-permute-start.2
  19.7 6.4 %collective-permute-done.2.rows_ref = bf16[80,128]{1,0:T(8,128)(2,1)S(1)} collective-permute-done((bf16[80,128]{1,0:T(8,128)(2,1)S(1)}, bf16[80,128]{1,0:T(8,128)(2,1)S(1)}, u32[]{:S(2)}, u32[]{:S(2)}) %collective-permute-start.2) | collective-permute-done | bytes 20512 | tf_op jit(solution)/shard_map/ppermute | solution.py:455
  26.2 0.7 %shard_map.147 = (f32[128,256]{1,0:T(8,128)S(1)}, f32[128,256]{1,0:T(8,128)S(1)}, f32[128,256]{1,0:T(8,128)S(1)}, f32[128,128]{1,0:T(8,128)S(1)}) custom-call(bf16[128,1280]{1,0:T(8,128)(2,1)S(1)} %collective-permute-done.raw_ref, bf16[80,128]{1,0:T(8,128)(2,1)S(1)} %collective-permute-done.2.rows_ref, bf16[2,64,1280]{2,1,0:T(8,128)(2,1)S(1)} %get-tuple-element.36.patch_ref, ...), custom_call_target="tpu_custom_call" | custom-call | flops 293601280 | bytes 5732352 | tf_op jit(solution)/shard_map/pallas_call | solution.py:56
  26.9 0.7 %shard_map.148 = (bf16[128,128]{1,0:T(8,128)(2,1)S(1)}, bf16[128,640]{1,0:T(8,128)(2,1)S(1)}, f32[128,512]{1,0:T(8,128)S(1)}) custom-call(bf16[128,1280]{1,0:T(8,128)(2,1)S(1)} %collective-permute-done.1.raw_ref, bf16[80,128]{1,0:T(8,128)(2,1)S(1)} %collective-permute-done.2.rows_ref, bf16[2,64,1280]{2,1,0:T(8,128)(2,1)S(1)} %get-tuple-element.36.patch_ref, ...), custom_call_target="tpu_custom_call" | custom-call | flops 293601280 | bytes 6191104 | tf_op jit(solution)/shard_map/pallas_call | solution.py:56
  27.6 1.8 %collective-permute-start.3 = (bf16[128,640]{1,0:T(8,128)(2,1)S(1)}, bf16[128,640]{1,0:T(8,128)(2,1)S(1)}, u32[]{:S(2)}, u32[]{:S(2)}) collective-permute-start(bf16[128,640]{1,0:T(8,128)(2,1)S(1)} %get-tuple-element.43), channel_id=1, source_target_pairs={{0,4},{4,0},{1,5},{5,1},{2,6},{6,2},{3,7},{7,3},{8,12},{12,8},{9,1... | collective-permute-start | bytes 491528 | tf_op jit(solution)/shard_map/ppermute | solution.py:507
  29.4 0.3 collective-permute-start.5
  29.7 4.4 %collective-permute-done.5.small_got_ref = bf16[128,128]{1,0:T(8,128)(2,1)S(1)} collective-permute-done((bf16[128,128]{1,0:T(8,128)(2,1)S(1)}, bf16[128,128]{1,0:T(8,128)(2,1)S(1)}, u32[]{:S(2)}, u32[]{:S(2)}) %collective-permute-start.5) | collective-permute-done | bytes 32800 | tf_op jit(solution)/shard_map/ppermute | solution.py:506
  34.3 1.0 %shard_map.150 = (bf16[128,64]{1,0:T(8,128)(2,1)S(1)}, f32[128,64]{1,0:T(8,128)S(1)}) custom-call(bf16[4,128,1280]{2,1,0:T(8,128)(2,1)S(1)} %get-tuple-element.48.hidden_ref, bf16[128,5120]{1,0:T(8,128)(2,1)S(1)} %copy-done.3, bf16[64,5120]{1,0:T(8,128)(2,1)S(1)} %copy-done.2, f32[64,128]{1,0:T(8,128)S(1)} %get-tuple-element.49.gap_ref), custom_call_target="tpu_custom_call" | custom-call | flops 167772160 | bytes 3358720 | tf_op jit(solution)/shard_map/pallas_call | solution.py:56
  35.3 0.2 collective-permute-done.6.lora_far_ref
  35.5 0.2 shard_map.151
  35.7 0.9 %shard_map.152 = (f32[128,128]{1,0:T(8,128)S(1)}, f32[128,128]{1,0:T(8,128)S(1)}) custom-call(f32[128,512]{1,0:T(8,128)S(1)} %get-tuple-element.34.own_kept_ref.kept_ref, bf16[128,640]{1,0:T(8,128)(2,1)S(1)} %collective-permute-done.3.got_ref, f32[128,128]{1,0:T(8,128)S(1)} %get-tuple-element.51.low_rank_ref, ...), custom_call_target="tpu_custom_call" | custom-call | bytes 851968 | tf_op jit(solution)/shard_map/pallas_call | solution.py:56
  36.6 0.4 collective-permute-start.7
  37.0 0.9 %collective-permute-done.7.got_ref = f32[128,128]{1,0:T(8,128)S(1)} collective-permute-done((f32[128,128]{1,0:T(8,128)S(1)}, f32[128,128]{1,0:T(8,128)S(1)}, u32[]{:S(2)}, u32[]{:S(2)}) %collective-permute-start.7) | collective-permute-done | bytes 65568 | tf_op jit(solution)/shard_map/ppermute | solution.py:532
  38.0 1.8 %collective-permute-start.8 = (bf16[96,128]{1,0:T(8,128)(2,1)S(1)}, bf16[96,128]{1,0:T(8,128)(2,1)S(1)}, u32[]{:S(2)}, u32[]{:S(2)}) collective-permute-start(bf16[96,128]{1,0:T(8,128)(2,1)S(1)} %get-tuple-element.57), channel_id=1, source_target_pairs={{0,2},{1,3},{2,0},{3,1},{4,6},{5,7},{6,4},{7,5},{8,10},{9,11},{10,... | collective-permute-start | bytes 73736 | tf_op jit(solution)/shard_map/ppermute | solution.py:536
  39.8 1.4 %collective-permute-start.10 = (bf16[96,128]{1,0:T(8,128)(2,1)S(1)}, bf16[96,128]{1,0:T(8,128)(2,1)S(1)}, u32[]{:S(2)}, u32[]{:S(2)}) collective-permute-start(bf16[96,128]{1,0:T(8,128)(2,1)S(1)} %get-tuple-element.58), channel_id=1, source_target_pairs={{0,6},{1,7},{2,4},{3,5},{4,2},{5,3},{6,0},{7,1},{8,14},{9,15},{10,... | collective-permute-start | bytes 73736 | tf_op jit(solution)/shard_map/ppermute | solution.py:537
  41.2 0.3 collective-permute-start.9
  41.5 0.3 collective-permute-done.8
  41.9 2.7 %collective-permute-done.10 = bf16[96,128]{1,0:T(8,128)(2,1)S(1)} collective-permute-done((bf16[96,128]{1,0:T(8,128)(2,1)S(1)}, bf16[96,128]{1,0:T(8,128)(2,1)S(1)}, u32[]{:S(2)}, u32[]{:S(2)}) %collective-permute-start.10) | collective-permute-done | bytes 24608 | tf_op jit(solution)/shard_map/ppermute | solution.py:537
  44.6 0.5 collective-permute-done.9
  45.1 3.6 %collective-permute-start.13 = (bf16[96,128]{1,0:T(8,128)(2,1)S(1)}, bf16[96,128]{1,0:T(8,128)(2,1)S(1)}, u32[]{:S(2)}, u32[]{:S(2)}) collective-permute-start(bf16[96,128]{1,0:T(8,128)(2,1)S(1)} %add_convert_fusion.refs_0_), channel_id=1, source_target_pairs={{0,24},{8,16},{16,8},{24,0},{1,25},{9,17},{17,9},{25,1},{2,26},{10... | collective-permute-start | bytes 73736 | tf_op jit(solution)/shard_map/ppermute | solution.py:545
  48.7 0.8 %collective-permute-start.11 = (bf16[96,128]{1,0:T(8,128)(2,1)S(1)}, bf16[96,128]{1,0:T(8,128)(2,1)S(1)}, u32[]{:S(2)}, u32[]{:S(2)}) collective-permute-start(bf16[96,128]{1,0:T(8,128)(2,1)S(1)} %add_convert_fusion.refs_0_), channel_id=1, source_target_pairs={{0,8},{8,0},{16,24},{24,16},{1,9},{9,1},{17,25},{25,17},{2,10},{10... | collective-permute-start | bytes 73736 | tf_op jit(solution)/shard_map/ppermute | solution.py:545
  49.5 1.3 %collective-permute-done.13.refs_3_ = bf16[96,128]{1,0:T(8,128)(2,1)S(1)} collective-permute-done((bf16[96,128]{1,0:T(8,128)(2,1)S(1)}, bf16[96,128]{1,0:T(8,128)(2,1)S(1)}, u32[]{:S(2)}, u32[]{:S(2)}) %collective-permute-start.13) | collective-permute-done | bytes 24608 | tf_op jit(solution)/shard_map/ppermute | solution.py:545
  50.8 2.7 %collective-permute-done.12.refs_2_ = bf16[96,128]{1,0:T(8,128)(2,1)S(1)} collective-permute-done((bf16[96,128]{1,0:T(8,128)(2,1)S(1)}, bf16[96,128]{1,0:T(8,128)(2,1)S(1)}, u32[]{:S(2)}, u32[]{:S(2)}) %collective-permute-start.12) | collective-permute-done | bytes 24608 | tf_op jit(solution)/shard_map/ppermute | solution.py:545
  53.5 0.1 shard_map.154.mine_ref
  53.7 1.2 %collective-permute-done.14.theirs_ref = f32[40,128]{1,0:T(8,128)S(1)} collective-permute-done((f32[40,128]{1,0:T(8,128)S(1)}, f32[40,128]{1,0:T(8,128)S(1)}, u32[]{:S(2)}, u32[]{:S(2)}) %collective-permute-start.14) | collective-permute-done | bytes 20512 | tf_op jit(solution)/shard_map/ppermute | solution.py:547
  54.9 0.8 %shard_map.155 = f32[64,128]{1,0:T(8,128)} custom-call(f32[40,128]{1,0:T(8,128)S(1)} %shard_map.154.mine_ref, f32[40,128]{1,0:T(8,128)S(1)} %collective-permute-done.14.theirs_ref), custom_call_target="tpu_custom_call" | custom-call | bytes 73728 | tf_op jit(solution)/shard_map/pallas_call | solution.py:56
  (23 shorter events, 0.4 us)
Async XLA Ops:
  1.0 10.7 %collective-permute-start = (bf16[128,1280]{1,0:T(8,128)(2,1)S(1)}, bf16[128,1280]{1,0:T(8,128)(2,1)S(1)}, u32[]{:S(2)}, u32[]{:S(2)}) collective-permute-start(bf16[128,1280]{1,0:T(8,128)(2,1)S(1)} %constant_dynamic-slice_fusion), channel_id=1, source_target_pairs={{0,4},{4,0},{1,5},{5,1},{2,6},{6,2},{3,7},{7,3},{8,12},{12,8},{9,1... | collective-permute-start | bytes 983048 | tf_op jit(solution)/shard_map/ppermute | solution.py:428
  11.7 15.1 %collective-permute-start.1 = (bf16[128,1280]{1,0:T(8,128)(2,1)S(1)}, bf16[128,1280]{1,0:T(8,128)(2,1)S(1)}, u32[]{:S(2)}, u32[]{:S(2)}) collective-permute-start(bf16[128,1280]{1,0:T(8,128)(2,1)S(1)} %collective-permute-done.raw_ref), channel_id=1, source_target_pairs={{0,1},{1,0},{2,3},{3,2},{4,5},{5,4},{6,7},{7,6},{8,9},{9,8},{10,11... | collective-permute-start | bytes 983048 | tf_op jit(solution)/shard_map/ppermute | solution.py:487
  12.4 2.7 %copy-start = (bf16[2560,256]{1,0:T(8,128)(2,1)S(1)}, bf16[2560,256]{1,0:T(8,128)(2,1)}, u32[]{:S(2)}) copy-start(bf16[2560,256]{1,0:T(8,128)(2,1)} %q_ref.5) | copy-start | bytes 3932164
  12.4 2.8 %copy-start.1 = (bf16[2560,256]{1,0:T(8,128)(2,1)S(1)}, bf16[2560,256]{1,0:T(8,128)(2,1)}, u32[]{:S(2)}) copy-start(bf16[2560,256]{1,0:T(8,128)(2,1)} %k_ref.5) | copy-start | bytes 3932164
  17.6 12.1 %collective-permute-start.4 = (bf16[128,896]{1,0:T(8,128)(2,1)S(1)}, bf16[128,896]{1,0:T(8,128)(2,1)S(1)}, u32[]{:S(2)}, u32[]{:S(2)}) collective-permute-start(bf16[128,896]{1,0:T(8,128)(2,1)S(1)} %get-tuple-element.45), channel_id=1, source_target_pairs={{0,4},{4,0},{1,5},{5,1},{2,6},{6,2},{3,7},{7,3},{8,12},{12,8},{9,1... | collective-permute-start | bytes 688136 | tf_op jit(solution)/shard_map/ppermute | solution.py:480
  19.4 6.7 %collective-permute-start.2 = (bf16[80,128]{1,0:T(8,128)(2,1)S(1)}, bf16[80,128]{1,0:T(8,128)(2,1)S(1)}, u32[]{:S(2)}, u32[]{:S(2)}) collective-permute-start(bf16[80,128]{1,0:T(8,128)(2,1)S(1)} %get-tuple-element.35), channel_id=1, source_target_pairs={{0,4},{4,0},{1,5},{5,1},{2,6},{6,2},{3,7},{7,3},{8,12},{12,8},{9,1... | collective-permute-start | bytes 61448 | tf_op jit(solution)/shard_map/ppermute | solution.py:455
  26.9 7.4 %copy-start.2 = (bf16[64,5120]{1,0:T(8,128)(2,1)S(1)}, bf16[64,5120]{1,0:T(8,128)(2,1)}, u32[]{:S(2)}) copy-start(bf16[64,5120]{1,0:T(8,128)(2,1)} %readout_ref.1) | copy-start | bytes 1966084
  26.9 7.4 %copy-start.3 = (bf16[128,5120]{1,0:T(8,128)(2,1)S(1)}, bf16[128,5120]{1,0:T(8,128)(2,1)}, u32[]{:S(2)}) copy-start(bf16[128,5120]{1,0:T(8,128)(2,1)} %up_ref.2) | copy-start | bytes 3932164
  27.6 8.1 %collective-permute-start.3 = (bf16[128,640]{1,0:T(8,128)(2,1)S(1)}, bf16[128,640]{1,0:T(8,128)(2,1)S(1)}, u32[]{:S(2)}, u32[]{:S(2)}) collective-permute-start(bf16[128,640]{1,0:T(8,128)(2,1)S(1)} %get-tuple-element.43), channel_id=1, source_target_pairs={{0,4},{4,0},{1,5},{5,1},{2,6},{6,2},{3,7},{7,3},{8,12},{12,8},{9,1... | collective-permute-start | bytes 491528 | tf_op jit(solution)/shard_map/ppermute | solution.py:507
  29.4 4.7 %collective-permute-start.5 = (bf16[128,128]{1,0:T(8,128)(2,1)S(1)}, bf16[128,128]{1,0:T(8,128)(2,1)S(1)}, u32[]{:S(2)}, u32[]{:S(2)}) collective-permute-start(bf16[128,128]{1,0:T(8,128)(2,1)S(1)} %get-tuple-element.46), channel_id=1, source_target_pairs={{0,4},{4,0},{1,5},{5,1},{2,6},{6,2},{3,7},{7,3},{8,12},{12,8},{9,1... | collective-permute-start | bytes 98312 | tf_op jit(solution)/shard_map/ppermute | solution.py:506
  34.2 1.3 %collective-permute-start.6 = (bf16[128,128]{1,0:T(8,128)(2,1)S(1)}, bf16[128,128]{1,0:T(8,128)(2,1)S(1)}, u32[]{:S(2)}, u32[]{:S(2)}) collective-permute-start(bf16[128,128]{1,0:T(8,128)(2,1)S(1)} %shard_map.149.lora_ref), channel_id=1, source_target_pairs={{0,1},{1,0},{2,3},{3,2},{4,5},{5,4},{6,7},{7,6},{8,9},{9,8},{10,11... | collective-permute-start | bytes 98312 | tf_op jit(solution)/shard_map/ppermute | solution.py:509
  34.3 1.2 %copy-start.4 = (bf16[128,256]{1,0:T(8,128)(2,1)S(1)}, bf16[128,256]{1,0:T(8,128)(2,1)}, u32[]{:S(2)}) copy-start(bf16[128,256]{1,0:T(8,128)(2,1)} %up_ref.3) | copy-start | bytes 196612
  34.3 1.2 %copy-start.5 = (bf16[256,128]{1,0:T(8,128)(2,1)S(1)}, bf16[256,128]{1,0:T(8,128)(2,1)}, u32[]{:S(2)}) copy-start(bf16[256,128]{1,0:T(8,128)(2,1)} %down_ref.1) | copy-start | bytes 196612
  36.6 1.3 %collective-permute-start.7 = (f32[128,128]{1,0:T(8,128)S(1)}, f32[128,128]{1,0:T(8,128)S(1)}, u32[]{:S(2)}, u32[]{:S(2)}) collective-permute-start(f32[128,128]{1,0:T(8,128)S(1)} %get-tuple-element.56), channel_id=1, source_target_pairs={{0,1},{1,0},{2,3},{3,2},{4,5},{5,4},{6,7},{7,6},{8,9},{9,8},{10,11... | collective-permute-start | bytes 196616 | tf_op jit(solution)/shard_map/ppermute | solution.py:532
  38.0 3.8 %collective-permute-start.8 = (bf16[96,128]{1,0:T(8,128)(2,1)S(1)}, bf16[96,128]{1,0:T(8,128)(2,1)S(1)}, u32[]{:S(2)}, u32[]{:S(2)}) collective-permute-start(bf16[96,128]{1,0:T(8,128)(2,1)S(1)} %get-tuple-element.57), channel_id=1, source_target_pairs={{0,2},{1,3},{2,0},{3,1},{4,6},{5,7},{6,4},{7,5},{8,10},{9,11},{10,... | collective-permute-start | bytes 73736 | tf_op jit(solution)/shard_map/ppermute | solution.py:536
  39.8 4.8 %collective-permute-start.10 = (bf16[96,128]{1,0:T(8,128)(2,1)S(1)}, bf16[96,128]{1,0:T(8,128)(2,1)S(1)}, u32[]{:S(2)}, u32[]{:S(2)}) collective-permute-start(bf16[96,128]{1,0:T(8,128)(2,1)S(1)} %get-tuple-element.58), channel_id=1, source_target_pairs={{0,6},{1,7},{2,4},{3,5},{4,2},{5,3},{6,0},{7,1},{8,14},{9,15},{10,... | collective-permute-start | bytes 73736 | tf_op jit(solution)/shard_map/ppermute | solution.py:537
  41.2 3.8 %collective-permute-start.9 = (bf16[96,128]{1,0:T(8,128)(2,1)S(1)}, bf16[96,128]{1,0:T(8,128)(2,1)S(1)}, u32[]{:S(2)}, u32[]{:S(2)}) collective-permute-start(bf16[96,128]{1,0:T(8,128)(2,1)S(1)} %get-tuple-element.58), channel_id=1, source_target_pairs={{0,4},{4,0},{1,5},{5,1},{2,6},{6,2},{3,7},{7,3},{8,12},{12,8},{9,1... | collective-permute-start | bytes 73736 | tf_op jit(solution)/shard_map/ppermute | solution.py:535
  45.1 5.7 %collective-permute-start.13 = (bf16[96,128]{1,0:T(8,128)(2,1)S(1)}, bf16[96,128]{1,0:T(8,128)(2,1)S(1)}, u32[]{:S(2)}, u32[]{:S(2)}) collective-permute-start(bf16[96,128]{1,0:T(8,128)(2,1)S(1)} %add_convert_fusion.refs_0_), channel_id=1, source_target_pairs={{0,24},{8,16},{16,8},{24,0},{1,25},{9,17},{17,9},{25,1},{2,26},{10... | collective-permute-start | bytes 73736 | tf_op jit(solution)/shard_map/ppermute | solution.py:545
  48.7 4.7 %collective-permute-start.12 = (bf16[96,128]{1,0:T(8,128)(2,1)S(1)}, bf16[96,128]{1,0:T(8,128)(2,1)S(1)}, u32[]{:S(2)}, u32[]{:S(2)}) collective-permute-start(bf16[96,128]{1,0:T(8,128)(2,1)S(1)} %add_convert_fusion.refs_0_), channel_id=1, source_target_pairs={{0,16},{8,24},{16,0},{24,8},{1,17},{9,25},{17,1},{25,9},{2,18},{10... | collective-permute-start | bytes 73736 | tf_op jit(solution)/shard_map/ppermute | solution.py:545
  48.7 4.7 %collective-permute-start.11 = (bf16[96,128]{1,0:T(8,128)(2,1)S(1)}, bf16[96,128]{1,0:T(8,128)(2,1)S(1)}, u32[]{:S(2)}, u32[]{:S(2)}) collective-permute-start(bf16[96,128]{1,0:T(8,128)(2,1)S(1)} %add_convert_fusion.refs_0_), channel_id=1, source_target_pairs={{0,8},{8,0},{16,24},{24,16},{1,9},{9,1},{17,25},{25,17},{2,10},{10... | collective-permute-start | bytes 73736 | tf_op jit(solution)/shard_map/ppermute | solution.py:545
  53.6 1.3 %collective-permute-start.14 = (f32[40,128]{1,0:T(8,128)S(1)}, f32[40,128]{1,0:T(8,128)S(1)}, u32[]{:S(2)}, u32[]{:S(2)}) collective-permute-start(f32[40,128]{1,0:T(8,128)S(1)} %shard_map.154.mine_ref), channel_id=1, source_target_pairs={{0,1},{1,0},{2,3},{3,2},{4,5},{5,4},{6,7},{7,6},{8,9},{9,8},{10,11... | collective-permute-start | bytes 61448 | tf_op jit(solution)/shard_map/ppermute | solution.py:547

commit v8 on v7

--- a/solution.py
+++ b/solution.py
@@ -333,16 +333,17 @@
         sets_v[i, :tokens] = block
         sets_v[i, tokens:] = set_ref[i]
     terms = jnp.zeros(terms_v.shape, F32)
+    rows = 2 * tokens
     for start in range(0, columns, HEAD_SIZE):
         span = slice(start, start + HEAD_SIZE)
-        keys, values = sets_v[2, :, span], sets_v[3, :, span]
-        for kind in range(2):
-            scores = contract_final_axis(sets_v[kind, :, span], keys)
-            top = jnp.max(scores, axis=1, keepdims=True)
-            probs = jnp.exp(scores - top)
-            mass = jnp.sum(probs, axis=1, keepdims=True)
-            attn = (dot(probs.astype(BF16), values) / mass).astype(BF16)
-            terms = terms + dot(attn, mixes_ref[kind, span, :])
+        queries = jnp.concatenate([sets_v[0, :, span], sets_v[1, :, span]], axis=0)
+        scores = contract_final_axis(queries, sets_v[2, :, span])
+        probs = jnp.exp(scores - jnp.max(scores, axis=1, keepdims=True))
+        mass = jnp.sum(probs, axis=1, keepdims=True)
+        attn = (dot(probs.astype(BF16), sets_v[3, :, span]) * (1.0 / mass)).astype(BF16)
+        attn = jnp.concatenate([attn[:rows], attn[rows:]], axis=1)
+        mixes = jnp.concatenate([mixes_ref[0, span, :], mixes_ref[1, span, :]], axis=0)
+        terms = terms + dot(attn, mixes)
     terms_v[...] = terms
     terms_v[:tokens, :channels] = terms[:tokens, :channels] + base_ref[...]
     share = tokens // 2

time: 55.9 us -> 55.6 us (level)
  no operation moved by 1% of the time
where the time goes in v8:
time: 55.6 us; the launch traced here: 55.5 us
  waiting for transfers between devices  28.4 us (51%)
  starting transfers between devices  15.7 us (28%)
  Pallas kernels  9.44 us (17%)
  local copies, waits for them, and re-layouts  1.12 us (2%)
  between operations  0.83 us (1%)
    pallas_call x11, Pallas kernels, run(): pl.pallas_call(kernel, out_shape=shapes, in_specs=specs or [VMEM] * len(a...  9.44 us
    ppermute x1, waiting for transfers between devices, paired_local(): near = lax.ppermute(message, 'seq', to_x)  7.71 us
    ppermute x1, waiting for transfers between devices, paired_local(): other_rows = lax.ppermute(rows, 'seq', to_x)  6.44 us
    ppermute x3, starting transfers between devices, paired_local(): totals.append(lax.ppermute(total, 'group', to_group))  4.45 us
    ppermute x1, waiting for transfers between devices, paired_local(): small_got = lax.ppermute(small_sent, 'seq', to_x)  4.45 us
    ppermute x3, waiting for transfers between devices, paired_local(): totals.append(lax.ppermute(total, 'group', to_group))  3.93 us
    ppermute x1, starting transfers between devices, paired_local(): near = lax.ppermute(message, 'seq', to_x)  3.03 us
    ppermute x1, waiting for transfers between devices, paired_local(): from_xy = lax.ppermute(cross, ('seq', 'head'), to_xy)  2.71 us
  transfers between devices with their start and end apart: 15, of which 11 were waited for; matrix products, arithmetic and copies ran while one was open for 0% of the time, Pallas kernels for 14%

profile of v8, /device:TPU:0, one launch (start us, length us, event | category | flops | bytes accessed | tf_op | source)
XLA Modules:
  0.0 55.5 jit_solution(3734986014916103563)
XLA Ops:
  0.0 1.0 %constant_dynamic-slice_fusion = bf16[128,1280]{1,0:T(8,128)(2,1)S(1)} fusion(bf16[128,5120]{1,0:T(8,128)(2,1)} %stream_hbm.1, s32[]{:T(128)S(6)} %select_n.11), kind=kLoop, calls=%fused_computation.1 | loop fusion | bytes 655364 | tf_op jit(solution)/shard_map/dynamic_slice | solution.py:45
  1.0 3.0 %collective-permute-start = (bf16[128,1280]{1,0:T(8,128)(2,1)S(1)}, bf16[128,1280]{1,0:T(8,128)(2,1)S(1)}, u32[]{:S(2)}, u32[]{:S(2)}) collective-permute-start(bf16[128,1280]{1,0:T(8,128)(2,1)S(1)} %constant_dynamic-slice_fusion), channel_id=1, source_target_pairs={{0,4},{4,0},{1,5},{5,1},{2,6},{6,2},{3,7},{7,3},{8,12},{12,8},{9,1... | collective-permute-start | bytes 983048 | tf_op jit(solution)/shard_map/ppermute | solution.py:429
  4.0 7.7 %collective-permute-done.raw_ref = bf16[128,1280]{1,0:T(8,128)(2,1)S(1)} collective-permute-done((bf16[128,1280]{1,0:T(8,128)(2,1)S(1)}, bf16[128,1280]{1,0:T(8,128)(2,1)S(1)}, u32[]{:S(2)}, u32[]{:S(2)}) %collective-permute-start) | collective-permute-done | bytes 327712 | tf_op jit(solution)/shard_map/ppermute | solution.py:429
  12.4 2.6 %shard_map.145 = (bf16[128,2560]{1,0:T(8,128)(2,1)S(1)}, bf16[80,128]{1,0:T(8,128)(2,1)S(1)}, f32[64,128]{1,0:T(8,128)S(1)}, bf16[4,128,1280]{2,1,0:T(8,128)(2,1...) custom-call(s32[1]{0:T(128)S(6)} %copy.16.step_any, ...), custom_call_target="tpu_custom_call" | custom-call | bytes 6998020 | tf_op jit(solution)/shard_map/pallas_call | solution.py:56
  15.2 2.5 %shard_map.146 = (bf16[128,896]{1,0:T(8,128)(2,1)S(1)}, f32[128,512]{1,0:T(8,128)S(1)}, f32[128,64]{1,0:T(8,128)S(1)}, bf16[2560,128]{1,0:T(8,128)(2,1)S(1)}) custom-call(bf16[128,2560]{1,0:T(8,128)(2,1)S(1)} %get-tuple-element.32.normed_ref, bf16[2560,256]{1,0:T(8,128)(2,1)S(1)} %copy-done, bf16[2560,256]{1,0:T(8,128)(2,1)S(1)} %copy-done.1, ...), custom_call_target="tpu_custom_call" | custom-call | flops 587202560 | bytes 8388608 | tf_op jit(solution)/shard_map/pallas_call | solution.py:56
  17.6 1.8 %collective-permute-start.4 = (bf16[128,896]{1,0:T(8,128)(2,1)S(1)}, bf16[128,896]{1,0:T(8,128)(2,1)S(1)}, u32[]{:S(2)}, u32[]{:S(2)}) collective-permute-start(bf16[128,896]{1,0:T(8,128)(2,1)S(1)} %get-tuple-element.45), channel_id=1, source_target_pairs={{0,4},{4,0},{1,5},{5,1},{2,6},{6,2},{3,7},{7,3},{8,12},{12,8},{9,1... | collective-permute-start | bytes 688136 | tf_op jit(solution)/shard_map/ppermute | solution.py:481
  19.4 0.3 collective-permute-start.2
  19.7 6.4 %collective-permute-done.2.rows_ref = bf16[80,128]{1,0:T(8,128)(2,1)S(1)} collective-permute-done((bf16[80,128]{1,0:T(8,128)(2,1)S(1)}, bf16[80,128]{1,0:T(8,128)(2,1)S(1)}, u32[]{:S(2)}, u32[]{:S(2)}) %collective-permute-start.2) | collective-permute-done | bytes 20512 | tf_op jit(solution)/shard_map/ppermute | solution.py:456
  26.2 0.7 %shard_map.147 = (f32[128,256]{1,0:T(8,128)S(1)}, f32[128,256]{1,0:T(8,128)S(1)}, f32[128,256]{1,0:T(8,128)S(1)}, f32[128,128]{1,0:T(8,128)S(1)}) custom-call(bf16[128,1280]{1,0:T(8,128)(2,1)S(1)} %collective-permute-done.raw_ref, bf16[80,128]{1,0:T(8,128)(2,1)S(1)} %collective-permute-done.2.rows_ref, bf16[2,64,1280]{2,1,0:T(8,128)(2,1)S(1)} %get-tuple-element.36.patch_ref, ...), custom_call_target="tpu_custom_call" | custom-call | flops 293601280 | bytes 5732352 | tf_op jit(solution)/shard_map/pallas_call | solution.py:56
  26.9 0.7 %shard_map.148 = (bf16[128,128]{1,0:T(8,128)(2,1)S(1)}, bf16[128,640]{1,0:T(8,128)(2,1)S(1)}, f32[128,512]{1,0:T(8,128)S(1)}) custom-call(bf16[128,1280]{1,0:T(8,128)(2,1)S(1)} %collective-permute-done.1.raw_ref, bf16[80,128]{1,0:T(8,128)(2,1)S(1)} %collective-permute-done.2.rows_ref, bf16[2,64,1280]{2,1,0:T(8,128)(2,1)S(1)} %get-tuple-element.36.patch_ref, ...), custom_call_target="tpu_custom_call" | custom-call | flops 293601280 | bytes 6191104 | tf_op jit(solution)/shard_map/pallas_call | solution.py:56
  27.6 1.8 %collective-permute-start.3 = (bf16[128,640]{1,0:T(8,128)(2,1)S(1)}, bf16[128,640]{1,0:T(8,128)(2,1)S(1)}, u32[]{:S(2)}, u32[]{:S(2)}) collective-permute-start(bf16[128,640]{1,0:T(8,128)(2,1)S(1)} %get-tuple-element.43), channel_id=1, source_target_pairs={{0,4},{4,0},{1,5},{5,1},{2,6},{6,2},{3,7},{7,3},{8,12},{12,8},{9,1... | collective-permute-start | bytes 491528 | tf_op jit(solution)/shard_map/ppermute | solution.py:508
  29.4 0.3 collective-permute-start.5
  29.7 4.4 %collective-permute-done.5.small_got_ref = bf16[128,128]{1,0:T(8,128)(2,1)S(1)} collective-permute-done((bf16[128,128]{1,0:T(8,128)(2,1)S(1)}, bf16[128,128]{1,0:T(8,128)(2,1)S(1)}, u32[]{:S(2)}, u32[]{:S(2)}) %collective-permute-start.5) | collective-permute-done | bytes 32800 | tf_op jit(solution)/shard_map/ppermute | solution.py:507
  34.3 1.0 %shard_map.150 = (bf16[128,64]{1,0:T(8,128)(2,1)S(1)}, f32[128,64]{1,0:T(8,128)S(1)}) custom-call(bf16[4,128,1280]{2,1,0:T(8,128)(2,1)S(1)} %get-tuple-element.48.hidden_ref, bf16[128,5120]{1,0:T(8,128)(2,1)S(1)} %copy-done.3, bf16[64,5120]{1,0:T(8,128)(2,1)S(1)} %copy-done.2, f32[64,128]{1,0:T(8,128)S(1)} %get-tuple-element.49.gap_ref), custom_call_target="tpu_custom_call" | custom-call | flops 167772160 | bytes 3358720 | tf_op jit(solution)/shard_map/pallas_call | solution.py:56
  35.3 0.2 collective-permute-done.6.lora_far_ref
  35.5 0.2 shard_map.151
  35.7 0.7 %shard_map.152 = (f32[128,128]{1,0:T(8,128)S(1)}, f32[128,128]{1,0:T(8,128)S(1)}) custom-call(f32[128,512]{1,0:T(8,128)S(1)} %get-tuple-element.34.own_kept_ref.kept_ref, bf16[128,640]{1,0:T(8,128)(2,1)S(1)} %collective-permute-done.3.got_ref, f32[128,128]{1,0:T(8,128)S(1)} %get-tuple-element.51.low_rank_ref, ...), custom_call_target="tpu_custom_call" | custom-call | bytes 851968 | tf_op jit(solution)/shard_map/pallas_call | solution.py:56
  36.4 0.4 collective-permute-start.7
  36.8 0.9 %collective-permute-done.7.got_ref = f32[128,128]{1,0:T(8,128)S(1)} collective-permute-done((f32[128,128]{1,0:T(8,128)S(1)}, f32[128,128]{1,0:T(8,128)S(1)}, u32[]{:S(2)}, u32[]{:S(2)}) %collective-permute-start.7) | collective-permute-done | bytes 65568 | tf_op jit(solution)/shard_map/ppermute | solution.py:533
  37.8 1.8 %collective-permute-start.8 = (bf16[96,128]{1,0:T(8,128)(2,1)S(1)}, bf16[96,128]{1,0:T(8,128)(2,1)S(1)}, u32[]{:S(2)}, u32[]{:S(2)}) collective-permute-start(bf16[96,128]{1,0:T(8,128)(2,1)S(1)} %get-tuple-element.57), channel_id=1, source_target_pairs={{0,2},{1,3},{2,0},{3,1},{4,6},{5,7},{6,4},{7,5},{8,10},{9,11},{10,... | collective-permute-start | bytes 73736 | tf_op jit(solution)/shard_map/ppermute | solution.py:537
  39.6 1.4 %collective-permute-start.10 = (bf16[96,128]{1,0:T(8,128)(2,1)S(1)}, bf16[96,128]{1,0:T(8,128)(2,1)S(1)}, u32[]{:S(2)}, u32[]{:S(2)}) collective-permute-start(bf16[96,128]{1,0:T(8,128)(2,1)S(1)} %get-tuple-element.58), channel_id=1, source_target_pairs={{0,6},{1,7},{2,4},{3,5},{4,2},{5,3},{6,0},{7,1},{8,14},{9,15},{10,... | collective-permute-start | bytes 73736 | tf_op jit(solution)/shard_map/ppermute | solution.py:538
  41.0 0.3 collective-permute-start.9
  41.3 0.3 collective-permute-done.8
  41.6 2.7 %collective-permute-done.10 = bf16[96,128]{1,0:T(8,128)(2,1)S(1)} collective-permute-done((bf16[96,128]{1,0:T(8,128)(2,1)S(1)}, bf16[96,128]{1,0:T(8,128)(2,1)S(1)}, u32[]{:S(2)}, u32[]{:S(2)}) %collective-permute-start.10) | collective-permute-done | bytes 24608 | tf_op jit(solution)/shard_map/ppermute | solution.py:538
  44.4 0.5 collective-permute-done.9
  44.9 3.7 %collective-permute-start.13 = (bf16[96,128]{1,0:T(8,128)(2,1)S(1)}, bf16[96,128]{1,0:T(8,128)(2,1)S(1)}, u32[]{:S(2)}, u32[]{:S(2)}) collective-permute-start(bf16[96,128]{1,0:T(8,128)(2,1)S(1)} %add_convert_fusion.refs_0_), channel_id=1, source_target_pairs={{0,24},{8,16},{16,8},{24,0},{1,25},{9,17},{17,9},{25,1},{2,26},{10... | collective-permute-start | bytes 73736 | tf_op jit(solution)/shard_map/ppermute | solution.py:546
  48.5 0.8 %collective-permute-start.11 = (bf16[96,128]{1,0:T(8,128)(2,1)S(1)}, bf16[96,128]{1,0:T(8,128)(2,1)S(1)}, u32[]{:S(2)}, u32[]{:S(2)}) collective-permute-start(bf16[96,128]{1,0:T(8,128)(2,1)S(1)} %add_convert_fusion.refs_0_), channel_id=1, source_target_pairs={{0,8},{8,0},{16,24},{24,16},{1,9},{9,1},{17,25},{25,17},{2,10},{10... | collective-permute-start | bytes 73736 | tf_op jit(solution)/shard_map/ppermute | solution.py:546
  49.3 1.3 %collective-permute-done.13.refs_3_ = bf16[96,128]{1,0:T(8,128)(2,1)S(1)} collective-permute-done((bf16[96,128]{1,0:T(8,128)(2,1)S(1)}, bf16[96,128]{1,0:T(8,128)(2,1)S(1)}, u32[]{:S(2)}, u32[]{:S(2)}) %collective-permute-start.13) | collective-permute-done | bytes 24608 | tf_op jit(solution)/shard_map/ppermute | solution.py:546
  50.6 2.7 %collective-permute-done.12.refs_2_ = bf16[96,128]{1,0:T(8,128)(2,1)S(1)} collective-permute-done((bf16[96,128]{1,0:T(8,128)(2,1)S(1)}, bf16[96,128]{1,0:T(8,128)(2,1)S(1)}, u32[]{:S(2)}, u32[]{:S(2)}) %collective-permute-start.12) | collective-permute-done | bytes 24608 | tf_op jit(solution)/shard_map/ppermute | solution.py:546
  53.2 0.1 shard_map.154.mine_ref
  53.5 1.2 %collective-permute-done.14.theirs_ref = f32[40,128]{1,0:T(8,128)S(1)} collective-permute-done((f32[40,128]{1,0:T(8,128)S(1)}, f32[40,128]{1,0:T(8,128)S(1)}, u32[]{:S(2)}, u32[]{:S(2)}) %collective-permute-start.14) | collective-permute-done | bytes 20512 | tf_op jit(solution)/shard_map/ppermute | solution.py:548
  54.6 0.8 %shard_map.155 = f32[64,128]{1,0:T(8,128)} custom-call(f32[40,128]{1,0:T(8,128)S(1)} %shard_map.154.mine_ref, f32[40,128]{1,0:T(8,128)S(1)} %collective-permute-done.14.theirs_ref), custom_call_target="tpu_custom_call" | custom-call | bytes 73728 | tf_op jit(solution)/shard_map/pallas_call | solution.py:56
  (23 shorter events, 0.4 us)
Async XLA Ops:
  1.0 10.7 %collective-permute-start = (bf16[128,1280]{1,0:T(8,128)(2,1)S(1)}, bf16[128,1280]{1,0:T(8,128)(2,1)S(1)}, u32[]{:S(2)}, u32[]{:S(2)}) collective-permute-start(bf16[128,1280]{1,0:T(8,128)(2,1)S(1)} %constant_dynamic-slice_fusion), channel_id=1, source_target_pairs={{0,4},{4,0},{1,5},{5,1},{2,6},{6,2},{3,7},{7,3},{8,12},{12,8},{9,1... | collective-permute-start | bytes 983048 | tf_op jit(solution)/shard_map/ppermute | solution.py:429
  11.7 15.1 %collective-permute-start.1 = (bf16[128,1280]{1,0:T(8,128)(2,1)S(1)}, bf16[128,1280]{1,0:T(8,128)(2,1)S(1)}, u32[]{:S(2)}, u32[]{:S(2)}) collective-permute-start(bf16[128,1280]{1,0:T(8,128)(2,1)S(1)} %collective-permute-done.raw_ref), channel_id=1, source_target_pairs={{0,1},{1,0},{2,3},{3,2},{4,5},{5,4},{6,7},{7,6},{8,9},{9,8},{10,11... | collective-permute-start | bytes 983048 | tf_op jit(solution)/shard_map/ppermute | solution.py:488
  12.4 2.7 %copy-start = (bf16[2560,256]{1,0:T(8,128)(2,1)S(1)}, bf16[2560,256]{1,0:T(8,128)(2,1)}, u32[]{:S(2)}) copy-start(bf16[2560,256]{1,0:T(8,128)(2,1)} %q_ref.5) | copy-start | bytes 3932164
  12.4 2.8 %copy-start.1 = (bf16[2560,256]{1,0:T(8,128)(2,1)S(1)}, bf16[2560,256]{1,0:T(8,128)(2,1)}, u32[]{:S(2)}) copy-start(bf16[2560,256]{1,0:T(8,128)(2,1)} %k_ref.5) | copy-start | bytes 3932164
  17.6 12.1 %collective-permute-start.4 = (bf16[128,896]{1,0:T(8,128)(2,1)S(1)}, bf16[128,896]{1,0:T(8,128)(2,1)S(1)}, u32[]{:S(2)}, u32[]{:S(2)}) collective-permute-start(bf16[128,896]{1,0:T(8,128)(2,1)S(1)} %get-tuple-element.45), channel_id=1, source_target_pairs={{0,4},{4,0},{1,5},{5,1},{2,6},{6,2},{3,7},{7,3},{8,12},{12,8},{9,1... | collective-permute-start | bytes 688136 | tf_op jit(solution)/shard_map/ppermute | solution.py:481
  19.4 6.7 %collective-permute-start.2 = (bf16[80,128]{1,0:T(8,128)(2,1)S(1)}, bf16[80,128]{1,0:T(8,128)(2,1)S(1)}, u32[]{:S(2)}, u32[]{:S(2)}) collective-permute-start(bf16[80,128]{1,0:T(8,128)(2,1)S(1)} %get-tuple-element.35), channel_id=1, source_target_pairs={{0,4},{4,0},{1,5},{5,1},{2,6},{6,2},{3,7},{7,3},{8,12},{12,8},{9,1... | collective-permute-start | bytes 61448 | tf_op jit(solution)/shard_map/ppermute | solution.py:456
  26.9 7.4 %copy-start.2 = (bf16[64,5120]{1,0:T(8,128)(2,1)S(1)}, bf16[64,5120]{1,0:T(8,128)(2,1)}, u32[]{:S(2)}) copy-start(bf16[64,5120]{1,0:T(8,128)(2,1)} %readout_ref.1) | copy-start | bytes 1966084
  26.9 7.4 %copy-start.3 = (bf16[128,5120]{1,0:T(8,128)(2,1)S(1)}, bf16[128,5120]{1,0:T(8,128)(2,1)}, u32[]{:S(2)}) copy-start(bf16[128,5120]{1,0:T(8,128)(2,1)} %up_ref.2) | copy-start | bytes 3932164
  27.6 8.1 %collective-permute-start.3 = (bf16[128,640]{1,0:T(8,128)(2,1)S(1)}, bf16[128,640]{1,0:T(8,128)(2,1)S(1)}, u32[]{:S(2)}, u32[]{:S(2)}) collective-permute-start(bf16[128,640]{1,0:T(8,128)(2,1)S(1)} %get-tuple-element.43), channel_id=1, source_target_pairs={{0,4},{4,0},{1,5},{5,1},{2,6},{6,2},{3,7},{7,3},{8,12},{12,8},{9,1... | collective-permute-start | bytes 491528 | tf_op jit(solution)/shard_map/ppermute | solution.py:508
  29.4 4.7 %collective-permute-start.5 = (bf16[128,128]{1,0:T(8,128)(2,1)S(1)}, bf16[128,128]{1,0:T(8,128)(2,1)S(1)}, u32[]{:S(2)}, u32[]{:S(2)}) collective-permute-start(bf16[128,128]{1,0:T(8,128)(2,1)S(1)} %get-tuple-element.46), channel_id=1, source_target_pairs={{0,4},{4,0},{1,5},{5,1},{2,6},{6,2},{3,7},{7,3},{8,12},{12,8},{9,1... | collective-permute-start | bytes 98312 | tf_op jit(solution)/shard_map/ppermute | solution.py:507
  34.2 1.3 %collective-permute-start.6 = (bf16[128,128]{1,0:T(8,128)(2,1)S(1)}, bf16[128,128]{1,0:T(8,128)(2,1)S(1)}, u32[]{:S(2)}, u32[]{:S(2)}) collective-permute-start(bf16[128,128]{1,0:T(8,128)(2,1)S(1)} %shard_map.149.lora_ref), channel_id=1, source_target_pairs={{0,1},{1,0},{2,3},{3,2},{4,5},{5,4},{6,7},{7,6},{8,9},{9,8},{10,11... | collective-permute-start | bytes 98312 | tf_op jit(solution)/shard_map/ppermute | solution.py:510
  34.3 1.2 %copy-start.4 = (bf16[128,256]{1,0:T(8,128)(2,1)S(1)}, bf16[128,256]{1,0:T(8,128)(2,1)}, u32[]{:S(2)}) copy-start(bf16[128,256]{1,0:T(8,128)(2,1)} %up_ref.3) | copy-start | bytes 196612
  34.3 1.2 %copy-start.5 = (bf16[256,128]{1,0:T(8,128)(2,1)S(1)}, bf16[256,128]{1,0:T(8,128)(2,1)}, u32[]{:S(2)}) copy-start(bf16[256,128]{1,0:T(8,128)(2,1)} %down_ref.1) | copy-start | bytes 196612
  36.4 1.3 %collective-permute-start.7 = (f32[128,128]{1,0:T(8,128)S(1)}, f32[128,128]{1,0:T(8,128)S(1)}, u32[]{:S(2)}, u32[]{:S(2)}) collective-permute-start(f32[128,128]{1,0:T(8,128)S(1)} %get-tuple-element.56), channel_id=1, source_target_pairs={{0,1},{1,0},{2,3},{3,2},{4,5},{5,4},{6,7},{7,6},{8,9},{9,8},{10,11... | collective-permute-start | bytes 196616 | tf_op jit(solution)/shard_map/ppermute | solution.py:533
  37.8 3.8 %collective-permute-start.8 = (bf16[96,128]{1,0:T(8,128)(2,1)S(1)}, bf16[96,128]{1,0:T(8,128)(2,1)S(1)}, u32[]{:S(2)}, u32[]{:S(2)}) collective-permute-start(bf16[96,128]{1,0:T(8,128)(2,1)S(1)} %get-tuple-element.57), channel_id=1, source_target_pairs={{0,2},{1,3},{2,0},{3,1},{4,6},{5,7},{6,4},{7,5},{8,10},{9,11},{10,... | collective-permute-start | bytes 73736 | tf_op jit(solution)/shard_map/ppermute | solution.py:537
  39.6 4.8 %collective-permute-start.10 = (bf16[96,128]{1,0:T(8,128)(2,1)S(1)}, bf16[96,128]{1,0:T(8,128)(2,1)S(1)}, u32[]{:S(2)}, u32[]{:S(2)}) collective-permute-start(bf16[96,128]{1,0:T(8,128)(2,1)S(1)} %get-tuple-element.58), channel_id=1, source_target_pairs={{0,6},{1,7},{2,4},{3,5},{4,2},{5,3},{6,0},{7,1},{8,14},{9,15},{10,... | collective-permute-start | bytes 73736 | tf_op jit(solution)/shard_map/ppermute | solution.py:538
  41.0 3.8 %collective-permute-start.9 = (bf16[96,128]{1,0:T(8,128)(2,1)S(1)}, bf16[96,128]{1,0:T(8,128)(2,1)S(1)}, u32[]{:S(2)}, u32[]{:S(2)}) collective-permute-start(bf16[96,128]{1,0:T(8,128)(2,1)S(1)} %get-tuple-element.58), channel_id=1, source_target_pairs={{0,4},{4,0},{1,5},{5,1},{2,6},{6,2},{3,7},{7,3},{8,12},{12,8},{9,1... | collective-permute-start | bytes 73736 | tf_op jit(solution)/shard_map/ppermute | solution.py:536
  44.9 5.7 %collective-permute-start.13 = (bf16[96,128]{1,0:T(8,128)(2,1)S(1)}, bf16[96,128]{1,0:T(8,128)(2,1)S(1)}, u32[]{:S(2)}, u32[]{:S(2)}) collective-permute-start(bf16[96,128]{1,0:T(8,128)(2,1)S(1)} %add_convert_fusion.refs_0_), channel_id=1, source_target_pairs={{0,24},{8,16},{16,8},{24,0},{1,25},{9,17},{17,9},{25,1},{2,26},{10... | collective-permute-start | bytes 73736 | tf_op jit(solution)/shard_map/ppermute | solution.py:546
  48.5 4.7 %collective-permute-start.12 = (bf16[96,128]{1,0:T(8,128)(2,1)S(1)}, bf16[96,128]{1,0:T(8,128)(2,1)S(1)}, u32[]{:S(2)}, u32[]{:S(2)}) collective-permute-start(bf16[96,128]{1,0:T(8,128)(2,1)S(1)} %add_convert_fusion.refs_0_), channel_id=1, source_target_pairs={{0,16},{8,24},{16,0},{24,8},{1,17},{9,25},{17,1},{25,9},{2,18},{10... | collective-permute-start | bytes 73736 | tf_op jit(solution)/shard_map/ppermute | solution.py:546
  48.5 4.7 %collective-permute-start.11 = (bf16[96,128]{1,0:T(8,128)(2,1)S(1)}, bf16[96,128]{1,0:T(8,128)(2,1)S(1)}, u32[]{:S(2)}, u32[]{:S(2)}) collective-permute-start(bf16[96,128]{1,0:T(8,128)(2,1)S(1)} %add_convert_fusion.refs_0_), channel_id=1, source_target_pairs={{0,8},{8,0},{16,24},{24,16},{1,9},{9,1},{17,25},{25,17},{2,10},{10... | collective-permute-start | bytes 73736 | tf_op jit(solution)/shard_map/ppermute | solution.py:546
  53.4 1.3 %collective-permute-start.14 = (f32[40,128]{1,0:T(8,128)S(1)}, f32[40,128]{1,0:T(8,128)S(1)}, u32[]{:S(2)}, u32[]{:S(2)}) collective-permute-start(f32[40,128]{1,0:T(8,128)S(1)} %shard_map.154.mine_ref), channel_id=1, source_target_pairs={{0,1},{1,0},{2,3},{3,2},{4,5},{5,4},{6,7},{7,6},{8,9},{9,8},{10,11... | collective-permute-start | bytes 61448 | tf_op jit(solution)/shard_map/ppermute | solution.py:548

commit v9 on v8

--- a/solution.py
+++ b/solution.py
@@ -164,10 +164,10 @@
     return jnp.where(index == 0, x[:, :half], x[:, half:])
 
 
-def partial_outputs(parts, seq, lora_blocks, sent_ref, kept_ref):
+def partial_outputs(parts, seq, query_terms, lora_blocks, sent_ref, kept_ref):
     q, k, v, lora = parts
     columns = q.shape[1] // 2
-    blocks = [*high_low(pick(1 - seq, q)), *high_low(pick(1 - seq, k))]
+    blocks = [*high_low(pick(1 - seq, q))[:query_terms], *high_low(pick(1 - seq, k))]
     blocks += [pick(1 - seq, v).astype(BF16), *lora_blocks]
     for i, block in enumerate(blocks):
         sent_ref[:, i * columns : (i + 1) * columns] = block
@@ -201,7 +201,7 @@
     copies[0].wait()
     lora = dot(normed, down_v[...])
     parts.append(lora)
-    partial_outputs(parts, seq, [half_rows(lora)], sent_ref, kept_ref)
+    partial_outputs(parts, seq, 2, [half_rows(lora)], sent_ref, kept_ref)
     for copy in copies[1:]:
         copy.wait()
     mix_v[...] = contract_final_axis(output_v[...], readout_v[...])
@@ -260,10 +260,10 @@
     near = (near_q_ref, near_k_ref, near_v_ref, near_down_ref)
     parts = [part + ref[...] for part, ref in zip(parts, near)]
     small_ref[...] = half_rows(parts[3])
-    partial_outputs(parts, lax.axis_index("seq"), [], sent_ref, kept_ref)
-
-
-def finish(kept_ref, got_ref, low_rank):
+    partial_outputs(parts, lax.axis_index("seq"), 1, [], sent_ref, kept_ref)
+
+
+def finish(kept_ref, got_ref, query_terms, low_rank):
     columns = low_rank.shape[1]
 
     def got(i):
@@ -273,12 +273,13 @@
         return kept_ref[:, i * columns : (i + 1) * columns]
 
     scale = HEAD_SIZE ** (-0.5)
-    base = kept(0) + (got(0) + got(1))
+    n = query_terms
+    base = kept(0) + sum(got(i) for i in reversed(range(n)))
     return (
         (base * scale).astype(BF16),
         ((base + low_rank) * scale).astype(BF16),
-        (kept(1) + (got(2) + got(3))).astype(BF16),
-        (kept(2) + got(4)).astype(BF16),
+        (kept(1) + (got(n) + got(n + 1))).astype(BF16),
+        (kept(2) + got(n + 2)).astype(BF16),
     )
 
 
@@ -311,7 +312,7 @@
     own = jnp.concatenate([low[:share], high[:share]], axis=0)
     other = jnp.concatenate([low[share:], high[share:]], axis=0)
     low_rank_ref[...] = dot(own, up)
-    for i, block in enumerate(finish(kept_ref, got_ref, dot(other, up))):
+    for i, block in enumerate(finish(kept_ref, got_ref, 2, dot(other, up))):
         set_ref[i] = block
     got = got_ref[:, -2 * channels :].astype(F32)
     mix_full = mix_ref[...] + (got[:, :channels] + swap_halves(got)[:, :channels])
@@ -329,7 +330,7 @@
     core = lax.axis_index("head") % 2
     tokens, channels = base_ref.shape
     columns = set_ref.shape[2]
-    for i, block in enumerate(finish(kept_ref, got_ref, low_rank_ref[...])):
+    for i, block in enumerate(finish(kept_ref, got_ref, 1, low_rank_ref[...])):
         sets_v[i, :tokens] = block
         sets_v[i, tokens:] = set_ref[i]
     terms = jnp.zeros(terms_v.shape, F32)
@@ -498,7 +499,7 @@
         far_kernel,
         [
             ((tokens, rank), BF16),
-            ((tokens, 5 * columns), BF16),
+            ((tokens, 4 * columns), BF16),
             ((tokens, 4 * columns), F32),
         ],
         (far, *shared, *near_parts),

time: 55.6 us -> 54.9 us (0.987)
  waiting for transfers between devices: 28.4 us -> 27.7 us
    ppermute x1, waiting for transfers between devices: 4.45 us -> 3.74 us  [paired_local(): small_got = lax.ppermute(small_sent, 'seq', to_x)]
where the time goes in v9:
time: 54.9 us; the launch traced here: 54.7 us
  waiting for transfers between devices  27.7 us (50%)
  starting transfers between devices  15.7 us (29%)
  Pallas kernels  9.43 us (17%)
  local copies, waits for them, and re-layouts  1.12 us (2%)
  between operations  0.83 us (2%)
    pallas_call x11, Pallas kernels, run(): pl.pallas_call(kernel, out_shape=shapes, in_specs=specs or [VMEM] * len(a...  9.43 us
    ppermute x1, waiting for transfers between devices, paired_local(): near = lax.ppermute(message, 'seq', to_x)  7.71 us
    ppermute x1, waiting for transfers between devices, paired_local(): other_rows = lax.ppermute(rows, 'seq', to_x)  6.44 us
    ppermute x3, starting transfers between devices, paired_local(): totals.append(lax.ppermute(total, 'group', to_group))  4.45 us
    ppermute x3, waiting for transfers between devices, paired_local(): totals.append(lax.ppermute(total, 'group', to_group))  3.91 us
    ppermute x1, waiting for transfers between devices, paired_local(): small_got = lax.ppermute(small_sent, 'seq', to_x)  3.74 us
    ppermute x1, starting transfers between devices, paired_local(): near = lax.ppermute(message, 'seq', to_x)  3.03 us
    ppermute x1, waiting for transfers between devices, paired_local(): from_xy = lax.ppermute(cross, ('seq', 'head'), to_xy)  2.69 us
  transfers between devices with their start and end apart: 15, of which 11 were waited for; matrix products, arithmetic and copies ran while one was open for 0% of the time, Pallas kernels for 14%

profile of v9, /device:TPU:0, one launch (start us, length us, event | category | flops | bytes accessed | tf_op | source)
XLA Modules:
  0.0 54.7 jit_solution(13144496344367886471)
XLA Ops:
  0.0 1.0 %constant_dynamic-slice_fusion = bf16[128,1280]{1,0:T(8,128)(2,1)S(1)} fusion(bf16[128,5120]{1,0:T(8,128)(2,1)} %stream_hbm.1, s32[]{:T(128)S(6)} %select_n.11), kind=kLoop, calls=%fused_computation.1 | loop fusion | bytes 655364 | tf_op jit(solution)/shard_map/dynamic_slice | solution.py:45
  1.0 3.0 %collective-permute-start = (bf16[128,1280]{1,0:T(8,128)(2,1)S(1)}, bf16[128,1280]{1,0:T(8,128)(2,1)S(1)}, u32[]{:S(2)}, u32[]{:S(2)}) collective-permute-start(bf16[128,1280]{1,0:T(8,128)(2,1)S(1)} %constant_dynamic-slice_fusion), channel_id=1, source_target_pairs={{0,4},{4,0},{1,5},{5,1},{2,6},{6,2},{3,7},{7,3},{8,12},{12,8},{9,1... | collective-permute-start | bytes 983048 | tf_op jit(solution)/shard_map/ppermute | solution.py:430
  4.0 7.7 %collective-permute-done.raw_ref = bf16[128,1280]{1,0:T(8,128)(2,1)S(1)} collective-permute-done((bf16[128,1280]{1,0:T(8,128)(2,1)S(1)}, bf16[128,1280]{1,0:T(8,128)(2,1)S(1)}, u32[]{:S(2)}, u32[]{:S(2)}) %collective-permute-start) | collective-permute-done | bytes 327712 | tf_op jit(solution)/shard_map/ppermute | solution.py:430
  12.4 2.6 %shard_map.145 = (bf16[128,2560]{1,0:T(8,128)(2,1)S(1)}, bf16[80,128]{1,0:T(8,128)(2,1)S(1)}, f32[64,128]{1,0:T(8,128)S(1)}, bf16[4,128,1280]{2,1,0:T(8,128)(2,1...) custom-call(s32[1]{0:T(128)S(6)} %copy.16.step_any, ...), custom_call_target="tpu_custom_call" | custom-call | bytes 6998020 | tf_op jit(solution)/shard_map/pallas_call | solution.py:56
  15.2 2.5 %shard_map.146 = (bf16[128,896]{1,0:T(8,128)(2,1)S(1)}, f32[128,512]{1,0:T(8,128)S(1)}, f32[128,64]{1,0:T(8,128)S(1)}, bf16[2560,128]{1,0:T(8,128)(2,1)S(1)}) custom-call(bf16[128,2560]{1,0:T(8,128)(2,1)S(1)} %get-tuple-element.32.normed_ref, bf16[2560,256]{1,0:T(8,128)(2,1)S(1)} %copy-done, bf16[2560,256]{1,0:T(8,128)(2,1)S(1)} %copy-done.1, ...), custom_call_target="tpu_custom_call" | custom-call | flops 587202560 | bytes 8388608 | tf_op jit(solution)/shard_map/pallas_call | solution.py:56
  17.6 1.8 %collective-permute-start.4 = (bf16[128,896]{1,0:T(8,128)(2,1)S(1)}, bf16[128,896]{1,0:T(8,128)(2,1)S(1)}, u32[]{:S(2)}, u32[]{:S(2)}) collective-permute-start(bf16[128,896]{1,0:T(8,128)(2,1)S(1)} %get-tuple-element.45), channel_id=1, source_target_pairs={{0,4},{4,0},{1,5},{5,1},{2,6},{6,2},{3,7},{7,3},{8,12},{12,8},{9,1... | collective-permute-start | bytes 688136 | tf_op jit(solution)/shard_map/ppermute | solution.py:482
  19.4 0.3 collective-permute-start.2
  19.7 6.4 %collective-permute-done.2.rows_ref = bf16[80,128]{1,0:T(8,128)(2,1)S(1)} collective-permute-done((bf16[80,128]{1,0:T(8,128)(2,1)S(1)}, bf16[80,128]{1,0:T(8,128)(2,1)S(1)}, u32[]{:S(2)}, u32[]{:S(2)}) %collective-permute-start.2) | collective-permute-done | bytes 20512 | tf_op jit(solution)/shard_map/ppermute | solution.py:457
  26.2 0.7 %shard_map.147 = (f32[128,256]{1,0:T(8,128)S(1)}, f32[128,256]{1,0:T(8,128)S(1)}, f32[128,256]{1,0:T(8,128)S(1)}, f32[128,128]{1,0:T(8,128)S(1)}) custom-call(bf16[128,1280]{1,0:T(8,128)(2,1)S(1)} %collective-permute-done.raw_ref, bf16[80,128]{1,0:T(8,128)(2,1)S(1)} %collective-permute-done.2.rows_ref, bf16[2,64,1280]{2,1,0:T(8,128)(2,1)S(1)} %get-tuple-element.36.patch_ref, ...), custom_call_target="tpu_custom_call" | custom-call | flops 293601280 | bytes 5732352 | tf_op jit(solution)/shard_map/pallas_call | solution.py:56
  26.9 0.7 %shard_map.148 = (bf16[128,128]{1,0:T(8,128)(2,1)S(1)}, bf16[128,512]{1,0:T(8,128)(2,1)S(1)}, f32[128,512]{1,0:T(8,128)S(1)}) custom-call(bf16[128,1280]{1,0:T(8,128)(2,1)S(1)} %collective-permute-done.1.raw_ref, bf16[80,128]{1,0:T(8,128)(2,1)S(1)} %collective-permute-done.2.rows_ref, bf16[2,64,1280]{2,1,0:T(8,128)(2,1)S(1)} %get-tuple-element.36.patch_ref, ...), custom_call_target="tpu_custom_call" | custom-call | flops 293601280 | bytes 6158336 | tf_op jit(solution)/shard_map/pallas_call | solution.py:56
  27.6 1.8 %collective-permute-start.3 = (bf16[128,512]{1,0:T(8,128)(2,1)S(1)}, bf16[128,512]{1,0:T(8,128)(2,1)S(1)}, u32[]{:S(2)}, u32[]{:S(2)}) collective-permute-start(bf16[128,512]{1,0:T(8,128)(2,1)S(1)} %get-tuple-element.43), channel_id=1, source_target_pairs={{0,4},{4,0},{1,5},{5,1},{2,6},{6,2},{3,7},{7,3},{8,12},{12,8},{9,1... | collective-permute-start | bytes 393224 | tf_op jit(solution)/shard_map/ppermute | solution.py:509
  29.4 0.3 collective-permute-start.5
  29.7 3.7 %collective-permute-done.5.small_got_ref = bf16[128,128]{1,0:T(8,128)(2,1)S(1)} collective-permute-done((bf16[128,128]{1,0:T(8,128)(2,1)S(1)}, bf16[128,128]{1,0:T(8,128)(2,1)S(1)}, u32[]{:S(2)}, u32[]{:S(2)}) %collective-permute-start.5) | collective-permute-done | bytes 32800 | tf_op jit(solution)/shard_map/ppermute | solution.py:508
  33.6 1.0 %shard_map.150 = (bf16[128,64]{1,0:T(8,128)(2,1)S(1)}, f32[128,64]{1,0:T(8,128)S(1)}) custom-call(bf16[4,128,1280]{2,1,0:T(8,128)(2,1)S(1)} %get-tuple-element.48.hidden_ref, bf16[128,5120]{1,0:T(8,128)(2,1)S(1)} %copy-done.3, bf16[64,5120]{1,0:T(8,128)(2,1)S(1)} %copy-done.2, f32[64,128]{1,0:T(8,128)S(1)} %get-tuple-element.49.gap_ref), custom_call_target="tpu_custom_call" | custom-call | flops 167772160 | bytes 3358720 | tf_op jit(solution)/shard_map/pallas_call | solution.py:56
  34.6 0.2 collective-permute-done.6.lora_far_ref
  34.8 0.2 shard_map.151
  35.0 0.7 %shard_map.152 = (f32[128,128]{1,0:T(8,128)S(1)}, f32[128,128]{1,0:T(8,128)S(1)}) custom-call(f32[128,512]{1,0:T(8,128)S(1)} %get-tuple-element.34.own_kept_ref.kept_ref, bf16[128,512]{1,0:T(8,128)(2,1)S(1)} %collective-permute-done.3.got_ref, f32[128,128]{1,0:T(8,128)S(1)} %get-tuple-element.51.low_rank_ref, ...), custom_call_target="tpu_custom_call" | custom-call | bytes 819200 | tf_op jit(solution)/shard_map/pallas_call | solution.py:56
  35.7 0.4 collective-permute-start.7
  36.1 0.9 %collective-permute-done.7.got_ref = f32[128,128]{1,0:T(8,128)S(1)} collective-permute-done((f32[128,128]{1,0:T(8,128)S(1)}, f32[128,128]{1,0:T(8,128)S(1)}, u32[]{:S(2)}, u32[]{:S(2)}) %collective-permute-start.7) | collective-permute-done | bytes 65568 | tf_op jit(solution)/shard_map/ppermute | solution.py:534
  37.1 1.8 %collective-permute-start.8 = (bf16[96,128]{1,0:T(8,128)(2,1)S(1)}, bf16[96,128]{1,0:T(8,128)(2,1)S(1)}, u32[]{:S(2)}, u32[]{:S(2)}) collective-permute-start(bf16[96,128]{1,0:T(8,128)(2,1)S(1)} %get-tuple-element.57), channel_id=1, source_target_pairs={{0,2},{1,3},{2,0},{3,1},{4,6},{5,7},{6,4},{7,5},{8,10},{9,11},{10,... | collective-permute-start | bytes 73736 | tf_op jit(solution)/shard_map/ppermute | solution.py:538
  38.9 1.4 %collective-permute-start.10 = (bf16[96,128]{1,0:T(8,128)(2,1)S(1)}, bf16[96,128]{1,0:T(8,128)(2,1)S(1)}, u32[]{:S(2)}, u32[]{:S(2)}) collective-permute-start(bf16[96,128]{1,0:T(8,128)(2,1)S(1)} %get-tuple-element.58), channel_id=1, source_target_pairs={{0,6},{1,7},{2,4},{3,5},{4,2},{5,3},{6,0},{7,1},{8,14},{9,15},{10,... | collective-permute-start | bytes 73736 | tf_op jit(solution)/shard_map/ppermute | solution.py:539
  40.3 0.3 collective-permute-start.9
  40.6 0.3 collective-permute-done.8
  40.9 2.7 %collective-permute-done.10 = bf16[96,128]{1,0:T(8,128)(2,1)S(1)} collective-permute-done((bf16[96,128]{1,0:T(8,128)(2,1)S(1)}, bf16[96,128]{1,0:T(8,128)(2,1)S(1)}, u32[]{:S(2)}, u32[]{:S(2)}) %collective-permute-start.10) | collective-permute-done | bytes 24608 | tf_op jit(solution)/shard_map/ppermute | solution.py:539
  43.6 0.5 collective-permute-done.9
  44.2 3.6 %collective-permute-start.13 = (bf16[96,128]{1,0:T(8,128)(2,1)S(1)}, bf16[96,128]{1,0:T(8,128)(2,1)S(1)}, u32[]{:S(2)}, u32[]{:S(2)}) collective-permute-start(bf16[96,128]{1,0:T(8,128)(2,1)S(1)} %add_convert_fusion.refs_0_), channel_id=1, source_target_pairs={{0,24},{8,16},{16,8},{24,0},{1,25},{9,17},{17,9},{25,1},{2,26},{10... | collective-permute-start | bytes 73736 | tf_op jit(solution)/shard_map/ppermute | solution.py:547
  47.8 0.8 %collective-permute-start.11 = (bf16[96,128]{1,0:T(8,128)(2,1)S(1)}, bf16[96,128]{1,0:T(8,128)(2,1)S(1)}, u32[]{:S(2)}, u32[]{:S(2)}) collective-permute-start(bf16[96,128]{1,0:T(8,128)(2,1)S(1)} %add_convert_fusion.refs_0_), channel_id=1, source_target_pairs={{0,8},{8,0},{16,24},{24,16},{1,9},{9,1},{17,25},{25,17},{2,10},{10... | collective-permute-start | bytes 73736 | tf_op jit(solution)/shard_map/ppermute | solution.py:547
  48.6 1.3 %collective-permute-done.13.refs_3_ = bf16[96,128]{1,0:T(8,128)(2,1)S(1)} collective-permute-done((bf16[96,128]{1,0:T(8,128)(2,1)S(1)}, bf16[96,128]{1,0:T(8,128)(2,1)S(1)}, u32[]{:S(2)}, u32[]{:S(2)}) %collective-permute-start.13) | collective-permute-done | bytes 24608 | tf_op jit(solution)/shard_map/ppermute | solution.py:547
  49.9 2.7 %collective-permute-done.12.refs_2_ = bf16[96,128]{1,0:T(8,128)(2,1)S(1)} collective-permute-done((bf16[96,128]{1,0:T(8,128)(2,1)S(1)}, bf16[96,128]{1,0:T(8,128)(2,1)S(1)}, u32[]{:S(2)}, u32[]{:S(2)}) %collective-permute-start.12) | collective-permute-done | bytes 24608 | tf_op jit(solution)/shard_map/ppermute | solution.py:547
  52.5 0.1 shard_map.154.mine_ref
  52.8 1.2 %collective-permute-done.14.theirs_ref = f32[40,128]{1,0:T(8,128)S(1)} collective-permute-done((f32[40,128]{1,0:T(8,128)S(1)}, f32[40,128]{1,0:T(8,128)S(1)}, u32[]{:S(2)}, u32[]{:S(2)}) %collective-permute-start.14) | collective-permute-done | bytes 20512 | tf_op jit(solution)/shard_map/ppermute | solution.py:549
  53.9 0.8 %shard_map.155 = f32[64,128]{1,0:T(8,128)} custom-call(f32[40,128]{1,0:T(8,128)S(1)} %shard_map.154.mine_ref, f32[40,128]{1,0:T(8,128)S(1)} %collective-permute-done.14.theirs_ref), custom_call_target="tpu_custom_call" | custom-call | bytes 73728 | tf_op jit(solution)/shard_map/pallas_call | solution.py:56
  (23 shorter events, 0.4 us)
Async XLA Ops:
  1.0 10.7 %collective-permute-start = (bf16[128,1280]{1,0:T(8,128)(2,1)S(1)}, bf16[128,1280]{1,0:T(8,128)(2,1)S(1)}, u32[]{:S(2)}, u32[]{:S(2)}) collective-permute-start(bf16[128,1280]{1,0:T(8,128)(2,1)S(1)} %constant_dynamic-slice_fusion), channel_id=1, source_target_pairs={{0,4},{4,0},{1,5},{5,1},{2,6},{6,2},{3,7},{7,3},{8,12},{12,8},{9,1... | collective-permute-start | bytes 983048 | tf_op jit(solution)/shard_map/ppermute | solution.py:430
  11.7 15.1 %collective-permute-start.1 = (bf16[128,1280]{1,0:T(8,128)(2,1)S(1)}, bf16[128,1280]{1,0:T(8,128)(2,1)S(1)}, u32[]{:S(2)}, u32[]{:S(2)}) collective-permute-start(bf16[128,1280]{1,0:T(8,128)(2,1)S(1)} %collective-permute-done.raw_ref), channel_id=1, source_target_pairs={{0,1},{1,0},{2,3},{3,2},{4,5},{5,4},{6,7},{7,6},{8,9},{9,8},{10,11... | collective-permute-start | bytes 983048 | tf_op jit(solution)/shard_map/ppermute | solution.py:489
  12.4 2.7 %copy-start = (bf16[2560,256]{1,0:T(8,128)(2,1)S(1)}, bf16[2560,256]{1,0:T(8,128)(2,1)}, u32[]{:S(2)}) copy-start(bf16[2560,256]{1,0:T(8,128)(2,1)} %q_ref.5) | copy-start | bytes 3932164
  12.4 2.8 %copy-start.1 = (bf16[2560,256]{1,0:T(8,128)(2,1)S(1)}, bf16[2560,256]{1,0:T(8,128)(2,1)}, u32[]{:S(2)}) copy-start(bf16[2560,256]{1,0:T(8,128)(2,1)} %k_ref.5) | copy-start | bytes 3932164
  17.6 12.1 %collective-permute-start.4 = (bf16[128,896]{1,0:T(8,128)(2,1)S(1)}, bf16[128,896]{1,0:T(8,128)(2,1)S(1)}, u32[]{:S(2)}, u32[]{:S(2)}) collective-permute-start(bf16[128,896]{1,0:T(8,128)(2,1)S(1)} %get-tuple-element.45), channel_id=1, source_target_pairs={{0,4},{4,0},{1,5},{5,1},{2,6},{6,2},{3,7},{7,3},{8,12},{12,8},{9,1... | collective-permute-start | bytes 688136 | tf_op jit(solution)/shard_map/ppermute | solution.py:482
  19.4 6.7 %collective-permute-start.2 = (bf16[80,128]{1,0:T(8,128)(2,1)S(1)}, bf16[80,128]{1,0:T(8,128)(2,1)S(1)}, u32[]{:S(2)}, u32[]{:S(2)}) collective-permute-start(bf16[80,128]{1,0:T(8,128)(2,1)S(1)} %get-tuple-element.35), channel_id=1, source_target_pairs={{0,4},{4,0},{1,5},{5,1},{2,6},{6,2},{3,7},{7,3},{8,12},{12,8},{9,1... | collective-permute-start | bytes 61448 | tf_op jit(solution)/shard_map/ppermute | solution.py:457
  26.9 6.7 %copy-start.2 = (bf16[64,5120]{1,0:T(8,128)(2,1)S(1)}, bf16[64,5120]{1,0:T(8,128)(2,1)}, u32[]{:S(2)}) copy-start(bf16[64,5120]{1,0:T(8,128)(2,1)} %readout_ref.1) | copy-start | bytes 1966084
  26.9 6.7 %copy-start.3 = (bf16[128,5120]{1,0:T(8,128)(2,1)S(1)}, bf16[128,5120]{1,0:T(8,128)(2,1)}, u32[]{:S(2)}) copy-start(bf16[128,5120]{1,0:T(8,128)(2,1)} %up_ref.2) | copy-start | bytes 3932164
  27.6 7.4 %collective-permute-start.3 = (bf16[128,512]{1,0:T(8,128)(2,1)S(1)}, bf16[128,512]{1,0:T(8,128)(2,1)S(1)}, u32[]{:S(2)}, u32[]{:S(2)}) collective-permute-start(bf16[128,512]{1,0:T(8,128)(2,1)S(1)} %get-tuple-element.43), channel_id=1, source_target_pairs={{0,4},{4,0},{1,5},{5,1},{2,6},{6,2},{3,7},{7,3},{8,12},{12,8},{9,1... | collective-permute-start | bytes 393224 | tf_op jit(solution)/shard_map/ppermute | solution.py:509
  29.4 4.0 %collective-permute-start.5 = (bf16[128,128]{1,0:T(8,128)(2,1)S(1)}, bf16[128,128]{1,0:T(8,128)(2,1)S(1)}, u32[]{:S(2)}, u32[]{:S(2)}) collective-permute-start(bf16[128,128]{1,0:T(8,128)(2,1)S(1)} %get-tuple-element.46), channel_id=1, source_target_pairs={{0,4},{4,0},{1,5},{5,1},{2,6},{6,2},{3,7},{7,3},{8,12},{12,8},{9,1... | collective-permute-start | bytes 98312 | tf_op jit(solution)/shard_map/ppermute | solution.py:508
  33.5 1.3 %collective-permute-start.6 = (bf16[128,128]{1,0:T(8,128)(2,1)S(1)}, bf16[128,128]{1,0:T(8,128)(2,1)S(1)}, u32[]{:S(2)}, u32[]{:S(2)}) collective-permute-start(bf16[128,128]{1,0:T(8,128)(2,1)S(1)} %shard_map.149.lora_ref), channel_id=1, source_target_pairs={{0,1},{1,0},{2,3},{3,2},{4,5},{5,4},{6,7},{7,6},{8,9},{9,8},{10,11... | collective-permute-start | bytes 98312 | tf_op jit(solution)/shard_map/ppermute | solution.py:511
  33.6 1.2 %copy-start.4 = (bf16[128,256]{1,0:T(8,128)(2,1)S(1)}, bf16[128,256]{1,0:T(8,128)(2,1)}, u32[]{:S(2)}) copy-start(bf16[128,256]{1,0:T(8,128)(2,1)} %up_ref.3) | copy-start | bytes 196612
  33.6 1.2 %copy-start.5 = (bf16[256,128]{1,0:T(8,128)(2,1)S(1)}, bf16[256,128]{1,0:T(8,128)(2,1)}, u32[]{:S(2)}) copy-start(bf16[256,128]{1,0:T(8,128)(2,1)} %down_ref.1) | copy-start | bytes 196612
  35.7 1.3 %collective-permute-start.7 = (f32[128,128]{1,0:T(8,128)S(1)}, f32[128,128]{1,0:T(8,128)S(1)}, u32[]{:S(2)}, u32[]{:S(2)}) collective-permute-start(f32[128,128]{1,0:T(8,128)S(1)} %get-tuple-element.56), channel_id=1, source_target_pairs={{0,1},{1,0},{2,3},{3,2},{4,5},{5,4},{6,7},{7,6},{8,9},{9,8},{10,11... | collective-permute-start | bytes 196616 | tf_op jit(solution)/shard_map/ppermute | solution.py:534
  37.1 3.8 %collective-permute-start.8 = (bf16[96,128]{1,0:T(8,128)(2,1)S(1)}, bf16[96,128]{1,0:T(8,128)(2,1)S(1)}, u32[]{:S(2)}, u32[]{:S(2)}) collective-permute-start(bf16[96,128]{1,0:T(8,128)(2,1)S(1)} %get-tuple-element.57), channel_id=1, source_target_pairs={{0,2},{1,3},{2,0},{3,1},{4,6},{5,7},{6,4},{7,5},{8,10},{9,11},{10,... | collective-permute-start | bytes 73736 | tf_op jit(solution)/shard_map/ppermute | solution.py:538
  38.9 4.7 %collective-permute-start.10 = (bf16[96,128]{1,0:T(8,128)(2,1)S(1)}, bf16[96,128]{1,0:T(8,128)(2,1)S(1)}, u32[]{:S(2)}, u32[]{:S(2)}) collective-permute-start(bf16[96,128]{1,0:T(8,128)(2,1)S(1)} %get-tuple-element.58), channel_id=1, source_target_pairs={{0,6},{1,7},{2,4},{3,5},{4,2},{5,3},{6,0},{7,1},{8,14},{9,15},{10,... | collective-permute-start | bytes 73736 | tf_op jit(solution)/shard_map/ppermute | solution.py:539
  40.3 3.8 %collective-permute-start.9 = (bf16[96,128]{1,0:T(8,128)(2,1)S(1)}, bf16[96,128]{1,0:T(8,128)(2,1)S(1)}, u32[]{:S(2)}, u32[]{:S(2)}) collective-permute-start(bf16[96,128]{1,0:T(8,128)(2,1)S(1)} %get-tuple-element.58), channel_id=1, source_target_pairs={{0,4},{4,0},{1,5},{5,1},{2,6},{6,2},{3,7},{7,3},{8,12},{12,8},{9,1... | collective-permute-start | bytes 73736 | tf_op jit(solution)/shard_map/ppermute | solution.py:537
  44.2 5.7 %collective-permute-start.13 = (bf16[96,128]{1,0:T(8,128)(2,1)S(1)}, bf16[96,128]{1,0:T(8,128)(2,1)S(1)}, u32[]{:S(2)}, u32[]{:S(2)}) collective-permute-start(bf16[96,128]{1,0:T(8,128)(2,1)S(1)} %add_convert_fusion.refs_0_), channel_id=1, source_target_pairs={{0,24},{8,16},{16,8},{24,0},{1,25},{9,17},{17,9},{25,1},{2,26},{10... | collective-permute-start | bytes 73736 | tf_op jit(solution)/shard_map/ppermute | solution.py:547
  47.8 4.7 %collective-permute-start.12 = (bf16[96,128]{1,0:T(8,128)(2,1)S(1)}, bf16[96,128]{1,0:T(8,128)(2,1)S(1)}, u32[]{:S(2)}, u32[]{:S(2)}) collective-permute-start(bf16[96,128]{1,0:T(8,128)(2,1)S(1)} %add_convert_fusion.refs_0_), channel_id=1, source_target_pairs={{0,16},{8,24},{16,0},{24,8},{1,17},{9,25},{17,1},{25,9},{2,18},{10... | collective-permute-start | bytes 73736 | tf_op jit(solution)/shard_map/ppermute | solution.py:547
  47.8 4.7 %collective-permute-start.11 = (bf16[96,128]{1,0:T(8,128)(2,1)S(1)}, bf16[96,128]{1,0:T(8,128)(2,1)S(1)}, u32[]{:S(2)}, u32[]{:S(2)}) collective-permute-start(bf16[96,128]{1,0:T(8,128)(2,1)S(1)} %add_convert_fusion.refs_0_), channel_id=1, source_target_pairs={{0,8},{8,0},{16,24},{24,16},{1,9},{9,1},{17,25},{25,17},{2,10},{10... | collective-permute-start | bytes 73736 | tf_op jit(solution)/shard_map/ppermute | solution.py:547
  52.7 1.3 %collective-permute-start.14 = (f32[40,128]{1,0:T(8,128)S(1)}, f32[40,128]{1,0:T(8,128)S(1)}, u32[]{:S(2)}, u32[]{:S(2)}) collective-permute-start(f32[40,128]{1,0:T(8,128)S(1)} %shard_map.154.mine_ref), channel_id=1, source_target_pairs={{0,1},{1,0},{2,3},{3,2},{4,5},{5,4},{6,7},{7,6},{8,9},{9,8},{10,11... | collective-permute-start | bytes 61448 | tf_op jit(solution)/shard_map/ppermute | solution.py:549

commit v10 on v9

--- a/solution.py
+++ b/solution.py
@@ -164,10 +164,10 @@
     return jnp.where(index == 0, x[:, :half], x[:, half:])
 
 
-def partial_outputs(parts, seq, query_terms, lora_blocks, sent_ref, kept_ref):
+def partial_outputs(parts, seq, terms, lora_blocks, sent_ref, kept_ref):
     q, k, v, lora = parts
     columns = q.shape[1] // 2
-    blocks = [*high_low(pick(1 - seq, q))[:query_terms], *high_low(pick(1 - seq, k))]
+    blocks = [*high_low(pick(1 - seq, q))[:terms], *high_low(pick(1 - seq, k))[:terms]]
     blocks += [pick(1 - seq, v).astype(BF16), *lora_blocks]
     for i, block in enumerate(blocks):
         sent_ref[:, i * columns : (i + 1) * columns] = block
@@ -263,7 +263,7 @@
     partial_outputs(parts, lax.axis_index("seq"), 1, [], sent_ref, kept_ref)
 
 
-def finish(kept_ref, got_ref, query_terms, low_rank):
+def finish(kept_ref, got_ref, terms, low_rank):
     columns = low_rank.shape[1]
 
     def got(i):
@@ -273,13 +273,16 @@
         return kept_ref[:, i * columns : (i + 1) * columns]
 
     scale = HEAD_SIZE ** (-0.5)
-    n = query_terms
-    base = kept(0) + sum(got(i) for i in reversed(range(n)))
+
+    def got_sum(start):
+        return sum(got(start + i) for i in reversed(range(terms)))
+
+    base = kept(0) + got_sum(0)
     return (
         (base * scale).astype(BF16),
         ((base + low_rank) * scale).astype(BF16),
-        (kept(1) + (got(n) + got(n + 1))).astype(BF16),
-        (kept(2) + got(n + 2)).astype(BF16),
+        (kept(1) + got_sum(terms)).astype(BF16),
+        (kept(2) + got(2 * terms)).astype(BF16),
     )
 
 
@@ -499,7 +502,7 @@
         far_kernel,
         [
             ((tokens, rank), BF16),
-            ((tokens, 4 * columns), BF16),
+            ((tokens, 3 * columns), BF16),
             ((tokens, 4 * columns), F32),
         ],
         (far, *shared, *near_parts),

time: 54.9 us -> 54.3 us (0.989)
  waiting for transfers between devices: 27.7 us -> 27 us
    ppermute x1, starting transfers between devices: 0.28 us -> 0.88 us  [paired_local(): from_x = lax.ppermute(cross, 'seq', to_x)]
  transfers between devices with their start and end apart: 15 -> 15, of which waited for: 11 -> 10; matrix products, arithmetic and copies ran while one was open for 0% -> 0% of each run, Pallas kernels for 14% -> 14%
where the time goes in v10:
time: 54.3 us; the launch traced here: 54.1 us
  waiting for transfers between devices  27 us (50%)
  starting transfers between devices  15.7 us (29%)
  Pallas kernels  9.43 us (17%)
  local copies, waits for them, and re-layouts  1.12 us (2%)
  between operations  0.83 us (2%)
    pallas_call x11, Pallas kernels, run(): pl.pallas_call(kernel, out_shape=shapes, in_specs=specs or [VMEM] * len(a...  9.43 us
    ppermute x1, waiting for transfers between devices, paired_local(): near = lax.ppermute(message, 'seq', to_x)  7.71 us
    ppermute x1, waiting for transfers between devices, paired_local(): other_rows = lax.ppermute(rows, 'seq', to_x)  6.44 us
    ppermute x3, starting transfers between devices, paired_local(): totals.append(lax.ppermute(total, 'group', to_group))  4.45 us
    ppermute x3, waiting for transfers between devices, paired_local(): totals.append(lax.ppermute(total, 'group', to_group))  3.94 us
    ppermute x1, waiting for transfers between devices, paired_local(): small_got = lax.ppermute(small_sent, 'seq', to_x)  3.64 us
    ppermute x1, starting transfers between devices, paired_local(): near = lax.ppermute(message, 'seq', to_x)  3.03 us
    ppermute x1, waiting for transfers between devices, paired_local(): from_xy = lax.ppermute(cross, ('seq', 'head'), to_xy)  2.57 us
  transfers between devices with their start and end apart: 15, of which 10 were waited for; matrix products, arithmetic and copies ran while one was open for 0% of the time, Pallas kernels for 14%

profile of v10, /device:TPU:0, one launch (start us, length us, event | category | flops | bytes accessed | tf_op | source)
XLA Modules:
  0.0 54.1 jit_solution(12447415426163381231)
XLA Ops:
  0.0 1.0 %constant_dynamic-slice_fusion = bf16[128,1280]{1,0:T(8,128)(2,1)S(1)} fusion(bf16[128,5120]{1,0:T(8,128)(2,1)} %stream_hbm.1, s32[]{:T(128)S(6)} %select_n.11), kind=kLoop, calls=%fused_computation.1 | loop fusion | bytes 655364 | tf_op jit(solution)/shard_map/dynamic_slice | solution.py:45
  1.0 3.0 %collective-permute-start = (bf16[128,1280]{1,0:T(8,128)(2,1)S(1)}, bf16[128,1280]{1,0:T(8,128)(2,1)S(1)}, u32[]{:S(2)}, u32[]{:S(2)}) collective-permute-start(bf16[128,1280]{1,0:T(8,128)(2,1)S(1)} %constant_dynamic-slice_fusion), channel_id=1, source_target_pairs={{0,4},{4,0},{1,5},{5,1},{2,6},{6,2},{3,7},{7,3},{8,12},{12,8},{9,1... | collective-permute-start | bytes 983048 | tf_op jit(solution)/shard_map/ppermute | solution.py:433
  4.0 7.7 %collective-permute-done.raw_ref = bf16[128,1280]{1,0:T(8,128)(2,1)S(1)} collective-permute-done((bf16[128,1280]{1,0:T(8,128)(2,1)S(1)}, bf16[128,1280]{1,0:T(8,128)(2,1)S(1)}, u32[]{:S(2)}, u32[]{:S(2)}) %collective-permute-start) | collective-permute-done | bytes 327712 | tf_op jit(solution)/shard_map/ppermute | solution.py:433
  12.4 2.6 %shard_map.145 = (bf16[128,2560]{1,0:T(8,128)(2,1)S(1)}, bf16[80,128]{1,0:T(8,128)(2,1)S(1)}, f32[64,128]{1,0:T(8,128)S(1)}, bf16[4,128,1280]{2,1,0:T(8,128)(2,1...) custom-call(s32[1]{0:T(128)S(6)} %copy.16.step_any, ...), custom_call_target="tpu_custom_call" | custom-call | bytes 6998020 | tf_op jit(solution)/shard_map/pallas_call | solution.py:56
  15.1 0.1 copy-done.1
  15.2 2.5 %shard_map.146 = (bf16[128,896]{1,0:T(8,128)(2,1)S(1)}, f32[128,512]{1,0:T(8,128)S(1)}, f32[128,64]{1,0:T(8,128)S(1)}, bf16[2560,128]{1,0:T(8,128)(2,1)S(1)}) custom-call(bf16[128,2560]{1,0:T(8,128)(2,1)S(1)} %get-tuple-element.32.normed_ref, bf16[2560,256]{1,0:T(8,128)(2,1)S(1)} %copy-done, bf16[2560,256]{1,0:T(8,128)(2,1)S(1)} %copy-done.1, ...), custom_call_target="tpu_custom_call" | custom-call | flops 587202560 | bytes 8388608 | tf_op jit(solution)/shard_map/pallas_call | solution.py:56
  17.6 1.8 %collective-permute-start.4 = (bf16[128,896]{1,0:T(8,128)(2,1)S(1)}, bf16[128,896]{1,0:T(8,128)(2,1)S(1)}, u32[]{:S(2)}, u32[]{:S(2)}) collective-permute-start(bf16[128,896]{1,0:T(8,128)(2,1)S(1)} %get-tuple-element.45), channel_id=1, source_target_pairs={{0,4},{4,0},{1,5},{5,1},{2,6},{6,2},{3,7},{7,3},{8,12},{12,8},{9,1... | collective-permute-start | bytes 688136 | tf_op jit(solution)/shard_map/ppermute | solution.py:485
  19.4 0.3 collective-permute-start.2
  19.7 6.4 %collective-permute-done.2.rows_ref = bf16[80,128]{1,0:T(8,128)(2,1)S(1)} collective-permute-done((bf16[80,128]{1,0:T(8,128)(2,1)S(1)}, bf16[80,128]{1,0:T(8,128)(2,1)S(1)}, u32[]{:S(2)}, u32[]{:S(2)}) %collective-permute-start.2) | collective-permute-done | bytes 20512 | tf_op jit(solution)/shard_map/ppermute | solution.py:460
  26.2 0.7 %shard_map.147 = (f32[128,256]{1,0:T(8,128)S(1)}, f32[128,256]{1,0:T(8,128)S(1)}, f32[128,256]{1,0:T(8,128)S(1)}, f32[128,128]{1,0:T(8,128)S(1)}) custom-call(bf16[128,1280]{1,0:T(8,128)(2,1)S(1)} %collective-permute-done.raw_ref, bf16[80,128]{1,0:T(8,128)(2,1)S(1)} %collective-permute-done.2.rows_ref, bf16[2,64,1280]{2,1,0:T(8,128)(2,1)S(1)} %get-tuple-element.36.patch_ref, ...), custom_call_target="tpu_custom_call" | custom-call | flops 293601280 | bytes 5732352 | tf_op jit(solution)/shard_map/pallas_call | solution.py:56
  26.9 0.7 %shard_map.148 = (bf16[128,128]{1,0:T(8,128)(2,1)S(1)}, bf16[128,384]{1,0:T(8,128)(2,1)S(1)}, f32[128,512]{1,0:T(8,128)S(1)}) custom-call(bf16[128,1280]{1,0:T(8,128)(2,1)S(1)} %collective-permute-done.1.raw_ref, bf16[80,128]{1,0:T(8,128)(2,1)S(1)} %collective-permute-done.2.rows_ref, bf16[2,64,1280]{2,1,0:T(8,128)(2,1)S(1)} %get-tuple-element.36.patch_ref, ...), custom_call_target="tpu_custom_call" | custom-call | flops 293601280 | bytes 6125568 | tf_op jit(solution)/shard_map/pallas_call | solution.py:56
  27.6 1.8 %collective-permute-start.3 = (bf16[128,384]{1,0:T(8,128)(2,1)S(1)}, bf16[128,384]{1,0:T(8,128)(2,1)S(1)}, u32[]{:S(2)}, u32[]{:S(2)}) collective-permute-start(bf16[128,384]{1,0:T(8,128)(2,1)S(1)} %get-tuple-element.43), channel_id=1, source_target_pairs={{0,4},{4,0},{1,5},{5,1},{2,6},{6,2},{3,7},{7,3},{8,12},{12,8},{9,1... | collective-permute-start | bytes 294920 | tf_op jit(solution)/shard_map/ppermute | solution.py:512
  29.4 0.3 collective-permute-start.5
  29.7 3.6 %collective-permute-done.5.small_got_ref = bf16[128,128]{1,0:T(8,128)(2,1)S(1)} collective-permute-done((bf16[128,128]{1,0:T(8,128)(2,1)S(1)}, bf16[128,128]{1,0:T(8,128)(2,1)S(1)}, u32[]{:S(2)}, u32[]{:S(2)}) %collective-permute-start.5) | collective-permute-done | bytes 32800 | tf_op jit(solution)/shard_map/ppermute | solution.py:511
  33.5 1.0 %shard_map.150 = (bf16[128,64]{1,0:T(8,128)(2,1)S(1)}, f32[128,64]{1,0:T(8,128)S(1)}) custom-call(bf16[4,128,1280]{2,1,0:T(8,128)(2,1)S(1)} %get-tuple-element.48.hidden_ref, bf16[128,5120]{1,0:T(8,128)(2,1)S(1)} %copy-done.3, bf16[64,5120]{1,0:T(8,128)(2,1)S(1)} %copy-done.2, f32[64,128]{1,0:T(8,128)S(1)} %get-tuple-element.49.gap_ref), custom_call_target="tpu_custom_call" | custom-call | flops 167772160 | bytes 3358720 | tf_op jit(solution)/shard_map/pallas_call | solution.py:56
  34.5 0.2 collective-permute-done.6.lora_far_ref
  34.7 0.2 shard_map.151
  34.9 0.7 %shard_map.152 = (f32[128,128]{1,0:T(8,128)S(1)}, f32[128,128]{1,0:T(8,128)S(1)}) custom-call(f32[128,512]{1,0:T(8,128)S(1)} %get-tuple-element.34.own_kept_ref.kept_ref, bf16[128,384]{1,0:T(8,128)(2,1)S(1)} %collective-permute-done.3.got_ref, f32[128,128]{1,0:T(8,128)S(1)} %get-tuple-element.51.low_rank_ref, ...), custom_call_target="tpu_custom_call" | custom-call | bytes 786432 | tf_op jit(solution)/shard_map/pallas_call | solution.py:56
  35.6 0.4 collective-permute-start.7
  36.0 1.0 %collective-permute-done.7.got_ref = f32[128,128]{1,0:T(8,128)S(1)} collective-permute-done((f32[128,128]{1,0:T(8,128)S(1)}, f32[128,128]{1,0:T(8,128)S(1)}, u32[]{:S(2)}, u32[]{:S(2)}) %collective-permute-start.7) | collective-permute-done | bytes 65568 | tf_op jit(solution)/shard_map/ppermute | solution.py:537
  37.0 1.5 %collective-permute-start.8 = (bf16[96,128]{1,0:T(8,128)(2,1)S(1)}, bf16[96,128]{1,0:T(8,128)(2,1)S(1)}, u32[]{:S(2)}, u32[]{:S(2)}) collective-permute-start(bf16[96,128]{1,0:T(8,128)(2,1)S(1)} %get-tuple-element.57), channel_id=1, source_target_pairs={{0,2},{1,3},{2,0},{3,1},{4,6},{5,7},{6,4},{7,5},{8,10},{9,11},{10,... | collective-permute-start | bytes 73736 | tf_op jit(solution)/shard_map/ppermute | solution.py:541
  38.5 1.1 %collective-permute-start.10 = (bf16[96,128]{1,0:T(8,128)(2,1)S(1)}, bf16[96,128]{1,0:T(8,128)(2,1)S(1)}, u32[]{:S(2)}, u32[]{:S(2)}) collective-permute-start(bf16[96,128]{1,0:T(8,128)(2,1)S(1)} %get-tuple-element.58), channel_id=1, source_target_pairs={{0,6},{1,7},{2,4},{3,5},{4,2},{5,3},{6,0},{7,1},{8,14},{9,15},{10,... | collective-permute-start | bytes 73736 | tf_op jit(solution)/shard_map/ppermute | solution.py:542
  39.6 0.9 %collective-permute-start.9 = (bf16[96,128]{1,0:T(8,128)(2,1)S(1)}, bf16[96,128]{1,0:T(8,128)(2,1)S(1)}, u32[]{:S(2)}, u32[]{:S(2)}) collective-permute-start(bf16[96,128]{1,0:T(8,128)(2,1)S(1)} %get-tuple-element.58), channel_id=1, source_target_pairs={{0,4},{4,0},{1,5},{5,1},{2,6},{6,2},{3,7},{7,3},{8,12},{12,8},{9,1... | collective-permute-start | bytes 73736 | tf_op jit(solution)/shard_map/ppermute | solution.py:540
  40.5 0.3 collective-permute-done.8
  40.8 2.6 %collective-permute-done.10 = bf16[96,128]{1,0:T(8,128)(2,1)S(1)} collective-permute-done((bf16[96,128]{1,0:T(8,128)(2,1)S(1)}, bf16[96,128]{1,0:T(8,128)(2,1)S(1)}, u32[]{:S(2)}, u32[]{:S(2)}) %collective-permute-start.10) | collective-permute-done | bytes 24608 | tf_op jit(solution)/shard_map/ppermute | solution.py:542
  43.5 3.7 %collective-permute-start.13 = (bf16[96,128]{1,0:T(8,128)(2,1)S(1)}, bf16[96,128]{1,0:T(8,128)(2,1)S(1)}, u32[]{:S(2)}, u32[]{:S(2)}) collective-permute-start(bf16[96,128]{1,0:T(8,128)(2,1)S(1)} %add_convert_fusion.refs_0_), channel_id=1, source_target_pairs={{0,24},{8,16},{16,8},{24,0},{1,25},{9,17},{17,9},{25,1},{2,26},{10... | collective-permute-start | bytes 73736 | tf_op jit(solution)/shard_map/ppermute | solution.py:550
  47.1 0.8 %collective-permute-start.11 = (bf16[96,128]{1,0:T(8,128)(2,1)S(1)}, bf16[96,128]{1,0:T(8,128)(2,1)S(1)}, u32[]{:S(2)}, u32[]{:S(2)}) collective-permute-start(bf16[96,128]{1,0:T(8,128)(2,1)S(1)} %add_convert_fusion.refs_0_), channel_id=1, source_target_pairs={{0,8},{8,0},{16,24},{24,16},{1,9},{9,1},{17,25},{25,17},{2,10},{10... | collective-permute-start | bytes 73736 | tf_op jit(solution)/shard_map/ppermute | solution.py:550
  47.9 1.2 %collective-permute-done.13.refs_3_ = bf16[96,128]{1,0:T(8,128)(2,1)S(1)} collective-permute-done((bf16[96,128]{1,0:T(8,128)(2,1)S(1)}, bf16[96,128]{1,0:T(8,128)(2,1)S(1)}, u32[]{:S(2)}, u32[]{:S(2)}) %collective-permute-start.13) | collective-permute-done | bytes 24608 | tf_op jit(solution)/shard_map/ppermute | solution.py:550
  49.1 2.7 %collective-permute-done.12.refs_2_ = bf16[96,128]{1,0:T(8,128)(2,1)S(1)} collective-permute-done((bf16[96,128]{1,0:T(8,128)(2,1)S(1)}, bf16[96,128]{1,0:T(8,128)(2,1)S(1)}, u32[]{:S(2)}, u32[]{:S(2)}) %collective-permute-start.12) | collective-permute-done | bytes 24608 | tf_op jit(solution)/shard_map/ppermute | solution.py:550
  51.9 0.1 shard_map.154.mine_ref
  52.1 1.2 %collective-permute-done.14.theirs_ref = f32[40,128]{1,0:T(8,128)S(1)} collective-permute-done((f32[40,128]{1,0:T(8,128)S(1)}, f32[40,128]{1,0:T(8,128)S(1)}, u32[]{:S(2)}, u32[]{:S(2)}) %collective-permute-start.14) | collective-permute-done | bytes 20512 | tf_op jit(solution)/shard_map/ppermute | solution.py:552
  53.3 0.8 %shard_map.155 = f32[64,128]{1,0:T(8,128)} custom-call(f32[40,128]{1,0:T(8,128)S(1)} %shard_map.154.mine_ref, f32[40,128]{1,0:T(8,128)S(1)} %collective-permute-done.14.theirs_ref), custom_call_target="tpu_custom_call" | custom-call | bytes 73728 | tf_op jit(solution)/shard_map/pallas_call | solution.py:56
  (23 shorter events, 0.3 us)
Async XLA Ops:
  1.0 10.7 %collective-permute-start = (bf16[128,1280]{1,0:T(8,128)(2,1)S(1)}, bf16[128,1280]{1,0:T(8,128)(2,1)S(1)}, u32[]{:S(2)}, u32[]{:S(2)}) collective-permute-start(bf16[128,1280]{1,0:T(8,128)(2,1)S(1)} %constant_dynamic-slice_fusion), channel_id=1, source_target_pairs={{0,4},{4,0},{1,5},{5,1},{2,6},{6,2},{3,7},{7,3},{8,12},{12,8},{9,1... | collective-permute-start | bytes 983048 | tf_op jit(solution)/shard_map/ppermute | solution.py:433
  11.7 15.1 %collective-permute-start.1 = (bf16[128,1280]{1,0:T(8,128)(2,1)S(1)}, bf16[128,1280]{1,0:T(8,128)(2,1)S(1)}, u32[]{:S(2)}, u32[]{:S(2)}) collective-permute-start(bf16[128,1280]{1,0:T(8,128)(2,1)S(1)} %collective-permute-done.raw_ref), channel_id=1, source_target_pairs={{0,1},{1,0},{2,3},{3,2},{4,5},{5,4},{6,7},{7,6},{8,9},{9,8},{10,11... | collective-permute-start | bytes 983048 | tf_op jit(solution)/shard_map/ppermute | solution.py:492
  12.4 2.7 %copy-start = (bf16[2560,256]{1,0:T(8,128)(2,1)S(1)}, bf16[2560,256]{1,0:T(8,128)(2,1)}, u32[]{:S(2)}) copy-start(bf16[2560,256]{1,0:T(8,128)(2,1)} %q_ref.5) | copy-start | bytes 3932164
  12.4 2.8 %copy-start.1 = (bf16[2560,256]{1,0:T(8,128)(2,1)S(1)}, bf16[2560,256]{1,0:T(8,128)(2,1)}, u32[]{:S(2)}) copy-start(bf16[2560,256]{1,0:T(8,128)(2,1)} %k_ref.5) | copy-start | bytes 3932164
  17.6 12.1 %collective-permute-start.4 = (bf16[128,896]{1,0:T(8,128)(2,1)S(1)}, bf16[128,896]{1,0:T(8,128)(2,1)S(1)}, u32[]{:S(2)}, u32[]{:S(2)}) collective-permute-start(bf16[128,896]{1,0:T(8,128)(2,1)S(1)} %get-tuple-element.45), channel_id=1, source_target_pairs={{0,4},{4,0},{1,5},{5,1},{2,6},{6,2},{3,7},{7,3},{8,12},{12,8},{9,1... | collective-permute-start | bytes 688136 | tf_op jit(solution)/shard_map/ppermute | solution.py:485
  19.4 6.7 %collective-permute-start.2 = (bf16[80,128]{1,0:T(8,128)(2,1)S(1)}, bf16[80,128]{1,0:T(8,128)(2,1)S(1)}, u32[]{:S(2)}, u32[]{:S(2)}) collective-permute-start(bf16[80,128]{1,0:T(8,128)(2,1)S(1)} %get-tuple-element.35), channel_id=1, source_target_pairs={{0,4},{4,0},{1,5},{5,1},{2,6},{6,2},{3,7},{7,3},{8,12},{12,8},{9,1... | collective-permute-start | bytes 61448 | tf_op jit(solution)/shard_map/ppermute | solution.py:460
  26.9 6.6 %copy-start.2 = (bf16[64,5120]{1,0:T(8,128)(2,1)S(1)}, bf16[64,5120]{1,0:T(8,128)(2,1)}, u32[]{:S(2)}) copy-start(bf16[64,5120]{1,0:T(8,128)(2,1)} %readout_ref.1) | copy-start | bytes 1966084
  26.9 6.6 %copy-start.3 = (bf16[128,5120]{1,0:T(8,128)(2,1)S(1)}, bf16[128,5120]{1,0:T(8,128)(2,1)}, u32[]{:S(2)}) copy-start(bf16[128,5120]{1,0:T(8,128)(2,1)} %up_ref.2) | copy-start | bytes 3932164
  27.6 7.3 %collective-permute-start.3 = (bf16[128,384]{1,0:T(8,128)(2,1)S(1)}, bf16[128,384]{1,0:T(8,128)(2,1)S(1)}, u32[]{:S(2)}, u32[]{:S(2)}) collective-permute-start(bf16[128,384]{1,0:T(8,128)(2,1)S(1)} %get-tuple-element.43), channel_id=1, source_target_pairs={{0,4},{4,0},{1,5},{5,1},{2,6},{6,2},{3,7},{7,3},{8,12},{12,8},{9,1... | collective-permute-start | bytes 294920 | tf_op jit(solution)/shard_map/ppermute | solution.py:512
  29.4 3.9 %collective-permute-start.5 = (bf16[128,128]{1,0:T(8,128)(2,1)S(1)}, bf16[128,128]{1,0:T(8,128)(2,1)S(1)}, u32[]{:S(2)}, u32[]{:S(2)}) collective-permute-start(bf16[128,128]{1,0:T(8,128)(2,1)S(1)} %get-tuple-element.46), channel_id=1, source_target_pairs={{0,4},{4,0},{1,5},{5,1},{2,6},{6,2},{3,7},{7,3},{8,12},{12,8},{9,1... | collective-permute-start | bytes 98312 | tf_op jit(solution)/shard_map/ppermute | solution.py:511
  33.4 1.3 %collective-permute-start.6 = (bf16[128,128]{1,0:T(8,128)(2,1)S(1)}, bf16[128,128]{1,0:T(8,128)(2,1)S(1)}, u32[]{:S(2)}, u32[]{:S(2)}) collective-permute-start(bf16[128,128]{1,0:T(8,128)(2,1)S(1)} %shard_map.149.lora_ref), channel_id=1, source_target_pairs={{0,1},{1,0},{2,3},{3,2},{4,5},{5,4},{6,7},{7,6},{8,9},{9,8},{10,11... | collective-permute-start | bytes 98312 | tf_op jit(solution)/shard_map/ppermute | solution.py:514
  33.5 1.2 %copy-start.4 = (bf16[128,256]{1,0:T(8,128)(2,1)S(1)}, bf16[128,256]{1,0:T(8,128)(2,1)}, u32[]{:S(2)}) copy-start(bf16[128,256]{1,0:T(8,128)(2,1)} %up_ref.3) | copy-start | bytes 196612
  33.5 1.2 %copy-start.5 = (bf16[256,128]{1,0:T(8,128)(2,1)S(1)}, bf16[256,128]{1,0:T(8,128)(2,1)}, u32[]{:S(2)}) copy-start(bf16[256,128]{1,0:T(8,128)(2,1)} %down_ref.1) | copy-start | bytes 196612
  35.6 1.3 %collective-permute-start.7 = (f32[128,128]{1,0:T(8,128)S(1)}, f32[128,128]{1,0:T(8,128)S(1)}, u32[]{:S(2)}, u32[]{:S(2)}) collective-permute-start(f32[128,128]{1,0:T(8,128)S(1)} %get-tuple-element.56), channel_id=1, source_target_pairs={{0,1},{1,0},{2,3},{3,2},{4,5},{5,4},{6,7},{7,6},{8,9},{9,8},{10,11... | collective-permute-start | bytes 196616 | tf_op jit(solution)/shard_map/ppermute | solution.py:537
  37.0 3.8 %collective-permute-start.8 = (bf16[96,128]{1,0:T(8,128)(2,1)S(1)}, bf16[96,128]{1,0:T(8,128)(2,1)S(1)}, u32[]{:S(2)}, u32[]{:S(2)}) collective-permute-start(bf16[96,128]{1,0:T(8,128)(2,1)S(1)} %get-tuple-element.57), channel_id=1, source_target_pairs={{0,2},{1,3},{2,0},{3,1},{4,6},{5,7},{6,4},{7,5},{8,10},{9,11},{10,... | collective-permute-start | bytes 73736 | tf_op jit(solution)/shard_map/ppermute | solution.py:541
  38.5 4.9 %collective-permute-start.10 = (bf16[96,128]{1,0:T(8,128)(2,1)S(1)}, bf16[96,128]{1,0:T(8,128)(2,1)S(1)}, u32[]{:S(2)}, u32[]{:S(2)}) collective-permute-start(bf16[96,128]{1,0:T(8,128)(2,1)S(1)} %get-tuple-element.58), channel_id=1, source_target_pairs={{0,6},{1,7},{2,4},{3,5},{4,2},{5,3},{6,0},{7,1},{8,14},{9,15},{10,... | collective-permute-start | bytes 73736 | tf_op jit(solution)/shard_map/ppermute | solution.py:542
  39.6 3.8 %collective-permute-start.9 = (bf16[96,128]{1,0:T(8,128)(2,1)S(1)}, bf16[96,128]{1,0:T(8,128)(2,1)S(1)}, u32[]{:S(2)}, u32[]{:S(2)}) collective-permute-start(bf16[96,128]{1,0:T(8,128)(2,1)S(1)} %get-tuple-element.58), channel_id=1, source_target_pairs={{0,4},{4,0},{1,5},{5,1},{2,6},{6,2},{3,7},{7,3},{8,12},{12,8},{9,1... | collective-permute-start | bytes 73736 | tf_op jit(solution)/shard_map/ppermute | solution.py:540
  43.5 5.7 %collective-permute-start.13 = (bf16[96,128]{1,0:T(8,128)(2,1)S(1)}, bf16[96,128]{1,0:T(8,128)(2,1)S(1)}, u32[]{:S(2)}, u32[]{:S(2)}) collective-permute-start(bf16[96,128]{1,0:T(8,128)(2,1)S(1)} %add_convert_fusion.refs_0_), channel_id=1, source_target_pairs={{0,24},{8,16},{16,8},{24,0},{1,25},{9,17},{17,9},{25,1},{2,26},{10... | collective-permute-start | bytes 73736 | tf_op jit(solution)/shard_map/ppermute | solution.py:550
  47.1 4.7 %collective-permute-start.12 = (bf16[96,128]{1,0:T(8,128)(2,1)S(1)}, bf16[96,128]{1,0:T(8,128)(2,1)S(1)}, u32[]{:S(2)}, u32[]{:S(2)}) collective-permute-start(bf16[96,128]{1,0:T(8,128)(2,1)S(1)} %add_convert_fusion.refs_0_), channel_id=1, source_target_pairs={{0,16},{8,24},{16,0},{24,8},{1,17},{9,25},{17,1},{25,9},{2,18},{10... | collective-permute-start | bytes 73736 | tf_op jit(solution)/shard_map/ppermute | solution.py:550
  47.1 4.7 %collective-permute-start.11 = (bf16[96,128]{1,0:T(8,128)(2,1)S(1)}, bf16[96,128]{1,0:T(8,128)(2,1)S(1)}, u32[]{:S(2)}, u32[]{:S(2)}) collective-permute-start(bf16[96,128]{1,0:T(8,128)(2,1)S(1)} %add_convert_fusion.refs_0_), channel_id=1, source_target_pairs={{0,8},{8,0},{16,24},{24,16},{1,9},{9,1},{17,25},{25,17},{2,10},{10... | collective-permute-start | bytes 73736 | tf_op jit(solution)/shard_map/ppermute | solution.py:550
  52.0 1.3 %collective-permute-start.14 = (f32[40,128]{1,0:T(8,128)S(1)}, f32[40,128]{1,0:T(8,128)S(1)}, u32[]{:S(2)}, u32[]{:S(2)}) collective-permute-start(f32[40,128]{1,0:T(8,128)S(1)} %shard_map.154.mine_ref), channel_id=1, source_target_pairs={{0,1},{1,0},{2,3},{3,2},{4,5},{5,4},{6,7},{7,6},{8,9},{9,8},{10,11... | collective-permute-start | bytes 61448 | tf_op jit(solution)/shard_map/ppermute | solution.py:552

commit v11 on v10

--- a/solution.py
+++ b/solution.py
@@ -82,9 +82,13 @@
     return high, (x - high.astype(F32)).astype(BF16)
 
 
+def pass_kernel(message_ref, *refs):
+    pass
+
+
 def first_kernel(
-    step_any, latents_hbm, noise_hbm, stream_hbm, patch_hbm, gain_hbm, value_hbm,
-    normed_ref, rows_ref, gap_ref, hidden_ref, gain_ref, patch_ref, value_ref,
+    step_any, latents_hbm, noise_hbm, stream_hbm, patch_hbm, gain_hbm,
+    normed_ref, rows_ref, gap_ref, hidden_ref, gain_ref, patch_ref,
     step_s, latents_v, noise_v, stream_v, patch_v, gain_v, sems,
 ):
     parts, tokens, quarter = stream_v.shape
@@ -111,8 +115,6 @@
         for copy in large[j]:
             copy.start()
     gain_copy.start()
-    value_copy = pltpu.make_async_copy(value_hbm, value_ref, sems.at[sems.shape[0] - 1])
-    value_copy.start()
     for copy in small:
         copy.wait()
     level = (jnp.full((8, 128), step_s[0], jnp.int32).astype(F32) + 1.0) / 1000.0
@@ -156,8 +158,6 @@
                 hidden_ref[j].astype(F32) * inverse * gain
             ).astype(BF16)
 
-    value_copy.wait()
-
 
 def pick(index, x):
     half = x.shape[1] // 2
@@ -182,14 +182,13 @@
 
 
 def own_kernel(
-    normed_ref, q_ref, k_ref, v_ref, down_hbm, output_hbm, readout_hbm,
+    normed_ref, q_ref, k_ref, v_ref, down_hbm, output_v, readout_hbm,
     sent_ref, kept_ref, mix_ref, down_v,
-    output_v, readout_v, mix_v, sems,
+    readout_v, mix_v, sems,
 ):
     seq = lax.axis_index("seq")
     copies = [
         pltpu.make_async_copy(down_hbm, down_v, sems.at[0]),
-        pltpu.make_async_copy(output_hbm, output_v, sems.at[1]),
         pltpu.make_async_copy(
             readout_hbm.at[:, aligned(seq, readout_v.shape[1])], readout_v, sems.at[2]
         ),
@@ -430,11 +429,23 @@
 
     target = (1 - lax.axis_index("seq")) * 2 + lax.axis_index("head") % 2
     message = columns_of(stream, target, quarter)
+    for _ in range(2):
+        message = pl.pallas_call(
+            pass_kernel,
+            out_shape=jax.ShapeDtypeStruct(message.shape, BF16),
+            in_specs=[VMEM] + [HBM] * 4,
+            out_specs=VMEM,
+            input_output_aliases={0: 0},
+            compiler_params=pltpu.CompilerParams(vmem_limit_bytes=1 << 20),
+        )(message, *(
+            pltpu.with_memory_space_constraint(x, pltpu.HBM)
+            for x in (query_matrix, key_matrix, value_matrix, output_matrix)
+        ))
     near = lax.ppermute(message, "seq", to_x)
     inputs = (
-        latents.T, noise.T, stream, patch_embed_weight, prenorm_gain_vector, value_matrix,
-    )
-    normed, rows, gap, hidden, gain, patch, value = run(
+        latents.T, noise.T, stream, patch_embed_weight, prenorm_gain_vector,
+    )
+    normed, rows, gap, hidden, gain, patch = run(
         first_kernel,
         [
             ((tokens, half_width), BF16),
@@ -443,10 +454,9 @@
             ((4, tokens, quarter), BF16),
             ((2, quarter), F32),
             ((2, channels, quarter), BF16),
-            (value_matrix.shape, BF16),
         ],
         [step, *(pltpu.with_memory_space_constraint(x, pltpu.HBM) for x in inputs)],
-        [pl.BlockSpec(memory_space=pl.ANY)] + [HBM] * 6,
+        [pl.BlockSpec(memory_space=pl.ANY)] + [HBM] * 5,
         [
             pltpu.SMEM((1,), jnp.int32),
             pltpu.VMEM((channels, tokens), BF16),
@@ -467,15 +477,13 @@
             (adapter_query_down.shape, BF16),
         ],
         (
-            normed, query_matrix, key_matrix, value,
-            *(
-                pltpu.with_memory_space_constraint(x, pltpu.HBM)
-                for x in (adapter_query_down, output_matrix, velocity_readout_weight)
-            ),
+            normed, query_matrix, key_matrix, value_matrix,
+            pltpu.with_memory_space_constraint(adapter_query_down, pltpu.HBM),
+            output_matrix,
+            pltpu.with_memory_space_constraint(velocity_readout_weight, pltpu.HBM),
         ),
-        [VMEM] * 4 + [HBM] * 3,
+        [VMEM] * 4 + [HBM, VMEM, HBM],
         scratch=[
-            pltpu.VMEM(output_matrix.shape, BF16),
             pltpu.VMEM((channels, half_width), BF16),
             pltpu.VMEM((local_columns, channels), F32),
             pltpu.SemaphoreType.DMA((3,)),
@@ -490,7 +498,7 @@
         flops=8 * tokens * half_width * channels,
     )
     far = lax.ppermute(near, "head", to_core)
-    weights = (query_matrix, key_matrix, value, down)
+    weights = (query_matrix, key_matrix, value_matrix, down)
     shared = (other_rows, patch, gain, *weights)
     near_parts = run(
         near_kernel,
@@ -510,7 +518,11 @@
     )
     small_got = lax.ppermute(small_sent, "seq", to_x)
     other_got = lax.ppermute(other_sent, "seq", to_x)
-    (lora,) = run(lora_kernel, [((tokens, rank), BF16)], (own_kept, small_got, other_kept, own_got))
+    (lora,) = run(
+        lora_kernel,
+        [((tokens, rank), BF16)],
+        (own_kept, small_got, other_kept, own_got),
+    )
     lora_far = lax.ppermute(lora, "head", to_core)
     half_set, mixes, low_rank = run(
         half_kernel,

time: 54.3 us -> 54 us (level)
  no operation moved by 1% of the time
where the time goes in v11:
time: 54 us; the launch traced here: 53.8 us
  waiting for transfers between devices  27 us (50%)
  starting transfers between devices  15.7 us (29%)
  Pallas kernels  9.2 us (17%)
  local copies, waits for them, and re-layouts  1.04 us (2%)
  between operations  0.88 us (2%)
    pallas_call x11, Pallas kernels, run(): pl.pallas_call(kernel, out_shape=shapes, in_specs=specs or [VMEM] * len(a...  9.2 us
    ppermute x1, waiting for transfers between devices, paired_local(): near = lax.ppermute(message, 'seq', to_x)  7.71 us
    ppermute x1, waiting for transfers between devices, paired_local(): other_rows = lax.ppermute(rows, 'seq', to_x)  6.43 us
    ppermute x3, starting transfers between devices, paired_local(): totals.append(lax.ppermute(total, 'group', to_group))  4.45 us
    ppermute x3, waiting for transfers between devices, paired_local(): totals.append(lax.ppermute(total, 'group', to_group))  3.94 us
    ppermute x1, waiting for transfers between devices, paired_local(): small_got = lax.ppermute(small_sent, 'seq', to_x)  3.63 us
    ppermute x1, starting transfers between devices, paired_local(): near = lax.ppermute(message, 'seq', to_x)  3.03 us
    ppermute x1, waiting for transfers between devices, paired_local(): from_xy = lax.ppermute(cross, ('seq', 'head'), to_xy)  2.6 us
  transfers between devices with their start and end apart: 15, of which 10 were waited for; matrix products, arithmetic and copies ran while one was open for 0% of the time, Pallas kernels for 14%

profile of v11, /device:TPU:0, one launch (start us, length us, event | category | flops | bytes accessed | tf_op | source)
XLA Modules:
  0.0 53.8 jit_solution(14896252890684284355)
XLA Ops:
  0.0 1.0 %constant_dynamic-slice_fusion.message_ref = bf16[128,1280]{1,0:T(8,128)(2,1)S(1)} fusion(bf16[128,5120]{1,0:T(8,128)(2,1)} %stream_hbm.1, s32[]{:T(128)S(6)} %select_n.11), kind=kLoop, calls=%fused_computation.1 | loop fusion | bytes 655364 | tf_op jit(solution)/shard_map/dynamic_slice | solution.py:45
  1.1 3.0 %collective-permute-start = (bf16[128,1280]{1,0:T(8,128)(2,1)S(1)}, bf16[128,1280]{1,0:T(8,128)(2,1)S(1)}, u32[]{:S(2)}, u32[]{:S(2)}) collective-permute-start(bf16[128,1280]{1,0:T(8,128)(2,1)S(1)} %shard_map.148), channel_id=1, source_target_pairs={{0,4},{4,0},{1,5},{5,1},{2,6},{6,2},{3,7},{7,3},{8,12},{12,8},{9,1... | collective-permute-start | bytes 983048 | tf_op jit(solution)/shard_map/ppermute | solution.py:444
  4.1 7.7 %collective-permute-done.raw_ref = bf16[128,1280]{1,0:T(8,128)(2,1)S(1)} collective-permute-done((bf16[128,1280]{1,0:T(8,128)(2,1)S(1)}, bf16[128,1280]{1,0:T(8,128)(2,1)S(1)}, u32[]{:S(2)}, u32[]{:S(2)}) %collective-permute-start) | collective-permute-done | bytes 327712 | tf_op jit(solution)/shard_map/ppermute | solution.py:444
  12.5 2.5 %shard_map.145 = (bf16[128,2560]{1,0:T(8,128)(2,1)S(1)}, bf16[80,128]{1,0:T(8,128)(2,1)S(1)}, f32[64,128]{1,0:T(8,128)S(1)}, bf16[4,128,1280]{2,1,0:T(8,128)(2,1...) custom-call(s32[1]{0:T(128)S(6)} %copy.20.step_any, bf16[64,128]{1,0:T(8,128)(2,1)} %bitcast.3, ...), custom_call_target="tpu_custom_call" | custom-call | bytes 4376580 | tf_op jit(solution)/shard_map/pallas_call | solution.py:56
  15.0 2.4 %shard_map.146 = (bf16[128,896]{1,0:T(8,128)(2,1)S(1)}, f32[128,512]{1,0:T(8,128)S(1)}, f32[128,64]{1,0:T(8,128)S(1)}, bf16[2560,128]{1,0:T(8,128)(2,1)S(1)}) custom-call(bf16[128,2560]{1,0:T(8,128)(2,1)S(1)} %get-tuple-element.31.normed_ref, bf16[2560,256]{1,0:T(8,128)(2,1)S(1)} %copy-done, bf16[2560,256]{1,0:T(8,128)(2,1)S(1)} %copy-done.1, ...), custom_call_target="tpu_custom_call" | custom-call | flops 587202560 | bytes 8388608 | tf_op jit(solution)/shard_map/pallas_call | solution.py:56
  17.4 1.8 %collective-permute-start.4 = (bf16[128,896]{1,0:T(8,128)(2,1)S(1)}, bf16[128,896]{1,0:T(8,128)(2,1)S(1)}, u32[]{:S(2)}, u32[]{:S(2)}) collective-permute-start(bf16[128,896]{1,0:T(8,128)(2,1)S(1)} %get-tuple-element.43), channel_id=1, source_target_pairs={{0,4},{4,0},{1,5},{5,1},{2,6},{6,2},{3,7},{7,3},{8,12},{12,8},{9,1... | collective-permute-start | bytes 688136 | tf_op jit(solution)/shard_map/ppermute | solution.py:493
  19.2 0.3 collective-permute-start.2
  19.5 6.4 %collective-permute-done.2.rows_ref = bf16[80,128]{1,0:T(8,128)(2,1)S(1)} collective-permute-done((bf16[80,128]{1,0:T(8,128)(2,1)S(1)}, bf16[80,128]{1,0:T(8,128)(2,1)S(1)}, u32[]{:S(2)}, u32[]{:S(2)}) %collective-permute-start.2) | collective-permute-done | bytes 20512 | tf_op jit(solution)/shard_map/ppermute | solution.py:470
  25.9 0.7 %shard_map.149 = (f32[128,256]{1,0:T(8,128)S(1)}, f32[128,256]{1,0:T(8,128)S(1)}, f32[128,256]{1,0:T(8,128)S(1)}, f32[128,128]{1,0:T(8,128)S(1)}) custom-call(bf16[128,1280]{1,0:T(8,128)(2,1)S(1)} %collective-permute-done.raw_ref, bf16[80,128]{1,0:T(8,128)(2,1)S(1)} %collective-permute-done.2.rows_ref, bf16[2,64,1280]{2,1,0:T(8,128)(2,1)S(1)} %get-tuple-element.34.patch_ref, ...), custom_call_target="tpu_custom_call" | custom-call | flops 293601280 | bytes 5732352 | tf_op jit(solution)/shard_map/pallas_call | solution.py:56
  26.6 0.7 %shard_map.150 = (bf16[128,128]{1,0:T(8,128)(2,1)S(1)}, bf16[128,384]{1,0:T(8,128)(2,1)S(1)}, f32[128,512]{1,0:T(8,128)S(1)}) custom-call(bf16[128,1280]{1,0:T(8,128)(2,1)S(1)} %collective-permute-done.1.raw_ref, bf16[80,128]{1,0:T(8,128)(2,1)S(1)} %collective-permute-done.2.rows_ref, bf16[2,64,1280]{2,1,0:T(8,128)(2,1)S(1)} %get-tuple-element.34.patch_ref, ...), custom_call_target="tpu_custom_call" | custom-call | flops 293601280 | bytes 6125568 | tf_op jit(solution)/shard_map/pallas_call | solution.py:56
  27.4 1.8 %collective-permute-start.3 = (bf16[128,384]{1,0:T(8,128)(2,1)S(1)}, bf16[128,384]{1,0:T(8,128)(2,1)S(1)}, u32[]{:S(2)}, u32[]{:S(2)}) collective-permute-start(bf16[128,384]{1,0:T(8,128)(2,1)S(1)} %get-tuple-element.41), channel_id=1, source_target_pairs={{0,4},{4,0},{1,5},{5,1},{2,6},{6,2},{3,7},{7,3},{8,12},{12,8},{9,1... | collective-permute-start | bytes 294920 | tf_op jit(solution)/shard_map/ppermute | solution.py:520
  29.2 0.3 collective-permute-start.5
  29.5 3.6 %collective-permute-done.5.small_got_ref = bf16[128,128]{1,0:T(8,128)(2,1)S(1)} collective-permute-done((bf16[128,128]{1,0:T(8,128)(2,1)S(1)}, bf16[128,128]{1,0:T(8,128)(2,1)S(1)}, u32[]{:S(2)}, u32[]{:S(2)}) %collective-permute-start.5) | collective-permute-done | bytes 32800 | tf_op jit(solution)/shard_map/ppermute | solution.py:519
  33.2 1.0 %shard_map.152 = (bf16[128,64]{1,0:T(8,128)(2,1)S(1)}, f32[128,64]{1,0:T(8,128)S(1)}) custom-call(bf16[4,128,1280]{2,1,0:T(8,128)(2,1)S(1)} %get-tuple-element.46.hidden_ref, bf16[128,5120]{1,0:T(8,128)(2,1)S(1)} %copy-done.5, bf16[64,5120]{1,0:T(8,128)(2,1)S(1)} %copy-done.4, f32[64,128]{1,0:T(8,128)S(1)} %get-tuple-element.47.gap_ref), custom_call_target="tpu_custom_call" | custom-call | flops 167772160 | bytes 3358720 | tf_op jit(solution)/shard_map/pallas_call | solution.py:56
  34.2 0.2 collective-permute-done.6.lora_far_ref
  34.4 0.2 shard_map.153
  34.6 0.7 %shard_map.154 = (f32[128,128]{1,0:T(8,128)S(1)}, f32[128,128]{1,0:T(8,128)S(1)}) custom-call(f32[128,512]{1,0:T(8,128)S(1)} %get-tuple-element.32.own_kept_ref.kept_ref, bf16[128,384]{1,0:T(8,128)(2,1)S(1)} %collective-permute-done.3.got_ref, f32[128,128]{1,0:T(8,128)S(1)} %get-tuple-element.49.low_rank_ref, ...), custom_call_target="tpu_custom_call" | custom-call | bytes 786432 | tf_op jit(solution)/shard_map/pallas_call | solution.py:56
  35.3 0.4 collective-permute-start.7
  35.7 1.0 %collective-permute-done.7.got_ref = f32[128,128]{1,0:T(8,128)S(1)} collective-permute-done((f32[128,128]{1,0:T(8,128)S(1)}, f32[128,128]{1,0:T(8,128)S(1)}, u32[]{:S(2)}, u32[]{:S(2)}) %collective-permute-start.7) | collective-permute-done | bytes 65568 | tf_op jit(solution)/shard_map/ppermute | solution.py:549
  36.6 0.1 shard_map.155
  36.7 1.5 %collective-permute-start.8 = (bf16[96,128]{1,0:T(8,128)(2,1)S(1)}, bf16[96,128]{1,0:T(8,128)(2,1)S(1)}, u32[]{:S(2)}, u32[]{:S(2)}) collective-permute-start(bf16[96,128]{1,0:T(8,128)(2,1)S(1)} %get-tuple-element.55), channel_id=1, source_target_pairs={{0,2},{1,3},{2,0},{3,1},{4,6},{5,7},{6,4},{7,5},{8,10},{9,11},{10,... | collective-permute-start | bytes 73736 | tf_op jit(solution)/shard_map/ppermute | solution.py:553
  38.3 1.1 %collective-permute-start.10 = (bf16[96,128]{1,0:T(8,128)(2,1)S(1)}, bf16[96,128]{1,0:T(8,128)(2,1)S(1)}, u32[]{:S(2)}, u32[]{:S(2)}) collective-permute-start(bf16[96,128]{1,0:T(8,128)(2,1)S(1)} %get-tuple-element.56), channel_id=1, source_target_pairs={{0,6},{1,7},{2,4},{3,5},{4,2},{5,3},{6,0},{7,1},{8,14},{9,15},{10,... | collective-permute-start | bytes 73736 | tf_op jit(solution)/shard_map/ppermute | solution.py:554
  39.3 0.9 %collective-permute-start.9 = (bf16[96,128]{1,0:T(8,128)(2,1)S(1)}, bf16[96,128]{1,0:T(8,128)(2,1)S(1)}, u32[]{:S(2)}, u32[]{:S(2)}) collective-permute-start(bf16[96,128]{1,0:T(8,128)(2,1)S(1)} %get-tuple-element.56), channel_id=1, source_target_pairs={{0,4},{4,0},{1,5},{5,1},{2,6},{6,2},{3,7},{7,3},{8,12},{12,8},{9,1... | collective-permute-start | bytes 73736 | tf_op jit(solution)/shard_map/ppermute | solution.py:552
  40.2 0.3 collective-permute-done.8
  40.6 2.6 %collective-permute-done.10 = bf16[96,128]{1,0:T(8,128)(2,1)S(1)} collective-permute-done((bf16[96,128]{1,0:T(8,128)(2,1)S(1)}, bf16[96,128]{1,0:T(8,128)(2,1)S(1)}, u32[]{:S(2)}, u32[]{:S(2)}) %collective-permute-start.10) | collective-permute-done | bytes 24608 | tf_op jit(solution)/shard_map/ppermute | solution.py:554
  43.2 3.7 %collective-permute-start.13 = (bf16[96,128]{1,0:T(8,128)(2,1)S(1)}, bf16[96,128]{1,0:T(8,128)(2,1)S(1)}, u32[]{:S(2)}, u32[]{:S(2)}) collective-permute-start(bf16[96,128]{1,0:T(8,128)(2,1)S(1)} %add_convert_fusion.refs_0_), channel_id=1, source_target_pairs={{0,24},{8,16},{16,8},{24,0},{1,25},{9,17},{17,9},{25,1},{2,26},{10... | collective-permute-start | bytes 73736 | tf_op jit(solution)/shard_map/ppermute | solution.py:562
  46.9 0.8 %collective-permute-start.11 = (bf16[96,128]{1,0:T(8,128)(2,1)S(1)}, bf16[96,128]{1,0:T(8,128)(2,1)S(1)}, u32[]{:S(2)}, u32[]{:S(2)}) collective-permute-start(bf16[96,128]{1,0:T(8,128)(2,1)S(1)} %add_convert_fusion.refs_0_), channel_id=1, source_target_pairs={{0,8},{8,0},{16,24},{24,16},{1,9},{9,1},{17,25},{25,17},{2,10},{10... | collective-permute-start | bytes 73736 | tf_op jit(solution)/shard_map/ppermute | solution.py:562
  47.6 1.2 %collective-permute-done.13.refs_3_ = bf16[96,128]{1,0:T(8,128)(2,1)S(1)} collective-permute-done((bf16[96,128]{1,0:T(8,128)(2,1)S(1)}, bf16[96,128]{1,0:T(8,128)(2,1)S(1)}, u32[]{:S(2)}, u32[]{:S(2)}) %collective-permute-start.13) | collective-permute-done | bytes 24608 | tf_op jit(solution)/shard_map/ppermute | solution.py:562
  48.9 2.7 %collective-permute-done.12.refs_2_ = bf16[96,128]{1,0:T(8,128)(2,1)S(1)} collective-permute-done((bf16[96,128]{1,0:T(8,128)(2,1)S(1)}, bf16[96,128]{1,0:T(8,128)(2,1)S(1)}, u32[]{:S(2)}, u32[]{:S(2)}) %collective-permute-start.12) | collective-permute-done | bytes 24608 | tf_op jit(solution)/shard_map/ppermute | solution.py:562
  51.6 0.1 shard_map.156.mine_ref
  51.8 1.2 %collective-permute-done.14.theirs_ref = f32[40,128]{1,0:T(8,128)S(1)} collective-permute-done((f32[40,128]{1,0:T(8,128)S(1)}, f32[40,128]{1,0:T(8,128)S(1)}, u32[]{:S(2)}, u32[]{:S(2)}) %collective-permute-start.14) | collective-permute-done | bytes 20512 | tf_op jit(solution)/shard_map/ppermute | solution.py:564
  53.0 0.8 %shard_map.157 = f32[64,128]{1,0:T(8,128)} custom-call(f32[40,128]{1,0:T(8,128)S(1)} %shard_map.156.mine_ref, f32[40,128]{1,0:T(8,128)S(1)} %collective-permute-done.14.theirs_ref), custom_call_target="tpu_custom_call" | custom-call | bytes 73728 | tf_op jit(solution)/shard_map/pallas_call | solution.py:56
  (29 shorter events, 0.3 us)
Async XLA Ops:
  1.0 14.0 %copy-start.1 = (bf16[2560,256]{1,0:T(8,128)(2,1)S(1)}, bf16[2560,256]{1,0:T(8,128)(2,1)}, u32[]{:S(2)}) copy-start(bf16[2560,256]{1,0:T(8,128)(2,1)} %k_ref.5) | copy-start | bytes 3932164
  1.0 14.0 %copy-start.2 = (bf16[2560,256]{1,0:T(8,128)(2,1)S(1)}, bf16[2560,256]{1,0:T(8,128)(2,1)}, u32[]{:S(2)}) copy-start(bf16[2560,256]{1,0:T(8,128)(2,1)} %v_ref.5) | copy-start | bytes 3932164
  1.0 13.9 %copy-start.3 = (bf16[256,2560]{1,0:T(8,128)(2,1)S(1)}, bf16[256,2560]{1,0:T(8,128)(2,1)}, u32[]{:S(2)}) copy-start(bf16[256,2560]{1,0:T(8,128)(2,1)} %refs_3_.3) | copy-start | bytes 3932164
  1.1 13.9 %copy-start = (bf16[2560,256]{1,0:T(8,128)(2,1)S(1)}, bf16[2560,256]{1,0:T(8,128)(2,1)}, u32[]{:S(2)}) copy-start(bf16[2560,256]{1,0:T(8,128)(2,1)} %q_ref.5) | copy-start | bytes 3932164
  1.1 10.7 %collective-permute-start = (bf16[128,1280]{1,0:T(8,128)(2,1)S(1)}, bf16[128,1280]{1,0:T(8,128)(2,1)S(1)}, u32[]{:S(2)}, u32[]{:S(2)}) collective-permute-start(bf16[128,1280]{1,0:T(8,128)(2,1)S(1)} %shard_map.148), channel_id=1, source_target_pairs={{0,4},{4,0},{1,5},{5,1},{2,6},{6,2},{3,7},{7,3},{8,12},{12,8},{9,1... | collective-permute-start | bytes 983048 | tf_op jit(solution)/shard_map/ppermute | solution.py:444
  11.8 14.8 %collective-permute-start.1 = (bf16[128,1280]{1,0:T(8,128)(2,1)S(1)}, bf16[128,1280]{1,0:T(8,128)(2,1)S(1)}, u32[]{:S(2)}, u32[]{:S(2)}) collective-permute-start(bf16[128,1280]{1,0:T(8,128)(2,1)S(1)} %collective-permute-done.raw_ref), channel_id=1, source_target_pairs={{0,1},{1,0},{2,3},{3,2},{4,5},{5,4},{6,7},{7,6},{8,9},{9,8},{10,11... | collective-permute-start | bytes 983048 | tf_op jit(solution)/shard_map/ppermute | solution.py:500
  17.4 12.1 %collective-permute-start.4 = (bf16[128,896]{1,0:T(8,128)(2,1)S(1)}, bf16[128,896]{1,0:T(8,128)(2,1)S(1)}, u32[]{:S(2)}, u32[]{:S(2)}) collective-permute-start(bf16[128,896]{1,0:T(8,128)(2,1)S(1)} %get-tuple-element.43), channel_id=1, source_target_pairs={{0,4},{4,0},{1,5},{5,1},{2,6},{6,2},{3,7},{7,3},{8,12},{12,8},{9,1... | collective-permute-start | bytes 688136 | tf_op jit(solution)/shard_map/ppermute | solution.py:493
  19.2 6.7 %collective-permute-start.2 = (bf16[80,128]{1,0:T(8,128)(2,1)S(1)}, bf16[80,128]{1,0:T(8,128)(2,1)S(1)}, u32[]{:S(2)}, u32[]{:S(2)}) collective-permute-start(bf16[80,128]{1,0:T(8,128)(2,1)S(1)} %get-tuple-element.33), channel_id=1, source_target_pairs={{0,4},{4,0},{1,5},{5,1},{2,6},{6,2},{3,7},{7,3},{8,12},{12,8},{9,1... | collective-permute-start | bytes 61448 | tf_op jit(solution)/shard_map/ppermute | solution.py:470
  26.6 6.6 %copy-start.4 = (bf16[64,5120]{1,0:T(8,128)(2,1)S(1)}, bf16[64,5120]{1,0:T(8,128)(2,1)}, u32[]{:S(2)}) copy-start(bf16[64,5120]{1,0:T(8,128)(2,1)} %readout_ref.1) | copy-start | bytes 1966084
  26.6 6.6 %copy-start.5 = (bf16[128,5120]{1,0:T(8,128)(2,1)S(1)}, bf16[128,5120]{1,0:T(8,128)(2,1)}, u32[]{:S(2)}) copy-start(bf16[128,5120]{1,0:T(8,128)(2,1)} %up_ref.2) | copy-start | bytes 3932164
  27.4 7.3 %collective-permute-start.3 = (bf16[128,384]{1,0:T(8,128)(2,1)S(1)}, bf16[128,384]{1,0:T(8,128)(2,1)S(1)}, u32[]{:S(2)}, u32[]{:S(2)}) collective-permute-start(bf16[128,384]{1,0:T(8,128)(2,1)S(1)} %get-tuple-element.41), channel_id=1, source_target_pairs={{0,4},{4,0},{1,5},{5,1},{2,6},{6,2},{3,7},{7,3},{8,12},{12,8},{9,1... | collective-permute-start | bytes 294920 | tf_op jit(solution)/shard_map/ppermute | solution.py:520
  29.2 3.9 %collective-permute-start.5 = (bf16[128,128]{1,0:T(8,128)(2,1)S(1)}, bf16[128,128]{1,0:T(8,128)(2,1)S(1)}, u32[]{:S(2)}, u32[]{:S(2)}) collective-permute-start(bf16[128,128]{1,0:T(8,128)(2,1)S(1)} %get-tuple-element.44), channel_id=1, source_target_pairs={{0,4},{4,0},{1,5},{5,1},{2,6},{6,2},{3,7},{7,3},{8,12},{12,8},{9,1... | collective-permute-start | bytes 98312 | tf_op jit(solution)/shard_map/ppermute | solution.py:519
  33.1 1.3 %collective-permute-start.6 = (bf16[128,128]{1,0:T(8,128)(2,1)S(1)}, bf16[128,128]{1,0:T(8,128)(2,1)S(1)}, u32[]{:S(2)}, u32[]{:S(2)}) collective-permute-start(bf16[128,128]{1,0:T(8,128)(2,1)S(1)} %shard_map.151.lora_ref), channel_id=1, source_target_pairs={{0,1},{1,0},{2,3},{3,2},{4,5},{5,4},{6,7},{7,6},{8,9},{9,8},{10,11... | collective-permute-start | bytes 98312 | tf_op jit(solution)/shard_map/ppermute | solution.py:526
  33.2 1.2 %copy-start.6 = (bf16[128,256]{1,0:T(8,128)(2,1)S(1)}, bf16[128,256]{1,0:T(8,128)(2,1)}, u32[]{:S(2)}) copy-start(bf16[128,256]{1,0:T(8,128)(2,1)} %up_ref.3) | copy-start | bytes 196612
  33.2 1.2 %copy-start.7 = (bf16[256,128]{1,0:T(8,128)(2,1)S(1)}, bf16[256,128]{1,0:T(8,128)(2,1)}, u32[]{:S(2)}) copy-start(bf16[256,128]{1,0:T(8,128)(2,1)} %down_ref.1) | copy-start | bytes 196612
  35.3 1.3 %collective-permute-start.7 = (f32[128,128]{1,0:T(8,128)S(1)}, f32[128,128]{1,0:T(8,128)S(1)}, u32[]{:S(2)}, u32[]{:S(2)}) collective-permute-start(f32[128,128]{1,0:T(8,128)S(1)} %get-tuple-element.54), channel_id=1, source_target_pairs={{0,1},{1,0},{2,3},{3,2},{4,5},{5,4},{6,7},{7,6},{8,9},{9,8},{10,11... | collective-permute-start | bytes 196616 | tf_op jit(solution)/shard_map/ppermute | solution.py:549
  36.7 3.8 %collective-permute-start.8 = (bf16[96,128]{1,0:T(8,128)(2,1)S(1)}, bf16[96,128]{1,0:T(8,128)(2,1)S(1)}, u32[]{:S(2)}, u32[]{:S(2)}) collective-permute-start(bf16[96,128]{1,0:T(8,128)(2,1)S(1)} %get-tuple-element.55), channel_id=1, source_target_pairs={{0,2},{1,3},{2,0},{3,1},{4,6},{5,7},{6,4},{7,5},{8,10},{9,11},{10,... | collective-permute-start | bytes 73736 | tf_op jit(solution)/shard_map/ppermute | solution.py:553
  38.3 4.9 %collective-permute-start.10 = (bf16[96,128]{1,0:T(8,128)(2,1)S(1)}, bf16[96,128]{1,0:T(8,128)(2,1)S(1)}, u32[]{:S(2)}, u32[]{:S(2)}) collective-permute-start(bf16[96,128]{1,0:T(8,128)(2,1)S(1)} %get-tuple-element.56), channel_id=1, source_target_pairs={{0,6},{1,7},{2,4},{3,5},{4,2},{5,3},{6,0},{7,1},{8,14},{9,15},{10,... | collective-permute-start | bytes 73736 | tf_op jit(solution)/shard_map/ppermute | solution.py:554
  39.3 3.9 %collective-permute-start.9 = (bf16[96,128]{1,0:T(8,128)(2,1)S(1)}, bf16[96,128]{1,0:T(8,128)(2,1)S(1)}, u32[]{:S(2)}, u32[]{:S(2)}) collective-permute-start(bf16[96,128]{1,0:T(8,128)(2,1)S(1)} %get-tuple-element.56), channel_id=1, source_target_pairs={{0,4},{4,0},{1,5},{5,1},{2,6},{6,2},{3,7},{7,3},{8,12},{12,8},{9,1... | collective-permute-start | bytes 73736 | tf_op jit(solution)/shard_map/ppermute | solution.py:552
  43.2 5.7 %collective-permute-start.13 = (bf16[96,128]{1,0:T(8,128)(2,1)S(1)}, bf16[96,128]{1,0:T(8,128)(2,1)S(1)}, u32[]{:S(2)}, u32[]{:S(2)}) collective-permute-start(bf16[96,128]{1,0:T(8,128)(2,1)S(1)} %add_convert_fusion.refs_0_), channel_id=1, source_target_pairs={{0,24},{8,16},{16,8},{24,0},{1,25},{9,17},{17,9},{25,1},{2,26},{10... | collective-permute-start | bytes 73736 | tf_op jit(solution)/shard_map/ppermute | solution.py:562
  46.9 4.7 %collective-permute-start.12 = (bf16[96,128]{1,0:T(8,128)(2,1)S(1)}, bf16[96,128]{1,0:T(8,128)(2,1)S(1)}, u32[]{:S(2)}, u32[]{:S(2)}) collective-permute-start(bf16[96,128]{1,0:T(8,128)(2,1)S(1)} %add_convert_fusion.refs_0_), channel_id=1, source_target_pairs={{0,16},{8,24},{16,0},{24,8},{1,17},{9,25},{17,1},{25,9},{2,18},{10... | collective-permute-start | bytes 73736 | tf_op jit(solution)/shard_map/ppermute | solution.py:562
  46.9 4.7 %collective-permute-start.11 = (bf16[96,128]{1,0:T(8,128)(2,1)S(1)}, bf16[96,128]{1,0:T(8,128)(2,1)S(1)}, u32[]{:S(2)}, u32[]{:S(2)}) collective-permute-start(bf16[96,128]{1,0:T(8,128)(2,1)S(1)} %add_convert_fusion.refs_0_), channel_id=1, source_target_pairs={{0,8},{8,0},{16,24},{24,16},{1,9},{9,1},{17,25},{25,17},{2,10},{10... | collective-permute-start | bytes 73736 | tf_op jit(solution)/shard_map/ppermute | solution.py:562
  51.7 1.3 %collective-permute-start.14 = (f32[40,128]{1,0:T(8,128)S(1)}, f32[40,128]{1,0:T(8,128)S(1)}, u32[]{:S(2)}, u32[]{:S(2)}) collective-permute-start(f32[40,128]{1,0:T(8,128)S(1)} %shard_map.156.mine_ref), channel_id=1, source_target_pairs={{0,1},{1,0},{2,3},{3,2},{4,5},{5,4},{6,7},{7,6},{8,9},{9,8},{10,11... | collective-permute-start | bytes 61448 | tf_op jit(solution)/shard_map/ppermute | solution.py:564
